TPU v7x, 32 devices: a whole 2x2x4 slice. The times are simulated.
32 devices in a mesh: dp: 2 (over y), ctx: 4 (over x, core), tp: 4 (over z).
Axes of the slice: x: 2, y: 2, z: 4, core: 2. Of those that a mesh axis runs over, the one named last changes fastest.
Arguments:
- tokens: bfloat16 [2, 2048, 1024], P('dp', ('ctx', 'tp')), may hold values from -6 to 6
- attention_gain: float32 [1024], replicated, may hold values from 0.5 to 1.5
- query_weight: bfloat16 [1024, 1024], P(('dp', 'ctx'), 'tp'), may hold values from -0.1875 to 0.1875
- key_value_weight: bfloat16 [1024, 1024], P(('dp', 'ctx'), 'tp'), may hold values from -0.1875 to 0.1875
- query_gain: float32 [64], replicated, may hold values from 0.5 to 2.5, as said below
- key_gain: float32 [64], replicated, may hold values from 0.5 to 2.5, as said below
- output_weight: bfloat16 [1024, 1024], P('tp', ('dp', 'ctx')), may hold values from -3 to 3
- ffn_gain: float32 [1024], replicated, may hold values from 0.5 to 1.5
- gate_weight: bfloat16 [1024, 4608], P(('dp', 'ctx'), 'tp'), may hold values from -0.1875 to 0.1875
- up_weight: bfloat16 [1024, 4608], P(('dp', 'ctx'), 'tp'), may hold values from -0.1875 to 0.1875
- down_weight: bfloat16 [4608, 1024], P('tp', ('dp', 'ctx')), may hold values from -0.09375 to 0.09375
- cotangent: bfloat16 [2, 2048, 1024], P('dp', ('ctx', 'tp')), may hold values from -6 to 6
Outputs:
- block_out: bfloat16 [2, 2048, 1024], P('dp', ('ctx', 'tp'))
- grad_tokens: float32 [2, 2048, 1024], P('dp', ('ctx', 'tp'))
- softmax_logsumexp: float32 [2, 16, 2048], P('dp', 'tp', 'ctx')
- grad_attention_gain: float32 [1024], replicated
- grad_query_weight: float32 [1024, 1024], P(('dp', 'ctx'), 'tp')
- grad_keyval_weight: float32 [1024, 1024], P(('dp', 'ctx'), 'tp')
- grad_query_gain: float32 [64], replicated
- grad_key_gain: float32 [64], replicated
- grad_output_weight: float32 [1024, 1024], P('tp', ('dp', 'ctx'))
- grad_ffn_gain: float32 [1024], replicated
- grad_gate_weight: float32 [1024, 4608], P(('dp', 'ctx'), 'tp')
- grad_up_weight: float32 [1024, 4608], P(('dp', 'ctx'), 'tp')
- grad_down_weight: float32 [4608, 1024], P('tp', ('dp', 'ctx'))
Inputs may be any that keep to these rules, and one draw needn't show every extreme that they name: `query_gain`: positive scales of the 64 channels of a normalized query. `key_gain`: positive scales of the 64 channels of a normalized key.
All inputs are finite; a program needn't handle non-finite values.
Results may differ from a plain program's by a relative error of at most 0.015.
The roundings to bfloat16 on the way count: a program that leaves them out, or rounds other values in their place, can miss the bound.
Values may be sent and summed in bfloat16 or wider, within the bound.
No kernel may reach another device: no remote copies, remote signals or barrier semaphores. Data moves between devices by JAX's collectives and lax.ppermute only.
A program may use at most 128 MiB of HBM per device.

v0:
```python
import math

import jax
import jax.numpy as jnp
from jax import lax
from jax.sharding import PartitionSpec as P

epsilon = 1e-05
rope_base = 1000000.0
masked_score = -1e30


def norm_rows(values, gain):
    inverse = lax.rsqrt(jnp.mean(values * values, axis=-1, keepdims=True) + epsilon)
    normal = values * inverse
    return (normal * gain, normal, inverse)


def norm_back(grad_out, normal, inverse, gain):
    scaled = grad_out * gain
    grad_in = inverse * (scaled - normal * jnp.mean(scaled * normal, axis=-1, keepdims=True))
    return (grad_in, jnp.sum(grad_out * normal, axis=tuple(range(grad_out.ndim - 1))))


def rope_tables(positions, head_width):
    half_width = head_width // 2
    freq = jnp.exp(
        jnp.arange(half_width, dtype=jnp.float32) * (-2.0 * math.log(rope_base) / head_width)
    )
    angle = positions.astype(jnp.float32)[:, None] * freq[None, :]
    cosine = jnp.cos(angle)
    sine_vals = jnp.sin(angle)
    return (jnp.concatenate([cosine, cosine], -1), jnp.concatenate([sine_vals, sine_vals], -1))


def rotate(values, cosine, sine_vals):
    half_width = values.shape[-1] // 2
    turned = jnp.concatenate([-values[..., half_width:], values[..., :half_width]], -1)
    return values * cosine + turned * sine_vals


def unrotate(grads, cosine, sine_vals):
    half_width = grads.shape[-1] // 2
    scaled = grads * sine_vals
    return grads * cosine + jnp.concatenate(
        [scaled[..., half_width:], -scaled[..., :half_width]], -1
    )


def split_pairs(packed, pair_heads, head_width):
    row_count = packed.shape[0]
    shaped = packed.reshape(row_count, pair_heads, 2, head_width)
    return (shaped[:, :, 0].transpose(1, 0, 2), shaped[:, :, 1].transpose(1, 0, 2))


def join_pairs(key_part, value_part):
    pair_heads, row_count, head_width = key_part.shape
    return (
        jnp.stack([key_part, value_part], axis=1)
        .transpose(2, 0, 1, 3)
        .reshape(row_count, pair_heads * 2 * head_width)
    )


def on_device(
    tokens,
    attention_gain,
    query_weight,
    key_value_weight,
    query_gain,
    key_gain,
    output_weight,
    ffn_gain,
    gate_weight,
    up_weight,
    down_weight,
    cotangent,
):
    head_width = query_gain.shape[0]
    local_rows = tokens.shape[1]
    block_rows = local_rows * lax.axis_size("tp")
    ctx_count = lax.axis_size("ctx")
    query_heads = query_weight.shape[1] // head_width
    pair_heads = key_value_weight.shape[1] // (2 * head_width)
    pair_cols = key_value_weight.shape[1]
    query_group_count = query_heads // pair_heads
    score_scale = 1.0 / math.sqrt(head_width)

    def fetch_weights():
        return (
            lax.all_gather(query_weight, ("dp", "ctx"), axis=0, tiled=True),
            lax.all_gather(key_value_weight, ("dp", "ctx"), axis=0, tiled=True),
            lax.all_gather(output_weight, ("dp", "ctx"), axis=1, tiled=True),
            lax.all_gather(gate_weight, ("dp", "ctx"), axis=0, tiled=True),
            lax.all_gather(up_weight, ("dp", "ctx"), axis=0, tiled=True),
            lax.all_gather(down_weight, ("dp", "ctx"), axis=1, tiled=True),
        )

    full_query, full_pairs, full_output, full_gate, full_up, full_down = fetch_weights()
    resid_in = tokens[0].astype(jnp.float32)
    normed_wide, hat_first, inv_first = norm_rows(resid_in, attention_gain)
    rows_first = lax.all_gather(normed_wide.astype(jnp.bfloat16), "tp", axis=0, tiled=True)
    queries = (
        jnp.dot(rows_first, full_query, preferred_element_type=jnp.float32)
        .reshape(block_rows, query_heads, head_width)
        .transpose(1, 0, 2)
    )
    key_value_pairs = jnp.dot(rows_first, full_pairs, preferred_element_type=jnp.float32)
    key_raw, value_raw = split_pairs(key_value_pairs, pair_heads, head_width)
    qnorm, q_hat, q_inv = norm_rows(queries, query_gain)
    knorm, k_hat, k_inv = norm_rows(key_raw, key_gain)
    positions = lax.axis_index("ctx") * block_rows + jnp.arange(block_rows, dtype=jnp.int32)
    cosine, sine_vals = rope_tables(positions, head_width)
    rotary_query = rotate(qnorm, cosine, sine_vals).astype(jnp.bfloat16)
    rot_k = rotate(knorm, cosine, sine_vals).astype(jnp.bfloat16)
    pair_block = join_pairs(rot_k, value_raw.astype(jnp.bfloat16))
    query_group = rotary_query.reshape(pair_heads, query_group_count, block_rows, head_width)

    def attend(state, piece, start):
        run_max, run_total, run_acc = state
        keys_part, vals_part = split_pairs(piece, pair_heads, head_width)
        key_pos = start + jnp.arange(piece.shape[0], dtype=jnp.int32)
        valid = key_pos[None, :] <= positions[:, None]
        score = (
            jnp.einsum("hgqd,hkd->hgqk", query_group, keys_part, preferred_element_type=jnp.float32)
            * score_scale
        )
        score = jnp.where(valid, score, masked_score)
        new_max = jnp.maximum(run_max, jnp.max(score, axis=-1))
        weight = jnp.where(valid, jnp.exp(score - new_max[..., None]), 0.0)
        decay = jnp.exp(run_max - new_max)
        run_total = run_total * decay + jnp.sum(weight, axis=-1)
        run_acc = run_acc * decay[..., None] + jnp.einsum(
            "hgqk,hkd->hgqd",
            weight.astype(jnp.bfloat16),
            vals_part,
            preferred_element_type=jnp.float32,
        )
        return (new_max, run_total, run_acc)

    start_state = (
        jnp.full((pair_heads, query_group_count, block_rows), masked_score, jnp.float32),
        jnp.zeros((pair_heads, query_group_count, block_rows), jnp.float32),
        jnp.zeros((pair_heads, query_group_count, block_rows, head_width), jnp.float32),
    )
    piece = lax.all_gather(pair_block, "ctx", axis=0, tiled=True)
    row_count = piece.shape[0]

    def one_step(turn, state):
        part = lax.dynamic_slice_in_dim(piece, turn * block_rows, block_rows, 0)
        return attend(state, part, turn * block_rows)

    run_max, run_total, run_acc = lax.fori_loop(0, row_count // block_rows, one_step, start_state)
    softmax_logsumexp = run_max + jnp.log(run_total)
    attended_group = (run_acc / run_total[..., None]).astype(jnp.bfloat16)
    attended = (
        attended_group.reshape(query_heads, block_rows, head_width)
        .transpose(1, 0, 2)
        .reshape(block_rows, query_heads * head_width)
    )
    resid = resid_in + lax.psum_scatter(
        jnp.dot(attended, full_output, preferred_element_type=jnp.float32),
        "tp",
        scatter_dimension=0,
        tiled=True,
    )
    normed_fw, hat_second, inv_second = norm_rows(resid, ffn_gain)
    rows_second = lax.all_gather(normed_fw.astype(jnp.bfloat16), "tp", axis=0, tiled=True)
    gate = jnp.dot(rows_second, full_gate, preferred_element_type=jnp.float32)
    up_vals = jnp.dot(rows_second, full_up, preferred_element_type=jnp.float32)
    sigma = jax.nn.sigmoid(gate)
    mid = (gate * sigma * up_vals).astype(jnp.bfloat16)
    block_out = (
        resid
        + lax.psum_scatter(
            jnp.dot(mid, full_down, preferred_element_type=jnp.float32),
            "tp",
            scatter_dimension=0,
            tiled=True,
        )
    ).astype(jnp.bfloat16)[None]
    back_query, back_pairs, back_output, back_gate, back_up, back_down = fetch_weights()
    cot_rows = lax.all_gather(cotangent[0], "tp", axis=0, tiled=True)
    grad_down = jnp.dot(mid.T, cot_rows, preferred_element_type=jnp.float32)
    grad_mid = jnp.dot(cot_rows, back_down.T, preferred_element_type=jnp.float32)
    dgate = (grad_mid * up_vals * sigma * (1.0 + gate * (1.0 - sigma))).astype(jnp.bfloat16)
    dup_vals = (grad_mid * gate * sigma).astype(jnp.bfloat16)
    grad_gate = jnp.dot(rows_second.T, dgate, preferred_element_type=jnp.float32)
    grad_up = jnp.dot(rows_second.T, dup_vals, preferred_element_type=jnp.float32)
    grad_normed_f = lax.psum_scatter(
        jnp.dot(dgate, back_gate.T, preferred_element_type=jnp.float32)
        + jnp.dot(dup_vals, back_up.T, preferred_element_type=jnp.float32),
        "tp",
        scatter_dimension=0,
        tiled=True,
    )
    through_norm, grad_ffn_gain = norm_back(grad_normed_f, hat_second, inv_second, ffn_gain)
    grad_resid = cotangent[0].astype(jnp.float32) + through_norm
    resid_rows = lax.all_gather(grad_resid.astype(jnp.bfloat16), "tp", axis=0, tiled=True)
    grad_output = jnp.dot(attended.T, resid_rows, preferred_element_type=jnp.float32)
    grad_attended = jnp.dot(resid_rows, back_output.T, preferred_element_type=jnp.float32).astype(
        jnp.bfloat16
    )
    grad_group = (
        grad_attended.reshape(block_rows, query_heads, head_width)
        .transpose(1, 0, 2)
        .reshape(pair_heads, query_group_count, block_rows, head_width)
    )
    delta_rows = jnp.sum(
        grad_group.astype(jnp.float32) * attended_group.astype(jnp.float32), axis=-1
    )
    pairs_all = lax.all_gather(pair_block, "ctx", axis=0, tiled=True)

    def back_block(query_acc, index):
        piece = lax.dynamic_slice_in_dim(pairs_all, index * block_rows, block_rows, 0)
        keys_part, vals_part = split_pairs(piece, pair_heads, head_width)
        key_pos = index * block_rows + jnp.arange(block_rows, dtype=jnp.int32)
        valid = key_pos[None, :] <= positions[:, None]
        score = (
            jnp.einsum("hgqd,hkd->hgqk", query_group, keys_part, preferred_element_type=jnp.float32)
            * score_scale
        )
        prob = jnp.where(valid, jnp.exp(score - softmax_logsumexp[..., None]), 0.0)
        dprob = jnp.einsum(
            "hgqd,hkd->hgqk", grad_group, vals_part, preferred_element_type=jnp.float32
        )
        dscore = (prob * (dprob - delta_rows[..., None]) * score_scale).astype(jnp.bfloat16)
        query_acc = query_acc + jnp.einsum(
            "hgqk,hkd->hgqd", dscore, keys_part, preferred_element_type=jnp.float32
        )
        key_term = jnp.einsum(
            "hgqk,hgqd->hkd", dscore, query_group, preferred_element_type=jnp.float32
        )
        value_term = jnp.einsum(
            "hgqk,hgqd->hkd",
            prob.astype(jnp.bfloat16),
            grad_group,
            preferred_element_type=jnp.float32,
        )
        return (query_acc, join_pairs(key_term, value_term))

    grad_rot_group, pair_terms = lax.scan(
        back_block,
        jnp.zeros((pair_heads, query_group_count, block_rows, head_width), jnp.float32),
        jnp.arange(ctx_count, dtype=jnp.int32),
    )
    pair_terms = pair_terms.reshape(ctx_count * block_rows, pair_cols)
    pair_grads = lax.psum_scatter(pair_terms, "ctx", scatter_dimension=0, tiled=True)
    grad_rot_k, value_gradient = split_pairs(pair_grads, pair_heads, head_width)
    grad_rot_q = grad_rot_group.reshape(query_heads, block_rows, head_width)
    grad_query_raw, grad_query_gain = norm_back(
        unrotate(grad_rot_q, cosine, sine_vals), q_hat, q_inv, query_gain
    )
    raw_key_gradient, grad_key_gain = norm_back(
        unrotate(grad_rot_k, cosine, sine_vals), k_hat, k_inv, key_gain
    )
    grad_q16 = (
        grad_query_raw.transpose(1, 0, 2)
        .reshape(block_rows, query_heads * head_width)
        .astype(jnp.bfloat16)
    )
    pair_gradient16 = join_pairs(raw_key_gradient, value_gradient).astype(jnp.bfloat16)
    grad_query_w = jnp.dot(rows_first.T, grad_q16, preferred_element_type=jnp.float32)
    grad_keyval_w = jnp.dot(rows_first.T, pair_gradient16, preferred_element_type=jnp.float32)
    grad_normed_a = lax.psum_scatter(
        jnp.dot(grad_q16, back_query.T, preferred_element_type=jnp.float32)
        + jnp.dot(pair_gradient16, back_pairs.T, preferred_element_type=jnp.float32),
        "tp",
        scatter_dimension=0,
        tiled=True,
    )
    through_first, grad_attention_gain = norm_back(
        grad_normed_a, hat_first, inv_first, attention_gain
    )
    grad_tokens = (grad_resid + through_first)[None]
    shard_query, shard_pairs, shard_output, shard_gate, shard_up, shard_down = (
        lax.psum_scatter(grad_query_w, ("dp", "ctx"), scatter_dimension=0, tiled=True),
        lax.psum_scatter(grad_keyval_w, ("dp", "ctx"), scatter_dimension=0, tiled=True),
        lax.psum_scatter(grad_output, ("dp", "ctx"), scatter_dimension=1, tiled=True),
        lax.psum_scatter(grad_gate, ("dp", "ctx"), scatter_dimension=0, tiled=True),
        lax.psum_scatter(grad_up, ("dp", "ctx"), scatter_dimension=0, tiled=True),
        lax.psum_scatter(grad_down, ("dp", "ctx"), scatter_dimension=1, tiled=True),
    )
    total_attention_gain, total_query_gain, total_key_gain, total_ffn_gain = lax.psum(
        (grad_attention_gain, grad_query_gain, grad_key_gain, grad_ffn_gain), ("dp", "ctx", "tp")
    )
    stats_out = softmax_logsumexp.reshape(1, query_heads, block_rows)
    return (
        block_out,
        grad_tokens,
        stats_out,
        total_attention_gain,
        shard_query,
        shard_pairs,
        total_query_gain,
        total_key_gain,
        shard_output,
        total_ffn_gain,
        shard_gate,
        shard_up,
        shard_down,
    )


def solution(mesh):
    in_specs = (
        P("dp", ("ctx", "tp"), None),
        P(),
        P(("dp", "ctx"), "tp"),
        P(("dp", "ctx"), "tp"),
        P(),
        P(),
        P("tp", ("dp", "ctx")),
        P(),
        P(("dp", "ctx"), "tp"),
        P(("dp", "ctx"), "tp"),
        P("tp", ("dp", "ctx")),
        P("dp", ("ctx", "tp"), None),
    )
    out_specs = (
        P("dp", ("ctx", "tp"), None),
        P("dp", ("ctx", "tp"), None),
        P("dp", "tp", "ctx"),
        P(),
        P(("dp", "ctx"), "tp"),
        P(("dp", "ctx"), "tp"),
        P(),
        P(),
        P("tp", ("dp", "ctx")),
        P(),
        P(("dp", "ctx"), "tp"),
        P(("dp", "ctx"), "tp"),
        P("tp", ("dp", "ctx")),
    )
    return jax.shard_map(
        on_device, mesh=mesh, in_specs=in_specs, out_specs=out_specs, check_vma=False
    )
```

profile of v0, /device:TPU:0, one launch (start us, length us, event | category | flops | bytes accessed | tf_op | source)
XLA Modules:
  0.0 868.2 jit_solution(13250657018108856462)
XLA Ops:
  11.6 11.6 %all_gather.41 = bf16[1024,256]{1,0:T(8,128)(2,1)S(1)} all-gather(bf16[128,256]{1,0:T(8,128)(2,1)} %param.19), channel_id=1, replica_groups=mesh['dp'=2,'ctx'=4,'tp'=4] {'dp','ctx'}, dimensions={0}, use_global_device_ids=true | all-gather | bytes 589824 | tf_op jit(solution)/shard_map/all_gather | solution.py:92
  23.6 18.8 %all-gather.10.cloned.1.call-done = bf16[512,1024]{1,0:T(8,128)(2,1)} async-done(((bf16[128,1024]{1,0:T(8,128)(2,1)}), bf16[512,1024]{1,0:T(8,128)(2,1)}) %all-gather.10.cloned.1.call-update) | async-done | bytes 1048592 | tf_op jit(solution)/shard_map/all_gather | solution.py:102
  45.8 9.8 %all_gather.43 = bf16[1024,256]{1,0:T(8,128)(2,1)S(1)} all-gather(bf16[128,256]{1,0:T(8,128)(2,1)S(1)} %copy-done.35), channel_id=1, replica_groups=mesh['dp'=2,'ctx'=4,'tp'=4] {'dp','ctx'}, dimensions={0}, use_global_device_ids=true | all-gather | bytes 589824 | tf_op jit(solution)/shard_map/all_gather | solution.py:91
  55.6 11.1 %all_gather.44 = bf16[256,1024]{1,0:T(8,128)(2,1)S(1)} all-gather(bf16[256,128]{1,0:T(8,128)(2,1)S(1)} %copy-done.36), channel_id=1, replica_groups=mesh['dp'=2,'ctx'=4,'tp'=4] {'dp','ctx'}, dimensions={1}, use_global_device_ids=true | all-gather | bytes 589824 | tf_op jit(solution)/shard_map/all_gather | solution.py:93
  68.3 35.6 %while.31 = (s32[]{:T(128)}, f32[2,2,512]{2,1,0:T(2,128)S(1)}, f32[2,2,512]{2,1,0:T(2,128)S(1)}, f32[2,2,512,64]{2,3,1,0:T(8,128)S(1)}, bf16[2048,256]{0,1:T(8,1...) while((s32[]{:T(128)}, f32[2,2,512]{2,1,0:T(2,128)S(1)}, ...), condition=%wide.region_6.7_spmd.clone, body=%wide.region_3.6_spmd.clone.sunk | while | flops 282733568 | bytes 32645324 | solution.py:153
  108.3 41.3 %reduce-scatter.12.cloned.1.call-done = f32[128,1024]{1,0:T(8,128)} async-done(((f32[512,1024]{1,0:T(8,128)}), f32[128,1024]{1,0:T(8,128)}) %reduce-scatter.12.cloned.1.call-update) | async-done | bytes 524304 | tf_op jit(solution)/shard_map/reduce_scatter | solution.py:161
  154.0 24.9 %all-gather.14.cloned.1.call-done = bf16[512,1024]{1,0:T(8,128)(2,1)} async-done(((bf16[128,1024]{1,0:T(8,128)(2,1)}), bf16[512,1024]{1,0:T(8,128)(2,1)}) %all-gather.14.cloned.1.call-update) | async-done | bytes 1048592 | tf_op jit(solution)/shard_map/all_gather | solution.py:168
  178.9 5.1 fusion.63
  184.0 24.8 %all-gather.18.cloned.1.call-done = bf16[1024,1152]{1,0:T(8,128)(2,1)} async-done(((bf16[128,1152]{1,0:T(8,128)(2,1)}), bf16[1024,1152]{1,0:T(8,128)(2,1)}) %all-gather.18.cloned.1.call-update) | async-done | bytes 2359312 | tf_op jit(solution)/shard_map/all_gather | solution.py:95
  208.8 4.6 fusion.64
  213.4 24.9 %all-gather.24.cloned.1.call-done = bf16[1,512,1024]{2,1,0:T(8,128)(2,1)} async-done(((bf16[1,128,1024]{2,1,0:T(8,128)(2,1)}), bf16[1,512,1024]{2,1,0:T(8,128)(2,1)}) %all-gather.24.cloned.1.call-update) | async-done | bytes 1048592 | tf_op jit(solution)/shard_map/all_gather | solution.py:183
  238.3 30.4 %all-gather.20.cloned.1.call-done = bf16[1152,1024]{1,0:T(8,128)(2,1)} async-done(((bf16[1152,128]{1,0:T(8,128)(2,1)}), bf16[1152,1024]{1,0:T(8,128)(2,1)}) %all-gather.20.cloned.1.call-update) | async-done | bytes 2359312 | tf_op jit(solution)/shard_map/all_gather | solution.py:96
  268.7 6.9 multiply_convert_fusion
  281.1 43.7 %reduce-scatter.16.cloned.1.call-done = f32[128,1024]{1,0:T(8,128)} async-done(((f32[512,1024]{1,0:T(8,128)}), f32[128,1024]{1,0:T(8,128)}) %reduce-scatter.16.cloned.1.call-update) | async-done | bytes 524304 | tf_op jit(solution)/shard_map/reduce_scatter | solution.py:190
  329.0 27.0 %all-gather.22.cloned.1.call-done = bf16[512,1024]{1,0:T(8,128)(2,1)} async-done(((bf16[128,1024]{1,0:T(8,128)(2,1)}), bf16[512,1024]{1,0:T(8,128)(2,1)}) %all-gather.22.cloned.1.call-update) | async-done | bytes 1048592 | tf_op jit(solution)/shard_map/all_gather | solution.py:199
  357.8 82.0 %while.32 = (s32[]{:T(128)}, f32[2,2,512,64]{2,3,1,0:T(8,128)}, f32[4,512,256]{1,0,2:T(4,128)}, s32[4]{0:T(128)S(1)}, bf16[2048,256]{0,1:T(8,128)(2,1)}, /*index...) while((s32[]{:T(128)}, f32[2,2,512,64]{2,3,1,0:T(8,128)}, ...), condition=%wide.region_14.15_spmd.clone, body=%wide.region_13.14_spmd.clone.sunk | while | flops 683279360 | bytes 29655608 | solution.py:242
  365.1 11.0 %dynamic_update_slice.6 = f32[4,512,256]{1,0,2:T(4,128)} dynamic-update-slice(f32[4,512,256]{1,0,2:T(4,128)} %get-tuple-element.508, f32[1,512,256]{1,0,2:T(1,128)S(1)} %copy.112, s32[]{:T(128)} %get-tuple-element.506, s32[]{:T(128)} %constant.95.clone.1..sunk.1, s32[]{:T(128)} %constant.95.clone.1..sunk.1) | dynamic-update-slice | bytes 1048580 | tf_op jit(solution)/shard_map/while/body/jit(dynamic_update_index_in_dim)/dynamic_update_slice | solution.py:242
  384.8 11.0 %dynamic_update_slice.6 = f32[4,512,256]{1,0,2:T(4,128)} dynamic-update-slice(f32[4,512,256]{1,0,2:T(4,128)} %get-tuple-element.508, f32[1,512,256]{1,0,2:T(1,128)S(1)} %copy.112, s32[]{:T(128)} %get-tuple-element.506, s32[]{:T(128)} %constant.95.clone.1..sunk.1, s32[]{:T(128)} %constant.95.clone.1..sunk.1) | dynamic-update-slice | bytes 1048580 | tf_op jit(solution)/shard_map/while/body/jit(dynamic_update_index_in_dim)/dynamic_update_slice | solution.py:242
  405.6 11.0 %dynamic_update_slice.6 = f32[4,512,256]{1,0,2:T(4,128)} dynamic-update-slice(f32[4,512,256]{1,0,2:T(4,128)} %get-tuple-element.508, f32[1,512,256]{1,0,2:T(1,128)S(1)} %copy.112, s32[]{:T(128)} %get-tuple-element.506, s32[]{:T(128)} %constant.95.clone.1..sunk.1, s32[]{:T(128)} %constant.95.clone.1..sunk.1) | dynamic-update-slice | bytes 1048580 | tf_op jit(solution)/shard_map/while/body/jit(dynamic_update_index_in_dim)/dynamic_update_slice | solution.py:242
  426.4 11.0 %dynamic_update_slice.6 = f32[4,512,256]{1,0,2:T(4,128)} dynamic-update-slice(f32[4,512,256]{1,0,2:T(4,128)} %get-tuple-element.508, f32[1,512,256]{1,0,2:T(1,128)S(1)} %copy.112, s32[]{:T(128)} %get-tuple-element.506, s32[]{:T(128)} %constant.95.clone.1..sunk.1, s32[]{:T(128)} %constant.95.clone.1..sunk.1) | dynamic-update-slice | bytes 1048580 | tf_op jit(solution)/shard_map/while/body/jit(dynamic_update_index_in_dim)/dynamic_update_slice | solution.py:242
  440.4 3.9 copy.79
  447.6 27.4 %reduce-scatter.18.cloned.1.call-done = f32[512,256]{0,1:T(8,128)} async-done(((f32[2048,256]{0,1:T(8,128)}), f32[512,256]{0,1:T(8,128)}) %reduce-scatter.18.cloned.1.call-update) | async-done | bytes 524304 | tf_op jit(solution)/shard_map/reduce_scatter | solution.py:248
  480.3 5.0 fusion.65
  490.5 3.8 fusion.72
  506.1 17.9 %reduce-scatter.20.cloned.1.call-done = f32[128,1024]{1,0:T(8,128)} async-done(((f32[512,1024]{1,0:T(8,128)}), f32[128,1024]{1,0:T(8,128)}) %reduce-scatter.20.cloned.1.call-update) | async-done | bytes 524304 | tf_op jit(solution)/shard_map/reduce_scatter | solution.py:265
  525.3 42.3 %all-reduce = (f32[1024]{0:T(1024)}, f32[64]{0:T(128)}, f32[64]{0:T(128)}, f32[1024]{0:T(1024)}) all-reduce(f32[1024]{0:T(1024)S(1)} %get-tuple-element.262, f32[64]{0:T(128)S(1)} %copy-done.53, f32[64]{0:T(128)S(1)} %get-tuple-element.266, f32[1024]{0:T(1024)S(1)} %copy-done.42), channel_id=1, replica_groups=mesh['dp'=2,'ctx'=4,'tp'=4] {'dp','ctx','tp'}, use_global_device_ids=true, to_apply=%region_21.22 | all-reduce | flops 2176 | bytes 17408 | tf_op jit(solution)/shard_map/psum | solution.py:284
  572.3 54.3 %reduce-scatter.28.cloned.1.call-done = f32[128,1152]{1,0:T(8,128)} async-done(((f32[1024,1152]{1,0:T(8,128)}), f32[128,1152]{1,0:T(8,128)}) %reduce-scatter.28.cloned.1.call-update) | async-done | bytes 589840 | tf_op jit(solution)/shard_map/reduce_scatter | solution.py:280
  626.7 57.6 %reduce-scatter.30.cloned.1.call-done = f32[128,1152]{1,0:T(8,128)} async-done(((f32[1024,1152]{1,0:T(8,128)}), f32[128,1152]{1,0:T(8,128)}) %reduce-scatter.30.cloned.1.call-update) | async-done | bytes 589840 | tf_op jit(solution)/shard_map/reduce_scatter | solution.py:281
  684.2 57.6 %reduce-scatter.32.cloned.1.call-done = f32[1152,128]{1,0:T(8,128)} async-done(((f32[1152,1024]{1,0:T(8,128)}), f32[1152,128]{1,0:T(8,128)}) %reduce-scatter.32.cloned.1.call-update) | async-done | bytes 589840 | tf_op jit(solution)/shard_map/reduce_scatter | solution.py:282
  741.8 39.5 %reduce-scatter.26.cloned.1.call-done = f32[256,128]{1,0:T(8,128)} async-done(((f32[256,1024]{1,0:T(8,128)}), f32[256,128]{1,0:T(8,128)}) %reduce-scatter.26.cloned.1.call-update) | async-done | bytes 131088 | tf_op jit(solution)/shard_map/reduce_scatter | solution.py:279
  781.4 39.7 %reduce-scatter.22.cloned.1.call-done = f32[128,256]{1,0:T(8,128)} async-done(((f32[1024,256]{1,0:T(8,128)}), f32[128,256]{1,0:T(8,128)}) %reduce-scatter.22.cloned.1.call-update) | async-done | bytes 131088 | tf_op jit(solution)/shard_map/reduce_scatter | solution.py:277
  821.0 39.5 %reduce-scatter.24.cloned.1.call-done = f32[128,256]{1,0:T(8,128)} async-done(((f32[1024,256]{1,0:T(8,128)}), f32[128,256]{1,0:T(8,128)}) %reduce-scatter.24.cloned.1.call-update) | async-done | bytes 131088 | tf_op jit(solution)/shard_map/reduce_scatter | solution.py:278
  (365 shorter events, 130.5 us)
Async XLA Ops:
  8.0 34.3 %all-gather.10.cloned.1.call-start = ((), (), s32[]{:S(2)}) async-start(), calls=%async_computation.11 | async-start | bytes 1310720 | tf_op jit(solution)/shard_map/all_gather | solution.py:102
  8.1 36.1 %copy-start.47 = (f32[64]{0:T(128)S(1)}, f32[64]{0:T(128)}, u32[]{:S(2)}) copy-start(f32[64]{0:T(128)} %param.21) | copy-start | bytes 772
  11.5 56.8 %all-gather.12.cloned.1.call-start = ((), (), s32[]{:S(2)}) async-start(), calls=%async_computation.12 | async-start | bytes 1310720 | tf_op jit(solution)/shard_map/all_gather | solution.py:146
  23.5 43.9 %copy-start.18 = (f32[512,64]{0,1:T(8,128)}, f32[512,64]{0,1:T(8,128)S(1)}, u32[]{:S(2)}) copy-start(f32[512,64]{0,1:T(8,128)S(1)} %get-tuple-element.337) | copy-start | bytes 393220
  45.7 103.9 %reduce-scatter.12.cloned.1.call-start = ((), (), s32[]{:S(2)}) async-start(), calls=%async_computation.13 | async-start | bytes 2621440 | tf_op jit(solution)/shard_map/reduce_scatter | solution.py:161
  105.8 250.2 %copy-start.22 = (bf16[2,2,512,64]{2,3,1,0:T(8,128)(2,1)}, bf16[2,2,512,64]{2,3,1,0:T(8,128)(2,1)S(1)}, u32[]{:S(2)}) copy-start(bf16[2,2,512,64]{2,3,1,0:T(8,128)(2,1)S(1)} %divide_convert_fusion) | copy-start | bytes 786436
  105.8 43.8 %copy-start.10 = (bf16[1,128,1024]{2,1,0:T(8,128)(2,1)S(1)}, bf16[1,128,1024]{2,1,0:T(8,128)(2,1)}, u32[]{:S(2)}) copy-start(bf16[1,128,1024]{2,1,0:T(8,128)(2,1)} %param.16) | copy-start | bytes 786436
  107.6 43.2 %copy-start.34 = (f32[1024]{0:T(1024)S(1)}, f32[1024]{0:T(1024)}, u32[]{:S(2)}) copy-start(f32[1024]{0:T(1024)} %param.23) | copy-start | bytes 12292
  107.7 46.3 %all-gather.16.cloned.1.call-start = ((), (), s32[]{:S(2)}) async-start(), calls=%async_computation.15 | async-start | bytes 2654208 | tf_op jit(solution)/shard_map/all_gather | solution.py:94
  108.2 70.7 %all-gather.14.cloned.1.call-start = ((), (), s32[]{:S(2)}) async-start(), calls=%async_computation.14 | async-start | bytes 1310720 | tf_op jit(solution)/shard_map/all_gather | solution.py:168
  150.8 175.9 %copy-start.6 = (f32[128,1024]{1,0:T(8,128)}, f32[128,1024]{1,0:T(8,128)S(1)}, u32[]{:S(2)}) copy-start(f32[128,1024]{1,0:T(8,128)S(1)} %get-tuple-element.311) | copy-start | bytes 1572868
  150.8 175.9 %copy-start.45 = (f32[128]{0:T(128)}, f32[128]{0:T(128)S(1)}, u32[]{:S(2)}) copy-start(f32[128]{0:T(128)S(1)} %add_rsqrt_fusion.2) | copy-start | bytes 1540
  151.7 57.1 %all-gather.18.cloned.1.call-start = ((), (), s32[]{:S(2)}) async-start(), calls=%async_computation.16 | async-start | bytes 2654208 | tf_op jit(solution)/shard_map/all_gather | solution.py:95
  152.3 86.0 %all-gather.24.cloned.1.call-start = ((), (), s32[]{:S(2)}) async-start(), calls=%async_computation.29 | async-start | bytes 1310720 | tf_op jit(solution)/shard_map/all_gather | solution.py:183
  153.0 115.7 %all-gather.20.cloned.1.call-start = ((), (), s32[]{:S(2)}) async-start(), calls=%async_computation.17 | async-start | bytes 2654208 | tf_op jit(solution)/shard_map/all_gather | solution.py:96
  153.7 171.1 %reduce-scatter.16.cloned.1.call-start = ((), (), s32[]{:S(2)}) async-start(), calls=%async_computation.19 | async-start | bytes 2621440 | tf_op jit(solution)/shard_map/reduce_scatter | solution.py:190
  281.0 45.7 %copy-start.20 = (bf16[1,128,1024]{2,1,0:T(8,128)(2,1)S(1)}, bf16[1,128,1024]{2,1,0:T(8,128)(2,1)}, u32[]{:S(2)}) copy-start(bf16[1,128,1024]{2,1,0:T(8,128)(2,1)} %param.27) | copy-start | bytes 786436
  281.0 75.0 %all-gather.22.cloned.1.call-start = ((), (), s32[]{:S(2)}) async-start(), calls=%async_computation.20 | async-start | bytes 1310720 | tf_op jit(solution)/shard_map/all_gather | solution.py:199
  328.7 146.3 %reduce-scatter.18.cloned.1.call-start = ((), (), s32[]{:S(2)}) async-start(), calls=%async_computation.21 | async-start | bytes 2621440 | tf_op jit(solution)/shard_map/reduce_scatter | solution.py:248
  444.3 79.7 %reduce-scatter.20.cloned.1.call-start = ((), (), s32[]{:S(2)}) async-start(), calls=%async_computation.22 | async-start | bytes 2621440 | tf_op jit(solution)/shard_map/reduce_scatter | solution.py:265
  480.3 89.7 %reduce-scatter.14.cloned.1.call-start = ((), (), s32[]{:S(2)}) async-start(), calls=%async_computation.18 | async-start | bytes 2621440 | tf_op jit(solution)/shard_map/reduce_scatter | solution.py:175
  485.4 141.3 %reduce-scatter.28.cloned.1.call-start = ((), (), s32[]{:S(2)}) async-start(), calls=%async_computation.26 | async-start | bytes 5308416 | tf_op jit(solution)/shard_map/reduce_scatter | solution.py:280
  489.2 195.0 %reduce-scatter.30.cloned.1.call-start = ((), (), s32[]{:S(2)}) async-start(), calls=%async_computation.27 | async-start | bytes 5308416 | tf_op jit(solution)/shard_map/reduce_scatter | solution.py:281
  494.3 247.5 %reduce-scatter.32.cloned.1.call-start = ((), (), s32[]{:S(2)}) async-start(), calls=%async_computation.28 | async-start | bytes 5308416 | tf_op jit(solution)/shard_map/reduce_scatter | solution.py:282
  499.5 281.8 %reduce-scatter.26.cloned.1.call-start = ((), (), s32[]{:S(2)}) async-start(), calls=%async_computation.25 | async-start | bytes 1179648 | tf_op jit(solution)/shard_map/reduce_scatter | solution.py:279
  502.2 318.8 %reduce-scatter.22.cloned.1.call-start = ((), (), s32[]{:S(2)}) async-start(), calls=%async_computation.23 | async-start | bytes 1179648 | tf_op jit(solution)/shard_map/reduce_scatter | solution.py:277
  503.8 66.2 %copy-start.7 = (f32[128,1024]{1,0:T(8,128)S(1)}, f32[128,1024]{1,0:T(8,128)}, u32[]{:S(2)}) copy-start(f32[128,1024]{1,0:T(8,128)} %copy-done.6) | copy-start | bytes 1572868
  503.8 66.1 %copy-start.13 = (f32[128,1024]{1,0:T(8,128)S(1)}, f32[128,1024]{1,0:T(8,128)}, u32[]{:S(2)}) copy-start(f32[128,1024]{1,0:T(8,128)} %reduce-scatter.16.cloned.1.call-done) | copy-start | bytes 1572868
  503.9 66.1 %copy-start.21 = (bf16[1,128,1024]{2,1,0:T(8,128)(2,1)S(1)}, bf16[1,128,1024]{2,1,0:T(8,128)(2,1)}, u32[]{:S(2)}) copy-start(bf16[1,128,1024]{2,1,0:T(8,128)(2,1)} %param.27) | copy-start | bytes 786436
  503.9 66.1 %copy-start.46 = (f32[128]{0:T(128)S(1)}, f32[128]{0:T(128)}, u32[]{:S(2)}) copy-start(f32[128]{0:T(128)} %copy-done.45) | copy-start | bytes 1540
  503.9 66.1 %copy-start.52 = (f32[128]{0:T(128)S(1)}, f32[128]{0:T(128)}, u32[]{:S(2)}) copy-start(f32[128]{0:T(128)} %copy-done.51) | copy-start | bytes 1540
  503.9 356.7 %reduce-scatter.24.cloned.1.call-start = ((), (), s32[]{:S(2)}) async-start(), calls=%async_computation.24 | async-start | bytes 1179648 | tf_op jit(solution)/shard_map/reduce_scatter | solution.py:278
  (76 other events, 485.9 us)
Sparse Core Ops, SparseCore 0:
  11.6 30.6 all-gather.9
  45.8 16.0 all-gather.11
  107.8 41.7 reduce-scatter.11
  281.1 43.6 reduce-scatter.15
  328.8 27.1 all-gather.21
  444.4 30.5 reduce-scatter.17
Sparse Core Ops, SparseCore 1:
  110.0 26.8 all-gather.15
  151.8 27.1 all-gather.13
  180.7 28.0 all-gather.17
  210.4 27.9 all-gather.23
  240.2 28.4 all-gather.19
  480.3 43.6 reduce-scatter.19
  526.2 43.7 reduce-scatter.13
  573.9 52.7 reduce-scatter.27
  630.6 53.6 reduce-scatter.29
  688.3 53.5 reduce-scatter.31
  745.4 35.9 reduce-scatter.25
  785.1 35.9 reduce-scatter.21
  824.7 35.9 reduce-scatter.23
where the time goes:
time: 870 us; the launch traced here: 868 us
  waiting for transfers between devices  574 us (66%)
  matrix products  91.3 us (10%)
  blocking collectives  74.9 us (9%)
  local copies, waits for them, and re-layouts  71.7 us (8%)
  other arithmetic  34.3 us (4%)
  between operations  16.6 us (2%)
    reduce_scatter x1, waiting for transfers between devices, on_device(): lax.psum_scatter(grad_down, ('dp', 'ctx'), scatter_dimension=1, tiled=True)  57.6 us
    reduce_scatter x1, waiting for transfers between devices, on_device(): lax.psum_scatter(grad_up, ('dp', 'ctx'), scatter_dimension=0, tiled=True)  57.6 us
    reduce_scatter x1, waiting for transfers between devices, on_device(): lax.psum_scatter(grad_gate, ('dp', 'ctx'), scatter_dimension=0, tiled=True)  54.3 us
    dynamic_update_slice x8, local copies, waits for them, and re-layouts, on_device(): lax.scan(back_block, jnp.zeros((pair_heads, query_group_count, block_rows...  46.2 us
    reduce_scatter x1, waiting for transfers between devices, on_device(): lax.psum_scatter(jnp.dot(dgate, back_gate.T, preferred_element_type=jnp.f...  43.7 us
    psum x1, blocking collectives, on_device(): lax.psum((grad_attention_gain, grad_query_gain, grad_key_gain, grad_ffn_g...  42.3 us
    reduce_scatter x1, waiting for transfers between devices, on_device(): lax.psum_scatter(jnp.dot(attended, full_output, preferred_element_type=jn...  41.3 us
    reduce_scatter x1, waiting for transfers between devices, on_device(): lax.psum_scatter(grad_query_w, ('dp', 'ctx'), scatter_dimension=0, tiled=...  39.7 us
  transfers between devices with their start and end apart: 19, of which 17 were waited for; matrix products, arithmetic and copies ran while one was open for 5% of the time, Pallas kernels for 0%

commit v1 on v0

v1 whole, which is shorter than its diff:
```python
import math

import jax
import jax.numpy as jnp
from jax import lax
from jax.experimental import pallas as pl
from jax.experimental.pallas import tpu as pltpu
from jax.sharding import PartitionSpec as P

epsilon = 1e-05
rope_base = 1000000.0
f32 = jnp.float32
bf16 = jnp.bfloat16
exact = lax.Precision.HIGHEST
log2e = math.log2(math.e)


def mm(a, b):
    return lax.dot_general(a, b, (((1,), (0,)), ((), ())), preferred_element_type=f32)


def mm_nt(a, b):
    return lax.dot_general(a, b, (((1,), (1,)), ((), ())), preferred_element_type=f32)


def lanes(shape):
    return lax.broadcasted_iota(jnp.int32, shape, len(shape) - 1)


def rows_of(shape):
    return lax.broadcasted_iota(jnp.int32, shape, 0)


def sds(shape, dtype):
    return jax.ShapeDtypeStruct(shape, dtype)


VM = pl.BlockSpec(memory_space=pltpu.VMEM)
SM = pl.BlockSpec(memory_space=pltpu.SMEM)


def whole_call(body, outs, args, flops, name, scratch=(), scalars=True):
    moved = sum(math.prod(a.shape) * a.dtype.itemsize for a in list(args) + list(outs))
    specs = [VM] * len(args)
    if scalars:
        specs[0] = SM
    return pl.pallas_call(
        body,
        out_shape=list(outs),
        in_specs=specs,
        out_specs=[VM] * len(outs),
        scratch_shapes=list(scratch),
        cost_estimate=pl.CostEstimate(flops=int(flops), bytes_accessed=int(moved), transcendentals=0),
        name=name,
    )(*args)


def on_device(
    tokens,
    attention_gain,
    query_weight,
    key_value_weight,
    query_gain,
    key_gain,
    output_weight,
    ffn_gain,
    gate_weight,
    up_weight,
    down_weight,
    cotangent,
):
    hw = query_gain.shape[0]
    pw = 2 * hw
    R = tokens.shape[1]
    W = tokens.shape[2]
    NT = lax.axis_size("tp")
    NC = lax.axis_size("ctx")
    N = lax.axis_size("dp") * NC
    B = R * NT
    C = query_weight.shape[1]
    F = gate_weight.shape[1]
    QH = C // hw
    KH = key_value_weight.shape[1] // pw
    assert QH == 2 * KH
    H = W // 2
    blk = W // N
    scale = 1.0 / math.sqrt(hw)
    c2 = scale * log2e
    masks = list(range(0, N, 2)) + list(range(1, N, 2))
    me = lax.axis_index("dp") * NC + lax.axis_index("ctx")
    ctx = lax.axis_index("ctx")
    z = lax.axis_index("tp")
    where = jnp.stack([me, ctx, z]).astype(jnp.int32)
    aligned = blk % 128 == 0
    row_aligned = R % 128 == 0

    def plane(v, mask):
        return lax.ppermute(v, ("dp", "ctx"), [(i, i ^ mask) for i in range(N)])

    def column(v, mask):
        return lax.ppermute(v, "tp", [(i, i ^ mask) for i in range(NT)])

    def along(v, mask, keep):
        pairs = [(i, i ^ mask) for i in range(NC) if keep(i, i ^ mask)]
        return lax.ppermute(v, "ctx", pairs)

    def after(v, *deps):
        return lax.optimization_barrier((v,) + deps)[0]

    def gather_plane(own):
        if N == 8:
            half = own.shape[1] // 2
            fx, fy = plane(own, 2), plane(own, 4)
            top, low = plane(fx[:, :half], 4), plane(fy[:, half:], 2)
            mine = jnp.concatenate([own, fx, fy, top, low], axis=1)
        else:
            mine = jnp.concatenate([own] + [plane(own, r) for r in range(2, N, 2)], axis=1)
        return mine, plane(mine, 1)

    def scatter_plane(mine, other):
        got = plane(other, 1)
        m = mine.shape[1] * 2 // N
        parts = [
            mine[:, i * m : (i + 1) * m].astype(f32) + got[:, i * m : (i + 1) * m].astype(f32)
            for i in range(N // 2)
        ]
        if N == 8:
            half = m // 2
            far = parts[3].astype(bf16)
            tx, ty = plane(far[:, :half], 2), plane(far[:, half:], 4)
            ysend = jnp.concatenate(
                [parts[2][:, :half] + tx.astype(f32), parts[2][:, half:]], axis=1
            ).astype(bf16)
            xsend = jnp.concatenate(
                [parts[1][:, :half], parts[1][:, half:] + ty.astype(f32)], axis=1
            ).astype(bf16)
            return parts[0] + plane(xsend, 2).astype(f32) + plane(ysend, 4).astype(f32)
        total = parts[0]
        for i in range(1, N // 2):
            total = total + plane(parts[i].astype(bf16), 2 * i).astype(f32)
        return total

    def gather_column(own):
        return [own] + [column(own, k) for k in range(1, NT)]

    def spread_column(full):
        return [full[:R]] + [column(full[k * R : (k + 1) * R], k) for k in range(1, NT)]

    def slots(ref_rows, fallback):
        return fallback

    def take_cols(v, index, size, order):
        picks = index ^ jnp.array(order, jnp.int32)
        return jnp.take(v.reshape(v.shape[0], -1, size), picks, axis=1).reshape(v.shape)

    own_qkv = jnp.stack([query_weight, key_value_weight])
    own_out = output_weight.T

    def pre_body(s_ref, t_ref, c_ref, g_ref, n_ref, t_out, c_out, g_out):
        index = s_ref[0]
        for s, mask in enumerate(masks):
            if aligned:
                src = pl.ds(pl.multiple_of((index ^ mask) * blk, blk), blk)
            else:
                src = slice(s * blk, (s + 1) * blk)
            dst = slice(s * blk, (s + 1) * blk)
            t_out[:, dst] = t_ref[:, src]
            c_out[:, dst] = c_ref[:, src]
            g_out[:, dst] = g_ref[:, src]
        x = t_out[...].astype(f32)
        inv = lax.rsqrt(jnp.mean(x * x, axis=-1, keepdims=True) + epsilon)
        n_ref[...] = (x * inv * g_out[0:1, :]).astype(bf16)

    gains = jnp.stack([attention_gain, ffn_gain])
    t_in, c_in, g_in = tokens[0], cotangent[0], gains
    if not aligned:
        t_in, c_in, g_in = (take_cols(v, me, blk, masks) for v in (t_in, c_in, g_in))
    normed, tok, cot, gain2 = whole_call(
        pre_body,
        [sds((R, W), bf16), sds((R, W), bf16), sds((R, W), bf16), sds((2, W), f32)],
        (where, t_in, c_in, g_in),
        R * W * 8,
        "pre",
    )
    first_pieces = gather_column(normed)
    qkv_m, qkv_o = gather_plane(own_qkv)
    rows_first = jnp.concatenate(first_pieces, axis=0)

    out_cols = jnp.concatenate(gather_column(own_out), axis=1)
    out_m, out_o = gather_plane(after(out_cols, qkv_o)[None])
    own_ffn = jnp.stack([gate_weight, up_weight, down_weight.T])
    ffn_m, ffn_o = gather_plane(after(own_ffn, qkv_o))

    cot_rows = jnp.concatenate(gather_column(after(cot, rows_first)), axis=0)

    half_width = hw // 2
    freq = jnp.exp(jnp.arange(half_width, dtype=f32) * (-2.0 * math.log(rope_base) / hw))
    positions = ctx * B + (jnp.arange(B, dtype=jnp.int32) ^ (z * R))
    angle = positions.astype(f32)[:, None] * freq[None, :]
    cos_h, sin_h = jnp.cos(angle), jnp.sin(angle)
    cosine = jnp.tile(cos_h, (1, 2 * QH))
    sine = jnp.tile(jnp.concatenate([-sin_h, sin_h], -1), (1, QH))
    qg = jnp.tile(query_gain, QH)[None]
    kg = jnp.tile(jnp.concatenate([key_gain, jnp.ones_like(key_gain)]), KH)[None]

    def head_mean(x):
        n = x.shape[1]
        same = rows_of((n, n)) // hw == lanes((n, n)) // hw
        ones = jnp.where(same, 1.0 / hw, 0.0).astype(f32)
        return jnp.dot(x, ones, precision=exact, preferred_element_type=f32)

    def swap_halves(x):
        first = lanes(x.shape) % hw < half_width
        return jnp.where(
            first, pltpu.roll(x, x.shape[1] - half_width, 1), pltpu.roll(x, half_width, 1)
        )

    def qkv_body(r_ref, wm, wo, cs, sn, qg_ref, kg_ref, rq, pr, q_raw, p_raw):
        left, right = r_ref[:, :H], r_ref[:, H:]
        q = mm(left, wm[0]) + mm(right, wo[0])
        p = mm(left, wm[1]) + mm(right, wo[1])
        q_raw[...] = q
        p_raw[...] = p
        qn = q * lax.rsqrt(head_mean(q * q) + epsilon) * qg_ref[...]
        rq[...] = (qn * cs[...] + swap_halves(qn) * sn[...]).astype(bf16)
        kn = p * lax.rsqrt(head_mean(p * p) + epsilon) * kg_ref[...]
        kr = kn * cs[...] + swap_halves(kn) * sn[...]
        pr[...] = jnp.where(lanes(p.shape) % pw < hw, kr, p).astype(bf16)

    rot_q, pair, q_raw, p_raw = whole_call(
        qkv_body,
        [sds((B, C), bf16), sds((B, C), bf16), sds((B, C), f32), sds((B, C), f32)],
        (rows_first, qkv_m, qkv_o, cosine, sine, qg, kg),
        4 * B * W * C,
        "qkv",
        scalars=False,
    )

    earlier = lambda i, j: i < j
    kv_even = [pair] + [along(pair, r, earlier) for r in range(2, NC, 2)]
    kv_odd = [along(pair, 1, earlier)]
    for r in range(2, NC, 2):
        kv_odd.append(along(kv_even[r // 2], 1, lambda i, j: (i ^ 1 ^ j) == 0 and (i ^ r) < i))
    kv_all = jnp.stack([v for pq in zip(kv_even, kv_odd) for v in pq])

    def widen(x, part):
        moved = x if part == 0 else pltpu.roll(x, hw, 1)
        return jnp.where(lanes(x.shape) < hw, moved, 0.0)

    def widen_high(x, part):
        moved = x if part == 1 else pltpu.roll(x, hw, 1)
        return jnp.where(lanes(x.shape) >= hw, moved, 0.0)

    def causal(zz):
        key = rows_of((B, B)) ^ zz
        qry = lanes((B, B)) ^ zz
        return key <= qry

    def fwd_body(s_ref, q_ref, kv_ref, att_ref, lse_ref, qz, acc, tot):
        r, h = pl.program_id(0), pl.program_id(1)
        here = s_ref[1]

        @pl.when((r == 0) & (h == 0))
        def _():
            for hd in range(QH):
                x = q_ref[:, (hd // 2) * pw : (hd // 2 + 1) * pw].astype(f32)
                qz[hd] = widen(x, hd % 2).astype(bf16)

        def step(masked):
            kv = kv_ref[0]
            kvt = kv.astype(f32).T.astype(bf16)
            for g in range(2):
                hd = 2 * h + g
                e = jnp.exp2(mm_nt(kv, qz[hd]) * c2)
                if masked:
                    e = jnp.where(causal(s_ref[2] * R), e, 0.0)
                part = jnp.sum(e, axis=0, keepdims=True)
                o = mm(kvt, e.astype(bf16))
                if masked:
                    tot[hd] = jnp.broadcast_to(part, (8, B))
                    acc[hd] = o
                else:
                    tot[hd] += jnp.broadcast_to(part, (8, B))
                    acc[hd] += o

        @pl.when(r == 0)
        def _():
            step(True)

        @pl.when((here ^ r) < here)
        def _():
            step(False)

        @pl.when((r == NC - 1) & (h == KH - 1))
        def _():
            outs = [acc[hd][hw:] / tot[hd][0:1] for hd in range(QH)]
            att_ref[...] = jnp.concatenate(outs, axis=0).T.astype(bf16)
            for hd in range(QH):
                lse_ref[hd : hd + 1] = jnp.log(tot[hd][0:1])

    fixed = lambda shape: pl.BlockSpec(shape, lambda r, h: (0,) * len(shape))
    kv_spec = pl.BlockSpec((1, B, pw), lambda r, h: (r, 0, h))
    attended, lse = pl.pallas_call(
        fwd_body,
        grid=(NC, KH),
        out_shape=[sds((B, C), bf16), sds((QH, B), f32)],
        in_specs=[SM, fixed((B, C)), kv_spec],
        out_specs=[fixed((B, C)), fixed((QH, B))],
        scratch_shapes=[
            pltpu.VMEM((QH, B, pw), bf16),
            pltpu.VMEM((QH, pw, B), f32),
            pltpu.VMEM((QH, 8, B), f32),
        ],
        cost_estimate=pl.CostEstimate(
            flops=16 * QH * B * B * pw, bytes_accessed=4 * B * C * 2, transcendentals=4 * QH * B * B
        ),
        name="attention_forward",
    )(where, rot_q, kv_all)

    att_pieces = spread_column(attended)

    def out_body(*refs):
        pieces, (om, oo, t_ref, g_ref, res, nrm) = refs[:NT], refs[NT:]
        a = jnp.concatenate([p[...] for p in pieces], axis=1)
        x = t_ref[...].astype(f32) + jnp.concatenate([mm_nt(a, om[0]), mm_nt(a, oo[0])], axis=1)
        res[...] = x
        inv = lax.rsqrt(jnp.mean(x * x, axis=-1, keepdims=True) + epsilon)
        nrm[...] = (x * inv * g_ref[1:2, :]).astype(bf16)

    resid, normed_f = whole_call(
        out_body,
        [sds((R, W), f32), sds((R, W), bf16)],
        (*att_pieces, out_m, out_o, tok, gain2),
        2 * R * W * W,
        "out_norm",
        scalars=False,
    )
    rows_second = jnp.concatenate(gather_column(normed_f), axis=0)

    FB = 384 if F % 384 == 0 else F
    steps = F // FB

    def ffn_body(r_ref, c_ref, wm, wo, out, gnf, mid_r, dg_r, du_r, acc_o, acc_g):
        i = pl.program_id(0)
        rl, rr = r_ref[:, :H], r_ref[:, H:]
        gate = mm(rl, wm[0]) + mm(rr, wo[0])
        up = mm(rl, wm[1]) + mm(rr, wo[1])
        gmid = mm(c_ref[:, :H], wm[2]) + mm(c_ref[:, H:], wo[2])
        sig = jax.nn.sigmoid(gate)
        act = gate * sig
        mid = (act * up).astype(bf16)
        dg = (gmid * up * sig * (1.0 + gate * (1.0 - sig))).astype(bf16)
        du = (gmid * act).astype(bf16)
        mid_r[...] = mid
        dg_r[...] = dg
        du_r[...] = du
        for w, cols in ((wm, slice(0, H)), (wo, slice(H, W))):
            o = mm_nt(mid, w[2])
            g = mm_nt(dg, w[0]) + mm_nt(du, w[1])

            @pl.when(i == 0)
            def _():
                acc_o[:, cols] = o
                acc_g[:, cols] = g

            @pl.when(i > 0)
            def _():
                acc_o[:, cols] += o
                acc_g[:, cols] += g

        @pl.when(i == steps - 1)
        def _():
            out[...] = acc_o[...].astype(bf16)
            gnf[...] = acc_g[...].astype(bf16)

    one = lambda shape: pl.BlockSpec(shape, lambda i: (0,) * len(shape))
    wide = pl.BlockSpec((B, FB), lambda i: (0, i))
    w_spec = pl.BlockSpec((3, H, FB), lambda i: (0, 0, i))
    ffn_part, gnf_part, mid, dgate, dup = pl.pallas_call(
        ffn_body,
        grid=(steps,),
        out_shape=[sds((B, W), bf16), sds((B, W), bf16)] + [sds((B, F), bf16)] * 3,
        in_specs=[one((B, W)), one((B, W)), w_spec, w_spec],
        out_specs=[one((B, W)), one((B, W)), wide, wide, wide],
        scratch_shapes=[pltpu.VMEM((B, W), f32)] * 2,
        cost_estimate=pl.CostEstimate(
            flops=12 * B * W * F, bytes_accessed=6 * W * F + 6 * B * F, transcendentals=B * F
        ),
        name="ffn",
    )(rows_second, cot_rows, ffn_m, ffn_o)
    gnf_pieces = spread_column(gnf_part)

    def back_body(*refs):
        pieces, (res, c_ref, g_ref, om, oo, gres, rg, ga, gg) = refs[:NT], refs[NT:]
        grad = sum(p[...].astype(f32) for p in pieces)
        x = res[...]
        inv = lax.rsqrt(jnp.mean(x * x, axis=-1, keepdims=True) + epsilon)
        hat = x * inv
        gg[...] = jnp.sum(grad * hat, axis=0, keepdims=True)
        scaled = grad * g_ref[1:2, :]
        through = inv * (scaled - hat * jnp.mean(scaled * hat, axis=-1, keepdims=True))
        total = c_ref[...].astype(f32) + through
        gres[...] = total
        half = total.astype(bf16)
        rg[...] = half
        ga[...] = (mm(half[:, :H], om[0]) + mm(half[:, H:], oo[0])).astype(bf16)

    grad_resid, rg16, ga_full, ffn_gain_part = whole_call(
        back_body,
        [sds((R, W), f32), sds((R, W), bf16), sds((R, W), bf16), sds((1, W), f32)],
        (*gnf_pieces, resid, cot, gain2, out_m, out_o),
        2 * R * W * W,
        "second_back",
        scalars=False,
    )
    ga_pieces = [ga_full[:, :C]] + [
        column(ga_full[:, k * C : (k + 1) * C], k) for k in range(1, NT)
    ]
    grad_att = jnp.concatenate(ga_pieces, axis=0)

    def dw_body(r_ref, c_ref, mid_r, dg_r, du_r, gm, go, rt, ct):
        @pl.when(pl.program_id(0) == 0)
        def _():
            rt[...] = r_ref[...].T
            ct[...] = c_ref[...].T

        for k, (lhs, rhs) in enumerate(((rt, dg_r), (rt, du_r), (ct, mid_r))):
            gm[k] = mm(lhs[:H], rhs[...]).astype(bf16)
            go[k] = mm(lhs[H:], rhs[...]).astype(bf16)

    dwf_m, dwf_o = pl.pallas_call(
        dw_body,
        grid=(steps,),
        out_shape=[sds((3, H, F), bf16)] * 2,
        in_specs=[one((B, W)), one((B, W)), wide, wide, wide],
        out_specs=[w_spec, w_spec],
        scratch_shapes=[pltpu.VMEM((W, B), bf16)] * 2,
        cost_estimate=pl.CostEstimate(
            flops=6 * B * W * F, bytes_accessed=6 * W * F + 6 * B * F, transcendentals=0
        ),
        name="ffn_weights",
    )(rows_second, cot_rows, mid, dgate, dup)
    ffn_sum = scatter_plane(dwf_m, dwf_o)

    def bwd_body(s_ref, q_ref, d_ref, a_ref, l_ref, kv_ref, dq_ref, dkv_ref, qz, dz, acc, dl):
        r, h = pl.program_id(0), pl.program_id(1)
        here = s_ref[1]

        @pl.when((r == 0) & (h == 0))
        def _():
            for hd in range(QH):
                cols = slice((hd // 2) * pw, (hd // 2 + 1) * pw)
                qz[hd] = widen(q_ref[:, cols].astype(f32), hd % 2).astype(bf16)
                dz[hd] = widen_high(d_ref[:, cols].astype(f32), hd % 2).astype(bf16)
            prod = d_ref[...].astype(f32) * a_ref[...].astype(f32)
            for hd in range(QH):
                pick = jnp.where(lanes((8, C)) // hw == hd, 1.0, 0.0).astype(f32)
                dl[hd] = lax.dot_general(
                    pick, prod, (((1,), (1,)), ((), ())), precision=exact, preferred_element_type=f32
                )

        def step(masked):
            kv = kv_ref[0]
            kvt = kv.astype(f32).T.astype(bf16)
            total = None
            for g in range(2):
                hd = 2 * h + g
                q, d = qz[hd], dz[hd]
                shift = l_ref[hd] * log2e
                p = jnp.exp2(mm_nt(kv, q) * c2 - shift)
                if masked:
                    p = jnp.where(causal(s_ref[2] * R), p, 0.0)
                ds = (p * (mm_nt(kv, d) - dl[hd][0:1])).astype(bf16)
                t = jnp.where(lanes((B, pw)) < hw, mm(ds, q) * scale, mm(p.astype(bf16), d))
                total = t if total is None else total + t
                o = mm(kvt, ds)
                if masked:
                    acc[hd] = o
                else:
                    acc[hd] += o
            dkv_ref[0] = total.astype(bf16)

        @pl.when(r == 0)
        def _():
            step(True)

        @pl.when((here ^ r) < here)
        def _():
            step(False)

        @pl.when((here ^ r) > here)
        def _():
            dkv_ref[...] = jnp.zeros_like(dkv_ref)

        @pl.when((r == NC - 1) & (h == KH - 1))
        def _():
            outs = [acc[hd][:hw] for hd in range(QH)]
            dq_ref[...] = jnp.concatenate(outs, axis=0).T * scale

    grad_rot_q, dkv = pl.pallas_call(
        bwd_body,
        grid=(NC, KH),
        out_shape=[sds((B, C), f32), sds((NC, B, C), bf16)],
        in_specs=[SM, fixed((B, C)), fixed((B, C)), fixed((B, C)), fixed((QH, 1, B)), kv_spec],
        out_specs=[fixed((B, C)), kv_spec],
        scratch_shapes=[
            pltpu.VMEM((QH, B, pw), bf16),
            pltpu.VMEM((QH, B, pw), bf16),
            pltpu.VMEM((QH, pw, B), f32),
            pltpu.VMEM((QH, 8, B), f32),
        ],
        cost_estimate=pl.CostEstimate(
            flops=40 * QH * B * B * pw, bytes_accessed=8 * B * C * 2, transcendentals=4 * QH * B * B
        ),
        name="attention_backward",
    )(where, rot_q, grad_att, attended, lse[:, None, :], kv_all)

    later = lambda i, j: i > j
    odd = lax.ppermute(dkv[1::2], "ctx", [(i, i ^ 1) for i in range(NC)])
    pair_sum = dkv[0].astype(f32) + odd[0].astype(f32)
    for k in range(1, NC // 2):
        part = (dkv[2 * k].astype(f32) + odd[k].astype(f32)).astype(bf16)
        pair_sum = pair_sum + along(part, 2 * k, lambda i, j: i // 2 > j // 2).astype(f32)

    rg_rows = jnp.concatenate(gather_column(after(rg16, grad_att)), axis=0)
    ffn_pieces = spread_column(after(ffn_part, rg_rows))

    def dwo_body(g_ref, a_ref, gm, go):
        a = a_ref[...]
        gm[0] = lax.dot_general(
            g_ref[:, :H], a, (((0,), (0,)), ((), ())), preferred_element_type=f32
        ).astype(bf16)
        go[0] = lax.dot_general(
            g_ref[:, H:], a, (((0,), (0,)), ((), ())), preferred_element_type=f32
        ).astype(bf16)

    dwo_m, dwo_o = whole_call(
        dwo_body,
        [sds((1, H, C), bf16)] * 2,
        (rg_rows, attended),
        2 * B * W * C,
        "output_weights",
        scalars=False,
    )

    def qk_body(
        dq, dp, q_raw_r, p_raw_r, cs, sn, qg_ref, kg_ref, r_ref, wm, wo, g_ref,
        gna, gm, go, qgg, kgg, agg,
    ):
        def back(grad, raw, gain, live):
            turned = grad * cs[...] - swap_halves(grad) * sn[...]
            inv = lax.rsqrt(head_mean(raw * raw) + epsilon)
            hat = raw * inv
            scaled = turned * gain
            out = inv * (scaled - hat * head_mean(scaled * hat))
            gg = jnp.sum(turned * hat, axis=0, keepdims=True)
            if live is not None:
                out = jnp.where(live, out, grad)
            return out.astype(bf16), gg

        gq, qsum = back(dq[...], q_raw_r[...], qg_ref[...], None)
        live = lanes((B, C)) % pw < hw
        gp, ksum = back(dp[...], p_raw_r[...], kg_ref[...], live)
        qgg[...] = qsum
        kgg[...] = ksum
        both = jnp.concatenate([gq, gp], axis=1)
        for w, cols, gw in ((wm, slice(0, H), gm), (wo, slice(H, W), go)):
            part = mm_nt(gq, w[0]) + mm_nt(gp, w[1])
            gna[:, cols] = part.astype(bf16)
            rows = r_ref[:, cols]
            agg[:, cols] = (
                jnp.sum(part * rows.astype(f32), axis=0, keepdims=True) / g_ref[0:1, cols]
            )
            full = lax.dot_general(
                rows, both, (((0,), (0,)), ((), ())), preferred_element_type=f32
            ).astype(bf16)
            gw[0] = full[:, :C]
            gw[1] = full[:, C:]

    gna_part, dwq_m, dwq_o, qg_part, kg_part, att_gain_part = whole_call(
        qk_body,
        [
            sds((B, W), bf16),
            sds((2, H, C), bf16),
            sds((2, H, C), bf16),
            sds((1, C), f32),
            sds((1, C), f32),
            sds((1, W), f32),
        ],
        (
            grad_rot_q, pair_sum, q_raw, p_raw, cosine, sine, qg, kg,
            rows_first, qkv_m, qkv_o, gain2,
        ),
        8 * B * W * C,
        "projections_back",
        scalars=False,
    )
    gna_pieces = spread_column(gna_part)
    last_m = jnp.concatenate([dwq_m, dwo_m], axis=0)
    last_o = jnp.concatenate([dwq_o, dwo_o], axis=0)
    att_sum = scatter_plane(last_m, last_o)

    order_back = masks
    inverse_order = [order_back.index(m) for m in range(N)]
    gain_parts = jnp.concatenate([att_gain_part, ffn_gain_part], axis=0)
    slot_of = jnp.take(jnp.array(inverse_order, jnp.int32), me ^ jnp.arange(N, dtype=jnp.int32))
    gain_parts = jnp.take(gain_parts.reshape(2, N, blk), slot_of, axis=1).reshape(2 * W)
    q_part = qg_part.reshape(QH, hw).sum(0)
    k_part = kg_part.reshape(KH, 2, hw)[:, 0].sum(0)
    packed = jnp.concatenate([gain_parts, q_part, k_part]).reshape(-1, 128)
    packed = sum(gather_column(packed))
    bit = 1
    while bit < N:
        packed = packed + plane(packed, bit)
        bit *= 2
    packed = packed.reshape(-1)

    def end_body(*refs):
        s_ref, rest = refs[0], refs[1:]
        gp, fp, (t_ref, res, gres, g_ref, gt, bo) = rest[:NT], rest[NT : 2 * NT], rest[2 * NT :]
        index = s_ref[0]
        grad = sum(p[...].astype(f32) for p in gp)
        x = t_ref[...].astype(f32)
        inv = lax.rsqrt(jnp.mean(x * x, axis=-1, keepdims=True) + epsilon)
        hat = x * inv
        scaled = grad * g_ref[0:1, :]
        total = gres[...] + inv * (scaled - hat * jnp.mean(scaled * hat, axis=-1, keepdims=True))
        block = (res[...] + sum(p[...].astype(f32) for p in fp)).astype(bf16)
        for s, mask in enumerate(masks):
            src = slice(s * blk, (s + 1) * blk)
            if aligned:
                dst = pl.ds(pl.multiple_of((index ^ mask) * blk, blk), blk)
            else:
                dst = src
            gt[:, dst] = total[:, src]
            bo[:, dst] = block[:, src]

    grad_tokens, block_out = whole_call(
        end_body,
        [sds((R, W), f32), sds((R, W), bf16)],
        (where, *gna_pieces, *ffn_pieces, tok, resid, grad_resid, gain2),
        R * W * 16,
        "end",
    )
    if not aligned:
        back_cols = lambda v: jnp.take(
            v.reshape(R, N, blk), slot_of, axis=1
        ).reshape(R, W)
        grad_tokens, block_out = back_cols(grad_tokens), back_cols(block_out)

    lse_out = jnp.take(
        lse.reshape(QH, NT, R), z ^ jnp.arange(NT, dtype=jnp.int32), axis=1
    ).reshape(1, QH, B)
    return (
        block_out[None],
        grad_tokens[None],
        lse_out,
        packed[:W],
        att_sum[0],
        att_sum[1],
        packed[2 * W : 2 * W + hw],
        packed[2 * W + hw : 2 * W + 2 * hw],
        att_sum[2].T,
        packed[W : 2 * W],
        ffn_sum[0],
        ffn_sum[1],
        ffn_sum[2].T,
    )


def solution(mesh):
    in_specs = (
        P("dp", ("ctx", "tp"), None),
        P(),
        P(("dp", "ctx"), "tp"),
        P(("dp", "ctx"), "tp"),
        P(),
        P(),
        P("tp", ("dp", "ctx")),
        P(),
        P(("dp", "ctx"), "tp"),
        P(("dp", "ctx"), "tp"),
        P("tp", ("dp", "ctx")),
        P("dp", ("ctx", "tp"), None),
    )
    out_specs = (
        P("dp", ("ctx", "tp"), None),
        P("dp", ("ctx", "tp"), None),
        P("dp", "tp", "ctx"),
        P(),
        P(("dp", "ctx"), "tp"),
        P(("dp", "ctx"), "tp"),
        P(),
        P(),
        P("tp", ("dp", "ctx")),
        P(),
        P(("dp", "ctx"), "tp"),
        P(("dp", "ctx"), "tp"),
        P("tp", ("dp", "ctx")),
    )
    return jax.shard_map(
        on_device, mesh=mesh, in_specs=in_specs, out_specs=out_specs, check_vma=False
    )
```

time: 870 us -> 359 us (0.41)
  waiting for transfers between devices: 574 us -> 125 us
  starting transfers between devices: 1.47 us -> 101 us
  matrix products: 91.3 us -> 0 us
  blocking collectives: 74.9 us -> 0 us
  Pallas kernels: 0 us -> 68.6 us
  local copies, waits for them, and re-layouts: 71.7 us -> 40.4 us
  between operations: 16.6 us -> 1.48 us
  other arithmetic: 34.3 us -> 21.5 us
    reduce_scatter x11 -> x0, waiting for transfers between devices: 421 us -> none  [the longest x1 57.6 us: on_device(): lax.psum_scatter(grad_down, ('dp', 'ctx'), scatter_dimension=1, tiled=True)]
    all_gather x8 -> x0, waiting for transfers between devices: 151 us -> none  [the longest x1 30.4 us: fetch_weights(): lax.all_gather(down_weight, ('dp', 'ctx'), axis=1, tiled=True)]
    ppermute x0 -> x66, waiting for transfers between devices: none -> 125 us  [the longest x33 82.7 us: column(): return lax.ppermute(v, 'tp', [(i, i ^ mask) for i in range(NT)])]
    ppermute x0 -> x66, starting transfers between devices: none -> 101 us  [the longest x33 61.8 us: column(): return lax.ppermute(v, 'tp', [(i, i ^ mask) for i in range(NT)])]
    dot_general x46 -> x0, matrix products: 91.3 us -> none  [the longest x4 11.4 us: attend(): jnp.einsum('hgqd,hkd->hgqk', query_group, keys_part, preferred_element_ty...]
    pallas_call x0 -> x10, Pallas kernels: none -> 68.6 us  [the longest x6 24.8 us: whole_call(): pl.pallas_call(body, out_shape=list(outs), in_specs=specs, out_specs=[VM]...]
    dynamic_update_slice x8 -> x0, local copies, waits for them, and re-layouts: 46.2 us -> none  [on_device(): lax.scan(back_block, jnp.zeros((pair_heads, query_group_count, block_rows...]
    psum x1 -> x0, blocking collectives: 42.3 us -> none  [on_device(): lax.psum((grad_attention_gain, grad_query_gain, grad_key_gain, grad_ffn_g...]
  transfers between devices with their start and end apart: 19 -> 66, of which waited for: 17 -> 30; matrix products, arithmetic and copies ran while one was open for 5% -> 14% of each run, Pallas kernels for 0% -> 11%
where the time goes in v1:
time: 359 us; the launch traced here: 358 us
  waiting for transfers between devices  125 us (35%)
  starting transfers between devices  101 us (28%)
  Pallas kernels  68.6 us (19%)
  local copies, waits for them, and re-layouts  40.4 us (11%)
  other arithmetic  21.5 us (6%)
    ppermute x33, waiting for transfers between devices, column(): return lax.ppermute(v, 'tp', [(i, i ^ mask) for i in range(NT)])  82.7 us
    ppermute x33, starting transfers between devices, column(): return lax.ppermute(v, 'tp', [(i, i ^ mask) for i in range(NT)])  61.8 us
    ppermute x28, waiting for transfers between devices, plane(): return lax.ppermute(v, ('dp', 'ctx'), [(i, i ^ mask) for i in range(N)])  39.2 us
    ppermute x28, starting transfers between devices, plane(): return lax.ppermute(v, ('dp', 'ctx'), [(i, i ^ mask) for i in range(N)])  32.7 us
    pallas_call x6, Pallas kernels, whole_call(): pl.pallas_call(body, out_shape=list(outs), in_specs=specs, out_specs=[VM]...  24.8 us
    unnamed x106, local copies, waits for them, and re-layouts  19.2 us
    pallas_call x1, Pallas kernels, on_device(): pl.pallas_call(ffn_body, grid=(steps,), out_shape=[sds((B, W), bf16), sds...  16.7 us
    pallas_call x1, Pallas kernels, on_device(): pl.pallas_call(bwd_body, grid=(NC, KH), out_shape=[sds((B, C), f32), sds(...  10.5 us
  transfers between devices with their start and end apart: 66, of which 30 were waited for; matrix products, arithmetic and copies ran while one was open for 14% of the time, Pallas kernels for 11%

profile of v1, /device:TPU:0, one launch (start us, length us, event | category | flops | bytes accessed | tf_op | source)
XLA Modules:
  0.0 358.0 jit_solution(8705034246277915639)
XLA Ops:
  1.6 3.0 collective-permute-start.3
  28.7 9.9 %collective-permute-done.28 = bf16[3,128,1152]{2,1,0:T(8,128)(2,1)} collective-permute-done((bf16[3,128,1152]{2,1,0:T(8,128)(2,1)S(1)}, bf16[3,128,1152]{2,1,0:T(8,128)(2,1)}, u32[]{:S(2)}, u32[]{:S(2)}) %collective-permute-start.28) | collective-permute-done | bytes 884768 | tf_op jit(solution)/shard_map/ppermute | solution.py:98
  47.1 4.1 %collective-permute-done.30 = bf16[3,64,1152]{2,1,0:T(8,128)(2,1)S(1)} collective-permute-done((bf16[3,64,1152]{2,1,0:T(8,128)(2,1)S(1)}, bf16[3,64,1152]{2,1,0:T(8,128)(2,1)S(1)}, u32[]{:S(2)}, u32[]{:S(2)}) %collective-permute-start.30) | collective-permute-done | bytes 442400 | tf_op jit(solution)/shard_map/ppermute | solution.py:98
  62.1 8.3 %collective-permute-done.2 = bf16[128,1024]{1,0:T(8,128)(2,1)S(1)} collective-permute-done((bf16[128,1024]{1,0:T(8,128)(2,1)S(1)}, bf16[128,1024]{1,0:T(8,128)(2,1)S(1)}, u32[]{:S(2)}, u32[]{:S(2)}) %collective-permute-start.2) | collective-permute-done | bytes 262176 | tf_op jit(solution)/shard_map/ppermute | solution.py:101
  73.0 4.9 %qkv.1 = (bf16[512,256]{1,0:T(8,128)(2,1)}, bf16[512,256]{1,0:T(8,128)(2,1)}, f32[512,256]{1,0:T(8,128)}, f32[512,256]{1,0:T(8,128)}) custom-call(bf16[512,1024]{1,0:T(8,128)(2,1)} %copy-done.1, bf16[2,512,256]{2,1,0:T(8,128)(2,1)} %copy-done.5, bf16[2,512,256]{2,1,0:T(8,128)(2,1)} %copy-done.8, f32[512,256]{1,0:T(8,128)} %copy.40.cs, f32[512,256]{1,0:T(8,128)} %copy.41.sn, ...), custom_call_target="tpu_custom_call" | custom-call | flops 536870912 | bytes 4720640 | tf_op jit(solution)/shard_map/qkv/pallas_call | solution.py:47
  77.9 3.2 collective-permute-start.9
  84.2 3.1 collective-permute-done.9
  89.3 4.2 %collective-permute-start.25 = (bf16[128,1024]{1,0:T(8,128)(2,1)S(1)}, bf16[128,1024]{1,0:T(8,128)(2,1)S(1)}, u32[]{:S(2)}, u32[]{:S(2)}) collective-permute-start(bf16[128,1024]{1,0:T(8,128)(2,1)S(1)} %copy-done.13), channel_id=1, source_target_pairs={{0,1},{1,0},{2,3},{3,2},{4,5},{5,4},{6,7},{7,6},{8,9},{9,8},{10,11... | collective-permute-start | bytes 786440 | tf_op jit(solution)/shard_map/ppermute | solution.py:101
  95.5 6.9 %attention_forward.1 = (bf16[512,256]{1,0:T(8,128)(2,1)}, f32[4,512]{1,0:T(4,128)}) custom-call(s32[3]{0:T(128)} %pad_add_fusion.s_ref.refs_0_, bf16[512,256]{1,0:T(8,128)(2,1)} %get-tuple-element.54.q_ref, bf16[4,512,256]{2,1,0:T(8,128)(2,1)} %pad_maximum_fusion.kv_ref), custom_call_target="tpu_custom_call" | custom-call | flops 2147483648 | bytes 1048576 | tf_op jit(solution)/shard_map/attention_forward/pallas_call | solution.py:303
  115.1 5.8 %collective-permute-done.13.refs_3_ = bf16[128,256]{1,0:T(8,128)(2,1)S(1)} collective-permute-done((bf16[128,256]{1,0:T(8,128)(2,1)S(1)}, bf16[128,256]{1,0:T(8,128)(2,1)S(1)}, u32[]{:S(2)}, u32[]{:S(2)}) %collective-permute-start.13) | collective-permute-done | bytes 65568 | tf_op jit(solution)/shard_map/ppermute | solution.py:101
  121.9 3.4 out_norm.1
  125.3 6.3 %collective-permute-start.22 = (bf16[128,1024]{1,0:T(8,128)(2,1)}, bf16[128,1024]{1,0:T(8,128)(2,1)S(1)}, u32[]{:S(2)}, u32[]{:S(2)}) collective-permute-start(bf16[128,1024]{1,0:T(8,128)(2,1)} %get-tuple-element.60), channel_id=1, source_target_pairs={{0,1},{1,0},{2,3},{3,2},{4,5},{5,4},{6,7},{7,6},{8,9},{9,8},{10,11... | collective-permute-start | bytes 786440 | tf_op jit(solution)/shard_map/ppermute | solution.py:101
  136.5 4.5 %collective-permute-done.22 = bf16[128,1024]{1,0:T(8,128)(2,1)S(1)} collective-permute-done((bf16[128,1024]{1,0:T(8,128)(2,1)}, bf16[128,1024]{1,0:T(8,128)(2,1)S(1)}, u32[]{:S(2)}, u32[]{:S(2)}) %collective-permute-start.22) | collective-permute-done | bytes 262176 | tf_op jit(solution)/shard_map/ppermute | solution.py:101
  141.0 12.6 %collective-permute-done.23 = bf16[128,1024]{1,0:T(8,128)(2,1)S(1)} collective-permute-done((bf16[128,1024]{1,0:T(8,128)(2,1)}, bf16[128,1024]{1,0:T(8,128)(2,1)S(1)}, u32[]{:S(2)}, u32[]{:S(2)}) %collective-permute-start.23) | collective-permute-done | bytes 262176 | tf_op jit(solution)/shard_map/ppermute | solution.py:101
  154.7 16.7 %ffn.1 = (bf16[512,1024]{1,0:T(8,128)(2,1)}, bf16[512,1024]{1,0:T(8,128)(2,1)}, bf16[512,1152]{1,0:T(8,128)(2,1)}, bf16[512,1152]{1,0:T(8,128)(2,1)}, bf16[512,1152]{1,0:T(8,128)(2,1)}) custom-call(bf16[512,1024]{1,0:T(8,128)(2,1)} %copy-done.31, bf16[512,1024]{1,0:T(8,128)(2,1)} %constant_dynamic-update-slice_fusion.18.c_ref, ...), custom_call_target="tpu_custom_call" | custom-call | flops 7247757312 | bytes 10616832 | tf_op jit(solution)/shard_map/ffn/pallas_call | solution.py:379
  173.3 4.1 %collective-permute-start.33 = (bf16[128,1024]{1,0:T(8,128)(2,1)S(1)}, bf16[128,1024]{1,0:T(8,128)(2,1)S(1)}, u32[]{:S(2)}, u32[]{:S(2)}) collective-permute-start(bf16[128,1024]{1,0:T(8,128)(2,1)S(1)} %get-tuple-element.155), channel_id=1, source_target_pairs={{0,1},{1,0},{2,3},{3,2},{4,5},{5,4},{6,7},{7,6},{8,9},{9,8},{10,11... | collective-permute-start | bytes 786440 | tf_op jit(solution)/shard_map/ppermute | solution.py:101
  179.9 6.4 %collective-permute-done.33.refs_1_ = bf16[128,1024]{1,0:T(8,128)(2,1)S(1)} collective-permute-done((bf16[128,1024]{1,0:T(8,128)(2,1)S(1)}, bf16[128,1024]{1,0:T(8,128)(2,1)S(1)}, u32[]{:S(2)}, u32[]{:S(2)}) %collective-permute-start.33) | collective-permute-done | bytes 262176 | tf_op jit(solution)/shard_map/ppermute | solution.py:101
  186.3 11.4 %collective-permute-done.34.refs_2_ = bf16[128,1024]{1,0:T(8,128)(2,1)S(1)} collective-permute-done((bf16[128,1024]{1,0:T(8,128)(2,1)S(1)}, bf16[128,1024]{1,0:T(8,128)(2,1)S(1)}, u32[]{:S(2)}, u32[]{:S(2)}) %collective-permute-start.34) | collective-permute-done | bytes 262176 | tf_op jit(solution)/shard_map/ppermute | solution.py:101
  198.6 3.6 %second_back.1 = (f32[128,1024]{1,0:T(8,128)}, bf16[128,1024]{1,0:T(8,128)(2,1)}, bf16[128,1024]{1,0:T(8,128)(2,1)}, f32[1,1024]{1,0:T(1,128)}) custom-call(bf16[128,1024]{1,0:T(8,128)(2,1)} %get-tuple-element.156.refs_0_, bf16[128,1024]{1,0:T(8,128)(2,1)} %copy-done.25, bf16[128,1024]{1,0:T(8,128)(2,1)} %copy-done.26, bf16[128,1024]{1,0:T(8,128)(2,1)} %copy-done.27, ...), custom_call_target="tpu_custom_call" | custom-call | flops 268435456 | bytes 4993024 | tf_op jit(solution)/shard_map/second_back/pallas_call | solution.py:47
  205.2 4.2 %collective-permute-start.37 = (bf16[128,256]{1,0:T(8,128)(2,1)S(1)}, bf16[128,256]{1,0:T(8,128)(2,1)S(1)}, u32[]{:S(2)}, u32[]{:S(2)}) collective-permute-start(bf16[128,256]{1,0:T(8,128)(2,1)S(1)} %get-tuple-element.164), channel_id=1, source_target_pairs={{0,2},{1,3},{2,0},{3,1},{4,6},{5,7},{6,4},{7,5},{8,10},{9,11},{10,... | collective-permute-start | bytes 196616 | tf_op jit(solution)/shard_map/ppermute | solution.py:101
  214.4 10.5 %attention_backward.1 = (f32[512,256]{1,0:T(8,128)}, bf16[4,512,256]{2,1,0:T(8,128)(2,1)}) custom-call(s32[3]{0:T(128)} %pad_add_fusion.s_ref.refs_0_, bf16[512,256]{1,0:T(8,128)(2,1)} %get-tuple-element.54.q_ref, bf16[512,256]{1,0:T(8,128)(2,1)} %pad_maximum_fusion.6.d_ref, bf16[512,256]{1,0:T(8,128)(2,1)} %get-tuple-element.56.a_ref, ...), custom_call_target="tpu_custom_call" | custom-call | flops 5368709120 | bytes 2097152 | tf_op jit(solution)/shard_map/attention_backward/pallas_call | solution.py:500
  226.2 9.7 %ffn_weights.1 = (bf16[3,512,1152]{2,1,0:T(8,128)(2,1)}, bf16[3,512,1152]{2,1,0:T(8,128)(2,1)}) custom-call(bf16[512,1024]{1,0:T(8,128)(2,1)} %copy-done.31, bf16[512,1024]{1,0:T(8,128)(2,1)} %constant_dynamic-update-slice_fusion.18.c_ref, bf16[512,1152]{1,0:T(8,128)(2,1)} %get-tuple-element.88.mid_r, bf16[512,1152]{1,0:T(8,128)(2,1)} %get-tuple-element.89.dg_r, ...), custom_call_target="tpu_custom_call" | custom-call | flops 3623878656 | bytes 10616832 | tf_op jit(solution)/shard_map/ffn_weights/pallas_call | solution.py:431
  238.5 2.9 collective-permute-start.46
  242.8 7.0 %collective-permute-done.44 = bf16[128,1024]{1,0:T(8,128)(2,1)S(1)} collective-permute-done((bf16[128,1024]{1,0:T(8,128)(2,1)S(1)}, bf16[128,1024]{1,0:T(8,128)(2,1)S(1)}, u32[]{:S(2)}, u32[]{:S(2)}) %collective-permute-start.44) | collective-permute-done | bytes 262176 | tf_op jit(solution)/shard_map/ppermute | solution.py:101
  249.8 9.2 %collective-permute-done.45 = bf16[128,1024]{1,0:T(8,128)(2,1)S(1)} collective-permute-done((bf16[128,1024]{1,0:T(8,128)(2,1)S(1)}, bf16[128,1024]{1,0:T(8,128)(2,1)S(1)}, u32[]{:S(2)}, u32[]{:S(2)}) %collective-permute-start.45) | collective-permute-done | bytes 262176 | tf_op jit(solution)/shard_map/ppermute | solution.py:101
  260.0 7.5 %projections_back.1 = (bf16[512,1024]{1,0:T(8,128)(2,1)}, bf16[2,512,256]{2,1,0:T(8,128)(2,1)}, bf16[2,512,256]{2,1,0:T(8,128)(2,1)}, f32[1,256]{1,0:T(1,128)}, f32[1,256]{1,0:T(1,128)}, /*index=5*/f32[1,1024]{1,0:T(1,128)}) custom-call(f32[512,256]{1,0:T(8,128)} %get-tuple-element.68.dq, f32[512,256]{1,0:T(8,128)} %bitcast_add_fusion.dp, ...), custom_call_target="tpu_custom_call" | custom-call | flops 1073741824 | bytes 7356416 | tf_op jit(solution)/shard_map/projections_back/pallas_call | solution.py:47
  273.9 4.8 %collective-permute-start.51 = (f32[17,128]{1,0:T(8,128)S(1)}, f32[17,128]{1,0:T(8,128)S(1)}, u32[]{:S(2)}, u32[]{:S(2)}) collective-permute-start(f32[17,128]{1,0:T(8,128)S(1)} %bitcast.93), channel_id=1, source_target_pairs={{0,2},{1,3},{2,0},{3,1},{4,6},{5,7},{6,4},{7,5},{8,10},{9,11},{10,... | collective-permute-start | bytes 26120 | tf_op jit(solution)/shard_map/ppermute | solution.py:101
  284.2 8.4 %collective-permute-start.54 = (f32[17,128]{1,0:T(8,128)S(1)}, f32[17,128]{1,0:T(8,128)S(1)}, u32[]{:S(2)}, u32[]{:S(2)}) collective-permute-start(f32[17,128]{1,0:T(8,128)S(1)} %add.161), channel_id=1, source_target_pairs={{0,8},{4,12},{8,0},{12,4},{16,24},{20,28},{24,16},{28,20},{1,9},{5... | collective-permute-start | bytes 26120 | tf_op jit(solution)/shard_map/ppermute | solution.py:98
  309.2 7.5 %collective-permute-done.64 = bf16[3,64,1152]{2,1,0:T(8,128)(2,1)S(1)} collective-permute-done((bf16[3,64,1152]{2,1,0:T(8,128)(2,1)S(1)}, bf16[3,64,1152]{2,1,0:T(8,128)(2,1)S(1)}, u32[]{:S(2)}, u32[]{:S(2)}) %collective-permute-start.64) | collective-permute-done | bytes 442400 | tf_op jit(solution)/shard_map/ppermute | solution.py:98
  318.7 6.7 %collective-permute-done.62 = bf16[3,64,1152]{2,1,0:T(8,128)(2,1)S(1)} collective-permute-done((bf16[3,64,1152]{2,1,0:T(8,128)(2,1)S(1)}, bf16[3,64,1152]{2,1,0:T(8,128)(2,1)S(1)}, u32[]{:S(2)}, u32[]{:S(2)}) %collective-permute-start.62) | collective-permute-done | bytes 442400 | tf_op jit(solution)/shard_map/ppermute | solution.py:98
  334.5 9.5 %collective-permute-done.42.refs_3_ = bf16[128,1024]{1,0:T(8,128)(2,1)S(1)} collective-permute-done((bf16[128,1024]{1,0:T(8,128)(2,1)S(1)}, bf16[128,1024]{1,0:T(8,128)(2,1)S(1)}, u32[]{:S(2)}, u32[]{:S(2)}) %collective-permute-start.42) | collective-permute-done | bytes 262176 | tf_op jit(solution)/shard_map/ppermute | solution.py:101
  345.4 3.4 end.1
  (308 shorter events, 142.8 us)
Async XLA Ops:
  16.4 22.1 %collective-permute-start.28 = (bf16[3,128,1152]{2,1,0:T(8,128)(2,1)S(1)}, bf16[3,128,1152]{2,1,0:T(8,128)(2,1)}, u32[]{:S(2)}, u32[]{:S(2)}) collective-permute-start(bf16[3,128,1152]{2,1,0:T(8,128)(2,1)S(1)} %pad_maximum_fusion.1), channel_id=1, source_target_pairs={{0,8},{4,12},{8,0},{12,4},{16,24},{20,28},{24,16},{28,20},{1,9},{5... | collective-permute-start | bytes 2654216 | tf_op jit(solution)/shard_map/ppermute | solution.py:98
  18.0 22.8 %collective-permute-start.29 = (bf16[3,128,1152]{2,1,0:T(8,128)(2,1)S(1)}, bf16[3,128,1152]{2,1,0:T(8,128)(2,1)}, u32[]{:S(2)}, u32[]{:S(2)}) collective-permute-start(bf16[3,128,1152]{2,1,0:T(8,128)(2,1)S(1)} %pad_maximum_fusion.1), channel_id=1, source_target_pairs={{0,16},{4,20},{8,24},{12,28},{16,0},{20,4},{24,8},{28,12},{1,17},{... | collective-permute-start | bytes 2654216 | tf_op jit(solution)/shard_map/ppermute | solution.py:98
  21.2 40.8 %collective-permute-start = (bf16[128,1024]{1,0:T(8,128)(2,1)}, bf16[128,1024]{1,0:T(8,128)(2,1)S(1)}, u32[]{:S(2)}, u32[]{:S(2)}) collective-permute-start(bf16[128,1024]{1,0:T(8,128)(2,1)} %get-tuple-element.53), channel_id=1, source_target_pairs={{0,1},{1,0},{2,3},{3,2},{4,5},{5,4},{6,7},{7,6},{8,9},{9,8},{10,11... | collective-permute-start | bytes 786440 | tf_op jit(solution)/shard_map/ppermute | solution.py:101
  22.8 39.2 %collective-permute-start.1 = (bf16[128,1024]{1,0:T(8,128)(2,1)}, bf16[128,1024]{1,0:T(8,128)(2,1)S(1)}, u32[]{:S(2)}, u32[]{:S(2)}) collective-permute-start(bf16[128,1024]{1,0:T(8,128)(2,1)} %get-tuple-element.53), channel_id=1, source_target_pairs={{0,2},{1,3},{2,0},{3,1},{4,6},{5,7},{6,4},{7,5},{8,10},{9,11},{10,... | collective-permute-start | bytes 786440 | tf_op jit(solution)/shard_map/ppermute | solution.py:101
  26.2 29.3 %collective-permute-start.16 = (bf16[128,256]{1,0:T(8,128)(2,1)}, bf16[128,256]{1,0:T(8,128)(2,1)}, u32[]{:S(2)}, u32[]{:S(2)}) collective-permute-start(bf16[128,256]{1,0:T(8,128)(2,1)} %bitcast.16), channel_id=1, source_target_pairs={{0,3},{1,2},{2,1},{3,0},{4,7},{5,6},{6,5},{7,4},{8,11},{9,10},{10,... | collective-permute-start | bytes 196616 | tf_op jit(solution)/shard_map/ppermute | solution.py:101
  55.4 98.3 %collective-permute-start.32 = (bf16[3,512,1152]{2,1,0:T(8,128)(2,1)}, bf16[3,512,1152]{2,1,0:T(8,128)(2,1)}, u32[]{:S(2)}, u32[]{:S(2)}) collective-permute-start(bf16[3,512,1152]{2,1,0:T(8,128)(2,1)} %constant_dynamic-update-slice_fusion.22.wm), channel_id=1, source_target_pairs={{0,4},{4,0},{8,12},{12,8},{16,20},{20,16},{24,28},{28,24},{1,5},{5... | collective-permute-start | bytes 10616840 | tf_op jit(solution)/shard_map/ppermute | solution.py:98
  89.2 31.7 %collective-permute-start.21 = (bf16[1,512,1024]{2,1,0:T(8,128)(2,1)S(1)}, bf16[1,512,1024]{2,1,0:T(8,128)(2,1)S(1)}, u32[]{:S(2)}, u32[]{:S(2)}) collective-permute-start(bf16[1,512,1024]{2,1,0:T(8,128)(2,1)S(1)} %constant_dynamic-update-slice_fusion.9.refs_4_.refs_7_), channel_id=1, source_target_pairs={{0,4},{4,0},{8,12},{12,8},{16,20},{20,16},{24,28},{28,24},{1,5},{5... | collective-permute-start | bytes 3145736 | tf_op jit(solution)/shard_map/ppermute | solution.py:98
  89.3 16.6 %collective-permute-start.25 = (bf16[128,1024]{1,0:T(8,128)(2,1)S(1)}, bf16[128,1024]{1,0:T(8,128)(2,1)S(1)}, u32[]{:S(2)}, u32[]{:S(2)}) collective-permute-start(bf16[128,1024]{1,0:T(8,128)(2,1)S(1)} %copy-done.13), channel_id=1, source_target_pairs={{0,1},{1,0},{2,3},{3,2},{4,5},{5,4},{6,7},{7,6},{8,9},{9,8},{10,11... | collective-permute-start | bytes 786440 | tf_op jit(solution)/shard_map/ppermute | solution.py:101
  93.5 38.1 %collective-permute-start.26 = (bf16[128,1024]{1,0:T(8,128)(2,1)S(1)}, bf16[128,1024]{1,0:T(8,128)(2,1)S(1)}, u32[]{:S(2)}, u32[]{:S(2)}) collective-permute-start(bf16[128,1024]{1,0:T(8,128)(2,1)S(1)} %copy-done.13), channel_id=1, source_target_pairs={{0,2},{1,3},{2,0},{3,1},{4,6},{5,7},{6,4},{7,5},{8,10},{9,11},{10,... | collective-permute-start | bytes 786440 | tf_op jit(solution)/shard_map/ppermute | solution.py:101
  109.3 23.3 %collective-permute-start.27 = (bf16[128,1024]{1,0:T(8,128)(2,1)S(1)}, bf16[128,1024]{1,0:T(8,128)(2,1)S(1)}, u32[]{:S(2)}, u32[]{:S(2)}) collective-permute-start(bf16[128,1024]{1,0:T(8,128)(2,1)S(1)} %copy-done.13), channel_id=1, source_target_pairs={{0,3},{1,2},{2,1},{3,0},{4,7},{5,6},{6,5},{7,4},{8,11},{9,10},{10,... | collective-permute-start | bytes 786440 | tf_op jit(solution)/shard_map/ppermute | solution.py:101
  125.3 15.7 %collective-permute-start.22 = (bf16[128,1024]{1,0:T(8,128)(2,1)}, bf16[128,1024]{1,0:T(8,128)(2,1)S(1)}, u32[]{:S(2)}, u32[]{:S(2)}) collective-permute-start(bf16[128,1024]{1,0:T(8,128)(2,1)} %get-tuple-element.60), channel_id=1, source_target_pairs={{0,1},{1,0},{2,3},{3,2},{4,5},{5,4},{6,7},{7,6},{8,9},{9,8},{10,11... | collective-permute-start | bytes 786440 | tf_op jit(solution)/shard_map/ppermute | solution.py:101
  132.4 21.2 %collective-permute-start.23 = (bf16[128,1024]{1,0:T(8,128)(2,1)}, bf16[128,1024]{1,0:T(8,128)(2,1)S(1)}, u32[]{:S(2)}, u32[]{:S(2)}) collective-permute-start(bf16[128,1024]{1,0:T(8,128)(2,1)} %get-tuple-element.60), channel_id=1, source_target_pairs={{0,2},{1,3},{2,0},{3,1},{4,6},{5,7},{6,4},{7,5},{8,10},{9,11},{10,... | collective-permute-start | bytes 786440 | tf_op jit(solution)/shard_map/ppermute | solution.py:101
  133.3 20.4 %collective-permute-start.24 = (bf16[128,1024]{1,0:T(8,128)(2,1)}, bf16[128,1024]{1,0:T(8,128)(2,1)S(1)}, u32[]{:S(2)}, u32[]{:S(2)}) collective-permute-start(bf16[128,1024]{1,0:T(8,128)(2,1)} %get-tuple-element.60), channel_id=1, source_target_pairs={{0,3},{1,2},{2,1},{3,0},{4,7},{5,6},{6,5},{7,4},{8,11},{9,10},{10,... | collective-permute-start | bytes 786440 | tf_op jit(solution)/shard_map/ppermute | solution.py:101
  173.3 13.0 %collective-permute-start.33 = (bf16[128,1024]{1,0:T(8,128)(2,1)S(1)}, bf16[128,1024]{1,0:T(8,128)(2,1)S(1)}, u32[]{:S(2)}, u32[]{:S(2)}) collective-permute-start(bf16[128,1024]{1,0:T(8,128)(2,1)S(1)} %get-tuple-element.155), channel_id=1, source_target_pairs={{0,1},{1,0},{2,3},{3,2},{4,5},{5,4},{6,7},{7,6},{8,9},{9,8},{10,11... | collective-permute-start | bytes 786440 | tf_op jit(solution)/shard_map/ppermute | solution.py:101
  177.5 20.3 %collective-permute-start.34 = (bf16[128,1024]{1,0:T(8,128)(2,1)S(1)}, bf16[128,1024]{1,0:T(8,128)(2,1)S(1)}, u32[]{:S(2)}, u32[]{:S(2)}) collective-permute-start(bf16[128,1024]{1,0:T(8,128)(2,1)S(1)} %get-tuple-element.154), channel_id=1, source_target_pairs={{0,2},{1,3},{2,0},{3,1},{4,6},{5,7},{6,4},{7,5},{8,10},{9,11},{10,... | collective-permute-start | bytes 786440 | tf_op jit(solution)/shard_map/ppermute | solution.py:101
  177.6 20.1 %collective-permute-start.35 = (bf16[128,1024]{1,0:T(8,128)(2,1)S(1)}, bf16[128,1024]{1,0:T(8,128)(2,1)S(1)}, u32[]{:S(2)}, u32[]{:S(2)}) collective-permute-start(bf16[128,1024]{1,0:T(8,128)(2,1)S(1)} %get-tuple-element.153), channel_id=1, source_target_pairs={{0,3},{1,2},{2,1},{3,0},{4,7},{5,6},{6,5},{7,4},{8,11},{9,10},{10,... | collective-permute-start | bytes 786440 | tf_op jit(solution)/shard_map/ppermute | solution.py:101
  226.1 15.4 %collective-permute-start.39 = (bf16[2,512,256]{2,1,0:T(8,128)(2,1)S(1)}, bf16[2,512,256]{2,1,0:T(8,128)(2,1)S(1)}, u32[]{:S(2)}, u32[]{:S(2)}) collective-permute-start(bf16[2,512,256]{2,1,0:T(8,128)(2,1)S(1)} %slice.239), channel_id=1, source_target_pairs={{0,4},{4,0},{8,12},{12,8},{1,5},{5,1},{9,13},{13,9},{2,6},{6,2},{1... | collective-permute-start | bytes 1572872 | tf_op jit(solution)/shard_map/ppermute | solution.py:519
  235.9 66.9 %collective-permute-start.61 = (bf16[3,512,1152]{2,1,0:T(8,128)(2,1)}, bf16[3,512,1152]{2,1,0:T(8,128)(2,1)}, u32[]{:S(2)}, u32[]{:S(2)}) collective-permute-start(bf16[3,512,1152]{2,1,0:T(8,128)(2,1)} %get-tuple-element.92), channel_id=1, source_target_pairs={{0,4},{4,0},{8,12},{12,8},{16,20},{20,16},{24,28},{28,24},{1,5},{5... | collective-permute-start | bytes 10616840 | tf_op jit(solution)/shard_map/ppermute | solution.py:98
  236.9 12.9 %collective-permute-start.44 = (bf16[128,1024]{1,0:T(8,128)(2,1)S(1)}, bf16[128,1024]{1,0:T(8,128)(2,1)S(1)}, u32[]{:S(2)}, u32[]{:S(2)}) collective-permute-start(bf16[128,1024]{1,0:T(8,128)(2,1)S(1)} %copy-done.23), channel_id=1, source_target_pairs={{0,1},{1,0},{2,3},{3,2},{4,5},{5,4},{6,7},{7,6},{8,9},{9,8},{10,11... | collective-permute-start | bytes 786440 | tf_op jit(solution)/shard_map/ppermute | solution.py:101
  237.6 21.4 %collective-permute-start.45 = (bf16[128,1024]{1,0:T(8,128)(2,1)S(1)}, bf16[128,1024]{1,0:T(8,128)(2,1)S(1)}, u32[]{:S(2)}, u32[]{:S(2)}) collective-permute-start(bf16[128,1024]{1,0:T(8,128)(2,1)S(1)} %copy-done.23), channel_id=1, source_target_pairs={{0,2},{1,3},{2,0},{3,1},{4,6},{5,7},{6,4},{7,5},{8,10},{9,11},{10,... | collective-permute-start | bytes 786440 | tf_op jit(solution)/shard_map/ppermute | solution.py:101
  238.5 20.5 %collective-permute-start.46 = (bf16[128,1024]{1,0:T(8,128)(2,1)S(1)}, bf16[128,1024]{1,0:T(8,128)(2,1)S(1)}, u32[]{:S(2)}, u32[]{:S(2)}) collective-permute-start(bf16[128,1024]{1,0:T(8,128)(2,1)S(1)} %copy-done.23), channel_id=1, source_target_pairs={{0,3},{1,2},{2,1},{3,0},{4,7},{5,6},{6,5},{7,4},{8,11},{9,10},{10,... | collective-permute-start | bytes 786440 | tf_op jit(solution)/shard_map/ppermute | solution.py:101
  241.5 17.5 %collective-permute-start.40 = (bf16[512,256]{1,0:T(8,128)(2,1)S(1)}, bf16[512,256]{1,0:T(8,128)(2,1)S(1)}, u32[]{:S(2)}, u32[]{:S(2)}) collective-permute-start(bf16[512,256]{1,0:T(8,128)(2,1)S(1)} %fusion.2), channel_id=1, source_target_pairs={{8,0},{12,4},{9,1},{13,5},{10,2},{14,6},{11,3},{15,7},{24,16},{28,... | collective-permute-start | bytes 786440 | tf_op jit(solution)/shard_map/ppermute | solution.py:105
  281.8 20.4 %collective-permute-start.56 = (bf16[3,512,256]{2,1,0:T(8,128)(2,1)S(1)}, bf16[3,512,256]{2,1,0:T(8,128)(2,1)S(1)}, u32[]{:S(2)}, u32[]{:S(2)}) collective-permute-start(bf16[3,512,256]{2,1,0:T(8,128)(2,1)S(1)} %pad_maximum_fusion.4), channel_id=1, source_target_pairs={{0,4},{4,0},{8,12},{12,8},{16,20},{20,16},{24,28},{28,24},{1,5},{5... | collective-permute-start | bytes 2359304 | tf_op jit(solution)/shard_map/ppermute | solution.py:98
  293.4 34.3 %collective-permute-start.47 = (bf16[128,1024]{1,0:T(8,128)(2,1)S(1)}, bf16[128,1024]{1,0:T(8,128)(2,1)S(1)}, u32[]{:S(2)}, u32[]{:S(2)}) collective-permute-start(bf16[128,1024]{1,0:T(8,128)(2,1)S(1)} %get-tuple-element.147), channel_id=1, source_target_pairs={{0,1},{1,0},{2,3},{3,2},{4,5},{5,4},{6,7},{7,6},{8,9},{9,8},{10,11... | collective-permute-start | bytes 786440 | tf_op jit(solution)/shard_map/ppermute | solution.py:101
  295.4 33.2 %collective-permute-start.48 = (bf16[128,1024]{1,0:T(8,128)(2,1)S(1)}, bf16[128,1024]{1,0:T(8,128)(2,1)S(1)}, u32[]{:S(2)}, u32[]{:S(2)}) collective-permute-start(bf16[128,1024]{1,0:T(8,128)(2,1)S(1)} %get-tuple-element.146), channel_id=1, source_target_pairs={{0,2},{1,3},{2,0},{3,1},{4,6},{5,7},{6,4},{7,5},{8,10},{9,11},{10,... | collective-permute-start | bytes 786440 | tf_op jit(solution)/shard_map/ppermute | solution.py:101
  299.6 31.2 %collective-permute-start.49 = (bf16[128,1024]{1,0:T(8,128)(2,1)S(1)}, bf16[128,1024]{1,0:T(8,128)(2,1)S(1)}, u32[]{:S(2)}, u32[]{:S(2)}) collective-permute-start(bf16[128,1024]{1,0:T(8,128)(2,1)S(1)} %get-tuple-element.145), channel_id=1, source_target_pairs={{0,3},{1,2},{2,1},{3,0},{4,7},{5,6},{6,5},{7,4},{8,11},{9,10},{10,... | collective-permute-start | bytes 786440 | tf_op jit(solution)/shard_map/ppermute | solution.py:101
  307.9 25.5 %collective-permute-start.41 = (bf16[128,1024]{1,0:T(8,128)(2,1)S(1)}, bf16[128,1024]{1,0:T(8,128)(2,1)S(1)}, u32[]{:S(2)}, u32[]{:S(2)}) collective-permute-start(bf16[128,1024]{1,0:T(8,128)(2,1)S(1)} %get-tuple-element.151), channel_id=1, source_target_pairs={{0,1},{1,0},{2,3},{3,2},{4,5},{5,4},{6,7},{7,6},{8,9},{9,8},{10,11... | collective-permute-start | bytes 786440 | tf_op jit(solution)/shard_map/ppermute | solution.py:101
  325.5 18.5 %collective-permute-start.42 = (bf16[128,1024]{1,0:T(8,128)(2,1)S(1)}, bf16[128,1024]{1,0:T(8,128)(2,1)S(1)}, u32[]{:S(2)}, u32[]{:S(2)}) collective-permute-start(bf16[128,1024]{1,0:T(8,128)(2,1)S(1)} %get-tuple-element.150), channel_id=1, source_target_pairs={{0,2},{1,3},{2,0},{3,1},{4,6},{5,7},{6,4},{7,5},{8,10},{9,11},{10,... | collective-permute-start | bytes 786440 | tf_op jit(solution)/shard_map/ppermute | solution.py:101
  327.7 26.0 %collective-permute-start.65 = (bf16[3,128,1152]{2,1,0:T(8,128)(2,1)}, bf16[3,128,1152]{2,1,0:T(8,128)(2,1)}, u32[]{:S(2)}, u32[]{:S(2)}) collective-permute-start(bf16[3,128,1152]{2,1,0:T(8,128)(2,1)} %pad_maximum_fusion.3), channel_id=1, source_target_pairs={{0,16},{4,20},{8,24},{12,28},{16,0},{20,4},{24,8},{28,12},{1,17},{... | collective-permute-start | bytes 2654216 | tf_op jit(solution)/shard_map/ppermute | solution.py:98
  328.6 25.1 %collective-permute-start.63 = (bf16[3,128,1152]{2,1,0:T(8,128)(2,1)}, bf16[3,128,1152]{2,1,0:T(8,128)(2,1)}, u32[]{:S(2)}, u32[]{:S(2)}) collective-permute-start(bf16[3,128,1152]{2,1,0:T(8,128)(2,1)} %pad_maximum_fusion.2), channel_id=1, source_target_pairs={{0,8},{4,12},{8,0},{12,4},{16,24},{20,28},{24,16},{28,20},{1,9},{5... | collective-permute-start | bytes 2654216 | tf_op jit(solution)/shard_map/ppermute | solution.py:98
  330.8 14.5 %collective-permute-start.43 = (bf16[128,1024]{1,0:T(8,128)(2,1)S(1)}, bf16[128,1024]{1,0:T(8,128)(2,1)}, u32[]{:S(2)}, u32[]{:S(2)}) collective-permute-start(bf16[128,1024]{1,0:T(8,128)(2,1)S(1)} %get-tuple-element.149), channel_id=1, source_target_pairs={{0,3},{1,2},{2,1},{3,0},{4,7},{5,6},{6,5},{7,4},{8,11},{9,10},{10,... | collective-permute-start | bytes 786440 | tf_op jit(solution)/shard_map/ppermute | solution.py:101
  333.5 15.6 %collective-permute-start.60 = (bf16[3,128,256]{2,1,0:T(8,128)(2,1)}, bf16[3,128,256]{2,1,0:T(8,128)(2,1)}, u32[]{:S(2)}, u32[]{:S(2)}) collective-permute-start(bf16[3,128,256]{2,1,0:T(8,128)(2,1)} %pad_maximum_fusion.8), channel_id=1, source_target_pairs={{0,16},{4,20},{8,24},{12,28},{16,0},{20,4},{24,8},{28,12},{1,17},{... | collective-permute-start | bytes 589832 | tf_op jit(solution)/shard_map/ppermute | solution.py:98
  (73 other events, 618.6 us)

commit v2 on v1

--- a/solution.py
+++ b/solution.py
@@ -7,6 +7,7 @@
 from jax.experimental.pallas import tpu as pltpu
 from jax.sharding import PartitionSpec as P
 
+
 epsilon = 1e-05
 rope_base = 1000000.0
 f32 = jnp.float32
@@ -39,7 +40,7 @@
 SM = pl.BlockSpec(memory_space=pltpu.SMEM)
 
 
-def whole_call(body, outs, args, flops, name, scratch=(), scalars=True):
+def whole_call(body, outs, args, flops, scratch=(), scalars=True):
     moved = sum(math.prod(a.shape) * a.dtype.itemsize for a in list(args) + list(outs))
     specs = [VM] * len(args)
     if scalars:
@@ -51,7 +52,6 @@
         out_specs=[VM] * len(outs),
         scratch_shapes=list(scratch),
         cost_estimate=pl.CostEstimate(flops=int(flops), bytes_accessed=int(moved), transcendentals=0),
-        name=name,
     )(*args)
 
 
@@ -92,7 +92,6 @@
     z = lax.axis_index("tp")
     where = jnp.stack([me, ctx, z]).astype(jnp.int32)
     aligned = blk % 128 == 0
-    row_aligned = R % 128 == 0
 
     def plane(v, mask):
         return lax.ppermute(v, ("dp", "ctx"), [(i, i ^ mask) for i in range(N)])
@@ -107,47 +106,62 @@
     def after(v, *deps):
         return lax.optimization_barrier((v,) + deps)[0]
 
-    def gather_plane(own):
+    def gather_near(own):
         if N == 8:
+            return [own, plane(own, 2), plane(own, 4)]
+        return [own] + [plane(own, r) for r in range(2, N, 2)]
+
+    def gather_far(near):
+        if N == 8:
+            own, fx, fy = near
             half = own.shape[1] // 2
-            fx, fy = plane(own, 2), plane(own, 4)
-            top, low = plane(fx[:, :half], 4), plane(fy[:, half:], 2)
-            mine = jnp.concatenate([own, fx, fy, top, low], axis=1)
-        else:
-            mine = jnp.concatenate([own] + [plane(own, r) for r in range(2, N, 2)], axis=1)
+            top = plane(fx[:, :half], 4)
+            low = plane(fy[:, half:], 2)
+            near = near + [top, low]
+        mine = jnp.concatenate(near, axis=1)
         return mine, plane(mine, 1)
 
-    def scatter_plane(mine, other):
+    def scatter_core(mine, other):
         got = plane(other, 1)
         m = mine.shape[1] * 2 // N
-        parts = [
+        return [
             mine[:, i * m : (i + 1) * m].astype(f32) + got[:, i * m : (i + 1) * m].astype(f32)
             for i in range(N // 2)
         ]
-        if N == 8:
-            half = m // 2
-            far = parts[3].astype(bf16)
-            tx, ty = plane(far[:, :half], 2), plane(far[:, half:], 4)
-            ysend = jnp.concatenate(
-                [parts[2][:, :half] + tx.astype(f32), parts[2][:, half:]], axis=1
-            ).astype(bf16)
-            xsend = jnp.concatenate(
-                [parts[1][:, :half], parts[1][:, half:] + ty.astype(f32)], axis=1
-            ).astype(bf16)
-            return parts[0] + plane(xsend, 2).astype(f32) + plane(ysend, 4).astype(f32)
-        total = parts[0]
-        for i in range(1, N // 2):
-            total = total + plane(parts[i].astype(bf16), 2 * i).astype(f32)
+
+    def scatter_far(parts):
+        if N != 8:
+            return [p.astype(bf16) for p in parts[1:]]
+        half = parts[0].shape[1] // 2
+        far = parts[3].astype(bf16)
+        tx = plane(far[:, :half], 2)
+        ty = plane(far[:, half:], 4)
+        ysend = jnp.concatenate(
+            [parts[2][:, :half] + tx.astype(f32), parts[2][:, half:]], axis=1
+        ).astype(bf16)
+        xsend = jnp.concatenate(
+            [parts[1][:, :half], parts[1][:, half:] + ty.astype(f32)], axis=1
+        ).astype(bf16)
+        return [xsend, ysend]
+
+    def scatter_near(own, sends):
+        total = own
+        for i, v in enumerate(sends):
+            total = total + plane(v, 2 * (i + 1)).astype(f32)
         return total
 
     def gather_column(own):
         return [own] + [column(own, k) for k in range(1, NT)]
 
-    def spread_column(full):
-        return [full[:R]] + [column(full[k * R : (k + 1) * R], k) for k in range(1, NT)]
-
-    def slots(ref_rows, fallback):
-        return fallback
+    def spread_column(pieces):
+        return [pieces[0]] + [column(pieces[k], k) for k in range(1, NT)]
+
+    def put_slots(refs, value):
+        for k, ref in enumerate(refs):
+            ref[...] = value[k * R : (k + 1) * R].astype(ref.dtype)
+
+    def join_slots(refs):
+        return jnp.concatenate([ref[...] for ref in refs], axis=0)
 
     def take_cols(v, index, size, order):
         picks = index ^ jnp.array(order, jnp.int32)
@@ -180,18 +194,15 @@
         [sds((R, W), bf16), sds((R, W), bf16), sds((R, W), bf16), sds((2, W), f32)],
         (where, t_in, c_in, g_in),
         R * W * 8,
-        "pre",
     )
     first_pieces = gather_column(normed)
-    qkv_m, qkv_o = gather_plane(own_qkv)
-    rows_first = jnp.concatenate(first_pieces, axis=0)
-
-    out_cols = jnp.concatenate(gather_column(own_out), axis=1)
-    out_m, out_o = gather_plane(after(out_cols, qkv_o)[None])
+    qkv_near = gather_near(after(own_qkv, normed))
+    qkv_m, qkv_o = gather_far(qkv_near)
     own_ffn = jnp.stack([gate_weight, up_weight, down_weight.T])
-    ffn_m, ffn_o = gather_plane(after(own_ffn, qkv_o))
-
-    cot_rows = jnp.concatenate(gather_column(after(cot, rows_first)), axis=0)
+    ffn_near = gather_near(after(own_ffn, *qkv_near))
+
+    out_cols = jnp.concatenate(gather_column(after(own_out, *first_pieces)), axis=1)
+    cot_pieces = gather_column(after(cot, *first_pieces))
 
     half_width = hw // 2
     freq = jnp.exp(jnp.arange(half_width, dtype=f32) * (-2.0 * math.log(rope_base) / hw))
@@ -215,8 +226,10 @@
             first, pltpu.roll(x, x.shape[1] - half_width, 1), pltpu.roll(x, half_width, 1)
         )
 
-    def qkv_body(r_ref, wm, wo, cs, sn, qg_ref, kg_ref, rq, pr, q_raw, p_raw):
-        left, right = r_ref[:, :H], r_ref[:, H:]
+    def qkv_body(*refs):
+        wm, wo, cs, sn, qg_ref, kg_ref, rq, pr, q_raw, p_raw = refs[NT:]
+        rows = join_slots(refs[:NT])
+        left, right = rows[:, :H], rows[:, H:]
         q = mm(left, wm[0]) + mm(right, wo[0])
         p = mm(left, wm[1]) + mm(right, wo[1])
         q_raw[...] = q
@@ -230,9 +243,8 @@
     rot_q, pair, q_raw, p_raw = whole_call(
         qkv_body,
         [sds((B, C), bf16), sds((B, C), bf16), sds((B, C), f32), sds((B, C), f32)],
-        (rows_first, qkv_m, qkv_o, cosine, sine, qg, kg),
+        (*first_pieces, qkv_m, qkv_o, cosine, sine, qg, kg),
         4 * B * W * C,
-        "qkv",
         scalars=False,
     )
 
@@ -240,8 +252,9 @@
     kv_even = [pair] + [along(pair, r, earlier) for r in range(2, NC, 2)]
     kv_odd = [along(pair, 1, earlier)]
     for r in range(2, NC, 2):
-        kv_odd.append(along(kv_even[r // 2], 1, lambda i, j: (i ^ 1 ^ j) == 0 and (i ^ r) < i))
+        kv_odd.append(along(kv_even[r // 2], 1, lambda i, j: (i ^ r) < i))
     kv_all = jnp.stack([v for pq in zip(kv_even, kv_odd) for v in pq])
+    out_m, out_o = gather_far(gather_near(out_cols[None]))
 
     def widen(x, part):
         moved = x if part == 0 else pltpu.roll(x, hw, 1)
@@ -256,7 +269,8 @@
         qry = lanes((B, B)) ^ zz
         return key <= qry
 
-    def fwd_body(s_ref, q_ref, kv_ref, att_ref, lse_ref, qz, acc, tot):
+    def fwd_body(s_ref, q_ref, kv_ref, *refs):
+        slot_refs, (att_ref, lse_ref, qz, acc, tot) = refs[:NT], refs[NT:]
         r, h = pl.program_id(0), pl.program_id(1)
         here = s_ref[1]
 
@@ -294,18 +308,20 @@
         @pl.when((r == NC - 1) & (h == KH - 1))
         def _():
             outs = [acc[hd][hw:] / tot[hd][0:1] for hd in range(QH)]
-            att_ref[...] = jnp.concatenate(outs, axis=0).T.astype(bf16)
+            att = jnp.concatenate(outs, axis=0).T.astype(bf16)
+            att_ref[...] = att
+            put_slots(slot_refs, att)
             for hd in range(QH):
                 lse_ref[hd : hd + 1] = jnp.log(tot[hd][0:1])
 
     fixed = lambda shape: pl.BlockSpec(shape, lambda r, h: (0,) * len(shape))
     kv_spec = pl.BlockSpec((1, B, pw), lambda r, h: (r, 0, h))
-    attended, lse = pl.pallas_call(
+    *att_slots, attended, lse = pl.pallas_call(
         fwd_body,
         grid=(NC, KH),
-        out_shape=[sds((B, C), bf16), sds((QH, B), f32)],
+        out_shape=[sds((R, C), bf16)] * NT + [sds((B, C), bf16), sds((QH, B), f32)],
         in_specs=[SM, fixed((B, C)), kv_spec],
-        out_specs=[fixed((B, C)), fixed((QH, B))],
+        out_specs=[fixed((R, C))] * NT + [fixed((B, C)), fixed((QH, B))],
         scratch_shapes=[
             pltpu.VMEM((QH, B, pw), bf16),
             pltpu.VMEM((QH, pw, B), f32),
@@ -317,7 +333,9 @@
         name="attention_forward",
     )(where, rot_q, kv_all)
 
-    att_pieces = spread_column(attended)
+    att_pieces = spread_column(att_slots)
+    _, *ffn_near = lax.optimization_barrier((attended, *ffn_near))
+    ffn_m, ffn_o = gather_far(list(ffn_near))
 
     def out_body(*refs):
         pieces, (om, oo, t_ref, g_ref, res, nrm) = refs[:NT], refs[NT:]
@@ -332,16 +350,25 @@
         [sds((R, W), f32), sds((R, W), bf16)],
         (*att_pieces, out_m, out_o, tok, gain2),
         2 * R * W * W,
-        "out_norm",
         scalars=False,
     )
-    rows_second = jnp.concatenate(gather_column(normed_f), axis=0)
+    second_pieces = gather_column(normed_f)
 
     FB = 384 if F % 384 == 0 else F
     steps = F // FB
 
-    def ffn_body(r_ref, c_ref, wm, wo, out, gnf, mid_r, dg_r, du_r, acc_o, acc_g):
+    def ffn_body(*refs):
+        r_in, c_in, (wm, wo) = refs[:NT], refs[NT : 2 * NT], refs[2 * NT : 2 * NT + 2]
+        refs = refs[2 * NT + 2 :]
+        outs, gnfs = refs[:NT], refs[NT : 2 * NT]
+        mid_r, dg_r, du_r, r_ref, c_ref, acc_o, acc_g = refs[2 * NT :]
         i = pl.program_id(0)
+
+        @pl.when(i == 0)
+        def _():
+            r_ref[...] = join_slots(r_in)
+            c_ref[...] = join_slots(c_in)
+
         rl, rr = r_ref[:, :H], r_ref[:, H:]
         gate = mm(rl, wm[0]) + mm(rr, wo[0])
         up = mm(rl, wm[1]) + mm(rr, wo[1])
@@ -370,28 +397,55 @@
 
         @pl.when(i == steps - 1)
         def _():
-            out[...] = acc_o[...].astype(bf16)
-            gnf[...] = acc_g[...].astype(bf16)
+            put_slots(outs, acc_o)
+            put_slots(gnfs, acc_g)
 
     one = lambda shape: pl.BlockSpec(shape, lambda i: (0,) * len(shape))
     wide = pl.BlockSpec((B, FB), lambda i: (0, i))
     w_spec = pl.BlockSpec((3, H, FB), lambda i: (0, 0, i))
-    ffn_part, gnf_part, mid, dgate, dup = pl.pallas_call(
+    *ffn_slots, mid, dgate, dup = pl.pallas_call(
         ffn_body,
         grid=(steps,),
-        out_shape=[sds((B, W), bf16), sds((B, W), bf16)] + [sds((B, F), bf16)] * 3,
-        in_specs=[one((B, W)), one((B, W)), w_spec, w_spec],
-        out_specs=[one((B, W)), one((B, W)), wide, wide, wide],
-        scratch_shapes=[pltpu.VMEM((B, W), f32)] * 2,
+        out_shape=[sds((R, W), bf16)] * (2 * NT) + [sds((B, F), bf16)] * 3,
+        in_specs=[one((R, W))] * (2 * NT) + [w_spec, w_spec],
+        out_specs=[one((R, W))] * (2 * NT) + [wide, wide, wide],
+        scratch_shapes=[pltpu.VMEM((B, W), bf16)] * 2 + [pltpu.VMEM((B, W), f32)] * 2,
         cost_estimate=pl.CostEstimate(
             flops=12 * B * W * F, bytes_accessed=6 * W * F + 6 * B * F, transcendentals=B * F
         ),
         name="ffn",
-    )(rows_second, cot_rows, ffn_m, ffn_o)
-    gnf_pieces = spread_column(gnf_part)
+    )(*second_pieces, *cot_pieces, ffn_m, ffn_o)
+    gnf_pieces = spread_column(ffn_slots[NT:])
+
+    def dw_body(*refs):
+        r_in, c_in, (mid_r, dg_r, du_r, gm, go, rt, ct) = refs[:NT], refs[NT : 2 * NT], refs[2 * NT :]
+
+        @pl.when(pl.program_id(0) == 0)
+        def _():
+            rt[...] = join_slots(r_in).T
+            ct[...] = join_slots(c_in).T
+
+        for k, (lhs, rhs) in enumerate(((rt, dg_r), (rt, du_r), (ct, mid_r))):
+            gm[k] = mm(lhs[:H], rhs[...]).astype(bf16)
+            go[k] = mm(lhs[H:], rhs[...]).astype(bf16)
+
+    dwf_m, dwf_o = pl.pallas_call(
+        dw_body,
+        grid=(steps,),
+        out_shape=[sds((3, H, F), bf16)] * 2,
+        in_specs=[one((R, W))] * (2 * NT) + [wide, wide, wide],
+        out_specs=[w_spec, w_spec],
+        scratch_shapes=[pltpu.VMEM((W, B), bf16)] * 2,
+        cost_estimate=pl.CostEstimate(
+            flops=6 * B * W * F, bytes_accessed=6 * W * F + 6 * B * F, transcendentals=0
+        ),
+        name="ffn_weights",
+    )(*second_pieces, *cot_pieces, mid, dgate, dup)
+    ffn_parts = scatter_core(dwf_m, dwf_o)
+    gnf_pieces, ffn_parts = lax.optimization_barrier((gnf_pieces, ffn_parts))
 
     def back_body(*refs):
-        pieces, (res, c_ref, g_ref, om, oo, gres, rg, ga, gg) = refs[:NT], refs[NT:]
+        pieces, (res, c_ref, g_ref, om, oo, gres, rg, gg, *gas) = refs[:NT], refs[NT:]
         grad = sum(p[...].astype(f32) for p in pieces)
         x = res[...]
         inv = lax.rsqrt(jnp.mean(x * x, axis=-1, keepdims=True) + epsilon)
@@ -403,44 +457,22 @@
         gres[...] = total
         half = total.astype(bf16)
         rg[...] = half
-        ga[...] = (mm(half[:, :H], om[0]) + mm(half[:, H:], oo[0])).astype(bf16)
-
-    grad_resid, rg16, ga_full, ffn_gain_part = whole_call(
+        ga = (mm(half[:, :H], om[0]) + mm(half[:, H:], oo[0])).astype(bf16)
+        for k, ref in enumerate(gas):
+            ref[...] = ga[:, k * C : (k + 1) * C]
+
+    grad_resid, rg16, ffn_gain_part, *ga_slots = whole_call(
         back_body,
-        [sds((R, W), f32), sds((R, W), bf16), sds((R, W), bf16), sds((1, W), f32)],
+        [sds((R, W), f32), sds((R, W), bf16), sds((1, W), f32)] + [sds((R, C), bf16)] * NT,
         (*gnf_pieces, resid, cot, gain2, out_m, out_o),
         2 * R * W * W,
-        "second_back",
         scalars=False,
     )
-    ga_pieces = [ga_full[:, :C]] + [
-        column(ga_full[:, k * C : (k + 1) * C], k) for k in range(1, NT)
-    ]
+    ga_pieces = spread_column(ga_slots)
     grad_att = jnp.concatenate(ga_pieces, axis=0)
-
-    def dw_body(r_ref, c_ref, mid_r, dg_r, du_r, gm, go, rt, ct):
-        @pl.when(pl.program_id(0) == 0)
-        def _():
-            rt[...] = r_ref[...].T
-            ct[...] = c_ref[...].T
-
-        for k, (lhs, rhs) in enumerate(((rt, dg_r), (rt, du_r), (ct, mid_r))):
-            gm[k] = mm(lhs[:H], rhs[...]).astype(bf16)
-            go[k] = mm(lhs[H:], rhs[...]).astype(bf16)
-
-    dwf_m, dwf_o = pl.pallas_call(
-        dw_body,
-        grid=(steps,),
-        out_shape=[sds((3, H, F), bf16)] * 2,
-        in_specs=[one((B, W)), one((B, W)), wide, wide, wide],
-        out_specs=[w_spec, w_spec],
-        scratch_shapes=[pltpu.VMEM((W, B), bf16)] * 2,
-        cost_estimate=pl.CostEstimate(
-            flops=6 * B * W * F, bytes_accessed=6 * W * F + 6 * B * F, transcendentals=0
-        ),
-        name="ffn_weights",
-    )(rows_second, cot_rows, mid, dgate, dup)
-    ffn_sum = scatter_plane(dwf_m, dwf_o)
+    ffn_sends = scatter_far(ffn_parts)
+    grad_att, ffn_sends = lax.optimization_barrier((grad_att, ffn_sends))
+    ffn_sum = scatter_near(ffn_parts[0], ffn_sends)
 
     def bwd_body(s_ref, q_ref, d_ref, a_ref, l_ref, kv_ref, dq_ref, dkv_ref, qz, dz, acc, dl):
         r, h = pl.program_id(0), pl.program_id(1)
@@ -515,38 +547,22 @@
         name="attention_backward",
     )(where, rot_q, grad_att, attended, lse[:, None, :], kv_all)
 
-    later = lambda i, j: i > j
     odd = lax.ppermute(dkv[1::2], "ctx", [(i, i ^ 1) for i in range(NC)])
     pair_sum = dkv[0].astype(f32) + odd[0].astype(f32)
     for k in range(1, NC // 2):
         part = (dkv[2 * k].astype(f32) + odd[k].astype(f32)).astype(bf16)
         pair_sum = pair_sum + along(part, 2 * k, lambda i, j: i // 2 > j // 2).astype(f32)
 
-    rg_rows = jnp.concatenate(gather_column(after(rg16, grad_att)), axis=0)
-    ffn_pieces = spread_column(after(ffn_part, rg_rows))
-
-    def dwo_body(g_ref, a_ref, gm, go):
-        a = a_ref[...]
-        gm[0] = lax.dot_general(
-            g_ref[:, :H], a, (((0,), (0,)), ((), ())), preferred_element_type=f32
-        ).astype(bf16)
-        go[0] = lax.dot_general(
-            g_ref[:, H:], a, (((0,), (0,)), ((), ())), preferred_element_type=f32
-        ).astype(bf16)
-
-    dwo_m, dwo_o = whole_call(
-        dwo_body,
-        [sds((1, H, C), bf16)] * 2,
-        (rg_rows, attended),
-        2 * B * W * C,
-        "output_weights",
-        scalars=False,
-    )
+    rg_rows = gather_column(after(rg16, grad_att))
+    out_slots = list(lax.optimization_barrier((*ffn_slots[:NT], grad_att))[:NT])
+    ffn_pieces = spread_column(out_slots)
 
     def qk_body(
-        dq, dp, q_raw_r, p_raw_r, cs, sn, qg_ref, kg_ref, r_ref, wm, wo, g_ref,
-        gna, gm, go, qgg, kgg, agg,
+        dq, dp, q_raw_r, p_raw_r, cs, sn, qg_ref, kg_ref, wm, wo, g_ref, *refs
     ):
+        r_in, gnas, (gm, go, qgg, kgg, agg) = refs[:NT], refs[NT : 2 * NT], refs[2 * NT :]
+        r_all = join_slots(r_in)
+
         def back(grad, raw, gain, live):
             turned = grad * cs[...] - swap_halves(grad) * sn[...]
             inv = lax.rsqrt(head_mean(raw * raw) + epsilon)
@@ -566,8 +582,9 @@
         both = jnp.concatenate([gq, gp], axis=1)
         for w, cols, gw in ((wm, slice(0, H), gm), (wo, slice(H, W), go)):
             part = mm_nt(gq, w[0]) + mm_nt(gp, w[1])
-            gna[:, cols] = part.astype(bf16)
-            rows = r_ref[:, cols]
+            for k, ref in enumerate(gnas):
+                ref[:, cols] = part[k * R : (k + 1) * R].astype(bf16)
+            rows = r_all[:, cols]
             agg[:, cols] = (
                 jnp.sum(part * rows.astype(f32), axis=0, keepdims=True) / g_ref[0:1, cols]
             )
@@ -577,10 +594,10 @@
             gw[0] = full[:, :C]
             gw[1] = full[:, C:]
 
-    gna_part, dwq_m, dwq_o, qg_part, kg_part, att_gain_part = whole_call(
+    *gna_slots, dwq_m, dwq_o, qg_part, kg_part, att_gain_part = whole_call(
         qk_body,
         [
-            sds((B, W), bf16),
+            *[sds((R, W), bf16)] * NT,
             sds((2, H, C), bf16),
             sds((2, H, C), bf16),
             sds((1, C), f32),
@@ -589,16 +606,32 @@
         ],
         (
             grad_rot_q, pair_sum, q_raw, p_raw, cosine, sine, qg, kg,
-            rows_first, qkv_m, qkv_o, gain2,
+            qkv_m, qkv_o, gain2, *first_pieces,
         ),
         8 * B * W * C,
-        "projections_back",
         scalars=False,
     )
-    gna_pieces = spread_column(gna_part)
+    gna_pieces = spread_column(gna_slots)
+    rg_rows = lax.optimization_barrier((*rg_rows, *gna_slots))[:NT]
+
+    def dwo_body(*refs):
+        a_ref, gm, go = refs[NT:]
+        a, g = a_ref[...], join_slots(refs[:NT])
+        gm[0] = lax.dot_general(
+            g[:, :H], a, (((0,), (0,)), ((), ())), preferred_element_type=f32
+        ).astype(bf16)
+        go[0] = lax.dot_general(
+            g[:, H:], a, (((0,), (0,)), ((), ())), preferred_element_type=f32
+        ).astype(bf16)
+
+    dwo_m, dwo_o = whole_call(
+        dwo_body, [sds((1, H, C), bf16)] * 2, (*rg_rows, attended), 2 * B * W * C, scalars=False
+    )
+
     last_m = jnp.concatenate([dwq_m, dwo_m], axis=0)
     last_o = jnp.concatenate([dwq_o, dwo_o], axis=0)
-    att_sum = scatter_plane(last_m, last_o)
+    att_parts = scatter_core(last_m, last_o)
+    att_sum = scatter_near(att_parts[0], scatter_far(att_parts))
 
     order_back = masks
     inverse_order = [order_back.index(m) for m in range(N)]
@@ -635,12 +668,14 @@
             gt[:, dst] = total[:, src]
             bo[:, dst] = block[:, src]
 
+    gna_pieces, att_sum, ffn_sum, packed = lax.optimization_barrier(
+        (gna_pieces, att_sum, ffn_sum, packed)
+    )
     grad_tokens, block_out = whole_call(
         end_body,
         [sds((R, W), f32), sds((R, W), bf16)],
         (where, *gna_pieces, *ffn_pieces, tok, resid, grad_resid, gain2),
         R * W * 16,
-        "end",
     )
     if not aligned:
         back_cols = lambda v: jnp.take(
@@ -698,6 +733,7 @@
         P(("dp", "ctx"), "tp"),
         P("tp", ("dp", "ctx")),
     )
+
     return jax.shard_map(
         on_device, mesh=mesh, in_specs=in_specs, out_specs=out_specs, check_vma=False
     )

time: 359 us -> 369 us (1.028)
  waiting for transfers between devices: 125 us -> 140 us
  local copies, waits for them, and re-layouts: 40.4 us -> 28.1 us
    ppermute x4, waiting for transfers between devices: 3.09 us -> 20.6 us  [along(): return lax.ppermute(v, 'ctx', pairs)]
    ppermute x33, waiting for transfers between devices: 82.7 us -> 67.1 us  [column(): return lax.ppermute(v, 'tp', [(i, i ^ mask) for i in range(NT)])]
    ppermute x28, waiting for transfers between devices: 39.2 us -> 51.1 us  [plane(): return lax.ppermute(v, ('dp', 'ctx'), [(i, i ^ mask) for i in range(N)])]
    unnamed x106 -> x94, local copies, waits for them, and re-layouts: 19.2 us -> 11.2 us
    slice x17 -> x12, local copies, waits for them, and re-layouts: 8.43 us -> 3.48 us  [the longest x2 1.23 us: scatter_far(): parts[1][:, :half]]
  transfers between devices with their start and end apart: 66 -> 66, of which waited for: 30 -> 32; matrix products, arithmetic and copies ran while one was open for 14% -> 11% of each run, Pallas kernels for 11% -> 7%
where the time goes in v2:
time: 369 us; the launch traced here: 366 us
  waiting for transfers between devices  140 us (38%)
  starting transfers between devices  103 us (28%)
  Pallas kernels  68.9 us (19%)
  local copies, waits for them, and re-layouts  28.1 us (8%)
  other arithmetic  24.9 us (7%)
    ppermute x33, waiting for transfers between devices, column(): return lax.ppermute(v, 'tp', [(i, i ^ mask) for i in range(NT)])  67.1 us
    ppermute x33, starting transfers between devices, column(): return lax.ppermute(v, 'tp', [(i, i ^ mask) for i in range(NT)])  60.8 us
    ppermute x28, waiting for transfers between devices, plane(): return lax.ppermute(v, ('dp', 'ctx'), [(i, i ^ mask) for i in range(N)])  51.1 us
    ppermute x28, starting transfers between devices, plane(): return lax.ppermute(v, ('dp', 'ctx'), [(i, i ^ mask) for i in range(N)])  34 us
    pallas_call x6, Pallas kernels, whole_call(): pl.pallas_call(body, out_shape=list(outs), in_specs=specs, out_specs=[VM]...  24.9 us
    ppermute x4, waiting for transfers between devices, along(): return lax.ppermute(v, 'ctx', pairs)  20.6 us
    pallas_call x1, Pallas kernels, on_device(): pl.pallas_call(ffn_body, grid=(steps,), out_shape=[sds((R, W), bf16)] * (...  17 us
    unnamed x94, local copies, waits for them, and re-layouts  11.2 us
  transfers between devices with their start and end apart: 66, of which 32 were waited for; matrix products, arithmetic and copies ran while one was open for 11% of the time, Pallas kernels for 7%

profile of v2, /device:TPU:0, one launch (start us, length us, event | category | flops | bytes accessed | tf_op | source)
XLA Modules:
  0.0 365.9 jit_solution(9008811233603715390)
XLA Ops:
  30.2 5.0 %shard_map.229 = (bf16[512,256]{1,0:T(8,128)(2,1)}, bf16[512,256]{1,0:T(8,128)(2,1)}, f32[512,256]{1,0:T(8,128)}, f32[512,256]{1,0:T(8,128)}) custom-call(bf16[128,1024]{1,0:T(8,128)(2,1)} %get-tuple-element.98.refs_0_, bf16[128,1024]{1,0:T(8,128)(2,1)} %copy-done.6, bf16[128,1024]{1,0:T(8,128)(2,1)} %copy-done.7, ...), custom_call_target="tpu_custom_call" | custom-call | flops 536870912 | bytes 4720640 | tf_op jit(solution)/shard_map/pallas_call | solution.py:48
  35.2 3.8 %collective-permute-start.9 = (bf16[512,256]{1,0:T(8,128)(2,1)}, bf16[512,256]{1,0:T(8,128)(2,1)S(1)}, u32[]{:S(2)}, u32[]{:S(2)}) collective-permute-start(bf16[512,256]{1,0:T(8,128)(2,1)} %get-tuple-element.101), channel_id=1, source_target_pairs={{0,8},{4,12},{1,9},{5,13},{2,10},{6,14},{3,11},{7,15},{16,24},{20,... | collective-permute-start | bytes 786440 | tf_op jit(solution)/shard_map/ppermute | solution.py:104
  40.6 13.3 %collective-permute-done.9 = bf16[512,256]{1,0:T(8,128)(2,1)S(1)} collective-permute-done((bf16[512,256]{1,0:T(8,128)(2,1)}, bf16[512,256]{1,0:T(8,128)(2,1)S(1)}, u32[]{:S(2)}, u32[]{:S(2)}) %collective-permute-start.9) | collective-permute-done | bytes 262176 | tf_op jit(solution)/shard_map/ppermute | solution.py:104
  56.8 7.0 %attention_forward.1 = (bf16[128,256]{1,0:T(8,128)(2,1)}, bf16[128,256]{1,0:T(8,128)(2,1)}, bf16[128,256]{1,0:T(8,128)(2,1)}, bf16[128,256]{1,0:T(8,128)(2,1)}, ...) custom-call(s32[3]{0:T(128)} %pad_add_fusion.s_ref.refs_0_, bf16[512,256]{1,0:T(8,128)(2,1)} %get-tuple-element.100.q_ref, ...), custom_call_target="tpu_custom_call" | custom-call | flops 2147483648 | bytes 1048576 | tf_op jit(solution)/shard_map/attention_forward/pallas_call | solution.py:319
  66.9 6.6 %collective-permute-start.31 = (bf16[3,64,1152]{2,1,0:T(8,128)(2,1)S(1)}, bf16[3,64,1152]{2,1,0:T(8,128)(2,1)S(1)}, u32[]{:S(2)}, u32[]{:S(2)}) collective-permute-start(bf16[3,64,1152]{2,1,0:T(8,128)(2,1)S(1)} %slice.159), channel_id=1, source_target_pairs={{0,8},{4,12},{8,0},{12,4},{16,24},{20,28},{24,16},{28,20},{1,9},{5... | collective-permute-start | bytes 1327112 | tf_op jit(solution)/shard_map/ppermute | solution.py:97
  78.3 6.2 %collective-permute-done.31 = bf16[3,64,1152]{2,1,0:T(8,128)(2,1)S(1)} collective-permute-done((bf16[3,64,1152]{2,1,0:T(8,128)(2,1)S(1)}, bf16[3,64,1152]{2,1,0:T(8,128)(2,1)S(1)}, u32[]{:S(2)}, u32[]{:S(2)}) %collective-permute-start.31) | collective-permute-done | bytes 442400 | tf_op jit(solution)/shard_map/ppermute | solution.py:97
  85.6 3.7 %collective-permute-start.16 = (bf16[128,256]{1,0:T(8,128)(2,1)S(1)}, bf16[128,256]{1,0:T(8,128)(2,1)S(1)}, u32[]{:S(2)}, u32[]{:S(2)}) collective-permute-start(bf16[128,256]{1,0:T(8,128)(2,1)S(1)} %bitcast.79), channel_id=1, source_target_pairs={{0,3},{1,2},{2,1},{3,0},{4,7},{5,6},{6,5},{7,4},{8,11},{9,10},{10,... | collective-permute-start | bytes 196616 | tf_op jit(solution)/shard_map/ppermute | solution.py:100
  97.9 4.9 %collective-permute-done.17 = bf16[1,128,1024]{2,1,0:T(8,128)(2,1)S(1)} collective-permute-done((bf16[1,128,1024]{2,1,0:T(8,128)(2,1)S(1)}, bf16[1,128,1024]{2,1,0:T(8,128)(2,1)S(1)}, u32[]{:S(2)}, u32[]{:S(2)}) %collective-permute-start.17) | collective-permute-done | bytes 262176 | tf_op jit(solution)/shard_map/ppermute | solution.py:97
  113.2 11.2 %collective-permute-done.11.refs_1_ = bf16[128,256]{1,0:T(8,128)(2,1)S(1)} collective-permute-done((bf16[128,256]{1,0:T(8,128)(2,1)S(1)}, bf16[128,256]{1,0:T(8,128)(2,1)S(1)}, u32[]{:S(2)}, u32[]{:S(2)}) %collective-permute-start.11) | collective-permute-done | bytes 65568 | tf_op jit(solution)/shard_map/ppermute | solution.py:100
  126.9 3.3 collective-permute-done.12.refs_2_
  130.2 3.4 collective-permute-start.13
  136.4 3.4 collective-permute-start.27
  140.8 3.4 shard_map.230
  145.2 3.4 collective-permute-start.24
  148.6 4.9 %collective-permute-done.22.refs_1_ = bf16[128,1024]{1,0:T(8,128)(2,1)S(1)} collective-permute-done((bf16[128,1024]{1,0:T(8,128)(2,1)}, bf16[128,1024]{1,0:T(8,128)(2,1)S(1)}, u32[]{:S(2)}, u32[]{:S(2)}) %collective-permute-start.22) | collective-permute-done | bytes 262176 | tf_op jit(solution)/shard_map/ppermute | solution.py:100
  153.6 12.6 %collective-permute-done.23.refs_2_ = bf16[128,1024]{1,0:T(8,128)(2,1)S(1)} collective-permute-done((bf16[128,1024]{1,0:T(8,128)(2,1)}, bf16[128,1024]{1,0:T(8,128)(2,1)S(1)}, u32[]{:S(2)}, u32[]{:S(2)}) %collective-permute-start.23) | collective-permute-done | bytes 262176 | tf_op jit(solution)/shard_map/ppermute | solution.py:100
  166.9 17.0 %ffn.1 = (bf16[128,1024]{1,0:T(8,128)(2,1)}, bf16[128,1024]{1,0:T(8,128)(2,1)}, bf16[128,1024]{1,0:T(8,128)(2,1)}, bf16[128,1024]{1,0:T(8,128)(2,1)}, bf16[128,1...) custom-call(bf16[128,1024]{1,0:T(8,128)(2,1)} %get-tuple-element.109, ...), custom_call_target="tpu_custom_call" | custom-call | flops 7247757312 | bytes 10616832 | tf_op jit(solution)/shard_map/ffn/pallas_call | solution.py:406
  183.9 9.4 %ffn_weights.1 = (bf16[3,512,1152]{2,1,0:T(8,128)(2,1)}, bf16[3,512,1152]{2,1,0:T(8,128)(2,1)}) custom-call(bf16[128,1024]{1,0:T(8,128)(2,1)} %get-tuple-element.109.refs_0_, bf16[128,1024]{1,0:T(8,128)(2,1)} %copy-done.32, bf16[128,1024]{1,0:T(8,128)(2,1)} %copy-done.33, bf16[128,1024]{1,0:T(8,128)(2,1)} %copy-done.34, ...), custom_call_target="tpu_custom_call" | custom-call | flops 3623878656 | bytes 10616832 | tf_op jit(solution)/shard_map/ffn_weights/pallas_call | solution.py:432
  193.4 4.5 %collective-permute-start.33 = (bf16[128,1024]{1,0:T(8,128)(2,1)}, bf16[128,1024]{1,0:T(8,128)(2,1)S(1)}, u32[]{:S(2)}, u32[]{:S(2)}) collective-permute-start(bf16[128,1024]{1,0:T(8,128)(2,1)} %get-tuple-element.118), channel_id=1, source_target_pairs={{0,1},{1,0},{2,3},{3,2},{4,5},{5,4},{6,7},{7,6},{8,9},{9,8},{10,11... | collective-permute-start | bytes 786440 | tf_op jit(solution)/shard_map/ppermute | solution.py:100
  200.4 3.6 convert_add_fusion.2
  205.3 4.7 %collective-permute-done.33.refs_1_ = bf16[128,1024]{1,0:T(8,128)(2,1)S(1)} collective-permute-done((bf16[128,1024]{1,0:T(8,128)(2,1)}, bf16[128,1024]{1,0:T(8,128)(2,1)S(1)}, u32[]{:S(2)}, u32[]{:S(2)}) %collective-permute-start.33) | collective-permute-done | bytes 262176 | tf_op jit(solution)/shard_map/ppermute | solution.py:100
  210.1 9.4 %collective-permute-done.34.refs_2_ = bf16[128,1024]{1,0:T(8,128)(2,1)S(1)} collective-permute-done((bf16[128,1024]{1,0:T(8,128)(2,1)}, bf16[128,1024]{1,0:T(8,128)(2,1)S(1)}, u32[]{:S(2)}, u32[]{:S(2)}) %collective-permute-start.34) | collective-permute-done | bytes 262176 | tf_op jit(solution)/shard_map/ppermute | solution.py:100
  221.7 3.5 shard_map.231
  227.5 4.6 %collective-permute-start.38 = (bf16[128,256]{1,0:T(8,128)(2,1)}, bf16[128,256]{1,0:T(8,128)(2,1)S(1)}, u32[]{:S(2)}, u32[]{:S(2)}) collective-permute-start(bf16[128,256]{1,0:T(8,128)(2,1)} %get-tuple-element.133), channel_id=1, source_target_pairs={{0,2},{1,3},{2,0},{3,1},{4,6},{5,7},{6,4},{7,5},{8,10},{9,11},{10,... | collective-permute-start | bytes 196616 | tf_op jit(solution)/shard_map/ppermute | solution.py:100
  240.2 4.5 %collective-permute-done.41 = bf16[3,64,1152]{2,1,0:T(8,128)(2,1)S(1)} collective-permute-done((bf16[3,64,1152]{2,1,0:T(8,128)(2,1)}, bf16[3,64,1152]{2,1,0:T(8,128)(2,1)S(1)}, u32[]{:S(2)}, u32[]{:S(2)}) %collective-permute-start.41) | collective-permute-done | bytes 442400 | tf_op jit(solution)/shard_map/ppermute | solution.py:97
  245.8 10.5 %attention_backward.1 = (f32[512,256]{1,0:T(8,128)}, bf16[4,512,256]{2,1,0:T(8,128)(2,1)}) custom-call(s32[3]{0:T(128)} %pad_add_fusion.s_ref.refs_0_, bf16[512,256]{1,0:T(8,128)(2,1)} %get-tuple-element.100.q_ref, bf16[512,256]{1,0:T(8,128)(2,1)} %pad_maximum_fusion.5.d_ref, bf16[512,256]{1,0:T(8,128)(2,1)} %get-tuple-element.112.a_ref, ...), custom_call_target="tpu_custom_call" | custom-call | flops 5368709120 | bytes 2097152 | tf_op jit(solution)/shard_map/attention_backward/pallas_call | solution.py:532
  266.5 7.4 %collective-permute-done.43 = bf16[512,256]{1,0:T(8,128)(2,1)S(1)} collective-permute-done((bf16[512,256]{1,0:T(8,128)(2,1)S(1)}, bf16[512,256]{1,0:T(8,128)(2,1)S(1)}, u32[]{:S(2)}, u32[]{:S(2)}) %collective-permute-start.43) | collective-permute-done | bytes 262176 | tf_op jit(solution)/shard_map/ppermute | solution.py:104
  275.7 7.6 %shard_map.232 = (bf16[128,1024]{1,0:T(8,128)(2,1)}, bf16[128,1024]{1,0:T(8,128)(2,1)}, bf16[128,1024]{1,0:T(8,128)(2,1)}, bf16[128,1024]{1,0:T(8,128)(2,1)}, bf...) custom-call(f32[512,256]{1,0:T(8,128)} %get-tuple-element.140.dq, ...), custom_call_target="tpu_custom_call" | custom-call | flops 1073741824 | bytes 7356416 | tf_op jit(solution)/shard_map/pallas_call | solution.py:48
  306.7 15.1 %collective-permute-done.62 = f32[17,128]{1,0:T(8,128)S(1)} collective-permute-done((f32[17,128]{1,0:T(8,128)S(1)}, f32[17,128]{1,0:T(8,128)S(1)}, u32[]{:S(2)}, u32[]{:S(2)}) %collective-permute-start.62) | collective-permute-done | bytes 8736 | tf_op jit(solution)/shard_map/ppermute | solution.py:97
  327.5 3.5 collective-permute-done.51
  349.7 12.0 %collective-permute-done.64.refs_7_ = bf16[128,1024]{1,0:T(8,128)(2,1)S(1)} collective-permute-done((bf16[128,1024]{1,0:T(8,128)(2,1)}, bf16[128,1024]{1,0:T(8,128)(2,1)S(1)}, u32[]{:S(2)}, u32[]{:S(2)}) %collective-permute-start.64) | collective-permute-done | bytes 262176 | tf_op jit(solution)/shard_map/ppermute | solution.py:100
  362.5 3.4 shard_map.233
  (289 shorter events, 147.7 us)
Async XLA Ops:
  4.7 23.9 %collective-permute-start = (bf16[128,1024]{1,0:T(8,128)(2,1)}, bf16[128,1024]{1,0:T(8,128)(2,1)S(1)}, u32[]{:S(2)}, u32[]{:S(2)}) collective-permute-start(bf16[128,1024]{1,0:T(8,128)(2,1)} %get-tuple-element.98.refs_0_), channel_id=1, source_target_pairs={{0,1},{1,0},{2,3},{3,2},{4,5},{5,4},{6,7},{7,6},{8,9},{9,8},{10,11... | collective-permute-start | bytes 786440 | tf_op jit(solution)/shard_map/ppermute | solution.py:100
  7.7 21.5 %collective-permute-start.1 = (bf16[128,1024]{1,0:T(8,128)(2,1)}, bf16[128,1024]{1,0:T(8,128)(2,1)S(1)}, u32[]{:S(2)}, u32[]{:S(2)}) collective-permute-start(bf16[128,1024]{1,0:T(8,128)(2,1)} %get-tuple-element.98.refs_0_), channel_id=1, source_target_pairs={{0,2},{1,3},{2,0},{3,1},{4,6},{5,7},{6,4},{7,5},{8,10},{9,11},{10,... | collective-permute-start | bytes 786440 | tf_op jit(solution)/shard_map/ppermute | solution.py:100
  10.3 18.9 %collective-permute-start.2 = (bf16[128,1024]{1,0:T(8,128)(2,1)}, bf16[128,1024]{1,0:T(8,128)(2,1)}, u32[]{:S(2)}, u32[]{:S(2)}) collective-permute-start(bf16[128,1024]{1,0:T(8,128)(2,1)} %get-tuple-element.98.refs_0_), channel_id=1, source_target_pairs={{0,3},{1,2},{2,1},{3,0},{4,7},{5,6},{6,5},{7,4},{8,11},{9,10},{10,... | collective-permute-start | bytes 786440 | tf_op jit(solution)/shard_map/ppermute | solution.py:100
  27.6 36.2 %collective-permute-start.28 = (bf16[3,128,1152]{2,1,0:T(8,128)(2,1)S(1)}, bf16[3,128,1152]{2,1,0:T(8,128)(2,1)S(1)}, u32[]{:S(2)}, u32[]{:S(2)}) collective-permute-start(bf16[3,128,1152]{2,1,0:T(8,128)(2,1)S(1)} %pad_maximum_fusion.1), channel_id=1, source_target_pairs={{0,8},{4,12},{8,0},{12,4},{16,24},{20,28},{24,16},{28,20},{1,9},{5... | collective-permute-start | bytes 2654216 | tf_op jit(solution)/shard_map/ppermute | solution.py:97
  28.5 35.3 %collective-permute-start.29 = (bf16[3,128,1152]{2,1,0:T(8,128)(2,1)S(1)}, bf16[3,128,1152]{2,1,0:T(8,128)(2,1)}, u32[]{:S(2)}, u32[]{:S(2)}) collective-permute-start(bf16[3,128,1152]{2,1,0:T(8,128)(2,1)S(1)} %pad_maximum_fusion.1), channel_id=1, source_target_pairs={{0,16},{4,20},{8,24},{12,28},{16,0},{20,4},{24,8},{28,12},{1,17},{... | collective-permute-start | bytes 2654216 | tf_op jit(solution)/shard_map/ppermute | solution.py:97
  35.2 18.7 %collective-permute-start.9 = (bf16[512,256]{1,0:T(8,128)(2,1)}, bf16[512,256]{1,0:T(8,128)(2,1)S(1)}, u32[]{:S(2)}, u32[]{:S(2)}) collective-permute-start(bf16[512,256]{1,0:T(8,128)(2,1)} %get-tuple-element.101), channel_id=1, source_target_pairs={{0,8},{4,12},{1,9},{5,13},{2,10},{6,14},{3,11},{7,15},{16,24},{20,... | collective-permute-start | bytes 786440 | tf_op jit(solution)/shard_map/ppermute | solution.py:104
  39.0 15.7 %collective-permute-start.8 = (bf16[512,256]{1,0:T(8,128)(2,1)}, bf16[512,256]{1,0:T(8,128)(2,1)S(1)}, u32[]{:S(2)}, u32[]{:S(2)}) collective-permute-start(bf16[512,256]{1,0:T(8,128)(2,1)} %get-tuple-element.101), channel_id=1, source_target_pairs={{0,4},{8,12},{1,5},{9,13},{2,6},{10,14},{3,7},{11,15},{16,20},{24,... | collective-permute-start | bytes 786440 | tf_op jit(solution)/shard_map/ppermute | solution.py:104
  64.9 12.6 %collective-permute-start.30 = (bf16[3,64,1152]{2,1,0:T(8,128)(2,1)S(1)}, bf16[3,64,1152]{2,1,0:T(8,128)(2,1)S(1)}, u32[]{:S(2)}, u32[]{:S(2)}) collective-permute-start(bf16[3,64,1152]{2,1,0:T(8,128)(2,1)S(1)} %slice.158), channel_id=1, source_target_pairs={{0,16},{4,20},{8,24},{12,28},{16,0},{20,4},{24,8},{28,12},{1,17},{... | collective-permute-start | bytes 1327112 | tf_op jit(solution)/shard_map/ppermute | solution.py:97
  66.9 17.6 %collective-permute-start.31 = (bf16[3,64,1152]{2,1,0:T(8,128)(2,1)S(1)}, bf16[3,64,1152]{2,1,0:T(8,128)(2,1)S(1)}, u32[]{:S(2)}, u32[]{:S(2)}) collective-permute-start(bf16[3,64,1152]{2,1,0:T(8,128)(2,1)S(1)} %slice.159), channel_id=1, source_target_pairs={{0,8},{4,12},{8,0},{12,4},{16,24},{20,28},{24,16},{28,20},{1,9},{5... | collective-permute-start | bytes 1327112 | tf_op jit(solution)/shard_map/ppermute | solution.py:97
  85.3 80.9 %collective-permute-start.32 = (bf16[3,512,1152]{2,1,0:T(8,128)(2,1)}, bf16[3,512,1152]{2,1,0:T(8,128)(2,1)}, u32[]{:S(2)}, u32[]{:S(2)}) collective-permute-start(bf16[3,512,1152]{2,1,0:T(8,128)(2,1)} %constant_dynamic-update-slice_fusion.10.refs_8_), channel_id=1, source_target_pairs={{0,4},{4,0},{8,12},{12,8},{16,20},{20,16},{24,28},{28,24},{1,5},{5... | collective-permute-start | bytes 10616840 | tf_op jit(solution)/shard_map/ppermute | solution.py:97
  109.5 30.4 %collective-permute-start.21 = (bf16[1,512,1024]{2,1,0:T(8,128)(2,1)S(1)}, bf16[1,512,1024]{2,1,0:T(8,128)(2,1)S(1)}, u32[]{:S(2)}, u32[]{:S(2)}) collective-permute-start(bf16[1,512,1024]{2,1,0:T(8,128)(2,1)S(1)} %constant_dynamic-update-slice_fusion.5.refs_4_.refs_7_), channel_id=1, source_target_pairs={{0,4},{4,0},{8,12},{12,8},{16,20},{20,16},{24,28},{28,24},{1,5},{5... | collective-permute-start | bytes 3145736 | tf_op jit(solution)/shard_map/ppermute | solution.py:97
  109.6 34.7 %collective-permute-start.25 = (bf16[128,1024]{1,0:T(8,128)(2,1)S(1)}, bf16[128,1024]{1,0:T(8,128)(2,1)S(1)}, u32[]{:S(2)}, u32[]{:S(2)}) collective-permute-start(bf16[128,1024]{1,0:T(8,128)(2,1)S(1)} %copy-done.17), channel_id=1, source_target_pairs={{0,1},{1,0},{2,3},{3,2},{4,5},{5,4},{6,7},{7,6},{8,9},{9,8},{10,11... | collective-permute-start | bytes 786440 | tf_op jit(solution)/shard_map/ppermute | solution.py:100
  111.1 34.0 %collective-permute-start.26 = (bf16[128,1024]{1,0:T(8,128)(2,1)S(1)}, bf16[128,1024]{1,0:T(8,128)(2,1)S(1)}, u32[]{:S(2)}, u32[]{:S(2)}) collective-permute-start(bf16[128,1024]{1,0:T(8,128)(2,1)S(1)} %copy-done.17), channel_id=1, source_target_pairs={{0,2},{1,3},{2,0},{3,1},{4,6},{5,7},{6,4},{7,5},{8,10},{9,11},{10,... | collective-permute-start | bytes 786440 | tf_op jit(solution)/shard_map/ppermute | solution.py:100
  136.4 12.2 %collective-permute-start.27 = (bf16[128,1024]{1,0:T(8,128)(2,1)S(1)}, bf16[128,1024]{1,0:T(8,128)(2,1)S(1)}, u32[]{:S(2)}, u32[]{:S(2)}) collective-permute-start(bf16[128,1024]{1,0:T(8,128)(2,1)S(1)} %copy-done.17), channel_id=1, source_target_pairs={{0,3},{1,2},{2,1},{3,0},{4,7},{5,6},{6,5},{7,4},{8,11},{9,10},{10,... | collective-permute-start | bytes 786440 | tf_op jit(solution)/shard_map/ppermute | solution.py:100
  144.2 21.9 %collective-permute-start.23 = (bf16[128,1024]{1,0:T(8,128)(2,1)}, bf16[128,1024]{1,0:T(8,128)(2,1)S(1)}, u32[]{:S(2)}, u32[]{:S(2)}) collective-permute-start(bf16[128,1024]{1,0:T(8,128)(2,1)} %get-tuple-element.109.refs_0_), channel_id=1, source_target_pairs={{0,2},{1,3},{2,0},{3,1},{4,6},{5,7},{6,4},{7,5},{8,10},{9,11},{10,... | collective-permute-start | bytes 786440 | tf_op jit(solution)/shard_map/ppermute | solution.py:100
  145.2 21.0 %collective-permute-start.24 = (bf16[128,1024]{1,0:T(8,128)(2,1)}, bf16[128,1024]{1,0:T(8,128)(2,1)S(1)}, u32[]{:S(2)}, u32[]{:S(2)}) collective-permute-start(bf16[128,1024]{1,0:T(8,128)(2,1)} %get-tuple-element.109.refs_0_), channel_id=1, source_target_pairs={{0,3},{1,2},{2,1},{3,0},{4,7},{5,6},{6,5},{7,4},{8,11},{9,10},{10,... | collective-permute-start | bytes 786440 | tf_op jit(solution)/shard_map/ppermute | solution.py:100
  193.4 16.7 %collective-permute-start.33 = (bf16[128,1024]{1,0:T(8,128)(2,1)}, bf16[128,1024]{1,0:T(8,128)(2,1)S(1)}, u32[]{:S(2)}, u32[]{:S(2)}) collective-permute-start(bf16[128,1024]{1,0:T(8,128)(2,1)} %get-tuple-element.118), channel_id=1, source_target_pairs={{0,1},{1,0},{2,3},{3,2},{4,5},{5,4},{6,7},{7,6},{8,9},{9,8},{10,11... | collective-permute-start | bytes 786440 | tf_op jit(solution)/shard_map/ppermute | solution.py:100
  197.9 21.6 %collective-permute-start.34 = (bf16[128,1024]{1,0:T(8,128)(2,1)}, bf16[128,1024]{1,0:T(8,128)(2,1)S(1)}, u32[]{:S(2)}, u32[]{:S(2)}) collective-permute-start(bf16[128,1024]{1,0:T(8,128)(2,1)} %get-tuple-element.119), channel_id=1, source_target_pairs={{0,2},{1,3},{2,0},{3,1},{4,6},{5,7},{6,4},{7,5},{8,10},{9,11},{10,... | collective-permute-start | bytes 786440 | tf_op jit(solution)/shard_map/ppermute | solution.py:100
  198.7 20.7 %collective-permute-start.35 = (bf16[128,1024]{1,0:T(8,128)(2,1)}, bf16[128,1024]{1,0:T(8,128)(2,1)S(1)}, u32[]{:S(2)}, u32[]{:S(2)}) collective-permute-start(bf16[128,1024]{1,0:T(8,128)(2,1)} %get-tuple-element.120), channel_id=1, source_target_pairs={{0,3},{1,2},{2,1},{3,0},{4,7},{5,6},{6,5},{7,4},{8,11},{9,10},{10,... | collective-permute-start | bytes 786440 | tf_op jit(solution)/shard_map/ppermute | solution.py:100
  220.6 17.6 %collective-permute-start.40 = (bf16[3,64,1152]{2,1,0:T(8,128)(2,1)}, bf16[3,64,1152]{2,1,0:T(8,128)(2,1)}, u32[]{:S(2)}, u32[]{:S(2)}) collective-permute-start(bf16[3,64,1152]{2,1,0:T(8,128)(2,1)} %get-tuple-element.236), channel_id=1, source_target_pairs={{0,16},{4,20},{8,24},{12,28},{16,0},{20,4},{24,8},{28,12},{1,17},{... | collective-permute-start | bytes 1327112 | tf_op jit(solution)/shard_map/ppermute | solution.py:97
  260.4 13.4 %collective-permute-start.43 = (bf16[512,256]{1,0:T(8,128)(2,1)S(1)}, bf16[512,256]{1,0:T(8,128)(2,1)S(1)}, u32[]{:S(2)}, u32[]{:S(2)}) collective-permute-start(bf16[512,256]{1,0:T(8,128)(2,1)S(1)} %fusion), channel_id=1, source_target_pairs={{8,0},{12,4},{9,1},{13,5},{10,2},{14,6},{11,3},{15,7},{24,16},{28,... | collective-permute-start | bytes 786440 | tf_op jit(solution)/shard_map/ppermute | solution.py:104
  262.0 30.4 %collective-permute-start.47 = (bf16[128,1024]{1,0:T(8,128)(2,1)S(1)}, bf16[128,1024]{1,0:T(8,128)(2,1)}, u32[]{:S(2)}, u32[]{:S(2)}) collective-permute-start(bf16[128,1024]{1,0:T(8,128)(2,1)S(1)} %copy-done.10), channel_id=1, source_target_pairs={{0,1},{1,0},{2,3},{3,2},{4,5},{5,4},{6,7},{7,6},{8,9},{9,8},{10,11... | collective-permute-start | bytes 786440 | tf_op jit(solution)/shard_map/ppermute | solution.py:100
  263.9 29.9 %collective-permute-start.48 = (bf16[128,1024]{1,0:T(8,128)(2,1)S(1)}, bf16[128,1024]{1,0:T(8,128)(2,1)}, u32[]{:S(2)}, u32[]{:S(2)}) collective-permute-start(bf16[128,1024]{1,0:T(8,128)(2,1)S(1)} %copy-done.10), channel_id=1, source_target_pairs={{0,2},{1,3},{2,0},{3,1},{4,6},{5,7},{6,4},{7,5},{8,10},{9,11},{10,... | collective-permute-start | bytes 786440 | tf_op jit(solution)/shard_map/ppermute | solution.py:100
  264.9 28.9 %collective-permute-start.49 = (bf16[128,1024]{1,0:T(8,128)(2,1)S(1)}, bf16[128,1024]{1,0:T(8,128)(2,1)}, u32[]{:S(2)}, u32[]{:S(2)}) collective-permute-start(bf16[128,1024]{1,0:T(8,128)(2,1)S(1)} %copy-done.10), channel_id=1, source_target_pairs={{0,3},{1,2},{2,1},{3,0},{4,7},{5,6},{6,5},{7,4},{8,11},{9,10},{10,... | collective-permute-start | bytes 786440 | tf_op jit(solution)/shard_map/ppermute | solution.py:100
  299.6 33.7 %collective-permute-start.56 = (bf16[3,128,1152]{2,1,0:T(8,128)(2,1)}, bf16[3,128,1152]{2,1,0:T(8,128)(2,1)S(1)}, u32[]{:S(2)}, u32[]{:S(2)}) collective-permute-start(bf16[3,128,1152]{2,1,0:T(8,128)(2,1)} %pad_maximum_fusion.3), channel_id=1, source_target_pairs={{0,16},{4,20},{8,24},{12,28},{16,0},{20,4},{24,8},{28,12},{1,17},{... | collective-permute-start | bytes 2654216 | tf_op jit(solution)/shard_map/ppermute | solution.py:97
  300.7 33.8 %collective-permute-start.55 = (bf16[3,128,1152]{2,1,0:T(8,128)(2,1)}, bf16[3,128,1152]{2,1,0:T(8,128)(2,1)S(1)}, u32[]{:S(2)}, u32[]{:S(2)}) collective-permute-start(bf16[3,128,1152]{2,1,0:T(8,128)(2,1)} %pad_maximum_fusion.2), channel_id=1, source_target_pairs={{0,8},{4,12},{8,0},{12,4},{16,24},{20,28},{24,16},{28,20},{1,9},{5... | collective-permute-start | bytes 2654216 | tf_op jit(solution)/shard_map/ppermute | solution.py:97
  302.7 39.5 %collective-permute-start.44 = (bf16[128,1024]{1,0:T(8,128)(2,1)}, bf16[128,1024]{1,0:T(8,128)(2,1)S(1)}, u32[]{:S(2)}, u32[]{:S(2)}) collective-permute-start(bf16[128,1024]{1,0:T(8,128)(2,1)} %get-tuple-element.145), channel_id=1, source_target_pairs={{0,1},{1,0},{2,3},{3,2},{4,5},{5,4},{6,7},{7,6},{8,9},{9,8},{10,11... | collective-permute-start | bytes 786440 | tf_op jit(solution)/shard_map/ppermute | solution.py:100
  303.7 41.0 %collective-permute-start.45 = (bf16[128,1024]{1,0:T(8,128)(2,1)}, bf16[128,1024]{1,0:T(8,128)(2,1)S(1)}, u32[]{:S(2)}, u32[]{:S(2)}) collective-permute-start(bf16[128,1024]{1,0:T(8,128)(2,1)} %get-tuple-element.146), channel_id=1, source_target_pairs={{0,2},{1,3},{2,0},{3,1},{4,6},{5,7},{6,4},{7,5},{8,10},{9,11},{10,... | collective-permute-start | bytes 786440 | tf_op jit(solution)/shard_map/ppermute | solution.py:100
  305.6 16.2 %collective-permute-start.62 = (f32[17,128]{1,0:T(8,128)S(1)}, f32[17,128]{1,0:T(8,128)S(1)}, u32[]{:S(2)}, u32[]{:S(2)}) collective-permute-start(f32[17,128]{1,0:T(8,128)S(1)} %add.176), channel_id=1, source_target_pairs={{0,16},{4,20},{8,24},{12,28},{16,0},{20,4},{24,8},{28,12},{1,17},{... | collective-permute-start | bytes 26120 | tf_op jit(solution)/shard_map/ppermute | solution.py:97
  331.0 13.8 %collective-permute-start.46 = (bf16[128,1024]{1,0:T(8,128)(2,1)S(1)}, bf16[128,1024]{1,0:T(8,128)(2,1)S(1)}, u32[]{:S(2)}, u32[]{:S(2)}) collective-permute-start(bf16[128,1024]{1,0:T(8,128)(2,1)S(1)} %copy-done.28), channel_id=1, source_target_pairs={{0,3},{1,2},{2,1},{3,0},{4,7},{5,6},{6,5},{7,4},{8,11},{9,10},{10,... | collective-permute-start | bytes 786440 | tf_op jit(solution)/shard_map/ppermute | solution.py:100
  341.1 20.6 %collective-permute-start.64 = (bf16[128,1024]{1,0:T(8,128)(2,1)}, bf16[128,1024]{1,0:T(8,128)(2,1)S(1)}, u32[]{:S(2)}, u32[]{:S(2)}) collective-permute-start(bf16[128,1024]{1,0:T(8,128)(2,1)} %get-tuple-element.175), channel_id=1, source_target_pairs={{0,2},{1,3},{2,0},{3,1},{4,6},{5,7},{6,4},{7,5},{8,10},{9,11},{10,... | collective-permute-start | bytes 786440 | tf_op jit(solution)/shard_map/ppermute | solution.py:100
  342.2 19.5 %collective-permute-start.65 = (bf16[128,1024]{1,0:T(8,128)(2,1)}, bf16[128,1024]{1,0:T(8,128)(2,1)S(1)}, u32[]{:S(2)}, u32[]{:S(2)}) collective-permute-start(bf16[128,1024]{1,0:T(8,128)(2,1)} %get-tuple-element.176), channel_id=1, source_target_pairs={{0,3},{1,2},{2,1},{3,0},{4,7},{5,6},{6,5},{7,4},{8,11},{9,10},{10,... | collective-permute-start | bytes 786440 | tf_op jit(solution)/shard_map/ppermute | solution.py:100
  (73 other events, 628.3 us)

commit v3 on v2

--- a/solution.py
+++ b/solution.py
@@ -92,6 +92,7 @@
     z = lax.axis_index("tp")
     where = jnp.stack([me, ctx, z]).astype(jnp.int32)
     aligned = blk % 128 == 0
+    assert R == blk
 
     def plane(v, mask):
         return lax.ppermute(v, ("dp", "ctx"), [(i, i ^ mask) for i in range(N)])
@@ -107,48 +108,58 @@
         return lax.optimization_barrier((v,) + deps)[0]
 
     def gather_near(own):
-        if N == 8:
-            return [own, plane(own, 2), plane(own, 4)]
         return [own] + [plane(own, r) for r in range(2, N, 2)]
 
-    def gather_far(near):
-        if N == 8:
-            own, fx, fy = near
-            half = own.shape[1] // 2
-            top = plane(fx[:, :half], 4)
-            low = plane(fy[:, half:], 2)
-            near = near + [top, low]
+    def gather_core(near):
         mine = jnp.concatenate(near, axis=1)
         return mine, plane(mine, 1)
 
-    def scatter_core(mine, other):
-        got = plane(other, 1)
-        m = mine.shape[1] * 2 // N
-        return [
-            mine[:, i * m : (i + 1) * m].astype(f32) + got[:, i * m : (i + 1) * m].astype(f32)
-            for i in range(N // 2)
-        ]
-
-    def scatter_far(parts):
-        if N != 8:
-            return [p.astype(bf16) for p in parts[1:]]
-        half = parts[0].shape[1] // 2
-        far = parts[3].astype(bf16)
-        tx = plane(far[:, :half], 2)
-        ty = plane(far[:, half:], 4)
-        ysend = jnp.concatenate(
-            [parts[2][:, :half] + tx.astype(f32), parts[2][:, half:]], axis=1
-        ).astype(bf16)
-        xsend = jnp.concatenate(
-            [parts[1][:, :half], parts[1][:, half:] + ty.astype(f32)], axis=1
-        ).astype(bf16)
-        return [xsend, ysend]
-
-    def scatter_near(own, sends):
-        total = own
-        for i, v in enumerate(sends):
-            total = total + plane(v, 2 * (i + 1)).astype(f32)
-        return total
+    def merge_core(mine, got):
+        kinds, half, cols = mine.shape
+        m = half * 2 // N
+
+        def body(a, b, first, *rest):
+            for i in range(N // 2):
+                rows = slice(i * m, (i + 1) * m)
+                total = a[0, rows].astype(f32) + b[0, rows].astype(f32)
+                if i == 0:
+                    first[0] = total
+                else:
+                    rest[i - 1][0] = total.astype(bf16)
+
+        big = pl.BlockSpec((1, half, cols), lambda k: (k, 0, 0))
+        small = pl.BlockSpec((1, m, cols), lambda k: (k, 0, 0))
+        own, *sends = pl.pallas_call(
+            body,
+            grid=(kinds,),
+            out_shape=[sds((kinds, m, cols), f32)] + [sds((kinds, m, cols), bf16)] * (N // 2 - 1),
+            in_specs=[big, big],
+            out_specs=[small] * (N // 2),
+            cost_estimate=pl.CostEstimate(
+                flops=kinds * half * cols, bytes_accessed=7 * kinds * half * cols, transcendentals=0
+            ),
+        )(mine, got)
+        return own, sends
+
+    def close_sum(own, parts):
+        kinds, m, cols = own.shape
+
+        def body(first, *refs):
+            parts, outs = refs[: len(parts_in)], refs[len(parts_in) :]
+            for k in range(kinds):
+                total = first[k]
+                for p in parts:
+                    total = total + p[k].astype(f32)
+                outs[k][...] = total if k < kinds - 1 else total.T
+
+        parts_in = parts
+        return whole_call(
+            body,
+            [sds((m, cols), f32)] * (kinds - 1) + [sds((cols, m), f32)],
+            (own, *parts),
+            own.size * N,
+            scalars=False,
+        )
 
     def gather_column(own):
         return [own] + [column(own, k) for k in range(1, NT)]
@@ -168,9 +179,8 @@
         return jnp.take(v.reshape(v.shape[0], -1, size), picks, axis=1).reshape(v.shape)
 
     own_qkv = jnp.stack([query_weight, key_value_weight])
-    own_out = output_weight.T
-
-    def pre_body(s_ref, t_ref, c_ref, g_ref, n_ref, t_out, c_out, g_out):
+
+    def pre_body(s_ref, t_ref, c_ref, g_ref, o_ref, n_ref, t_out, c_out, g_out):
         index = s_ref[0]
         for s, mask in enumerate(masks):
             if aligned:
@@ -183,7 +193,8 @@
             g_out[:, dst] = g_ref[:, src]
         x = t_out[...].astype(f32)
         inv = lax.rsqrt(jnp.mean(x * x, axis=-1, keepdims=True) + epsilon)
-        n_ref[...] = (x * inv * g_out[0:1, :]).astype(bf16)
+        n_ref[:, :W] = (x * inv * g_out[0:1, :]).astype(bf16)
+        n_ref[:, W:] = o_ref[...].T
 
     gains = jnp.stack([attention_gain, ffn_gain])
     t_in, c_in, g_in = tokens[0], cotangent[0], gains
@@ -191,17 +202,17 @@
         t_in, c_in, g_in = (take_cols(v, me, blk, masks) for v in (t_in, c_in, g_in))
     normed, tok, cot, gain2 = whole_call(
         pre_body,
-        [sds((R, W), bf16), sds((R, W), bf16), sds((R, W), bf16), sds((2, W), f32)],
-        (where, t_in, c_in, g_in),
+        [sds((R, W + C), bf16), sds((R, W), bf16), sds((R, W), bf16), sds((2, W), f32)],
+        (where, t_in, c_in, g_in, output_weight),
         R * W * 8,
     )
     first_pieces = gather_column(normed)
     qkv_near = gather_near(after(own_qkv, normed))
-    qkv_m, qkv_o = gather_far(qkv_near)
+    qkv_m, qkv_o = gather_core(qkv_near)
     own_ffn = jnp.stack([gate_weight, up_weight, down_weight.T])
-    ffn_near = gather_near(after(own_ffn, *qkv_near))
-
-    out_cols = jnp.concatenate(gather_column(after(own_out, *first_pieces)), axis=1)
+    ffn_near = gather_near(after(own_ffn, normed))
+    out_cols = jnp.concatenate([p[:, W:] for p in first_pieces], axis=1)[None]
+    out_near = gather_near(out_cols)
     cot_pieces = gather_column(after(cot, *first_pieces))
 
     half_width = hw // 2
@@ -217,8 +228,12 @@
     def head_mean(x):
         n = x.shape[1]
         same = rows_of((n, n)) // hw == lanes((n, n)) // hw
-        ones = jnp.where(same, 1.0 / hw, 0.0).astype(f32)
-        return jnp.dot(x, ones, precision=exact, preferred_element_type=f32)
+        ones = jnp.where(same, 1.0 / hw, 0.0).astype(bf16)
+        high = x.astype(bf16)
+        rest = x - high.astype(f32)
+        low = rest.astype(bf16)
+        tail = (rest - low.astype(f32)).astype(bf16)
+        return mm(high, ones) + mm(low, ones) + mm(tail, ones)
 
     def swap_halves(x):
         first = lanes(x.shape) % hw < half_width
@@ -229,7 +244,7 @@
     def qkv_body(*refs):
         wm, wo, cs, sn, qg_ref, kg_ref, rq, pr, q_raw, p_raw = refs[NT:]
         rows = join_slots(refs[:NT])
-        left, right = rows[:, :H], rows[:, H:]
+        left, right = rows[:, :H], rows[:, H:W]
         q = mm(left, wm[0]) + mm(right, wo[0])
         p = mm(left, wm[1]) + mm(right, wo[1])
         q_raw[...] = q
@@ -253,8 +268,8 @@
     kv_odd = [along(pair, 1, earlier)]
     for r in range(2, NC, 2):
         kv_odd.append(along(kv_even[r // 2], 1, lambda i, j: (i ^ r) < i))
-    kv_all = jnp.stack([v for pq in zip(kv_even, kv_odd) for v in pq])
-    out_m, out_o = gather_far(gather_near(out_cols[None]))
+    kv_pieces = [v for pq in zip(kv_even, kv_odd) for v in pq]
+    out_m, out_o = gather_core(out_near)
 
     def widen(x, part):
         moved = x if part == 0 else pltpu.roll(x, hw, 1)
@@ -269,8 +284,9 @@
         qry = lanes((B, B)) ^ zz
         return key <= qry
 
-    def fwd_body(s_ref, q_ref, kv_ref, *refs):
-        slot_refs, (att_ref, lse_ref, qz, acc, tot) = refs[:NT], refs[NT:]
+    def fwd_body(s_ref, q_ref, *refs):
+        kv_in, slot_refs = refs[:NC], refs[NC : NC + NT]
+        att_ref, lse_ref, qz, acc, tot, kv_ref = refs[NC + NT :]
         r, h = pl.program_id(0), pl.program_id(1)
         here = s_ref[1]
 
@@ -279,9 +295,11 @@
             for hd in range(QH):
                 x = q_ref[:, (hd // 2) * pw : (hd // 2 + 1) * pw].astype(f32)
                 qz[hd] = widen(x, hd % 2).astype(bf16)
+            for k in range(NC):
+                kv_ref[k] = kv_in[k][...]
 
         def step(masked):
-            kv = kv_ref[0]
+            kv = kv_ref[r, :, pl.ds(pl.multiple_of(h * pw, pw), pw)]
             kvt = kv.astype(f32).T.astype(bf16)
             for g in range(2):
                 hd = 2 * h + g
@@ -312,30 +330,29 @@
             att_ref[...] = att
             put_slots(slot_refs, att)
             for hd in range(QH):
-                lse_ref[hd : hd + 1] = jnp.log(tot[hd][0:1])
+                lse_ref[hd] = jnp.log(tot[hd][0:1])
 
     fixed = lambda shape: pl.BlockSpec(shape, lambda r, h: (0,) * len(shape))
-    kv_spec = pl.BlockSpec((1, B, pw), lambda r, h: (r, 0, h))
     *att_slots, attended, lse = pl.pallas_call(
         fwd_body,
         grid=(NC, KH),
-        out_shape=[sds((R, C), bf16)] * NT + [sds((B, C), bf16), sds((QH, B), f32)],
-        in_specs=[SM, fixed((B, C)), kv_spec],
-        out_specs=[fixed((R, C))] * NT + [fixed((B, C)), fixed((QH, B))],
+        out_shape=[sds((R, C), bf16)] * NT + [sds((B, C), bf16), sds((QH, 1, B), f32)],
+        in_specs=[SM] + [fixed((B, C))] * (1 + NC),
+        out_specs=[fixed((R, C))] * NT + [fixed((B, C)), fixed((QH, 1, B))],
         scratch_shapes=[
             pltpu.VMEM((QH, B, pw), bf16),
             pltpu.VMEM((QH, pw, B), f32),
             pltpu.VMEM((QH, 8, B), f32),
+            pltpu.VMEM((NC, B, C), bf16),
         ],
         cost_estimate=pl.CostEstimate(
             flops=16 * QH * B * B * pw, bytes_accessed=4 * B * C * 2, transcendentals=4 * QH * B * B
         ),
         name="attention_forward",
-    )(where, rot_q, kv_all)
+    )(where, rot_q, *kv_pieces)
 
     att_pieces = spread_column(att_slots)
-    _, *ffn_near = lax.optimization_barrier((attended, *ffn_near))
-    ffn_m, ffn_o = gather_far(list(ffn_near))
+    ffn_m, ffn_o = gather_core(ffn_near)
 
     def out_body(*refs):
         pieces, (om, oo, t_ref, g_ref, res, nrm) = refs[:NT], refs[NT:]
@@ -441,11 +458,14 @@
         ),
         name="ffn_weights",
     )(*second_pieces, *cot_pieces, mid, dgate, dup)
-    ffn_parts = scatter_core(dwf_m, dwf_o)
-    gnf_pieces, ffn_parts = lax.optimization_barrier((gnf_pieces, ffn_parts))
+    ffn_own, ffn_sends = merge_core(dwf_m, plane(dwf_o, 1))
+    gnf_pieces, ffn_own, ffn_sends = lax.optimization_barrier((gnf_pieces, ffn_own, ffn_sends))
+    ffn_got = [plane(v, 2 * (i + 1)) for i, v in enumerate(ffn_sends)]
 
     def back_body(*refs):
-        pieces, (res, c_ref, g_ref, om, oo, gres, rg, gg, *gas) = refs[:NT], refs[NT:]
+        pieces, outs_in = refs[:NT], refs[NT : 2 * NT]
+        res, c_ref, g_ref, om, oo, gres, gg, *more = refs[2 * NT :]
+        gas, both = more[:NT], more[NT:]
         grad = sum(p[...].astype(f32) for p in pieces)
         x = res[...]
         inv = lax.rsqrt(jnp.mean(x * x, axis=-1, keepdims=True) + epsilon)
@@ -456,43 +476,62 @@
         total = c_ref[...].astype(f32) + through
         gres[...] = total
         half = total.astype(bf16)
-        rg[...] = half
+        for k, ref in enumerate(both):
+            ref[:R] = half
+            ref[R:] = outs_in[k][...]
         ga = (mm(half[:, :H], om[0]) + mm(half[:, H:], oo[0])).astype(bf16)
         for k, ref in enumerate(gas):
             ref[...] = ga[:, k * C : (k + 1) * C]
 
-    grad_resid, rg16, ffn_gain_part, *ga_slots = whole_call(
+    grad_resid, ffn_gain_part, *ga_slots = whole_call(
         back_body,
-        [sds((R, W), f32), sds((R, W), bf16), sds((1, W), f32)] + [sds((R, C), bf16)] * NT,
-        (*gnf_pieces, resid, cot, gain2, out_m, out_o),
+        [sds((R, W), f32), sds((1, W), f32)]
+        + [sds((R, C), bf16)] * NT
+        + [sds((2 * R, W), bf16)] * NT,
+        (*gnf_pieces, *ffn_slots[:NT], resid, cot, gain2, out_m, out_o),
         2 * R * W * W,
         scalars=False,
     )
+    ga_slots, both_slots = ga_slots[:NT], ga_slots[NT:]
     ga_pieces = spread_column(ga_slots)
-    grad_att = jnp.concatenate(ga_pieces, axis=0)
-    ffn_sends = scatter_far(ffn_parts)
-    grad_att, ffn_sends = lax.optimization_barrier((grad_att, ffn_sends))
-    ffn_sum = scatter_near(ffn_parts[0], ffn_sends)
-
-    def bwd_body(s_ref, q_ref, d_ref, a_ref, l_ref, kv_ref, dq_ref, dkv_ref, qz, dz, acc, dl):
+    *both_slots, ga_pieces = lax.optimization_barrier((*both_slots, ga_pieces))
+    both_pieces = spread_column(both_slots)
+
+    def bwd_body(s_ref, q_ref, a_ref, l_ref, *refs):
+        d_in, kv_in = refs[:NT], refs[NT : NT + NC]
+        dq_ref, even, odd, qz, dz, acc, dl, kv_ref = refs[NT + NC :]
         r, h = pl.program_id(0), pl.program_id(1)
         here = s_ref[1]
 
         @pl.when((r == 0) & (h == 0))
         def _():
+            d_all = join_slots(d_in).astype(f32)
             for hd in range(QH):
                 cols = slice((hd // 2) * pw, (hd // 2 + 1) * pw)
                 qz[hd] = widen(q_ref[:, cols].astype(f32), hd % 2).astype(bf16)
-                dz[hd] = widen_high(d_ref[:, cols].astype(f32), hd % 2).astype(bf16)
-            prod = d_ref[...].astype(f32) * a_ref[...].astype(f32)
+                dz[hd] = widen_high(d_all[:, cols], hd % 2).astype(bf16)
+            for k in range(NC):
+                kv_ref[k] = kv_in[k][...]
+            prod = d_all * a_ref[...].astype(f32)
             for hd in range(QH):
                 pick = jnp.where(lanes((8, C)) // hw == hd, 1.0, 0.0).astype(f32)
                 dl[hd] = lax.dot_general(
                     pick, prod, (((1,), (1,)), ((), ())), precision=exact, preferred_element_type=f32
                 )
 
+        here_cols = pl.ds(pl.multiple_of(h * pw, pw), pw)
+
+        def put(value):
+            @pl.when(r % 2 == 0)
+            def _():
+                even[r // 2, :, here_cols] = value
+
+            @pl.when(r % 2 == 1)
+            def _():
+                odd[r // 2, :, here_cols] = value
+
         def step(masked):
-            kv = kv_ref[0]
+            kv = kv_ref[r, :, here_cols]
             kvt = kv.astype(f32).T.astype(bf16)
             total = None
             for g in range(2):
@@ -510,7 +549,7 @@
                     acc[hd] = o
                 else:
                     acc[hd] += o
-            dkv_ref[0] = total.astype(bf16)
+            put(total.astype(bf16))
 
         @pl.when(r == 0)
         def _():
@@ -522,46 +561,46 @@
 
         @pl.when((here ^ r) > here)
         def _():
-            dkv_ref[...] = jnp.zeros_like(dkv_ref)
+            put(jnp.zeros((B, pw), bf16))
 
         @pl.when((r == NC - 1) & (h == KH - 1))
         def _():
             outs = [acc[hd][:hw] for hd in range(QH)]
             dq_ref[...] = jnp.concatenate(outs, axis=0).T * scale
 
-    grad_rot_q, dkv = pl.pallas_call(
+    grad_rot_q, dkv_even, dkv_odd = pl.pallas_call(
         bwd_body,
         grid=(NC, KH),
-        out_shape=[sds((B, C), f32), sds((NC, B, C), bf16)],
-        in_specs=[SM, fixed((B, C)), fixed((B, C)), fixed((B, C)), fixed((QH, 1, B)), kv_spec],
-        out_specs=[fixed((B, C)), kv_spec],
+        out_shape=[sds((B, C), f32)] + [sds((NC // 2, B, C), bf16)] * 2,
+        in_specs=[SM, fixed((B, C)), fixed((B, C)), fixed((QH, 1, B))]
+        + [fixed((R, C))] * NT
+        + [fixed((B, C))] * NC,
+        out_specs=[fixed((B, C))] + [fixed((NC // 2, B, C))] * 2,
         scratch_shapes=[
             pltpu.VMEM((QH, B, pw), bf16),
             pltpu.VMEM((QH, B, pw), bf16),
             pltpu.VMEM((QH, pw, B), f32),
             pltpu.VMEM((QH, 8, B), f32),
+            pltpu.VMEM((NC, B, C), bf16),
         ],
         cost_estimate=pl.CostEstimate(
             flops=40 * QH * B * B * pw, bytes_accessed=8 * B * C * 2, transcendentals=4 * QH * B * B
         ),
         name="attention_backward",
-    )(where, rot_q, grad_att, attended, lse[:, None, :], kv_all)
-
-    odd = lax.ppermute(dkv[1::2], "ctx", [(i, i ^ 1) for i in range(NC)])
-    pair_sum = dkv[0].astype(f32) + odd[0].astype(f32)
+    )(where, rot_q, attended, lse, *ga_pieces, *kv_pieces)
+
+    odd = lax.ppermute(dkv_odd, "ctx", [(i, i ^ 1) for i in range(NC)])
+    pair_parts = []
     for k in range(1, NC // 2):
-        part = (dkv[2 * k].astype(f32) + odd[k].astype(f32)).astype(bf16)
-        pair_sum = pair_sum + along(part, 2 * k, lambda i, j: i // 2 > j // 2).astype(f32)
-
-    rg_rows = gather_column(after(rg16, grad_att))
-    out_slots = list(lax.optimization_barrier((*ffn_slots[:NT], grad_att))[:NT])
-    ffn_pieces = spread_column(out_slots)
-
-    def qk_body(
-        dq, dp, q_raw_r, p_raw_r, cs, sn, qg_ref, kg_ref, wm, wo, g_ref, *refs
-    ):
-        r_in, gnas, (gm, go, qgg, kgg, agg) = refs[:NT], refs[NT : 2 * NT], refs[2 * NT :]
-        r_all = join_slots(r_in)
+        part = (dkv_even[k].astype(f32) + odd[k].astype(f32)).astype(bf16)
+        pair_parts.append(along(part, 2 * k, lambda i, j: i // 2 > j // 2))
+
+    def qk_body(s_ref, dq, even, odd_ref, q_raw_r, p_raw_r, cs, sn, qg_ref, kg_ref, wm, wo, g_ref, fg_ref, *refs):
+        index = s_ref[0]
+        n_parts = len(pair_parts)
+        parts, r_in, gnas = refs[:n_parts], refs[n_parts : n_parts + NT], refs[n_parts + NT : n_parts + 2 * NT]
+        both_ref, pack = refs[n_parts + 2 * NT :]
+        r_all = jnp.concatenate([ref[:, :W] for ref in r_in], axis=0)
 
         def back(grad, raw, gain, live):
             turned = grad * cs[...] - swap_halves(grad) * sn[...]
@@ -574,79 +613,70 @@
                 out = jnp.where(live, out, grad)
             return out.astype(bf16), gg
 
+        dp = even[0].astype(f32) + odd_ref[0].astype(f32)
+        for p in parts:
+            dp = dp + p[...].astype(f32)
         gq, qsum = back(dq[...], q_raw_r[...], qg_ref[...], None)
         live = lanes((B, C)) % pw < hw
-        gp, ksum = back(dp[...], p_raw_r[...], kg_ref[...], live)
-        qgg[...] = qsum
-        kgg[...] = ksum
-        both = jnp.concatenate([gq, gp], axis=1)
-        for w, cols, gw in ((wm, slice(0, H), gm), (wo, slice(H, W), go)):
+        gp, ksum = back(dp, p_raw_r[...], kg_ref[...], live)
+        both_ref[...] = jnp.concatenate([gq, gp], axis=1)
+        pack[...] = jnp.zeros_like(pack)
+        for w, cols, first in ((wm, slice(0, H), 0), (wo, slice(H, W), N // 2)):
             part = mm_nt(gq, w[0]) + mm_nt(gp, w[1])
             for k, ref in enumerate(gnas):
                 ref[:, cols] = part[k * R : (k + 1) * R].astype(bf16)
-            rows = r_all[:, cols]
-            agg[:, cols] = (
-                jnp.sum(part * rows.astype(f32), axis=0, keepdims=True) / g_ref[0:1, cols]
-            )
-            full = lax.dot_general(
-                rows, both, (((0,), (0,)), ((), ())), preferred_element_type=f32
-            ).astype(bf16)
-            gw[0] = full[:, :C]
-            gw[1] = full[:, C:]
-
-    *gna_slots, dwq_m, dwq_o, qg_part, kg_part, att_gain_part = whole_call(
+            agg = jnp.sum(part * r_all[:, cols].astype(f32), axis=0, keepdims=True) / g_ref[0:1, cols]
+            for i in range(N // 2):
+                to = index ^ masks[first + i]
+                pack[pl.ds(to, 1), :] = agg[:, i * blk : (i + 1) * blk]
+                pack[pl.ds(N + to, 1), :] = fg_ref[:, (first + i) * blk : (first + i + 1) * blk]
+        heads_q = sum(qsum[:, i * pw : (i + 1) * pw] for i in range(KH))
+        heads_q = heads_q + pltpu.roll(heads_q, hw, 1)
+        heads_k = sum(ksum[:, i * pw : (i + 1) * pw] for i in range(KH))
+        pack[2 * N : 2 * N + 1, :hw] = heads_q[:, :hw]
+        pack[2 * N + 1 : 2 * N + 2, :hw] = heads_k[:, :hw]
+
+    *gna_slots, both16, packed = whole_call(
         qk_body,
-        [
-            *[sds((R, W), bf16)] * NT,
-            sds((2, H, C), bf16),
-            sds((2, H, C), bf16),
-            sds((1, C), f32),
-            sds((1, C), f32),
-            sds((1, W), f32),
-        ],
+        [sds((R, W), bf16)] * NT + [sds((B, 2 * C), bf16), sds((2 * N + 8, blk), f32)],
         (
-            grad_rot_q, pair_sum, q_raw, p_raw, cosine, sine, qg, kg,
-            qkv_m, qkv_o, gain2, *first_pieces,
+            where, grad_rot_q, dkv_even, odd, q_raw, p_raw, cosine, sine, qg, kg,
+            qkv_m, qkv_o, gain2, ffn_gain_part, *pair_parts, *first_pieces,
         ),
-        8 * B * W * C,
+        4 * B * W * C,
+    )
+    gna_pieces = spread_column(gna_slots)
+
+    *both_pieces, both16 = lax.optimization_barrier((*both_pieces, both16))
+
+    def last_body(*refs):
+        r_in, g_in, (a_ref, b_ref, gm, go) = refs[:NT], refs[NT : 2 * NT], refs[2 * NT :]
+        rt = jnp.concatenate([ref[:, :W] for ref in r_in], axis=0).T
+        gt = jnp.concatenate([ref[:R] for ref in g_in], axis=0).T
+        for ref, rows in ((gm, slice(0, H)), (go, slice(H, W))):
+            full = mm(rt[rows], b_ref[...]).astype(bf16)
+            ref[0] = full[:, :C]
+            ref[1] = full[:, C:]
+            ref[2] = mm(gt[rows], a_ref[...]).astype(bf16)
+
+    last_m, last_o = whole_call(
+        last_body,
+        [sds((3, H, C), bf16)] * 2,
+        (*first_pieces, *both_pieces, attended, both16),
+        6 * B * W * C,
         scalars=False,
     )
-    gna_pieces = spread_column(gna_slots)
-    rg_rows = lax.optimization_barrier((*rg_rows, *gna_slots))[:NT]
-
-    def dwo_body(*refs):
-        a_ref, gm, go = refs[NT:]
-        a, g = a_ref[...], join_slots(refs[:NT])
-        gm[0] = lax.dot_general(
-            g[:, :H], a, (((0,), (0,)), ((), ())), preferred_element_type=f32
-        ).astype(bf16)
-        go[0] = lax.dot_general(
-            g[:, H:], a, (((0,), (0,)), ((), ())), preferred_element_type=f32
-        ).astype(bf16)
-
-    dwo_m, dwo_o = whole_call(
-        dwo_body, [sds((1, H, C), bf16)] * 2, (*rg_rows, attended), 2 * B * W * C, scalars=False
-    )
-
-    last_m = jnp.concatenate([dwq_m, dwo_m], axis=0)
-    last_o = jnp.concatenate([dwq_o, dwo_o], axis=0)
-    att_parts = scatter_core(last_m, last_o)
-    att_sum = scatter_near(att_parts[0], scatter_far(att_parts))
-
-    order_back = masks
-    inverse_order = [order_back.index(m) for m in range(N)]
-    gain_parts = jnp.concatenate([att_gain_part, ffn_gain_part], axis=0)
-    slot_of = jnp.take(jnp.array(inverse_order, jnp.int32), me ^ jnp.arange(N, dtype=jnp.int32))
-    gain_parts = jnp.take(gain_parts.reshape(2, N, blk), slot_of, axis=1).reshape(2 * W)
-    q_part = qg_part.reshape(QH, hw).sum(0)
-    k_part = kg_part.reshape(KH, 2, hw)[:, 0].sum(0)
-    packed = jnp.concatenate([gain_parts, q_part, k_part]).reshape(-1, 128)
+    att_own, att_sends = merge_core(last_m, plane(last_o, 1))
+    att_got = [plane(v, 2 * (i + 1)) for i, v in enumerate(att_sends)]
+
     packed = sum(gather_column(packed))
     bit = 1
     while bit < N:
         packed = packed + plane(packed, bit)
         bit *= 2
-    packed = packed.reshape(-1)
+
+    grad_gate, grad_up, grad_down = close_sum(ffn_own, ffn_got)
+    grad_query, grad_pairs, grad_output = close_sum(att_own, att_got)
 
     def end_body(*refs):
         s_ref, rest = refs[0], refs[1:]
@@ -658,7 +688,7 @@
         hat = x * inv
         scaled = grad * g_ref[0:1, :]
         total = gres[...] + inv * (scaled - hat * jnp.mean(scaled * hat, axis=-1, keepdims=True))
-        block = (res[...] + sum(p[...].astype(f32) for p in fp)).astype(bf16)
+        block = (res[...] + sum(p[R:].astype(f32) for p in fp)).astype(bf16)
         for s, mask in enumerate(masks):
             src = slice(s * blk, (s + 1) * blk)
             if aligned:
@@ -668,16 +698,18 @@
             gt[:, dst] = total[:, src]
             bo[:, dst] = block[:, src]
 
-    gna_pieces, att_sum, ffn_sum, packed = lax.optimization_barrier(
-        (gna_pieces, att_sum, ffn_sum, packed)
+    gna_pieces, packed, grad_down, grad_output = lax.optimization_barrier(
+        (gna_pieces, packed, grad_down, grad_output)
     )
     grad_tokens, block_out = whole_call(
         end_body,
         [sds((R, W), f32), sds((R, W), bf16)],
-        (where, *gna_pieces, *ffn_pieces, tok, resid, grad_resid, gain2),
+        (where, *gna_pieces, *both_pieces, tok, resid, grad_resid, gain2),
         R * W * 16,
     )
     if not aligned:
+        inverse = [masks.index(m) for m in range(N)]
+        slot_of = jnp.take(jnp.array(inverse), me ^ jnp.arange(N, dtype=jnp.int32))
         back_cols = lambda v: jnp.take(
             v.reshape(R, N, blk), slot_of, axis=1
         ).reshape(R, W)
@@ -690,16 +722,16 @@
         block_out[None],
         grad_tokens[None],
         lse_out,
-        packed[:W],
-        att_sum[0],
-        att_sum[1],
-        packed[2 * W : 2 * W + hw],
-        packed[2 * W + hw : 2 * W + 2 * hw],
-        att_sum[2].T,
-        packed[W : 2 * W],
-        ffn_sum[0],
-        ffn_sum[1],
-        ffn_sum[2].T,
+        packed[:N].reshape(W),
+        grad_query,
+        grad_pairs,
+        packed[2 * N, :hw],
+        packed[2 * N + 1, :hw],
+        grad_output,
+        packed[N : 2 * N].reshape(W),
+        grad_gate,
+        grad_up,
+        grad_down,
     )
 
 

time: 369 us -> 394 us (1.068)
  waiting for transfers between devices: 140 us -> 164 us
  other arithmetic: 24.9 us -> 6.35 us
  Pallas kernels: 68.9 us -> 83.5 us
  starting transfers between devices: 103 us -> 113 us
  local copies, waits for them, and re-layouts: 28.1 us -> 23.2 us
    ppermute x28 -> x23, waiting for transfers between devices: 51.1 us -> 65.5 us  [plane(): return lax.ppermute(v, ('dp', 'ctx'), [(i, i ^ mask) for i in range(N)])]
    ppermute x33 -> x27, starting transfers between devices: 60.8 us -> 71.1 us  [column(): return lax.ppermute(v, 'tp', [(i, i ^ mask) for i in range(NT)])]
    pallas_call x6 -> x9, Pallas kernels: 24.9 us -> 34.6 us  [whole_call(): pl.pallas_call(body, out_shape=list(outs), in_specs=specs, out_specs=[VM]...]
    ppermute x33 -> x27, waiting for transfers between devices: 67.1 us -> 75.9 us  [column(): return lax.ppermute(v, 'tp', [(i, i ^ mask) for i in range(NT)])]
    pallas_call x1 -> x3, Pallas kernels: 10.5 us -> 17.9 us  [the longest x2 9.05 us: merge_core(): pl.pallas_call(body, grid=(kinds,), out_shape=[sds((kinds, m, cols), f32)...]
    add x6 -> x0, other arithmetic: 7.34 us -> none  [the longest x3 5.09 us: scatter_core(): mine[:, i * m:(i + 1) * m].astype(f32)]
    slice x15 -> x4, local copies, waits for them, and re-layouts: 5.78 us -> 0.02 us  [on_device(): out_cols = jnp.concatenate([p[:, W:] for p in first_pieces], axis=1)[None]]
    unnamed x94 -> x91, local copies, waits for them, and re-layouts: 11.2 us -> 14.5 us
  transfers between devices with their start and end apart: 66 -> 55, of which waited for: 32 -> 28; matrix products, arithmetic and copies ran while one was open for 11% -> 4% of each run, Pallas kernels for 7% -> 9%
where the time goes in v3:
time: 394 us; the launch traced here: 391 us
  waiting for transfers between devices  164 us (42%)
  starting transfers between devices  113 us (29%)
  Pallas kernels  83.5 us (21%)
  local copies, waits for them, and re-layouts  23.2 us (6%)
  other arithmetic  6.35 us (2%)
    ppermute x27, waiting for transfers between devices, column(): return lax.ppermute(v, 'tp', [(i, i ^ mask) for i in range(NT)])  75.9 us
    ppermute x27, starting transfers between devices, column(): return lax.ppermute(v, 'tp', [(i, i ^ mask) for i in range(NT)])  71.1 us
    ppermute x23, waiting for transfers between devices, plane(): return lax.ppermute(v, ('dp', 'ctx'), [(i, i ^ mask) for i in range(N)])  65.5 us
    pallas_call x9, Pallas kernels, whole_call(): pl.pallas_call(body, out_shape=list(outs), in_specs=specs, out_specs=[VM]...  34.6 us
    ppermute x23, starting transfers between devices, plane(): return lax.ppermute(v, ('dp', 'ctx'), [(i, i ^ mask) for i in range(N)])  34.6 us
    ppermute x4, waiting for transfers between devices, along(): return lax.ppermute(v, 'ctx', pairs)  22.3 us
    pallas_call x1, Pallas kernels, on_device(): pl.pallas_call(ffn_body, grid=(steps,), out_shape=[sds((R, W), bf16)] * (...  16.9 us
    unnamed x91, local copies, waits for them, and re-layouts  14.5 us
  transfers between devices with their start and end apart: 55, of which 28 were waited for; matrix products, arithmetic and copies ran while one was open for 4% of the time, Pallas kernels for 9%

profile of v3, /device:TPU:0, one launch (start us, length us, event | category | flops | bytes accessed | tf_op | source)
XLA Modules:
  0.0 391.0 jit_solution(15035367105137339435)
XLA Ops:
  12.6 17.9 %collective-permute-done.23 = bf16[3,128,1152]{2,1,0:T(8,128)(2,1)S(1)} collective-permute-done((bf16[3,128,1152]{2,1,0:T(8,128)(2,1)S(1)}, bf16[3,128,1152]{2,1,0:T(8,128)(2,1)S(1)}, u32[]{:S(2)}, u32[]{:S(2)}) %collective-permute-start.23) | collective-permute-done | bytes 884768 | tf_op jit(solution)/shard_map/ppermute | solution.py:98
  31.5 18.6 %collective-permute-done.24 = bf16[3,128,1152]{2,1,0:T(8,128)(2,1)S(1)} collective-permute-done((bf16[3,128,1152]{2,1,0:T(8,128)(2,1)S(1)}, bf16[3,128,1152]{2,1,0:T(8,128)(2,1)S(1)}, u32[]{:S(2)}, u32[]{:S(2)}) %collective-permute-start.24) | collective-permute-done | bytes 884768 | tf_op jit(solution)/shard_map/ppermute | solution.py:98
  68.5 9.9 %collective-permute-done.2.refs_3_.refs_4_ = bf16[128,1280]{1,0:T(8,128)(2,1)S(1)} collective-permute-done((bf16[128,1280]{1,0:T(8,128)(2,1)S(1)}, bf16[128,1280]{1,0:T(8,128)(2,1)S(1)}, u32[]{:S(2)}, u32[]{:S(2)}) %collective-permute-start.2) | collective-permute-done | bytes 327712 | tf_op jit(solution)/shard_map/ppermute | solution.py:101
  84.3 5.2 %collective-permute-done.15 = bf16[1,128,1024]{2,1,0:T(8,128)(2,1)S(1)} collective-permute-done((bf16[1,128,1024]{2,1,0:T(8,128)(2,1)S(1)}, bf16[1,128,1024]{2,1,0:T(8,128)(2,1)S(1)}, u32[]{:S(2)}, u32[]{:S(2)}) %collective-permute-start.15) | collective-permute-done | bytes 262176 | tf_op jit(solution)/shard_map/ppermute | solution.py:98
  99.1 4.6 %shard_map.220 = (bf16[512,256]{1,0:T(8,128)(2,1)}, bf16[512,256]{1,0:T(8,128)(2,1)}, f32[512,256]{1,0:T(8,128)}, f32[512,256]{1,0:T(8,128)}) custom-call(bf16[128,1280]{1,0:T(8,128)(2,1)} %get-tuple-element.110.refs_0_.refs_1_, bf16[128,1280]{1,0:T(8,128)(2,1)} %copy-done.4, bf16[128,1280]{1,0:T(8,128)(2,1)} %copy-done.5, bf16[128,1280]{1,0:T(8,128)(2,1)} %copy-done.6, ...), custom_call_target="tpu_custom_call" | custom-call | flops 536870912 | bytes 4982784 | tf_op jit(solution)/shard_map/pallas_call | solution.py:48
  107.9 4.4 %collective-permute-done.8.refs_2_.refs_6_ = bf16[512,256]{1,0:T(8,128)(2,1)S(1)} collective-permute-done((bf16[512,256]{1,0:T(8,128)(2,1)}, bf16[512,256]{1,0:T(8,128)(2,1)S(1)}, u32[]{:S(2)}, u32[]{:S(2)}) %collective-permute-start.8) | collective-permute-done | bytes 262176 | tf_op jit(solution)/shard_map/ppermute | solution.py:105
  113.2 7.5 %collective-permute-start.20 = (bf16[128,1024]{1,0:T(8,128)(2,1)S(1)}, bf16[128,1024]{1,0:T(8,128)(2,1)}, u32[]{:S(2)}, u32[]{:S(2)}) collective-permute-start(bf16[128,1024]{1,0:T(8,128)(2,1)S(1)} %copy-done.15), channel_id=1, source_target_pairs={{0,1},{1,0},{2,3},{3,2},{4,5},{5,4},{6,7},{7,6},{8,9},{9,8},{10,11... | collective-permute-start | bytes 786440 | tf_op jit(solution)/shard_map/ppermute | solution.py:101
  122.5 4.7 %attention_forward.1 = (bf16[128,256]{1,0:T(8,128)(2,1)}, bf16[128,256]{1,0:T(8,128)(2,1)}, bf16[128,256]{1,0:T(8,128)(2,1)}, bf16[128,256]{1,0:T(8,128)(2,1)}, ...) custom-call(s32[3]{0:T(128)} %pad_add_fusion.s_ref.refs_0_, bf16[512,256]{1,0:T(8,128)(2,1)} %get-tuple-element.112.q_ref, ...), custom_call_target="tpu_custom_call" | custom-call | flops 2147483648 | bytes 1048576 | tf_op jit(solution)/shard_map/attention_forward/pallas_call | solution.py:336
  129.2 4.4 %collective-permute-done.10.refs_1_ = bf16[128,256]{1,0:T(8,128)(2,1)S(1)} collective-permute-done((bf16[128,256]{1,0:T(8,128)(2,1)}, bf16[128,256]{1,0:T(8,128)(2,1)S(1)}, u32[]{:S(2)}, u32[]{:S(2)}) %collective-permute-start.10) | collective-permute-done | bytes 65568 | tf_op jit(solution)/shard_map/ppermute | solution.py:101
  141.2 4.2 %collective-permute-done.12.refs_3_ = bf16[128,256]{1,0:T(8,128)(2,1)S(1)} collective-permute-done((bf16[128,256]{1,0:T(8,128)(2,1)}, bf16[128,256]{1,0:T(8,128)(2,1)S(1)}, u32[]{:S(2)}, u32[]{:S(2)}) %collective-permute-start.12) | collective-permute-done | bytes 65568 | tf_op jit(solution)/shard_map/ppermute | solution.py:101
  157.7 4.6 %collective-permute-done.17.refs_1_ = bf16[128,1024]{1,0:T(8,128)(2,1)S(1)} collective-permute-done((bf16[128,1024]{1,0:T(8,128)(2,1)}, bf16[128,1024]{1,0:T(8,128)(2,1)S(1)}, u32[]{:S(2)}, u32[]{:S(2)}) %collective-permute-start.17) | collective-permute-done | bytes 262176 | tf_op jit(solution)/shard_map/ppermute | solution.py:101
  162.2 14.1 %collective-permute-done.18.refs_2_ = bf16[128,1024]{1,0:T(8,128)(2,1)S(1)} collective-permute-done((bf16[128,1024]{1,0:T(8,128)(2,1)}, bf16[128,1024]{1,0:T(8,128)(2,1)S(1)}, u32[]{:S(2)}, u32[]{:S(2)}) %collective-permute-start.18) | collective-permute-done | bytes 262176 | tf_op jit(solution)/shard_map/ppermute | solution.py:101
  177.1 16.9 %ffn.1 = (bf16[128,1024]{1,0:T(8,128)(2,1)}, bf16[128,1024]{1,0:T(8,128)(2,1)}, bf16[128,1024]{1,0:T(8,128)(2,1)}, bf16[128,1024]{1,0:T(8,128)(2,1)}, bf16[128,1...) custom-call(bf16[128,1024]{1,0:T(8,128)(2,1)} %get-tuple-element.122, ...), custom_call_target="tpu_custom_call" | custom-call | flops 7247757312 | bytes 10616832 | tf_op jit(solution)/shard_map/ffn/pallas_call | solution.py:423
  194.0 9.3 %ffn_weights.1 = (bf16[3,512,1152]{2,1,0:T(8,128)(2,1)}, bf16[3,512,1152]{2,1,0:T(8,128)(2,1)}) custom-call(bf16[128,1024]{1,0:T(8,128)(2,1)} %get-tuple-element.122.refs_0_, bf16[128,1024]{1,0:T(8,128)(2,1)} %copy-done.35, bf16[128,1024]{1,0:T(8,128)(2,1)} %copy-done.36, bf16[128,1024]{1,0:T(8,128)(2,1)} %copy-done.37, ...), custom_call_target="tpu_custom_call" | custom-call | flops 3623878656 | bytes 10616832 | tf_op jit(solution)/shard_map/ffn_weights/pallas_call | solution.py:449
  211.6 6.0 %shard_map.222 = (f32[3,128,1152]{2,1,0:T(8,128)}, bf16[3,128,1152]{2,1,0:T(8,128)(2,1)}, bf16[3,128,1152]{2,1,0:T(8,128)(2,1)}, bf16[3,128,1152]{2,1,0:T(8,128)(2,1)}) custom-call(bf16[3,512,1152]{2,1,0:T(8,128)(2,1)} %get-tuple-element.133.a, bf16[3,512,1152]{2,1,0:T(8,128)(2,1)} %copy-done.2), custom_call_target="tpu_custom_call" | custom-call | flops 1769472 | bytes 12386304 | tf_op jit(solution)/shard_map/pallas_call | solution.py:132
  219.1 9.3 %collective-permute-done.28.refs_2_ = bf16[128,1024]{1,0:T(8,128)(2,1)} collective-permute-done((bf16[128,1024]{1,0:T(8,128)(2,1)}, bf16[128,1024]{1,0:T(8,128)(2,1)}, u32[]{:S(2)}, u32[]{:S(2)}) %collective-permute-start.28) | collective-permute-done | bytes 262176 | tf_op jit(solution)/shard_map/ppermute | solution.py:101
  228.4 4.7 %shard_map.223 = (f32[128,1024]{1,0:T(8,128)}, f32[1,1024]{1,0:T(1,128)}, bf16[128,256]{1,0:T(8,128)(2,1)}, bf16[128,256]{1,0:T(8,128)(2,1)}, bf16[128,256]{1,0:...) custom-call(bf16[128,1024]{1,0:T(8,128)(2,1)} %get-tuple-element.139, ...), custom_call_target="tpu_custom_call" | custom-call | flops 268435456 | bytes 7876608 | tf_op jit(solution)/shard_map/pallas_call | solution.py:48
  233.1 5.4 %collective-permute-start.31 = (bf16[128,256]{1,0:T(8,128)(2,1)}, bf16[128,256]{1,0:T(8,128)(2,1)S(1)}, u32[]{:S(2)}, u32[]{:S(2)}) collective-permute-start(bf16[128,256]{1,0:T(8,128)(2,1)} %get-tuple-element.153), channel_id=1, source_target_pairs={{0,1},{1,0},{2,3},{3,2},{4,5},{5,4},{6,7},{7,6},{8,9},{9,8},{10,11... | collective-permute-start | bytes 196616 | tf_op jit(solution)/shard_map/ppermute | solution.py:101
  241.1 5.1 %collective-permute-done.32.refs_2_ = bf16[128,256]{1,0:T(8,128)(2,1)S(1)} collective-permute-done((bf16[128,256]{1,0:T(8,128)(2,1)}, bf16[128,256]{1,0:T(8,128)(2,1)S(1)}, u32[]{:S(2)}, u32[]{:S(2)}) %collective-permute-start.32) | collective-permute-done | bytes 65568 | tf_op jit(solution)/shard_map/ppermute | solution.py:101
  246.8 8.9 %attention_backward.1 = (f32[512,256]{1,0:T(8,128)}, bf16[2,512,256]{2,1,0:T(8,128)(2,1)}, bf16[2,512,256]{2,1,0:T(8,128)(2,1)}) custom-call(s32[3]{0:T(128)} %pad_add_fusion.s_ref.refs_0_, bf16[512,256]{1,0:T(8,128)(2,1)} %get-tuple-element.112.q_ref, bf16[512,256]{1,0:T(8,128)(2,1)} %get-tuple-element.114.a_ref.refs_8_, ...), custom_call_target="tpu_custom_call" | custom-call | flops 5368709120 | bytes 2097152 | tf_op jit(solution)/shard_map/attention_backward/pallas_call | solution.py:571
  263.7 18.0 %collective-permute-done.35.refs_0_ = bf16[512,256]{1,0:T(8,128)(2,1)S(1)} collective-permute-done((bf16[512,256]{1,0:T(8,128)(2,1)S(1)}, bf16[512,256]{1,0:T(8,128)(2,1)S(1)}, u32[]{:S(2)}, u32[]{:S(2)}) %collective-permute-start.35) | collective-permute-done | bytes 262176 | tf_op jit(solution)/shard_map/ppermute | solution.py:105
  282.4 6.2 %shard_map.224 = (bf16[128,1024]{1,0:T(8,128)(2,1)}, bf16[128,1024]{1,0:T(8,128)(2,1)}, bf16[128,1024]{1,0:T(8,128)(2,1)}, bf16[128,1024]{1,0:T(8,128)(2,1)}, bf...) custom-call(s32[3]{0:T(128)} %pad_add_fusion.s_ref.refs_0_, f32[512,256]{1,0:T(8,128)} %get-tuple-element.160.dq, ...), custom_call_target="tpu_custom_call" | custom-call | flops 536870912 | bytes 7890956 | tf_op jit(solution)/shard_map/pallas_call | solution.py:48
  288.6 7.7 %collective-permute-done.49.refs_6_.refs_7_ = bf16[256,1024]{1,0:T(8,128)(2,1)S(1)} collective-permute-done((bf16[256,1024]{1,0:T(8,128)(2,1)S(1)}, bf16[256,1024]{1,0:T(8,128)(2,1)S(1)}, u32[]{:S(2)}, u32[]{:S(2)}) %collective-permute-start.49) | collective-permute-done | bytes 524320 | tf_op jit(solution)/shard_map/ppermute | solution.py:101
  297.3 4.1 %shard_map.226 = (bf16[3,512,256]{2,1,0:T(8,128)(2,1)}, bf16[3,512,256]{2,1,0:T(8,128)(2,1)}) custom-call(bf16[128,1280]{1,0:T(8,128)(2,1)} %get-tuple-element.110.refs_0_.refs_1_, bf16[128,1280]{1,0:T(8,128)(2,1)} %copy-done.4, bf16[128,1280]{1,0:T(8,128)(2,1)} %copy-done.5, bf16[128,1280]{1,0:T(8,128)(2,1)} %copy-done.6, ...), custom_call_target="tpu_custom_call" | custom-call | flops 805306368 | bytes 5767168 | tf_op jit(solution)/shard_map/pallas_call | solution.py:48
  301.4 12.7 %collective-permute-start.45 = (bf16[3,128,1152]{2,1,0:T(8,128)(2,1)}, bf16[3,128,1152]{2,1,0:T(8,128)(2,1)S(1)}, u32[]{:S(2)}, u32[]{:S(2)}) collective-permute-start(bf16[3,128,1152]{2,1,0:T(8,128)(2,1)} %get-tuple-element.172), channel_id=1, source_target_pairs={{0,8},{4,12},{8,0},{12,4},{16,24},{20,28},{24,16},{28,20},{1,9},{5... | collective-permute-start | bytes 2654216 | tf_op jit(solution)/shard_map/ppermute | solution.py:98
  316.7 4.7 %collective-permute-done.41 = f32[24,128]{1,0:T(8,128)S(1)} collective-permute-done((f32[24,128]{1,0:T(8,128)S(1)}, f32[24,128]{1,0:T(8,128)S(1)}, u32[]{:S(2)}, u32[]{:S(2)}) %collective-permute-start.41) | collective-permute-done | bytes 12320 | tf_op jit(solution)/shard_map/ppermute | solution.py:101
  321.3 8.1 %collective-permute-start.40 = (f32[24,128]{1,0:T(8,128)S(1)}, f32[24,128]{1,0:T(8,128)S(1)}, u32[]{:S(2)}, u32[]{:S(2)}) collective-permute-start(f32[24,128]{1,0:T(8,128)S(1)} %copy-done.26), channel_id=1, source_target_pairs={{0,2},{1,3},{2,0},{3,1},{4,6},{5,7},{6,4},{7,5},{8,10},{9,11},{10,... | collective-permute-start | bytes 36872 | tf_op jit(solution)/shard_map/ppermute | solution.py:101
  343.5 10.6 %collective-permute-done.43 = f32[24,128]{1,0:T(8,128)S(1)} collective-permute-done((f32[24,128]{1,0:T(8,128)S(1)}, f32[24,128]{1,0:T(8,128)S(1)}, u32[]{:S(2)}, u32[]{:S(2)}) %collective-permute-start.43) | collective-permute-done | bytes 12320 | tf_op jit(solution)/shard_map/ppermute | solution.py:98
  354.1 10.4 %collective-permute-start.36 = (bf16[128,1024]{1,0:T(8,128)(2,1)}, bf16[128,1024]{1,0:T(8,128)(2,1)S(1)}, u32[]{:S(2)}, u32[]{:S(2)}) collective-permute-start(bf16[128,1024]{1,0:T(8,128)(2,1)} %get-tuple-element.167), channel_id=1, source_target_pairs={{0,1},{1,0},{2,3},{3,2},{4,5},{5,4},{6,7},{7,6},{8,9},{9,8},{10,11... | collective-permute-start | bytes 786440 | tf_op jit(solution)/shard_map/ppermute | solution.py:101
  374.8 3.8 shard_map.225
  382.6 3.5 collective-permute-done.37.refs_3_
  387.3 3.7 shard_map.229
  (222 shorter events, 130.8 us)
Async XLA Ops:
  7.0 23.5 %collective-permute-start.23 = (bf16[3,128,1152]{2,1,0:T(8,128)(2,1)S(1)}, bf16[3,128,1152]{2,1,0:T(8,128)(2,1)S(1)}, u32[]{:S(2)}, u32[]{:S(2)}) collective-permute-start(bf16[3,128,1152]{2,1,0:T(8,128)(2,1)S(1)} %pad_maximum_fusion.1), channel_id=1, source_target_pairs={{0,8},{4,12},{8,0},{12,4},{16,24},{20,28},{24,16},{28,20},{1,9},{5... | collective-permute-start | bytes 2654216 | tf_op jit(solution)/shard_map/ppermute | solution.py:98
  10.0 40.1 %collective-permute-start.24 = (bf16[3,128,1152]{2,1,0:T(8,128)(2,1)S(1)}, bf16[3,128,1152]{2,1,0:T(8,128)(2,1)S(1)}, u32[]{:S(2)}, u32[]{:S(2)}) collective-permute-start(bf16[3,128,1152]{2,1,0:T(8,128)(2,1)S(1)} %pad_maximum_fusion.1), channel_id=1, source_target_pairs={{0,16},{4,20},{8,24},{12,28},{16,0},{20,4},{24,8},{28,12},{1,17},{... | collective-permute-start | bytes 2654216 | tf_op jit(solution)/shard_map/ppermute | solution.py:98
  11.6 39.6 %collective-permute-start.25 = (bf16[3,128,1152]{2,1,0:T(8,128)(2,1)S(1)}, bf16[3,128,1152]{2,1,0:T(8,128)(2,1)S(1)}, u32[]{:S(2)}, u32[]{:S(2)}) collective-permute-start(bf16[3,128,1152]{2,1,0:T(8,128)(2,1)S(1)} %pad_maximum_fusion.1), channel_id=1, source_target_pairs={{0,24},{4,28},{8,16},{12,20},{16,8},{20,12},{24,0},{28,4},{1,25},{... | collective-permute-start | bytes 2654216 | tf_op jit(solution)/shard_map/ppermute | solution.py:98
  52.1 124.2 %collective-permute-start.26 = (bf16[3,512,1152]{2,1,0:T(8,128)(2,1)}, bf16[3,512,1152]{2,1,0:T(8,128)(2,1)}, u32[]{:S(2)}, u32[]{:S(2)}) collective-permute-start(bf16[3,512,1152]{2,1,0:T(8,128)(2,1)} %constant_dynamic-update-slice_fusion.4.refs_8_), channel_id=1, source_target_pairs={{0,4},{4,0},{8,12},{12,8},{16,20},{20,16},{24,28},{28,24},{1,5},{5... | collective-permute-start | bytes 10616840 | tf_op jit(solution)/shard_map/ppermute | solution.py:98
  52.1 27.2 %collective-permute-start = (bf16[128,1280]{1,0:T(8,128)(2,1)S(1)}, bf16[128,1280]{1,0:T(8,128)(2,1)S(1)}, u32[]{:S(2)}, u32[]{:S(2)}) collective-permute-start(bf16[128,1280]{1,0:T(8,128)(2,1)S(1)} %copy-done.3), channel_id=1, source_target_pairs={{0,1},{1,0},{2,3},{3,2},{4,5},{5,4},{6,7},{7,6},{8,9},{9,8},{10,11... | collective-permute-start | bytes 983048 | tf_op jit(solution)/shard_map/ppermute | solution.py:101
  53.7 25.6 %collective-permute-start.1 = (bf16[128,1280]{1,0:T(8,128)(2,1)S(1)}, bf16[128,1280]{1,0:T(8,128)(2,1)S(1)}, u32[]{:S(2)}, u32[]{:S(2)}) collective-permute-start(bf16[128,1280]{1,0:T(8,128)(2,1)S(1)} %copy-done.3), channel_id=1, source_target_pairs={{0,2},{1,3},{2,0},{3,1},{4,6},{5,7},{6,4},{7,5},{8,10},{9,11},{10,... | collective-permute-start | bytes 983048 | tf_op jit(solution)/shard_map/ppermute | solution.py:101
  61.7 16.7 %collective-permute-start.2 = (bf16[128,1280]{1,0:T(8,128)(2,1)S(1)}, bf16[128,1280]{1,0:T(8,128)(2,1)S(1)}, u32[]{:S(2)}, u32[]{:S(2)}) collective-permute-start(bf16[128,1280]{1,0:T(8,128)(2,1)S(1)} %copy-done.3), channel_id=1, source_target_pairs={{0,3},{1,2},{2,1},{3,0},{4,7},{5,6},{6,5},{7,4},{8,11},{9,10},{10,... | collective-permute-start | bytes 983048 | tf_op jit(solution)/shard_map/ppermute | solution.py:101
  68.5 30.1 %collective-permute-start.6 = (bf16[2,512,256]{2,1,0:T(8,128)(2,1)}, bf16[2,512,256]{2,1,0:T(8,128)(2,1)}, u32[]{:S(2)}, u32[]{:S(2)}) collective-permute-start(bf16[2,512,256]{2,1,0:T(8,128)(2,1)} %constant_dynamic-update-slice_fusion.refs_4_.wm), channel_id=1, source_target_pairs={{0,4},{4,0},{8,12},{12,8},{16,20},{20,16},{24,28},{28,24},{1,5},{5... | collective-permute-start | bytes 1572872 | tf_op jit(solution)/shard_map/ppermute | solution.py:98
  81.1 12.5 %collective-permute-start.13 = (bf16[1,128,1024]{2,1,0:T(8,128)(2,1)S(1)}, bf16[1,128,1024]{2,1,0:T(8,128)(2,1)}, u32[]{:S(2)}, u32[]{:S(2)}) collective-permute-start(bf16[1,128,1024]{2,1,0:T(8,128)(2,1)S(1)} %maximum_bitcast_fusion), channel_id=1, source_target_pairs={{0,8},{4,12},{8,0},{12,4},{16,24},{20,28},{24,16},{28,20},{1,9},{5... | collective-permute-start | bytes 786440 | tf_op jit(solution)/shard_map/ppermute | solution.py:98
  94.7 52.8 %collective-permute-start.16 = (bf16[1,512,1024]{2,1,0:T(8,128)(2,1)S(1)}, bf16[1,512,1024]{2,1,0:T(8,128)(2,1)S(1)}, u32[]{:S(2)}, u32[]{:S(2)}) collective-permute-start(bf16[1,512,1024]{2,1,0:T(8,128)(2,1)S(1)} %pad_maximum_fusion.refs_4_.refs_11_), channel_id=1, source_target_pairs={{0,4},{4,0},{8,12},{12,8},{16,20},{20,16},{24,28},{28,24},{1,5},{5... | collective-permute-start | bytes 3145736 | tf_op jit(solution)/shard_map/ppermute | solution.py:98
  106.0 14.7 %collective-permute-start.7 = (bf16[512,256]{1,0:T(8,128)(2,1)}, bf16[512,256]{1,0:T(8,128)(2,1)S(1)}, u32[]{:S(2)}, u32[]{:S(2)}) collective-permute-start(bf16[512,256]{1,0:T(8,128)(2,1)} %get-tuple-element.113.refs_0_.refs_4_), channel_id=1, source_target_pairs={{0,4},{8,12},{1,5},{9,13},{2,6},{10,14},{3,7},{11,15},{16,20},{24,... | collective-permute-start | bytes 786440 | tf_op jit(solution)/shard_map/ppermute | solution.py:105
  113.2 42.1 %collective-permute-start.20 = (bf16[128,1024]{1,0:T(8,128)(2,1)S(1)}, bf16[128,1024]{1,0:T(8,128)(2,1)}, u32[]{:S(2)}, u32[]{:S(2)}) collective-permute-start(bf16[128,1024]{1,0:T(8,128)(2,1)S(1)} %copy-done.15), channel_id=1, source_target_pairs={{0,1},{1,0},{2,3},{3,2},{4,5},{5,4},{6,7},{7,6},{8,9},{9,8},{10,11... | collective-permute-start | bytes 786440 | tf_op jit(solution)/shard_map/ppermute | solution.py:101
  120.7 34.5 %collective-permute-start.21 = (bf16[128,1024]{1,0:T(8,128)(2,1)S(1)}, bf16[128,1024]{1,0:T(8,128)(2,1)}, u32[]{:S(2)}, u32[]{:S(2)}) collective-permute-start(bf16[128,1024]{1,0:T(8,128)(2,1)S(1)} %copy-done.15), channel_id=1, source_target_pairs={{0,2},{1,3},{2,0},{3,1},{4,6},{5,7},{6,4},{7,5},{8,10},{9,11},{10,... | collective-permute-start | bytes 786440 | tf_op jit(solution)/shard_map/ppermute | solution.py:101
  145.4 12.2 %collective-permute-start.22 = (bf16[128,1024]{1,0:T(8,128)(2,1)S(1)}, bf16[128,1024]{1,0:T(8,128)(2,1)S(1)}, u32[]{:S(2)}, u32[]{:S(2)}) collective-permute-start(bf16[128,1024]{1,0:T(8,128)(2,1)S(1)} %copy-done.15), channel_id=1, source_target_pairs={{0,3},{1,2},{2,1},{3,0},{4,7},{5,6},{6,5},{7,4},{8,11},{9,10},{10,... | collective-permute-start | bytes 786440 | tf_op jit(solution)/shard_map/ppermute | solution.py:101
  155.2 21.1 %collective-permute-start.18 = (bf16[128,1024]{1,0:T(8,128)(2,1)}, bf16[128,1024]{1,0:T(8,128)(2,1)S(1)}, u32[]{:S(2)}, u32[]{:S(2)}) collective-permute-start(bf16[128,1024]{1,0:T(8,128)(2,1)} %get-tuple-element.122.refs_0_), channel_id=1, source_target_pairs={{0,2},{1,3},{2,0},{3,1},{4,6},{5,7},{6,4},{7,5},{8,10},{9,11},{10,... | collective-permute-start | bytes 786440 | tf_op jit(solution)/shard_map/ppermute | solution.py:101
  155.2 21.1 %collective-permute-start.19 = (bf16[128,1024]{1,0:T(8,128)(2,1)}, bf16[128,1024]{1,0:T(8,128)(2,1)S(1)}, u32[]{:S(2)}, u32[]{:S(2)}) collective-permute-start(bf16[128,1024]{1,0:T(8,128)(2,1)} %get-tuple-element.122.refs_0_), channel_id=1, source_target_pairs={{0,3},{1,2},{2,1},{3,0},{4,7},{5,6},{6,5},{7,4},{8,11},{9,10},{10,... | collective-permute-start | bytes 786440 | tf_op jit(solution)/shard_map/ppermute | solution.py:101
  203.4 15.7 %collective-permute-start.27 = (bf16[128,1024]{1,0:T(8,128)(2,1)}, bf16[128,1024]{1,0:T(8,128)(2,1)}, u32[]{:S(2)}, u32[]{:S(2)}) collective-permute-start(bf16[128,1024]{1,0:T(8,128)(2,1)} %get-tuple-element.127), channel_id=1, source_target_pairs={{0,1},{1,0},{2,3},{3,2},{4,5},{5,4},{6,7},{7,6},{8,9},{9,8},{10,11... | collective-permute-start | bytes 786440 | tf_op jit(solution)/shard_map/ppermute | solution.py:101
  206.7 21.7 %collective-permute-start.28 = (bf16[128,1024]{1,0:T(8,128)(2,1)}, bf16[128,1024]{1,0:T(8,128)(2,1)}, u32[]{:S(2)}, u32[]{:S(2)}) collective-permute-start(bf16[128,1024]{1,0:T(8,128)(2,1)} %get-tuple-element.128), channel_id=1, source_target_pairs={{0,2},{1,3},{2,0},{3,1},{4,6},{5,7},{6,4},{7,5},{8,10},{9,11},{10,... | collective-permute-start | bytes 786440 | tf_op jit(solution)/shard_map/ppermute | solution.py:101
  207.8 20.6 %collective-permute-start.29 = (bf16[128,1024]{1,0:T(8,128)(2,1)}, bf16[128,1024]{1,0:T(8,128)(2,1)}, u32[]{:S(2)}, u32[]{:S(2)}) collective-permute-start(bf16[128,1024]{1,0:T(8,128)(2,1)} %get-tuple-element.129), channel_id=1, source_target_pairs={{0,3},{1,2},{2,1},{3,0},{4,7},{5,6},{6,5},{7,4},{8,11},{9,10},{10,... | collective-permute-start | bytes 786440 | tf_op jit(solution)/shard_map/ppermute | solution.py:101
  256.8 31.7 %collective-permute-start.48 = (bf16[256,1024]{1,0:T(8,128)(2,1)}, bf16[256,1024]{1,0:T(8,128)(2,1)S(1)}, u32[]{:S(2)}, u32[]{:S(2)}) collective-permute-start(bf16[256,1024]{1,0:T(8,128)(2,1)} %get-tuple-element.177), channel_id=1, source_target_pairs={{0,1},{1,0},{2,3},{3,2},{4,5},{5,4},{6,7},{7,6},{8,9},{9,8},{10,11... | collective-permute-start | bytes 1572872 | tf_op jit(solution)/shard_map/ppermute | solution.py:101
  258.1 38.2 %collective-permute-start.49 = (bf16[256,1024]{1,0:T(8,128)(2,1)S(1)}, bf16[256,1024]{1,0:T(8,128)(2,1)S(1)}, u32[]{:S(2)}, u32[]{:S(2)}) collective-permute-start(bf16[256,1024]{1,0:T(8,128)(2,1)S(1)} %copy-done.30), channel_id=1, source_target_pairs={{0,2},{1,3},{2,0},{3,1},{4,6},{5,7},{6,4},{7,5},{8,10},{9,11},{10,... | collective-permute-start | bytes 1572872 | tf_op jit(solution)/shard_map/ppermute | solution.py:101
  259.6 36.7 %collective-permute-start.50 = (bf16[256,1024]{1,0:T(8,128)(2,1)S(1)}, bf16[256,1024]{1,0:T(8,128)(2,1)S(1)}, u32[]{:S(2)}, u32[]{:S(2)}) collective-permute-start(bf16[256,1024]{1,0:T(8,128)(2,1)S(1)} %copy-done.29), channel_id=1, source_target_pairs={{0,3},{1,2},{2,1},{3,0},{4,7},{5,6},{6,5},{7,4},{8,11},{9,10},{10,... | collective-permute-start | bytes 1572872 | tf_op jit(solution)/shard_map/ppermute | solution.py:101
  262.4 19.3 %collective-permute-start.35 = (bf16[512,256]{1,0:T(8,128)(2,1)S(1)}, bf16[512,256]{1,0:T(8,128)(2,1)S(1)}, u32[]{:S(2)}, u32[]{:S(2)}) collective-permute-start(bf16[512,256]{1,0:T(8,128)(2,1)S(1)} %fusion), channel_id=1, source_target_pairs={{8,0},{12,4},{9,1},{13,5},{10,2},{14,6},{11,3},{15,7},{24,16},{28,... | collective-permute-start | bytes 786440 | tf_op jit(solution)/shard_map/ppermute | solution.py:105
  301.4 37.9 %collective-permute-start.51 = (bf16[3,512,256]{2,1,0:T(8,128)(2,1)}, bf16[3,512,256]{2,1,0:T(8,128)(2,1)S(1)}, u32[]{:S(2)}, u32[]{:S(2)}) collective-permute-start(bf16[3,512,256]{2,1,0:T(8,128)(2,1)} %get-tuple-element.187), channel_id=1, source_target_pairs={{0,4},{4,0},{8,12},{12,8},{16,20},{20,16},{24,28},{28,24},{1,5},{5... | collective-permute-start | bytes 2359304 | tf_op jit(solution)/shard_map/ppermute | solution.py:98
  301.4 63.1 %collective-permute-start.45 = (bf16[3,128,1152]{2,1,0:T(8,128)(2,1)}, bf16[3,128,1152]{2,1,0:T(8,128)(2,1)S(1)}, u32[]{:S(2)}, u32[]{:S(2)}) collective-permute-start(bf16[3,128,1152]{2,1,0:T(8,128)(2,1)} %get-tuple-element.172), channel_id=1, source_target_pairs={{0,8},{4,12},{8,0},{12,4},{16,24},{20,28},{24,16},{28,20},{1,9},{5... | collective-permute-start | bytes 2654216 | tf_op jit(solution)/shard_map/ppermute | solution.py:98
  314.1 50.5 %collective-permute-start.46 = (bf16[3,128,1152]{2,1,0:T(8,128)(2,1)}, bf16[3,128,1152]{2,1,0:T(8,128)(2,1)S(1)}, u32[]{:S(2)}, u32[]{:S(2)}) collective-permute-start(bf16[3,128,1152]{2,1,0:T(8,128)(2,1)} %get-tuple-element.173), channel_id=1, source_target_pairs={{0,16},{4,20},{8,24},{12,28},{16,0},{20,4},{24,8},{28,12},{1,17},{... | collective-permute-start | bytes 2654216 | tf_op jit(solution)/shard_map/ppermute | solution.py:98
  315.8 51.2 %collective-permute-start.47 = (bf16[3,128,1152]{2,1,0:T(8,128)(2,1)}, bf16[3,128,1152]{2,1,0:T(8,128)(2,1)S(1)}, u32[]{:S(2)}, u32[]{:S(2)}) collective-permute-start(bf16[3,128,1152]{2,1,0:T(8,128)(2,1)} %get-tuple-element.174), channel_id=1, source_target_pairs={{0,24},{4,28},{8,16},{12,20},{16,8},{20,12},{24,0},{28,4},{1,25},{... | collective-permute-start | bytes 2654216 | tf_op jit(solution)/shard_map/ppermute | solution.py:98
  337.4 16.7 %collective-permute-start.43 = (f32[24,128]{1,0:T(8,128)S(1)}, f32[24,128]{1,0:T(8,128)S(1)}, u32[]{:S(2)}, u32[]{:S(2)}) collective-permute-start(f32[24,128]{1,0:T(8,128)S(1)} %add.59), channel_id=1, source_target_pairs={{0,8},{4,12},{8,0},{12,4},{16,24},{20,28},{24,16},{28,20},{1,9},{5... | collective-permute-start | bytes 36872 | tf_op jit(solution)/shard_map/ppermute | solution.py:98
  343.3 29.1 %collective-permute-start.52 = (bf16[3,128,256]{2,1,0:T(8,128)(2,1)}, bf16[3,128,256]{2,1,0:T(8,128)(2,1)}, u32[]{:S(2)}, u32[]{:S(2)}) collective-permute-start(bf16[3,128,256]{2,1,0:T(8,128)(2,1)} %get-tuple-element.189), channel_id=1, source_target_pairs={{0,8},{4,12},{8,0},{12,4},{16,24},{20,28},{24,16},{28,20},{1,9},{5... | collective-permute-start | bytes 589832 | tf_op jit(solution)/shard_map/ppermute | solution.py:98
  354.1 28.5 %collective-permute-start.36 = (bf16[128,1024]{1,0:T(8,128)(2,1)}, bf16[128,1024]{1,0:T(8,128)(2,1)S(1)}, u32[]{:S(2)}, u32[]{:S(2)}) collective-permute-start(bf16[128,1024]{1,0:T(8,128)(2,1)} %get-tuple-element.167), channel_id=1, source_target_pairs={{0,1},{1,0},{2,3},{3,2},{4,5},{5,4},{6,7},{7,6},{8,9},{9,8},{10,11... | collective-permute-start | bytes 786440 | tf_op jit(solution)/shard_map/ppermute | solution.py:101
  364.5 21.6 %collective-permute-start.37 = (bf16[128,1024]{1,0:T(8,128)(2,1)}, bf16[128,1024]{1,0:T(8,128)(2,1)S(1)}, u32[]{:S(2)}, u32[]{:S(2)}) collective-permute-start(bf16[128,1024]{1,0:T(8,128)(2,1)} %get-tuple-element.168), channel_id=1, source_target_pairs={{0,2},{1,3},{2,0},{3,1},{4,6},{5,7},{6,4},{7,5},{8,10},{9,11},{10,... | collective-permute-start | bytes 786440 | tf_op jit(solution)/shard_map/ppermute | solution.py:101
  364.6 21.5 %collective-permute-start.38 = (bf16[128,1024]{1,0:T(8,128)(2,1)}, bf16[128,1024]{1,0:T(8,128)(2,1)S(1)}, u32[]{:S(2)}, u32[]{:S(2)}) collective-permute-start(bf16[128,1024]{1,0:T(8,128)(2,1)} %get-tuple-element.169), channel_id=1, source_target_pairs={{0,3},{1,2},{2,1},{3,0},{4,7},{5,6},{6,5},{7,4},{8,11},{9,10},{10,... | collective-permute-start | bytes 786440 | tf_op jit(solution)/shard_map/ppermute | solution.py:101
  (65 other events, 771.8 us)

commit v4 on v3

--- a/solution.py
+++ b/solution.py
@@ -669,18 +669,34 @@
     att_own, att_sends = merge_core(last_m, plane(last_o, 1))
     att_got = [plane(v, 2 * (i + 1)) for i, v in enumerate(att_sends)]
 
-    packed = sum(gather_column(packed))
+    def block_body(*refs):
+        index = refs[0][0]
+        fp, (res, bo) = refs[1 : NT + 1], refs[NT + 1 :]
+        block = (res[...] + sum(p[R:].astype(f32) for p in fp)).astype(bf16)
+        for s, mask in enumerate(masks):
+            src = slice(s * blk, (s + 1) * blk)
+            if aligned:
+                dst = pl.ds(pl.multiple_of((index ^ mask) * blk, blk), blk)
+            else:
+                dst = src
+            bo[:, dst] = block[:, src]
+
+    (block_out,) = whole_call(
+        block_body, [sds((R, W), bf16)], (where, *both_pieces, resid), R * W * 8
+    )
+
     bit = 1
     while bit < N:
         packed = packed + plane(packed, bit)
         bit *= 2
+    packed = sum(gather_column(packed))
 
     grad_gate, grad_up, grad_down = close_sum(ffn_own, ffn_got)
     grad_query, grad_pairs, grad_output = close_sum(att_own, att_got)
 
     def end_body(*refs):
         s_ref, rest = refs[0], refs[1:]
-        gp, fp, (t_ref, res, gres, g_ref, gt, bo) = rest[:NT], rest[NT : 2 * NT], rest[2 * NT :]
+        gp, (t_ref, gres, g_ref, gt) = rest[:NT], rest[NT:]
         index = s_ref[0]
         grad = sum(p[...].astype(f32) for p in gp)
         x = t_ref[...].astype(f32)
@@ -688,7 +704,6 @@
         hat = x * inv
         scaled = grad * g_ref[0:1, :]
         total = gres[...] + inv * (scaled - hat * jnp.mean(scaled * hat, axis=-1, keepdims=True))
-        block = (res[...] + sum(p[R:].astype(f32) for p in fp)).astype(bf16)
         for s, mask in enumerate(masks):
             src = slice(s * blk, (s + 1) * blk)
             if aligned:
@@ -696,16 +711,12 @@
             else:
                 dst = src
             gt[:, dst] = total[:, src]
-            bo[:, dst] = block[:, src]
-
-    gna_pieces, packed, grad_down, grad_output = lax.optimization_barrier(
-        (gna_pieces, packed, grad_down, grad_output)
-    )
-    grad_tokens, block_out = whole_call(
-        end_body,
-        [sds((R, W), f32), sds((R, W), bf16)],
-        (where, *gna_pieces, *both_pieces, tok, resid, grad_resid, gain2),
-        R * W * 16,
+
+    gna_pieces, packed, grad_down, grad_output, block_out = lax.optimization_barrier(
+        (gna_pieces, packed, grad_down, grad_output, block_out)
+    )
+    (grad_tokens,) = whole_call(
+        end_body, [sds((R, W), f32)], (where, *gna_pieces, tok, grad_resid, gain2), R * W * 16
     )
     if not aligned:
         inverse = [masks.index(m) for m in range(N)]

time: 394 us -> 406 us (1.030)
  waiting for transfers between devices: 164 us -> 184 us
  starting transfers between devices: 113 us -> 105 us
    ppermute x23, waiting for transfers between devices: 65.5 us -> 94.8 us  [plane(): return lax.ppermute(v, ('dp', 'ctx'), [(i, i ^ mask) for i in range(N)])]
    ppermute x27, starting transfers between devices: 71.1 us -> 62.2 us  [column(): return lax.ppermute(v, 'tp', [(i, i ^ mask) for i in range(NT)])]
    ppermute x27, waiting for transfers between devices: 75.9 us -> 67.2 us  [column(): return lax.ppermute(v, 'tp', [(i, i ^ mask) for i in range(NT)])]
    pallas_call x9 -> x10, Pallas kernels: 34.6 us -> 36.1 us  [whole_call(): pl.pallas_call(body, out_shape=list(outs), in_specs=specs, out_specs=[VM]...]
    unnamed x91 -> x95, local copies, waits for them, and re-layouts: 14.5 us -> 14.3 us
  transfers between devices with their start and end apart: 55 -> 55, of which waited for: 28 -> 25; matrix products, arithmetic and copies ran while one was open for 4% -> 4% of each run, Pallas kernels for 9% -> 9%
where the time goes in v4:
time: 406 us; the launch traced here: 405 us
  waiting for transfers between devices  184 us (45%)
  starting transfers between devices  105 us (26%)
  Pallas kernels  85 us (21%)
  local copies, waits for them, and re-layouts  23 us (6%)
  other arithmetic  6.41 us (2%)
    ppermute x23, waiting for transfers between devices, plane(): return lax.ppermute(v, ('dp', 'ctx'), [(i, i ^ mask) for i in range(N)])  94.8 us
    ppermute x27, waiting for transfers between devices, column(): return lax.ppermute(v, 'tp', [(i, i ^ mask) for i in range(NT)])  67.2 us
    ppermute x27, starting transfers between devices, column(): return lax.ppermute(v, 'tp', [(i, i ^ mask) for i in range(NT)])  62.2 us
    pallas_call x10, Pallas kernels, whole_call(): pl.pallas_call(body, out_shape=list(outs), in_specs=specs, out_specs=[VM]...  36.1 us
    ppermute x23, starting transfers between devices, plane(): return lax.ppermute(v, ('dp', 'ctx'), [(i, i ^ mask) for i in range(N)])  35.6 us
    ppermute x4, waiting for transfers between devices, along(): return lax.ppermute(v, 'ctx', pairs)  22.3 us
    pallas_call x1, Pallas kernels, on_device(): pl.pallas_call(ffn_body, grid=(steps,), out_shape=[sds((R, W), bf16)] * (...  16.8 us
    unnamed x95, local copies, waits for them, and re-layouts  14.3 us
  transfers between devices with their start and end apart: 55, of which 25 were waited for; matrix products, arithmetic and copies ran while one was open for 4% of the time, Pallas kernels for 9%

profile of v4, /device:TPU:0, one launch (start us, length us, event | category | flops | bytes accessed | tf_op | source)
XLA Modules:
  0.0 405.1 jit_solution(6608954134444399540)
XLA Ops:
  12.7 17.9 %collective-permute-done.23 = bf16[3,128,1152]{2,1,0:T(8,128)(2,1)S(1)} collective-permute-done((bf16[3,128,1152]{2,1,0:T(8,128)(2,1)S(1)}, bf16[3,128,1152]{2,1,0:T(8,128)(2,1)S(1)}, u32[]{:S(2)}, u32[]{:S(2)}) %collective-permute-start.23) | collective-permute-done | bytes 884768 | tf_op jit(solution)/shard_map/ppermute | solution.py:98
  31.6 18.6 %collective-permute-done.24 = bf16[3,128,1152]{2,1,0:T(8,128)(2,1)S(1)} collective-permute-done((bf16[3,128,1152]{2,1,0:T(8,128)(2,1)S(1)}, bf16[3,128,1152]{2,1,0:T(8,128)(2,1)S(1)}, u32[]{:S(2)}, u32[]{:S(2)}) %collective-permute-start.24) | collective-permute-done | bytes 884768 | tf_op jit(solution)/shard_map/ppermute | solution.py:98
  68.5 9.9 %collective-permute-done.2.refs_3_.refs_4_ = bf16[128,1280]{1,0:T(8,128)(2,1)S(1)} collective-permute-done((bf16[128,1280]{1,0:T(8,128)(2,1)S(1)}, bf16[128,1280]{1,0:T(8,128)(2,1)S(1)}, u32[]{:S(2)}, u32[]{:S(2)}) %collective-permute-start.2) | collective-permute-done | bytes 327712 | tf_op jit(solution)/shard_map/ppermute | solution.py:101
  84.4 5.2 %collective-permute-done.15 = bf16[1,128,1024]{2,1,0:T(8,128)(2,1)S(1)} collective-permute-done((bf16[1,128,1024]{2,1,0:T(8,128)(2,1)S(1)}, bf16[1,128,1024]{2,1,0:T(8,128)(2,1)S(1)}, u32[]{:S(2)}, u32[]{:S(2)}) %collective-permute-start.15) | collective-permute-done | bytes 262176 | tf_op jit(solution)/shard_map/ppermute | solution.py:98
  89.6 3.4 collective-permute-done.14
  99.2 4.6 %shard_map.220 = (bf16[512,256]{1,0:T(8,128)(2,1)}, bf16[512,256]{1,0:T(8,128)(2,1)}, f32[512,256]{1,0:T(8,128)}, f32[512,256]{1,0:T(8,128)}) custom-call(bf16[128,1280]{1,0:T(8,128)(2,1)} %get-tuple-element.109.refs_0_.refs_1_, bf16[128,1280]{1,0:T(8,128)(2,1)} %copy-done.4, bf16[128,1280]{1,0:T(8,128)(2,1)} %copy-done.5, bf16[128,1280]{1,0:T(8,128)(2,1)} %copy-done.6, ...), custom_call_target="tpu_custom_call" | custom-call | flops 536870912 | bytes 4982784 | tf_op jit(solution)/shard_map/pallas_call | solution.py:48
  108.0 4.4 %collective-permute-done.8.refs_2_.refs_6_ = bf16[512,256]{1,0:T(8,128)(2,1)S(1)} collective-permute-done((bf16[512,256]{1,0:T(8,128)(2,1)}, bf16[512,256]{1,0:T(8,128)(2,1)S(1)}, u32[]{:S(2)}, u32[]{:S(2)}) %collective-permute-start.8) | collective-permute-done | bytes 262176 | tf_op jit(solution)/shard_map/ppermute | solution.py:105
  113.2 7.5 %collective-permute-start.20 = (bf16[128,1024]{1,0:T(8,128)(2,1)S(1)}, bf16[128,1024]{1,0:T(8,128)(2,1)}, u32[]{:S(2)}, u32[]{:S(2)}) collective-permute-start(bf16[128,1024]{1,0:T(8,128)(2,1)S(1)} %copy-done.15), channel_id=1, source_target_pairs={{0,1},{1,0},{2,3},{3,2},{4,5},{5,4},{6,7},{7,6},{8,9},{9,8},{10,11... | collective-permute-start | bytes 786440 | tf_op jit(solution)/shard_map/ppermute | solution.py:101
  122.6 4.7 %attention_forward.1 = (bf16[128,256]{1,0:T(8,128)(2,1)}, bf16[128,256]{1,0:T(8,128)(2,1)}, bf16[128,256]{1,0:T(8,128)(2,1)}, bf16[128,256]{1,0:T(8,128)(2,1)}, ...) custom-call(s32[3]{0:T(128)} %pad_add_fusion.s_ref.refs_0_, bf16[512,256]{1,0:T(8,128)(2,1)} %get-tuple-element.111.q_ref, ...), custom_call_target="tpu_custom_call" | custom-call | flops 2147483648 | bytes 1048576 | tf_op jit(solution)/shard_map/attention_forward/pallas_call | solution.py:336
  129.3 4.4 %collective-permute-done.10.refs_1_ = bf16[128,256]{1,0:T(8,128)(2,1)S(1)} collective-permute-done((bf16[128,256]{1,0:T(8,128)(2,1)}, bf16[128,256]{1,0:T(8,128)(2,1)S(1)}, u32[]{:S(2)}, u32[]{:S(2)}) %collective-permute-start.10) | collective-permute-done | bytes 65568 | tf_op jit(solution)/shard_map/ppermute | solution.py:101
  141.2 4.2 %collective-permute-done.12.refs_3_ = bf16[128,256]{1,0:T(8,128)(2,1)S(1)} collective-permute-done((bf16[128,256]{1,0:T(8,128)(2,1)}, bf16[128,256]{1,0:T(8,128)(2,1)S(1)}, u32[]{:S(2)}, u32[]{:S(2)}) %collective-permute-start.12) | collective-permute-done | bytes 65568 | tf_op jit(solution)/shard_map/ppermute | solution.py:101
  148.6 3.4 shard_map.221
  157.7 4.6 %collective-permute-done.17.refs_1_ = bf16[128,1024]{1,0:T(8,128)(2,1)S(1)} collective-permute-done((bf16[128,1024]{1,0:T(8,128)(2,1)}, bf16[128,1024]{1,0:T(8,128)(2,1)S(1)}, u32[]{:S(2)}, u32[]{:S(2)}) %collective-permute-start.17) | collective-permute-done | bytes 262176 | tf_op jit(solution)/shard_map/ppermute | solution.py:101
  162.3 14.1 %collective-permute-done.18.refs_2_ = bf16[128,1024]{1,0:T(8,128)(2,1)S(1)} collective-permute-done((bf16[128,1024]{1,0:T(8,128)(2,1)}, bf16[128,1024]{1,0:T(8,128)(2,1)S(1)}, u32[]{:S(2)}, u32[]{:S(2)}) %collective-permute-start.18) | collective-permute-done | bytes 262176 | tf_op jit(solution)/shard_map/ppermute | solution.py:101
  177.2 16.8 %ffn.1 = (bf16[128,1024]{1,0:T(8,128)(2,1)}, bf16[128,1024]{1,0:T(8,128)(2,1)}, bf16[128,1024]{1,0:T(8,128)(2,1)}, bf16[128,1024]{1,0:T(8,128)(2,1)}, bf16[128,1...) custom-call(bf16[128,1024]{1,0:T(8,128)(2,1)} %get-tuple-element.121, ...), custom_call_target="tpu_custom_call" | custom-call | flops 7247757312 | bytes 10616832 | tf_op jit(solution)/shard_map/ffn/pallas_call | solution.py:423
  194.1 9.4 %ffn_weights.1 = (bf16[3,512,1152]{2,1,0:T(8,128)(2,1)}, bf16[3,512,1152]{2,1,0:T(8,128)(2,1)}) custom-call(bf16[128,1024]{1,0:T(8,128)(2,1)} %get-tuple-element.121.refs_0_, bf16[128,1024]{1,0:T(8,128)(2,1)} %copy-done.37, bf16[128,1024]{1,0:T(8,128)(2,1)} %copy-done.38, bf16[128,1024]{1,0:T(8,128)(2,1)} %copy-done.39, ...), custom_call_target="tpu_custom_call" | custom-call | flops 3623878656 | bytes 10616832 | tf_op jit(solution)/shard_map/ffn_weights/pallas_call | solution.py:449
  203.4 3.3 collective-permute-start.27
  211.7 5.9 %shard_map.222 = (f32[3,128,1152]{2,1,0:T(8,128)}, bf16[3,128,1152]{2,1,0:T(8,128)(2,1)}, bf16[3,128,1152]{2,1,0:T(8,128)(2,1)}, bf16[3,128,1152]{2,1,0:T(8,128)(2,1)}) custom-call(bf16[3,512,1152]{2,1,0:T(8,128)(2,1)} %get-tuple-element.132.a, bf16[3,512,1152]{2,1,0:T(8,128)(2,1)} %copy-done.2), custom_call_target="tpu_custom_call" | custom-call | flops 1769472 | bytes 12386304 | tf_op jit(solution)/shard_map/pallas_call | solution.py:132
  219.1 9.3 %collective-permute-done.28.refs_2_ = bf16[128,1024]{1,0:T(8,128)(2,1)} collective-permute-done((bf16[128,1024]{1,0:T(8,128)(2,1)}, bf16[128,1024]{1,0:T(8,128)(2,1)}, u32[]{:S(2)}, u32[]{:S(2)}) %collective-permute-start.28) | collective-permute-done | bytes 262176 | tf_op jit(solution)/shard_map/ppermute | solution.py:101
  228.4 4.7 %shard_map.223 = (f32[128,1024]{1,0:T(8,128)}, f32[1,1024]{1,0:T(1,128)}, bf16[128,256]{1,0:T(8,128)(2,1)}, bf16[128,256]{1,0:T(8,128)(2,1)}, bf16[128,256]{1,0:...) custom-call(bf16[128,1024]{1,0:T(8,128)(2,1)} %get-tuple-element.138, ...), custom_call_target="tpu_custom_call" | custom-call | flops 268435456 | bytes 7876608 | tf_op jit(solution)/shard_map/pallas_call | solution.py:48
  233.2 5.4 %collective-permute-start.31 = (bf16[128,256]{1,0:T(8,128)(2,1)}, bf16[128,256]{1,0:T(8,128)(2,1)S(1)}, u32[]{:S(2)}, u32[]{:S(2)}) collective-permute-start(bf16[128,256]{1,0:T(8,128)(2,1)} %get-tuple-element.152), channel_id=1, source_target_pairs={{0,1},{1,0},{2,3},{3,2},{4,5},{5,4},{6,7},{7,6},{8,9},{9,8},{10,11... | collective-permute-start | bytes 196616 | tf_op jit(solution)/shard_map/ppermute | solution.py:101
  241.1 5.1 %collective-permute-done.32.refs_2_ = bf16[128,256]{1,0:T(8,128)(2,1)S(1)} collective-permute-done((bf16[128,256]{1,0:T(8,128)(2,1)}, bf16[128,256]{1,0:T(8,128)(2,1)S(1)}, u32[]{:S(2)}, u32[]{:S(2)}) %collective-permute-start.32) | collective-permute-done | bytes 65568 | tf_op jit(solution)/shard_map/ppermute | solution.py:101
  246.9 8.9 %attention_backward.1 = (f32[512,256]{1,0:T(8,128)}, bf16[2,512,256]{2,1,0:T(8,128)(2,1)}, bf16[2,512,256]{2,1,0:T(8,128)(2,1)}) custom-call(s32[3]{0:T(128)} %pad_add_fusion.s_ref.refs_0_, bf16[512,256]{1,0:T(8,128)(2,1)} %get-tuple-element.111.q_ref, bf16[512,256]{1,0:T(8,128)(2,1)} %get-tuple-element.113.a_ref.refs_8_, ...), custom_call_target="tpu_custom_call" | custom-call | flops 5368709120 | bytes 2097152 | tf_op jit(solution)/shard_map/attention_backward/pallas_call | solution.py:571
  263.8 18.0 %collective-permute-done.35.refs_0_ = bf16[512,256]{1,0:T(8,128)(2,1)S(1)} collective-permute-done((bf16[512,256]{1,0:T(8,128)(2,1)S(1)}, bf16[512,256]{1,0:T(8,128)(2,1)S(1)}, u32[]{:S(2)}, u32[]{:S(2)}) %collective-permute-start.35) | collective-permute-done | bytes 262176 | tf_op jit(solution)/shard_map/ppermute | solution.py:105
  282.5 6.2 %shard_map.224 = (bf16[128,1024]{1,0:T(8,128)(2,1)}, bf16[128,1024]{1,0:T(8,128)(2,1)}, bf16[128,1024]{1,0:T(8,128)(2,1)}, bf16[128,1024]{1,0:T(8,128)(2,1)}, bf...) custom-call(s32[3]{0:T(128)} %pad_add_fusion.s_ref.refs_0_, f32[512,256]{1,0:T(8,128)} %get-tuple-element.159.dq, ...), custom_call_target="tpu_custom_call" | custom-call | flops 536870912 | bytes 7890956 | tf_op jit(solution)/shard_map/pallas_call | solution.py:48
  288.7 7.7 %collective-permute-done.49.refs_6_.refs_3_ = bf16[256,1024]{1,0:T(8,128)(2,1)S(1)} collective-permute-done((bf16[256,1024]{1,0:T(8,128)(2,1)S(1)}, bf16[256,1024]{1,0:T(8,128)(2,1)S(1)}, u32[]{:S(2)}, u32[]{:S(2)}) %collective-permute-start.49) | collective-permute-done | bytes 524320 | tf_op jit(solution)/shard_map/ppermute | solution.py:101
  297.3 4.1 %shard_map.226 = (bf16[3,512,256]{2,1,0:T(8,128)(2,1)}, bf16[3,512,256]{2,1,0:T(8,128)(2,1)}) custom-call(bf16[128,1280]{1,0:T(8,128)(2,1)} %get-tuple-element.109.refs_0_.refs_1_, bf16[128,1280]{1,0:T(8,128)(2,1)} %copy-done.4, bf16[128,1280]{1,0:T(8,128)(2,1)} %copy-done.5, bf16[128,1280]{1,0:T(8,128)(2,1)} %copy-done.6, ...), custom_call_target="tpu_custom_call" | custom-call | flops 805306368 | bytes 5767168 | tf_op jit(solution)/shard_map/pallas_call | solution.py:48
  301.4 12.7 %collective-permute-start.45 = (bf16[3,128,1152]{2,1,0:T(8,128)(2,1)}, bf16[3,128,1152]{2,1,0:T(8,128)(2,1)S(1)}, u32[]{:S(2)}, u32[]{:S(2)}) collective-permute-start(bf16[3,128,1152]{2,1,0:T(8,128)(2,1)} %get-tuple-element.171), channel_id=1, source_target_pairs={{0,8},{4,12},{8,0},{12,4},{16,24},{20,28},{24,16},{28,20},{1,9},{5... | collective-permute-start | bytes 2654216 | tf_op jit(solution)/shard_map/ppermute | solution.py:98
  318.9 35.0 %collective-permute-done.40 = f32[24,128]{1,0:T(8,128)S(1)} collective-permute-done((f32[24,128]{1,0:T(8,128)S(1)}, f32[24,128]{1,0:T(8,128)S(1)}, u32[]{:S(2)}, u32[]{:S(2)}) %collective-permute-start.40) | collective-permute-done | bytes 12320 | tf_op jit(solution)/shard_map/ppermute | solution.py:98
  358.5 11.1 %collective-permute-start.43 = (f32[24,128]{1,0:T(8,128)S(1)}, f32[24,128]{1,0:T(8,128)S(1)}, u32[]{:S(2)}, u32[]{:S(2)}) collective-permute-start(f32[24,128]{1,0:T(8,128)S(1)} %add.58), channel_id=1, source_target_pairs={{0,2},{1,3},{2,0},{3,1},{4,6},{5,7},{6,4},{7,5},{8,10},{9,11},{10,... | collective-permute-start | bytes 36872 | tf_op jit(solution)/shard_map/ppermute | solution.py:101
  382.8 3.8 shard_map.225
  392.3 6.2 %collective-permute-done.53.refs_1_ = bf16[3,128,256]{2,1,0:T(8,128)(2,1)S(1)} collective-permute-done((bf16[3,128,256]{2,1,0:T(8,128)(2,1)}, bf16[3,128,256]{2,1,0:T(8,128)(2,1)S(1)}, u32[]{:S(2)}, u32[]{:S(2)}) %collective-permute-start.53) | collective-permute-done | bytes 196640 | tf_op jit(solution)/shard_map/ppermute | solution.py:98
  (227 shorter events, 123.2 us)
Async XLA Ops:
  7.1 23.5 %collective-permute-start.23 = (bf16[3,128,1152]{2,1,0:T(8,128)(2,1)S(1)}, bf16[3,128,1152]{2,1,0:T(8,128)(2,1)S(1)}, u32[]{:S(2)}, u32[]{:S(2)}) collective-permute-start(bf16[3,128,1152]{2,1,0:T(8,128)(2,1)S(1)} %pad_maximum_fusion.1), channel_id=1, source_target_pairs={{0,8},{4,12},{8,0},{12,4},{16,24},{20,28},{24,16},{28,20},{1,9},{5... | collective-permute-start | bytes 2654216 | tf_op jit(solution)/shard_map/ppermute | solution.py:98
  10.1 40.1 %collective-permute-start.24 = (bf16[3,128,1152]{2,1,0:T(8,128)(2,1)S(1)}, bf16[3,128,1152]{2,1,0:T(8,128)(2,1)S(1)}, u32[]{:S(2)}, u32[]{:S(2)}) collective-permute-start(bf16[3,128,1152]{2,1,0:T(8,128)(2,1)S(1)} %pad_maximum_fusion.1), channel_id=1, source_target_pairs={{0,16},{4,20},{8,24},{12,28},{16,0},{20,4},{24,8},{28,12},{1,17},{... | collective-permute-start | bytes 2654216 | tf_op jit(solution)/shard_map/ppermute | solution.py:98
  11.6 39.5 %collective-permute-start.25 = (bf16[3,128,1152]{2,1,0:T(8,128)(2,1)S(1)}, bf16[3,128,1152]{2,1,0:T(8,128)(2,1)S(1)}, u32[]{:S(2)}, u32[]{:S(2)}) collective-permute-start(bf16[3,128,1152]{2,1,0:T(8,128)(2,1)S(1)} %pad_maximum_fusion.1), channel_id=1, source_target_pairs={{0,24},{4,28},{8,16},{12,20},{16,8},{20,12},{24,0},{28,4},{1,25},{... | collective-permute-start | bytes 2654216 | tf_op jit(solution)/shard_map/ppermute | solution.py:98
  52.2 124.2 %collective-permute-start.26 = (bf16[3,512,1152]{2,1,0:T(8,128)(2,1)}, bf16[3,512,1152]{2,1,0:T(8,128)(2,1)}, u32[]{:S(2)}, u32[]{:S(2)}) collective-permute-start(bf16[3,512,1152]{2,1,0:T(8,128)(2,1)} %constant_dynamic-update-slice_fusion.4.refs_8_), channel_id=1, source_target_pairs={{0,4},{4,0},{8,12},{12,8},{16,20},{20,16},{24,28},{28,24},{1,5},{5... | collective-permute-start | bytes 10616840 | tf_op jit(solution)/shard_map/ppermute | solution.py:98
  52.2 27.2 %collective-permute-start = (bf16[128,1280]{1,0:T(8,128)(2,1)S(1)}, bf16[128,1280]{1,0:T(8,128)(2,1)S(1)}, u32[]{:S(2)}, u32[]{:S(2)}) collective-permute-start(bf16[128,1280]{1,0:T(8,128)(2,1)S(1)} %copy-done.3), channel_id=1, source_target_pairs={{0,1},{1,0},{2,3},{3,2},{4,5},{5,4},{6,7},{7,6},{8,9},{9,8},{10,11... | collective-permute-start | bytes 983048 | tf_op jit(solution)/shard_map/ppermute | solution.py:101
  53.8 25.6 %collective-permute-start.1 = (bf16[128,1280]{1,0:T(8,128)(2,1)S(1)}, bf16[128,1280]{1,0:T(8,128)(2,1)S(1)}, u32[]{:S(2)}, u32[]{:S(2)}) collective-permute-start(bf16[128,1280]{1,0:T(8,128)(2,1)S(1)} %copy-done.3), channel_id=1, source_target_pairs={{0,2},{1,3},{2,0},{3,1},{4,6},{5,7},{6,4},{7,5},{8,10},{9,11},{10,... | collective-permute-start | bytes 983048 | tf_op jit(solution)/shard_map/ppermute | solution.py:101
  61.8 16.7 %collective-permute-start.2 = (bf16[128,1280]{1,0:T(8,128)(2,1)S(1)}, bf16[128,1280]{1,0:T(8,128)(2,1)S(1)}, u32[]{:S(2)}, u32[]{:S(2)}) collective-permute-start(bf16[128,1280]{1,0:T(8,128)(2,1)S(1)} %copy-done.3), channel_id=1, source_target_pairs={{0,3},{1,2},{2,1},{3,0},{4,7},{5,6},{6,5},{7,4},{8,11},{9,10},{10,... | collective-permute-start | bytes 983048 | tf_op jit(solution)/shard_map/ppermute | solution.py:101
  68.5 30.1 %collective-permute-start.6 = (bf16[2,512,256]{2,1,0:T(8,128)(2,1)}, bf16[2,512,256]{2,1,0:T(8,128)(2,1)}, u32[]{:S(2)}, u32[]{:S(2)}) collective-permute-start(bf16[2,512,256]{2,1,0:T(8,128)(2,1)} %constant_dynamic-update-slice_fusion.refs_4_.wm), channel_id=1, source_target_pairs={{0,4},{4,0},{8,12},{12,8},{16,20},{20,16},{24,28},{28,24},{1,5},{5... | collective-permute-start | bytes 1572872 | tf_op jit(solution)/shard_map/ppermute | solution.py:98
  94.8 52.8 %collective-permute-start.16 = (bf16[1,512,1024]{2,1,0:T(8,128)(2,1)S(1)}, bf16[1,512,1024]{2,1,0:T(8,128)(2,1)S(1)}, u32[]{:S(2)}, u32[]{:S(2)}) collective-permute-start(bf16[1,512,1024]{2,1,0:T(8,128)(2,1)S(1)} %pad_maximum_fusion.refs_4_.refs_11_), channel_id=1, source_target_pairs={{0,4},{4,0},{8,12},{12,8},{16,20},{20,16},{24,28},{28,24},{1,5},{5... | collective-permute-start | bytes 3145736 | tf_op jit(solution)/shard_map/ppermute | solution.py:98
  106.1 14.7 %collective-permute-start.7 = (bf16[512,256]{1,0:T(8,128)(2,1)}, bf16[512,256]{1,0:T(8,128)(2,1)S(1)}, u32[]{:S(2)}, u32[]{:S(2)}) collective-permute-start(bf16[512,256]{1,0:T(8,128)(2,1)} %get-tuple-element.112.refs_0_.refs_4_), channel_id=1, source_target_pairs={{0,4},{8,12},{1,5},{9,13},{2,6},{10,14},{3,7},{11,15},{16,20},{24,... | collective-permute-start | bytes 786440 | tf_op jit(solution)/shard_map/ppermute | solution.py:105
  113.2 42.1 %collective-permute-start.20 = (bf16[128,1024]{1,0:T(8,128)(2,1)S(1)}, bf16[128,1024]{1,0:T(8,128)(2,1)}, u32[]{:S(2)}, u32[]{:S(2)}) collective-permute-start(bf16[128,1024]{1,0:T(8,128)(2,1)S(1)} %copy-done.15), channel_id=1, source_target_pairs={{0,1},{1,0},{2,3},{3,2},{4,5},{5,4},{6,7},{7,6},{8,9},{9,8},{10,11... | collective-permute-start | bytes 786440 | tf_op jit(solution)/shard_map/ppermute | solution.py:101
  120.8 34.5 %collective-permute-start.21 = (bf16[128,1024]{1,0:T(8,128)(2,1)S(1)}, bf16[128,1024]{1,0:T(8,128)(2,1)}, u32[]{:S(2)}, u32[]{:S(2)}) collective-permute-start(bf16[128,1024]{1,0:T(8,128)(2,1)S(1)} %copy-done.15), channel_id=1, source_target_pairs={{0,2},{1,3},{2,0},{3,1},{4,6},{5,7},{6,4},{7,5},{8,10},{9,11},{10,... | collective-permute-start | bytes 786440 | tf_op jit(solution)/shard_map/ppermute | solution.py:101
  155.3 21.1 %collective-permute-start.18 = (bf16[128,1024]{1,0:T(8,128)(2,1)}, bf16[128,1024]{1,0:T(8,128)(2,1)S(1)}, u32[]{:S(2)}, u32[]{:S(2)}) collective-permute-start(bf16[128,1024]{1,0:T(8,128)(2,1)} %get-tuple-element.121.refs_0_), channel_id=1, source_target_pairs={{0,2},{1,3},{2,0},{3,1},{4,6},{5,7},{6,4},{7,5},{8,10},{9,11},{10,... | collective-permute-start | bytes 786440 | tf_op jit(solution)/shard_map/ppermute | solution.py:101
  155.3 21.1 %collective-permute-start.19 = (bf16[128,1024]{1,0:T(8,128)(2,1)}, bf16[128,1024]{1,0:T(8,128)(2,1)S(1)}, u32[]{:S(2)}, u32[]{:S(2)}) collective-permute-start(bf16[128,1024]{1,0:T(8,128)(2,1)} %get-tuple-element.121.refs_0_), channel_id=1, source_target_pairs={{0,3},{1,2},{2,1},{3,0},{4,7},{5,6},{6,5},{7,4},{8,11},{9,10},{10,... | collective-permute-start | bytes 786440 | tf_op jit(solution)/shard_map/ppermute | solution.py:101
  203.4 15.7 %collective-permute-start.27 = (bf16[128,1024]{1,0:T(8,128)(2,1)}, bf16[128,1024]{1,0:T(8,128)(2,1)}, u32[]{:S(2)}, u32[]{:S(2)}) collective-permute-start(bf16[128,1024]{1,0:T(8,128)(2,1)} %get-tuple-element.126), channel_id=1, source_target_pairs={{0,1},{1,0},{2,3},{3,2},{4,5},{5,4},{6,7},{7,6},{8,9},{9,8},{10,11... | collective-permute-start | bytes 786440 | tf_op jit(solution)/shard_map/ppermute | solution.py:101
  206.8 21.7 %collective-permute-start.28 = (bf16[128,1024]{1,0:T(8,128)(2,1)}, bf16[128,1024]{1,0:T(8,128)(2,1)}, u32[]{:S(2)}, u32[]{:S(2)}) collective-permute-start(bf16[128,1024]{1,0:T(8,128)(2,1)} %get-tuple-element.127), channel_id=1, source_target_pairs={{0,2},{1,3},{2,0},{3,1},{4,6},{5,7},{6,4},{7,5},{8,10},{9,11},{10,... | collective-permute-start | bytes 786440 | tf_op jit(solution)/shard_map/ppermute | solution.py:101
  207.8 20.6 %collective-permute-start.29 = (bf16[128,1024]{1,0:T(8,128)(2,1)}, bf16[128,1024]{1,0:T(8,128)(2,1)}, u32[]{:S(2)}, u32[]{:S(2)}) collective-permute-start(bf16[128,1024]{1,0:T(8,128)(2,1)} %get-tuple-element.128), channel_id=1, source_target_pairs={{0,3},{1,2},{2,1},{3,0},{4,7},{5,6},{6,5},{7,4},{8,11},{9,10},{10,... | collective-permute-start | bytes 786440 | tf_op jit(solution)/shard_map/ppermute | solution.py:101
  256.9 31.8 %collective-permute-start.48 = (bf16[256,1024]{1,0:T(8,128)(2,1)}, bf16[256,1024]{1,0:T(8,128)(2,1)S(1)}, u32[]{:S(2)}, u32[]{:S(2)}) collective-permute-start(bf16[256,1024]{1,0:T(8,128)(2,1)} %get-tuple-element.176), channel_id=1, source_target_pairs={{0,1},{1,0},{2,3},{3,2},{4,5},{5,4},{6,7},{7,6},{8,9},{9,8},{10,11... | collective-permute-start | bytes 1572872 | tf_op jit(solution)/shard_map/ppermute | solution.py:101
  258.2 38.2 %collective-permute-start.49 = (bf16[256,1024]{1,0:T(8,128)(2,1)S(1)}, bf16[256,1024]{1,0:T(8,128)(2,1)S(1)}, u32[]{:S(2)}, u32[]{:S(2)}) collective-permute-start(bf16[256,1024]{1,0:T(8,128)(2,1)S(1)} %copy-done.32), channel_id=1, source_target_pairs={{0,2},{1,3},{2,0},{3,1},{4,6},{5,7},{6,4},{7,5},{8,10},{9,11},{10,... | collective-permute-start | bytes 1572872 | tf_op jit(solution)/shard_map/ppermute | solution.py:101
  259.7 36.6 %collective-permute-start.50 = (bf16[256,1024]{1,0:T(8,128)(2,1)S(1)}, bf16[256,1024]{1,0:T(8,128)(2,1)S(1)}, u32[]{:S(2)}, u32[]{:S(2)}) collective-permute-start(bf16[256,1024]{1,0:T(8,128)(2,1)S(1)} %copy-done.31), channel_id=1, source_target_pairs={{0,3},{1,2},{2,1},{3,0},{4,7},{5,6},{6,5},{7,4},{8,11},{9,10},{10,... | collective-permute-start | bytes 1572872 | tf_op jit(solution)/shard_map/ppermute | solution.py:101
  262.5 19.3 %collective-permute-start.35 = (bf16[512,256]{1,0:T(8,128)(2,1)S(1)}, bf16[512,256]{1,0:T(8,128)(2,1)S(1)}, u32[]{:S(2)}, u32[]{:S(2)}) collective-permute-start(bf16[512,256]{1,0:T(8,128)(2,1)S(1)} %fusion), channel_id=1, source_target_pairs={{8,0},{12,4},{9,1},{13,5},{10,2},{14,6},{11,3},{15,7},{24,16},{28,... | collective-permute-start | bytes 786440 | tf_op jit(solution)/shard_map/ppermute | solution.py:105
  301.4 57.1 %collective-permute-start.51 = (bf16[3,512,256]{2,1,0:T(8,128)(2,1)}, bf16[3,512,256]{2,1,0:T(8,128)(2,1)S(1)}, u32[]{:S(2)}, u32[]{:S(2)}) collective-permute-start(bf16[3,512,256]{2,1,0:T(8,128)(2,1)} %get-tuple-element.186), channel_id=1, source_target_pairs={{0,4},{4,0},{8,12},{12,8},{16,20},{20,16},{24,28},{28,24},{1,5},{5... | collective-permute-start | bytes 2359304 | tf_op jit(solution)/shard_map/ppermute | solution.py:98
  301.4 71.9 %collective-permute-start.45 = (bf16[3,128,1152]{2,1,0:T(8,128)(2,1)}, bf16[3,128,1152]{2,1,0:T(8,128)(2,1)S(1)}, u32[]{:S(2)}, u32[]{:S(2)}) collective-permute-start(bf16[3,128,1152]{2,1,0:T(8,128)(2,1)} %get-tuple-element.171), channel_id=1, source_target_pairs={{0,8},{4,12},{8,0},{12,4},{16,24},{20,28},{24,16},{28,20},{1,9},{5... | collective-permute-start | bytes 2654216 | tf_op jit(solution)/shard_map/ppermute | solution.py:98
  314.2 59.2 %collective-permute-start.46 = (bf16[3,128,1152]{2,1,0:T(8,128)(2,1)}, bf16[3,128,1152]{2,1,0:T(8,128)(2,1)S(1)}, u32[]{:S(2)}, u32[]{:S(2)}) collective-permute-start(bf16[3,128,1152]{2,1,0:T(8,128)(2,1)} %get-tuple-element.172), channel_id=1, source_target_pairs={{0,16},{4,20},{8,24},{12,28},{16,0},{20,4},{24,8},{28,12},{1,17},{... | collective-permute-start | bytes 2654216 | tf_op jit(solution)/shard_map/ppermute | solution.py:98
  315.9 59.1 %collective-permute-start.47 = (bf16[3,128,1152]{2,1,0:T(8,128)(2,1)}, bf16[3,128,1152]{2,1,0:T(8,128)(2,1)S(1)}, u32[]{:S(2)}, u32[]{:S(2)}) collective-permute-start(bf16[3,128,1152]{2,1,0:T(8,128)(2,1)} %get-tuple-element.173), channel_id=1, source_target_pairs={{0,24},{4,28},{8,16},{12,20},{16,8},{20,12},{24,0},{28,4},{1,25},{... | collective-permute-start | bytes 2654216 | tf_op jit(solution)/shard_map/ppermute | solution.py:98
  317.1 36.9 %collective-permute-start.40 = (f32[24,128]{1,0:T(8,128)S(1)}, f32[24,128]{1,0:T(8,128)S(1)}, u32[]{:S(2)}, u32[]{:S(2)}) collective-permute-start(f32[24,128]{1,0:T(8,128)S(1)} %add.56), channel_id=1, source_target_pairs={{0,8},{4,12},{8,0},{12,4},{16,24},{20,28},{24,16},{28,20},{1,9},{5... | collective-permute-start | bytes 36872 | tf_op jit(solution)/shard_map/ppermute | solution.py:98
  357.7 20.1 %collective-permute-start.44 = (f32[24,128]{1,0:T(8,128)S(1)}, f32[24,128]{1,0:T(8,128)S(1)}, u32[]{:S(2)}, u32[]{:S(2)}) collective-permute-start(f32[24,128]{1,0:T(8,128)S(1)} %add.58), channel_id=1, source_target_pairs={{0,3},{1,2},{2,1},{3,0},{4,7},{5,6},{6,5},{7,4},{8,11},{9,10},{10,... | collective-permute-start | bytes 36872 | tf_op jit(solution)/shard_map/ppermute | solution.py:101
  358.5 19.3 %collective-permute-start.43 = (f32[24,128]{1,0:T(8,128)S(1)}, f32[24,128]{1,0:T(8,128)S(1)}, u32[]{:S(2)}, u32[]{:S(2)}) collective-permute-start(f32[24,128]{1,0:T(8,128)S(1)} %add.58), channel_id=1, source_target_pairs={{0,2},{1,3},{2,0},{3,1},{4,6},{5,7},{6,4},{7,5},{8,10},{9,11},{10,... | collective-permute-start | bytes 36872 | tf_op jit(solution)/shard_map/ppermute | solution.py:101
  373.3 27.9 %collective-permute-start.36 = (bf16[128,1024]{1,0:T(8,128)(2,1)}, bf16[128,1024]{1,0:T(8,128)(2,1)S(1)}, u32[]{:S(2)}, u32[]{:S(2)}) collective-permute-start(bf16[128,1024]{1,0:T(8,128)(2,1)} %get-tuple-element.166), channel_id=1, source_target_pairs={{0,1},{1,0},{2,3},{3,2},{4,5},{5,4},{6,7},{7,6},{8,9},{9,8},{10,11... | collective-permute-start | bytes 786440 | tf_op jit(solution)/shard_map/ppermute | solution.py:101
  373.4 27.8 %collective-permute-start.37 = (bf16[128,1024]{1,0:T(8,128)(2,1)}, bf16[128,1024]{1,0:T(8,128)(2,1)S(1)}, u32[]{:S(2)}, u32[]{:S(2)}) collective-permute-start(bf16[128,1024]{1,0:T(8,128)(2,1)} %get-tuple-element.167), channel_id=1, source_target_pairs={{0,2},{1,3},{2,0},{3,1},{4,6},{5,7},{6,4},{7,5},{8,10},{9,11},{10,... | collective-permute-start | bytes 786440 | tf_op jit(solution)/shard_map/ppermute | solution.py:101
  374.9 26.3 %collective-permute-start.38 = (bf16[128,1024]{1,0:T(8,128)(2,1)}, bf16[128,1024]{1,0:T(8,128)(2,1)S(1)}, u32[]{:S(2)}, u32[]{:S(2)}) collective-permute-start(bf16[128,1024]{1,0:T(8,128)(2,1)} %get-tuple-element.168), channel_id=1, source_target_pairs={{0,3},{1,2},{2,1},{3,0},{4,7},{5,6},{6,5},{7,4},{8,11},{9,10},{10,... | collective-permute-start | bytes 786440 | tf_op jit(solution)/shard_map/ppermute | solution.py:101
  377.8 13.3 %collective-permute-start.52 = (bf16[3,128,256]{2,1,0:T(8,128)(2,1)}, bf16[3,128,256]{2,1,0:T(8,128)(2,1)}, u32[]{:S(2)}, u32[]{:S(2)}) collective-permute-start(bf16[3,128,256]{2,1,0:T(8,128)(2,1)} %get-tuple-element.188), channel_id=1, source_target_pairs={{0,8},{4,12},{8,0},{12,4},{16,24},{20,28},{24,16},{28,20},{1,9},{5... | collective-permute-start | bytes 589832 | tf_op jit(solution)/shard_map/ppermute | solution.py:98
  (67 other events, 794.0 us)

commit v5 on v4

--- a/solution.py
+++ b/solution.py
@@ -1,3 +1,4 @@
+import functools
 import math
 
 import jax
@@ -12,7 +13,6 @@
 rope_base = 1000000.0
 f32 = jnp.float32
 bf16 = jnp.bfloat16
-exact = lax.Precision.HIGHEST
 log2e = math.log2(math.e)
 
 
@@ -92,7 +92,6 @@
     z = lax.axis_index("tp")
     where = jnp.stack([me, ctx, z]).astype(jnp.int32)
     aligned = blk % 128 == 0
-    assert R == blk
 
     def plane(v, mask):
         return lax.ppermute(v, ("dp", "ctx"), [(i, i ^ mask) for i in range(N)])
@@ -127,11 +126,12 @@
                 else:
                     rest[i - 1][0] = total.astype(bf16)
 
-        big = pl.BlockSpec((1, half, cols), lambda k: (k, 0, 0))
-        small = pl.BlockSpec((1, m, cols), lambda k: (k, 0, 0))
+        part = 384 if cols % 384 == 0 else cols
+        big = pl.BlockSpec((1, half, part), lambda k, i: (k, 0, i))
+        small = pl.BlockSpec((1, m, part), lambda k, i: (k, 0, i))
         own, *sends = pl.pallas_call(
             body,
-            grid=(kinds,),
+            grid=(kinds, cols // part),
             out_shape=[sds((kinds, m, cols), f32)] + [sds((kinds, m, cols), bf16)] * (N // 2 - 1),
             in_specs=[big, big],
             out_specs=[small] * (N // 2),
@@ -180,7 +180,7 @@
 
     own_qkv = jnp.stack([query_weight, key_value_weight])
 
-    def pre_body(s_ref, t_ref, c_ref, g_ref, o_ref, n_ref, t_out, c_out, g_out):
+    def pre_body(s_ref, t_ref, c_ref, g_ref, o_ref, n_ref, t_out, c_out, g_out, ot_out):
         index = s_ref[0]
         for s, mask in enumerate(masks):
             if aligned:
@@ -193,16 +193,16 @@
             g_out[:, dst] = g_ref[:, src]
         x = t_out[...].astype(f32)
         inv = lax.rsqrt(jnp.mean(x * x, axis=-1, keepdims=True) + epsilon)
-        n_ref[:, :W] = (x * inv * g_out[0:1, :]).astype(bf16)
-        n_ref[:, W:] = o_ref[...].T
+        n_ref[...] = (x * inv * g_out[0:1, :]).astype(bf16)
+        ot_out[...] = o_ref[...].T
 
     gains = jnp.stack([attention_gain, ffn_gain])
     t_in, c_in, g_in = tokens[0], cotangent[0], gains
     if not aligned:
         t_in, c_in, g_in = (take_cols(v, me, blk, masks) for v in (t_in, c_in, g_in))
-    normed, tok, cot, gain2 = whole_call(
+    normed, tok, cot, gain2, own_out = whole_call(
         pre_body,
-        [sds((R, W + C), bf16), sds((R, W), bf16), sds((R, W), bf16), sds((2, W), f32)],
+        [sds((R, W), bf16)] * 3 + [sds((2, W), f32), sds((blk, C), bf16)],
         (where, t_in, c_in, g_in, output_weight),
         R * W * 8,
     )
@@ -211,9 +211,9 @@
     qkv_m, qkv_o = gather_core(qkv_near)
     own_ffn = jnp.stack([gate_weight, up_weight, down_weight.T])
     ffn_near = gather_near(after(own_ffn, normed))
-    out_cols = jnp.concatenate([p[:, W:] for p in first_pieces], axis=1)[None]
+    out_cols = jnp.concatenate(gather_column(own_out), axis=1)[None]
     out_near = gather_near(out_cols)
-    cot_pieces = gather_column(after(cot, *first_pieces))
+    cot_pieces = gather_column(cot)
 
     half_width = hw // 2
     freq = jnp.exp(jnp.arange(half_width, dtype=f32) * (-2.0 * math.log(rope_base) / hw))
@@ -225,15 +225,17 @@
     qg = jnp.tile(query_gain, QH)[None]
     kg = jnp.tile(jnp.concatenate([key_gain, jnp.ones_like(key_gain)]), KH)[None]
 
+    def three_terms(x):
+        high = x.astype(bf16)
+        rest = x - high.astype(f32)
+        low = rest.astype(bf16)
+        return high, low, (rest - low.astype(f32)).astype(bf16)
+
     def head_mean(x):
         n = x.shape[1]
         same = rows_of((n, n)) // hw == lanes((n, n)) // hw
         ones = jnp.where(same, 1.0 / hw, 0.0).astype(bf16)
-        high = x.astype(bf16)
-        rest = x - high.astype(f32)
-        low = rest.astype(bf16)
-        tail = (rest - low.astype(f32)).astype(bf16)
-        return mm(high, ones) + mm(low, ones) + mm(tail, ones)
+        return sum(mm(term, ones) for term in three_terms(x))
 
     def swap_halves(x):
         first = lanes(x.shape) % hw < half_width
@@ -244,7 +246,7 @@
     def qkv_body(*refs):
         wm, wo, cs, sn, qg_ref, kg_ref, rq, pr, q_raw, p_raw = refs[NT:]
         rows = join_slots(refs[:NT])
-        left, right = rows[:, :H], rows[:, H:W]
+        left, right = rows[:, :H], rows[:, H:]
         q = mm(left, wm[0]) + mm(right, wo[0])
         p = mm(left, wm[1]) + mm(right, wo[1])
         q_raw[...] = q
@@ -371,93 +373,78 @@
     )
     second_pieces = gather_column(normed_f)
 
-    FB = 384 if F % 384 == 0 else F
-    steps = F // FB
+    chunks = [slice(i, min(i + 256, F)) for i in range(0, F, 256)]
+
+    def hidden_body(*refs):
+        wm, wo, out = refs[NT:]
+        c = join_slots(refs[:NT])
+        for cols in chunks:
+            out[:, cols] = mm(c[:, :H], wm[2, :, cols]) + mm(c[:, H:], wo[2, :, cols])
+
+    (grad_mid,) = whole_call(
+        hidden_body, [sds((B, F), f32)], (*cot_pieces, ffn_m, ffn_o), 2 * B * W * F, scalars=False
+    )
 
     def ffn_body(*refs):
-        r_in, c_in, (wm, wo) = refs[:NT], refs[NT : 2 * NT], refs[2 * NT : 2 * NT + 2]
-        refs = refs[2 * NT + 2 :]
-        outs, gnfs = refs[:NT], refs[NT : 2 * NT]
-        mid_r, dg_r, du_r, r_ref, c_ref, acc_o, acc_g = refs[2 * NT :]
-        i = pl.program_id(0)
-
-        @pl.when(i == 0)
-        def _():
-            r_ref[...] = join_slots(r_in)
-            c_ref[...] = join_slots(c_in)
-
-        rl, rr = r_ref[:, :H], r_ref[:, H:]
-        gate = mm(rl, wm[0]) + mm(rr, wo[0])
-        up = mm(rl, wm[1]) + mm(rr, wo[1])
-        gmid = mm(c_ref[:, :H], wm[2]) + mm(c_ref[:, H:], wo[2])
-        sig = jax.nn.sigmoid(gate)
-        act = gate * sig
-        mid = (act * up).astype(bf16)
-        dg = (gmid * up * sig * (1.0 + gate * (1.0 - sig))).astype(bf16)
-        du = (gmid * act).astype(bf16)
-        mid_r[...] = mid
-        dg_r[...] = dg
-        du_r[...] = du
+        wm, wo, gmid_r, mid_r, dg_r, du_r = refs[NT : NT + 6]
+        gnfs = refs[NT + 6 :]
+        r = join_slots(refs[:NT])
+        rl, rr = r[:, :H], r[:, H:]
+        for cols in chunks:
+            gate = mm(rl, wm[0, :, cols]) + mm(rr, wo[0, :, cols])
+            up = mm(rl, wm[1, :, cols]) + mm(rr, wo[1, :, cols])
+            gmid = gmid_r[:, cols]
+            sig = jax.nn.sigmoid(gate)
+            act = gate * sig
+            mid_r[:, cols] = (act * up).astype(bf16)
+            dg_r[:, cols] = (gmid * up * sig * (1.0 + gate * (1.0 - sig))).astype(bf16)
+            du_r[:, cols] = (gmid * act).astype(bf16)
         for w, cols in ((wm, slice(0, H)), (wo, slice(H, W))):
-            o = mm_nt(mid, w[2])
-            g = mm_nt(dg, w[0]) + mm_nt(du, w[1])
-
-            @pl.when(i == 0)
-            def _():
-                acc_o[:, cols] = o
-                acc_g[:, cols] = g
-
-            @pl.when(i > 0)
-            def _():
-                acc_o[:, cols] += o
-                acc_g[:, cols] += g
-
-        @pl.when(i == steps - 1)
-        def _():
-            put_slots(outs, acc_o)
-            put_slots(gnfs, acc_g)
-
-    one = lambda shape: pl.BlockSpec(shape, lambda i: (0,) * len(shape))
-    wide = pl.BlockSpec((B, FB), lambda i: (0, i))
-    w_spec = pl.BlockSpec((3, H, FB), lambda i: (0, 0, i))
-    *ffn_slots, mid, dgate, dup = pl.pallas_call(
+            g = mm_nt(dg_r[...], w[0]) + mm_nt(du_r[...], w[1])
+            for k, ref in enumerate(gnfs):
+                ref[:, cols] = g[k * R : (k + 1) * R].astype(bf16)
+
+    mid, dgate, dup, *gnf_slots = whole_call(
         ffn_body,
-        grid=(steps,),
-        out_shape=[sds((R, W), bf16)] * (2 * NT) + [sds((B, F), bf16)] * 3,
-        in_specs=[one((R, W))] * (2 * NT) + [w_spec, w_spec],
-        out_specs=[one((R, W))] * (2 * NT) + [wide, wide, wide],
-        scratch_shapes=[pltpu.VMEM((B, W), bf16)] * 2 + [pltpu.VMEM((B, W), f32)] * 2,
-        cost_estimate=pl.CostEstimate(
-            flops=12 * B * W * F, bytes_accessed=6 * W * F + 6 * B * F, transcendentals=B * F
-        ),
-        name="ffn",
-    )(*second_pieces, *cot_pieces, ffn_m, ffn_o)
-    gnf_pieces = spread_column(ffn_slots[NT:])
-
-    def dw_body(*refs):
-        r_in, c_in, (mid_r, dg_r, du_r, gm, go, rt, ct) = refs[:NT], refs[NT : 2 * NT], refs[2 * NT :]
-
-        @pl.when(pl.program_id(0) == 0)
-        def _():
-            rt[...] = join_slots(r_in).T
-            ct[...] = join_slots(c_in).T
-
+        [sds((B, F), bf16)] * 3 + [sds((R, W), bf16)] * NT,
+        (*second_pieces, ffn_m, ffn_o, grad_mid),
+        8 * B * W * F,
+        scalars=False,
+    )
+    gnf_pieces = spread_column(gnf_slots)
+
+    def dw_body(cols, *refs):
+        c_in, (mid_r, dg_r, du_r, out) = refs[NT : 2 * NT], refs[2 * NT :]
+        rt = jnp.concatenate([ref[:, cols] for ref in refs[:NT]], axis=0).T
+        ct = jnp.concatenate([ref[:, cols] for ref in c_in], axis=0).T
         for k, (lhs, rhs) in enumerate(((rt, dg_r), (rt, du_r), (ct, mid_r))):
-            gm[k] = mm(lhs[:H], rhs[...]).astype(bf16)
-            go[k] = mm(lhs[H:], rhs[...]).astype(bf16)
-
-    dwf_m, dwf_o = pl.pallas_call(
-        dw_body,
-        grid=(steps,),
-        out_shape=[sds((3, H, F), bf16)] * 2,
-        in_specs=[one((R, W))] * (2 * NT) + [wide, wide, wide],
-        out_specs=[w_spec, w_spec],
-        scratch_shapes=[pltpu.VMEM((W, B), bf16)] * 2,
-        cost_estimate=pl.CostEstimate(
-            flops=6 * B * W * F, bytes_accessed=6 * W * F + 6 * B * F, transcendentals=0
-        ),
-        name="ffn_weights",
-    )(*second_pieces, *cot_pieces, mid, dgate, dup)
+            out[k] = mm(lhs, rhs[...]).astype(bf16)
+
+    def half_weights(cols, dg):
+        return whole_call(
+            functools.partial(dw_body, cols),
+            [sds((3, H, F), bf16)],
+            (*second_pieces, *cot_pieces, mid, dg, dup),
+            3 * B * W * F,
+            scalars=False,
+        )[0]
+
+    dwf_o = half_weights(slice(H, W), dgate)
+    dwf_m = half_weights(slice(0, H), after(dgate, dwf_o))
+
+    def out_part_body(m_ref, wm, wo, *outs):
+        for w, cols in ((wm, slice(0, H)), (wo, slice(H, W))):
+            o = mm_nt(m_ref[...], w[2])
+            for k, ref in enumerate(outs):
+                ref[:, cols] = o[k * R : (k + 1) * R].astype(bf16)
+
+    ffn_slots = whole_call(
+        out_part_body,
+        [sds((R, W), bf16)] * NT,
+        (after(mid, dwf_m), ffn_m, ffn_o),
+        2 * B * W * F,
+        scalars=False,
+    )
     ffn_own, ffn_sends = merge_core(dwf_m, plane(dwf_o, 1))
     gnf_pieces, ffn_own, ffn_sends = lax.optimization_barrier((gnf_pieces, ffn_own, ffn_sends))
     ffn_got = [plane(v, 2 * (i + 1)) for i, v in enumerate(ffn_sends)]
@@ -494,7 +481,6 @@
     )
     ga_slots, both_slots = ga_slots[:NT], ga_slots[NT:]
     ga_pieces = spread_column(ga_slots)
-    *both_slots, ga_pieces = lax.optimization_barrier((*both_slots, ga_pieces))
     both_pieces = spread_column(both_slots)
 
     def bwd_body(s_ref, q_ref, a_ref, l_ref, *refs):
@@ -513,11 +499,10 @@
             for k in range(NC):
                 kv_ref[k] = kv_in[k][...]
             prod = d_all * a_ref[...].astype(f32)
+            pick = jnp.where(lanes((8, C)) // hw == rows_of((8, C)), 1.0, 0.0).astype(bf16)
+            sums = sum(mm_nt(pick, term) for term in three_terms(prod))
             for hd in range(QH):
-                pick = jnp.where(lanes((8, C)) // hw == hd, 1.0, 0.0).astype(f32)
-                dl[hd] = lax.dot_general(
-                    pick, prod, (((1,), (1,)), ((), ())), precision=exact, preferred_element_type=f32
-                )
+                dl[hd] = jnp.broadcast_to(sums[hd : hd + 1], (8, B))
 
         here_cols = pl.ds(pl.multiple_of(h * pw, pw), pw)
 
@@ -600,7 +585,7 @@
         n_parts = len(pair_parts)
         parts, r_in, gnas = refs[:n_parts], refs[n_parts : n_parts + NT], refs[n_parts + NT : n_parts + 2 * NT]
         both_ref, pack = refs[n_parts + 2 * NT :]
-        r_all = jnp.concatenate([ref[:, :W] for ref in r_in], axis=0)
+        r_all = join_slots(r_in)
 
         def back(grad, raw, gain, live):
             turned = grad * cs[...] - swap_halves(grad) * sn[...]
@@ -647,23 +632,30 @@
     )
     gna_pieces = spread_column(gna_slots)
 
-    *both_pieces, both16 = lax.optimization_barrier((*both_pieces, both16))
-
-    def last_body(*refs):
-        r_in, g_in, (a_ref, b_ref, gm, go) = refs[:NT], refs[NT : 2 * NT], refs[2 * NT :]
-        rt = jnp.concatenate([ref[:, :W] for ref in r_in], axis=0).T
-        gt = jnp.concatenate([ref[:R] for ref in g_in], axis=0).T
+    def proj_body(*refs):
+        b_ref, gm, go = refs[NT:]
+        rt = join_slots(refs[:NT]).T
         for ref, rows in ((gm, slice(0, H)), (go, slice(H, W))):
             full = mm(rt[rows], b_ref[...]).astype(bf16)
             ref[0] = full[:, :C]
             ref[1] = full[:, C:]
+
+    proj_m, proj_o = whole_call(
+        proj_body, [sds((2, H, C), bf16)] * 2, (*first_pieces, both16), 4 * B * W * C, scalars=False
+    )
+
+    def last_body(*refs):
+        g_in, (a_ref, pm, po, gm, go) = refs[:NT], refs[NT:]
+        gt = jnp.concatenate([ref[:R] for ref in g_in], axis=0).T
+        for ref, part, rows in ((gm, pm, slice(0, H)), (go, po, slice(H, W))):
+            ref[:2] = part[...]
             ref[2] = mm(gt[rows], a_ref[...]).astype(bf16)
 
     last_m, last_o = whole_call(
         last_body,
         [sds((3, H, C), bf16)] * 2,
-        (*first_pieces, *both_pieces, attended, both16),
-        6 * B * W * C,
+        (*both_pieces, attended, proj_m, proj_o),
+        2 * B * W * C,
         scalars=False,
     )
     att_own, att_sends = merge_core(last_m, plane(last_o, 1))

time: 406 us -> 407 us (level)
  waiting for transfers between devices: 184 us -> 158 us
  Pallas kernels: 85 us -> 98 us
  starting transfers between devices: 105 us -> 110 us
  other arithmetic: 6.41 us -> 10.7 us
    pallas_call x10 -> x16, Pallas kernels: 36.1 us -> 75.1 us  [whole_call(): pl.pallas_call(body, out_shape=list(outs), in_specs=specs, out_specs=[VM]...]
    pallas_call x4 -> x2, Pallas kernels: 35.3 us -> 10.9 us  [merge_core(): pl.pallas_call(body, grid=(kinds, cols // part), out_shape=[sds((kinds, m...]
    ppermute x27 -> x30, waiting for transfers between devices: 67.2 us -> 46.4 us  [column(): return lax.ppermute(v, 'tp', [(i, i ^ mask) for i in range(NT)])]
    ppermute x23, waiting for transfers between devices: 94.8 us -> 88.4 us  [plane(): return lax.ppermute(v, ('dp', 'ctx'), [(i, i ^ mask) for i in range(N)])]
    ppermute x27 -> x30, starting transfers between devices: 62.2 us -> 63.5 us  [column(): return lax.ppermute(v, 'tp', [(i, i ^ mask) for i in range(NT)])]
    unnamed x95 -> x75, local copies, waits for them, and re-layouts: 14.3 us -> 13.5 us
  transfers between devices with their start and end apart: 55 -> 58, of which waited for: 25 -> 20; matrix products, arithmetic and copies ran while one was open for 4% -> 5% of each run, Pallas kernels for 9% -> 15%
where the time goes in v5:
time: 407 us; the launch traced here: 402 us
  waiting for transfers between devices  158 us (39%)
  starting transfers between devices  110 us (27%)
  Pallas kernels  98 us (24%)
  local copies, waits for them, and re-layouts  24 us (6%)
  other arithmetic  10.7 us (3%)
    ppermute x23, waiting for transfers between devices, plane(): return lax.ppermute(v, ('dp', 'ctx'), [(i, i ^ mask) for i in range(N)])  88.4 us
    pallas_call x16, Pallas kernels, whole_call(): pl.pallas_call(body, out_shape=list(outs), in_specs=specs, out_specs=[VM]...  75.1 us
    ppermute x30, starting transfers between devices, column(): return lax.ppermute(v, 'tp', [(i, i ^ mask) for i in range(NT)])  63.5 us
    ppermute x30, waiting for transfers between devices, column(): return lax.ppermute(v, 'tp', [(i, i ^ mask) for i in range(NT)])  46.4 us
    ppermute x23, starting transfers between devices, plane(): return lax.ppermute(v, ('dp', 'ctx'), [(i, i ^ mask) for i in range(N)])  38.1 us
    ppermute x4, waiting for transfers between devices, along(): return lax.ppermute(v, 'ctx', pairs)  23.2 us
    unnamed x75, local copies, waits for them, and re-layouts  13.5 us
    pallas_call x2, Pallas kernels, merge_core(): pl.pallas_call(body, grid=(kinds, cols // part), out_shape=[sds((kinds, m...  10.9 us
  transfers between devices with their start and end apart: 58, of which 20 were waited for; matrix products, arithmetic and copies ran while one was open for 5% of the time, Pallas kernels for 15%

profile of v5, /device:TPU:0, one launch (start us, length us, event | category | flops | bytes accessed | tf_op | source)
XLA Modules:
  0.0 402.0 jit_solution(3798790360973316660)
XLA Ops:
  13.8 17.9 %collective-permute-done.23 = bf16[3,128,1152]{2,1,0:T(8,128)(2,1)S(1)} collective-permute-done((bf16[3,128,1152]{2,1,0:T(8,128)(2,1)}, bf16[3,128,1152]{2,1,0:T(8,128)(2,1)S(1)}, u32[]{:S(2)}, u32[]{:S(2)}) %collective-permute-start.23) | collective-permute-done | bytes 884768 | tf_op jit(solution)/shard_map/ppermute | solution.py:97
  31.8 19.4 %collective-permute-done.24 = bf16[3,128,1152]{2,1,0:T(8,128)(2,1)S(1)} collective-permute-done((bf16[3,128,1152]{2,1,0:T(8,128)(2,1)}, bf16[3,128,1152]{2,1,0:T(8,128)(2,1)S(1)}, u32[]{:S(2)}, u32[]{:S(2)}) %collective-permute-start.24) | collective-permute-done | bytes 884768 | tf_op jit(solution)/shard_map/ppermute | solution.py:97
  70.3 4.1 %collective-permute-done.16 = bf16[1,128,1024]{2,1,0:T(8,128)(2,1)S(1)} collective-permute-done((bf16[1,128,1024]{2,1,0:T(8,128)(2,1)S(1)}, bf16[1,128,1024]{2,1,0:T(8,128)(2,1)S(1)}, u32[]{:S(2)}, u32[]{:S(2)}) %collective-permute-start.16) | collective-permute-done | bytes 262176 | tf_op jit(solution)/shard_map/ppermute | solution.py:97
  74.7 4.0 collective-permute-done.17
  92.9 3.7 collective-permute-done.1.refs_2_.refs_3_
  97.1 4.5 %shard_map.220 = (bf16[512,256]{1,0:T(8,128)(2,1)}, bf16[512,256]{1,0:T(8,128)(2,1)}, f32[512,256]{1,0:T(8,128)}, f32[512,256]{1,0:T(8,128)}) custom-call(bf16[128,1024]{1,0:T(8,128)(2,1)} %get-tuple-element.98.refs_0_.refs_1_, bf16[128,1024]{1,0:T(8,128)(2,1)} %collective-permute-done.refs_1_.refs_2_, ...), custom_call_target="tpu_custom_call" | custom-call | flops 536870912 | bytes 4720640 | tf_op jit(solution)/shard_map/pallas_call | solution.py:48
  101.6 5.2 %collective-permute-start.8 = (bf16[512,256]{1,0:T(8,128)(2,1)}, bf16[512,256]{1,0:T(8,128)(2,1)S(1)}, u32[]{:S(2)}, u32[]{:S(2)}) collective-permute-start(bf16[512,256]{1,0:T(8,128)(2,1)} %get-tuple-element.101.refs_0_.refs_4_), channel_id=1, source_target_pairs={{0,8},{4,12},{1,9},{5,13},{2,10},{6,14},{3,11},{7,15},{16,24},{20,... | collective-permute-start | bytes 786440 | tf_op jit(solution)/shard_map/ppermute | solution.py:104
  113.8 4.7 %attention_forward.1 = (bf16[128,256]{1,0:T(8,128)(2,1)}, bf16[128,256]{1,0:T(8,128)(2,1)}, bf16[128,256]{1,0:T(8,128)(2,1)}, bf16[128,256]{1,0:T(8,128)(2,1)}, ...) custom-call(s32[3]{0:T(128)} %pad_add_fusion.s_ref.refs_0_, bf16[512,256]{1,0:T(8,128)(2,1)} %get-tuple-element.100.q_ref, ...), custom_call_target="tpu_custom_call" | custom-call | flops 2147483648 | bytes 1048576 | tf_op jit(solution)/shard_map/attention_forward/pallas_call | solution.py:338
  118.5 4.1 %collective-permute-start.10 = (bf16[128,256]{1,0:T(8,128)(2,1)}, bf16[128,256]{1,0:T(8,128)(2,1)}, u32[]{:S(2)}, u32[]{:S(2)}) collective-permute-start(bf16[128,256]{1,0:T(8,128)(2,1)} %get-tuple-element.105), channel_id=1, source_target_pairs={{0,1},{1,0},{2,3},{3,2},{4,5},{5,4},{6,7},{7,6},{8,9},{9,8},{10,11... | collective-permute-start | bytes 196616 | tf_op jit(solution)/shard_map/ppermute | solution.py:100
  122.7 3.9 collective-permute-start.28
  129.8 11.7 %collective-permute-done.11.refs_2_ = bf16[128,256]{1,0:T(8,128)(2,1)} collective-permute-done((bf16[128,256]{1,0:T(8,128)(2,1)}, bf16[128,256]{1,0:T(8,128)(2,1)}, u32[]{:S(2)}, u32[]{:S(2)}) %collective-permute-start.11) | collective-permute-done | bytes 65568 | tf_op jit(solution)/shard_map/ppermute | solution.py:100
  143.9 4.1 %collective-permute-done.12.refs_3_ = bf16[128,256]{1,0:T(8,128)(2,1)} collective-permute-done((bf16[128,256]{1,0:T(8,128)(2,1)}, bf16[128,256]{1,0:T(8,128)(2,1)}, u32[]{:S(2)}, u32[]{:S(2)}) %collective-permute-start.12) | collective-permute-done | bytes 65568 | tf_op jit(solution)/shard_map/ppermute | solution.py:100
  159.4 6.4 %shard_map.222.refs_6_ = f32[512,1152]{1,0:T(8,128)} custom-call(bf16[128,1024]{1,0:T(8,128)(2,1)} %get-tuple-element.113.refs_0_.refs_4_.refs_9_, bf16[128,1024]{1,0:T(8,128)(2,1)} %collective-permute-done.27.refs_1_.refs_5_, bf16[128,1024]{1,0:T(8,128)(2,1)} %collective-permute-done.28.refs_2_.refs_6_, ...), custom_call_target="tpu_custom_call" | custom-call | flops 1207959552 | bytes 10485760 | tf_op jit(solution)/shard_map/pallas_call | solution.py:48
  166.5 10.6 %collective-permute-done.21.refs_2_ = bf16[128,1024]{1,0:T(8,128)(2,1)} collective-permute-done((bf16[128,1024]{1,0:T(8,128)(2,1)}, bf16[128,1024]{1,0:T(8,128)(2,1)}, u32[]{:S(2)}, u32[]{:S(2)}) %collective-permute-start.21) | collective-permute-done | bytes 262176 | tf_op jit(solution)/shard_map/ppermute | solution.py:100
  177.1 11.1 %shard_map.223 = (bf16[512,1152]{1,0:T(8,128)(2,1)}, bf16[512,1152]{1,0:T(8,128)(2,1)}, bf16[512,1152]{1,0:T(8,128)(2,1)}, bf16[128,1024]{1,0:T(8,128)(2,1)}, bf...) custom-call(bf16[128,1024]{1,0:T(8,128)(2,1)} %get-tuple-element.111.refs_0_, ...), custom_call_target="tpu_custom_call" | custom-call | flops 4831838208 | bytes 15073280 | tf_op jit(solution)/shard_map/pallas_call | solution.py:48
  188.3 6.7 %shard_map.224 = bf16[3,512,1152]{2,1,0:T(8,128)(2,1)} custom-call(bf16[128,1024]{1,0:T(8,128)(2,1)} %get-tuple-element.111.refs_0_, bf16[128,1024]{1,0:T(8,128)(2,1)} %collective-permute-done.20.refs_1_, bf16[128,1024]{1,0:T(8,128)(2,1)} %collective-permute-done.21.refs_2_, bf16[128,1024]{1,0:T(8,128)(2,1)} %collective-permute-done.22.refs_3_, ...), custom_call_target="tpu_custom_call" | custom-call | flops 1811939328 | bytes 9175040 | tf_op jit(solution)/shard_map/pallas_call | solution.py:48
  194.9 4.7 %collective-permute-start.30 = (bf16[128,1024]{1,0:T(8,128)(2,1)}, bf16[128,1024]{1,0:T(8,128)(2,1)}, u32[]{:S(2)}, u32[]{:S(2)}) collective-permute-start(bf16[128,1024]{1,0:T(8,128)(2,1)} %get-tuple-element.115), channel_id=1, source_target_pairs={{0,1},{1,0},{2,3},{3,2},{4,5},{5,4},{6,7},{7,6},{8,9},{9,8},{10,11... | collective-permute-start | bytes 786440 | tf_op jit(solution)/shard_map/ppermute | solution.py:100
  202.0 6.6 %shard_map.225.a = bf16[3,512,1152]{2,1,0:T(8,128)(2,1)} custom-call(bf16[128,1024]{1,0:T(8,128)(2,1)} %get-tuple-element.111.refs_0_, bf16[128,1024]{1,0:T(8,128)(2,1)} %collective-permute-done.20.refs_1_, bf16[128,1024]{1,0:T(8,128)(2,1)} %collective-permute-done.21.refs_2_, bf16[128,1024]{1,0:T(8,128)(2,1)} %collective-permute-done.22.refs_3_, ...), custom_call_target="tpu_custom_call" | custom-call | flops 1811939328 | bytes 9175040 | tf_op jit(solution)/shard_map/pallas_call | solution.py:48
  208.7 5.9 %shard_map.227 = (bf16[128,1024]{1,0:T(8,128)(2,1)}, bf16[128,1024]{1,0:T(8,128)(2,1)}, bf16[128,1024]{1,0:T(8,128)(2,1)}, bf16[128,1024]{1,0:T(8,128)(2,1)}) custom-call(bf16[512,1152]{1,0:T(8,128)(2,1)} %get-tuple-element.130.refs_8_.m_ref, bf16[3,512,1152]{2,1,0:T(8,128)(2,1)} %copy-done, bf16[3,512,1152]{2,1,0:T(8,128)(2,1)} %collective-permute-done.26.refs_5_.wo), custom_call_target="tpu_custom_call" | custom-call | flops 1207959552 | bytes 9306112 | tf_op jit(solution)/shard_map/pallas_call | solution.py:48
  216.3 7.7 %shard_map.226 = (f32[3,128,1152]{2,1,0:T(8,128)}, bf16[3,128,1152]{2,1,0:T(8,128)(2,1)}, bf16[3,128,1152]{2,1,0:T(8,128)(2,1)}, bf16[3,128,1152]{2,1,0:T(8,128)(2,1)}) custom-call(bf16[3,512,1152]{2,1,0:T(8,128)(2,1)} %shard_map.225.a, bf16[3,512,1152]{2,1,0:T(8,128)(2,1)} %copy-done.1), custom_call_target="tpu_custom_call" | custom-call | flops 1769472 | bytes 12386304 | tf_op jit(solution)/shard_map/pallas_call | solution.py:132
  224.1 4.8 %shard_map.228 = (f32[128,1024]{1,0:T(8,128)}, f32[1,1024]{1,0:T(1,128)}, bf16[128,256]{1,0:T(8,128)(2,1)}, bf16[128,256]{1,0:T(8,128)(2,1)}, bf16[128,256]{1,0:...) custom-call(bf16[128,1024]{1,0:T(8,128)(2,1)} %get-tuple-element.126, ...), custom_call_target="tpu_custom_call" | custom-call | flops 268435456 | bytes 7876608 | tf_op jit(solution)/shard_map/pallas_call | solution.py:48
  234.0 5.0 %collective-permute-done.35.refs_2_ = bf16[128,256]{1,0:T(8,128)(2,1)S(1)} collective-permute-done((bf16[128,256]{1,0:T(8,128)(2,1)}, bf16[128,256]{1,0:T(8,128)(2,1)S(1)}, u32[]{:S(2)}, u32[]{:S(2)}) %collective-permute-start.35) | collective-permute-done | bytes 65568 | tf_op jit(solution)/shard_map/ppermute | solution.py:100
  239.7 7.3 %attention_backward.1 = (f32[512,256]{1,0:T(8,128)}, bf16[2,512,256]{2,1,0:T(8,128)(2,1)}, bf16[2,512,256]{2,1,0:T(8,128)(2,1)}) custom-call(s32[3]{0:T(128)} %pad_add_fusion.s_ref.refs_0_, bf16[512,256]{1,0:T(8,128)(2,1)} %get-tuple-element.100.q_ref, bf16[512,256]{1,0:T(8,128)(2,1)} %get-tuple-element.102.a_ref.refs_4_, ...), custom_call_target="tpu_custom_call" | custom-call | flops 5368709120 | bytes 2097152 | tf_op jit(solution)/shard_map/attention_backward/pallas_call | solution.py:556
  254.9 20.4 %collective-permute-done.38.refs_0_ = bf16[512,256]{1,0:T(8,128)(2,1)S(1)} collective-permute-done((bf16[512,256]{1,0:T(8,128)(2,1)S(1)}, bf16[512,256]{1,0:T(8,128)(2,1)S(1)}, u32[]{:S(2)}, u32[]{:S(2)}) %collective-permute-start.38) | collective-permute-done | bytes 262176 | tf_op jit(solution)/shard_map/ppermute | solution.py:104
  276.0 6.1 %shard_map.229 = (bf16[128,1024]{1,0:T(8,128)(2,1)}, bf16[128,1024]{1,0:T(8,128)(2,1)}, bf16[128,1024]{1,0:T(8,128)(2,1)}, bf16[128,1024]{1,0:T(8,128)(2,1)}, bf...) custom-call(s32[3]{0:T(128)} %pad_add_fusion.s_ref.refs_0_, f32[512,256]{1,0:T(8,128)} %get-tuple-element.140.dq, ...), custom_call_target="tpu_custom_call" | custom-call | flops 536870912 | bytes 7628812 | tf_op jit(solution)/shard_map/pallas_call | solution.py:48
  289.2 3.5 shard_map.232
  292.7 14.4 %collective-permute-start.48 = (bf16[3,128,1152]{2,1,0:T(8,128)(2,1)}, bf16[3,128,1152]{2,1,0:T(8,128)(2,1)S(1)}, u32[]{:S(2)}, u32[]{:S(2)}) collective-permute-start(bf16[3,128,1152]{2,1,0:T(8,128)(2,1)} %get-tuple-element.152), channel_id=1, source_target_pairs={{0,8},{4,12},{8,0},{12,4},{16,24},{20,28},{24,16},{28,20},{1,9},{5... | collective-permute-start | bytes 2654216 | tf_op jit(solution)/shard_map/ppermute | solution.py:97
  312.7 34.2 %collective-permute-done.43 = f32[24,128]{1,0:T(8,128)S(1)} collective-permute-done((f32[24,128]{1,0:T(8,128)S(1)}, f32[24,128]{1,0:T(8,128)S(1)}, u32[]{:S(2)}, u32[]{:S(2)}) %collective-permute-start.43) | collective-permute-done | bytes 12320 | tf_op jit(solution)/shard_map/ppermute | solution.py:97
  351.5 10.4 %collective-permute-start.45 = (f32[24,128]{1,0:T(8,128)S(1)}, f32[24,128]{1,0:T(8,128)S(1)}, u32[]{:S(2)}, u32[]{:S(2)}) collective-permute-start(f32[24,128]{1,0:T(8,128)S(1)} %add.58), channel_id=1, source_target_pairs={{0,1},{1,0},{2,3},{3,2},{4,5},{5,4},{6,7},{7,6},{8,9},{9,8},{10,11... | collective-permute-start | bytes 36872 | tf_op jit(solution)/shard_map/ppermute | solution.py:100
  377.4 3.8 shard_map.230
  381.3 5.3 %collective-permute-done.47 = f32[24,128]{1,0:T(8,128)S(1)} collective-permute-done((f32[24,128]{1,0:T(8,128)S(1)}, f32[24,128]{1,0:T(8,128)S(1)}, u32[]{:S(2)}, u32[]{:S(2)}) %collective-permute-start.47) | collective-permute-done | bytes 12320 | tf_op jit(solution)/shard_map/ppermute | solution.py:100
  389.5 5.9 %collective-permute-done.56.refs_1_ = bf16[3,128,256]{2,1,0:T(8,128)(2,1)S(1)} collective-permute-done((bf16[3,128,256]{2,1,0:T(8,128)(2,1)}, bf16[3,128,256]{2,1,0:T(8,128)(2,1)S(1)}, u32[]{:S(2)}, u32[]{:S(2)}) %collective-permute-start.56) | collective-permute-done | bytes 196640 | tf_op jit(solution)/shard_map/ppermute | solution.py:97
  (213 shorter events, 132.9 us)
Async XLA Ops:
  7.9 23.7 %collective-permute-start.23 = (bf16[3,128,1152]{2,1,0:T(8,128)(2,1)}, bf16[3,128,1152]{2,1,0:T(8,128)(2,1)S(1)}, u32[]{:S(2)}, u32[]{:S(2)}) collective-permute-start(bf16[3,128,1152]{2,1,0:T(8,128)(2,1)} %pad_maximum_fusion.1), channel_id=1, source_target_pairs={{0,8},{4,12},{8,0},{12,4},{16,24},{20,28},{24,16},{28,20},{1,9},{5... | collective-permute-start | bytes 2654216 | tf_op jit(solution)/shard_map/ppermute | solution.py:97
  10.9 40.3 %collective-permute-start.24 = (bf16[3,128,1152]{2,1,0:T(8,128)(2,1)}, bf16[3,128,1152]{2,1,0:T(8,128)(2,1)S(1)}, u32[]{:S(2)}, u32[]{:S(2)}) collective-permute-start(bf16[3,128,1152]{2,1,0:T(8,128)(2,1)} %pad_maximum_fusion.1), channel_id=1, source_target_pairs={{0,16},{4,20},{8,24},{12,28},{16,0},{20,4},{24,8},{28,12},{1,17},{... | collective-permute-start | bytes 2654216 | tf_op jit(solution)/shard_map/ppermute | solution.py:97
  12.5 38.9 %collective-permute-start.25 = (bf16[3,128,1152]{2,1,0:T(8,128)(2,1)}, bf16[3,128,1152]{2,1,0:T(8,128)(2,1)S(1)}, u32[]{:S(2)}, u32[]{:S(2)}) collective-permute-start(bf16[3,128,1152]{2,1,0:T(8,128)(2,1)} %pad_maximum_fusion.1), channel_id=1, source_target_pairs={{0,24},{4,28},{8,16},{12,20},{16,8},{20,12},{24,0},{28,4},{1,25},{... | collective-permute-start | bytes 2654216 | tf_op jit(solution)/shard_map/ppermute | solution.py:97
  51.5 107.9 %collective-permute-start.26 = (bf16[3,512,1152]{2,1,0:T(8,128)(2,1)S(1)}, bf16[3,512,1152]{2,1,0:T(8,128)(2,1)}, u32[]{:S(2)}, u32[]{:S(2)}) collective-permute-start(bf16[3,512,1152]{2,1,0:T(8,128)(2,1)S(1)} %constant_dynamic-update-slice_fusion.4.refs_4_.wm), channel_id=1, source_target_pairs={{0,4},{4,0},{8,12},{12,8},{16,20},{20,16},{24,28},{28,24},{1,5},{5... | collective-permute-start | bytes 10616840 | tf_op jit(solution)/shard_map/ppermute | solution.py:97
  70.3 26.3 %collective-permute-start.6 = (bf16[2,512,256]{2,1,0:T(8,128)(2,1)}, bf16[2,512,256]{2,1,0:T(8,128)(2,1)}, u32[]{:S(2)}, u32[]{:S(2)}) collective-permute-start(bf16[2,512,256]{2,1,0:T(8,128)(2,1)} %constant_dynamic-update-slice_fusion.refs_4_.wm), channel_id=1, source_target_pairs={{0,4},{4,0},{8,12},{12,8},{16,20},{20,16},{24,28},{28,24},{1,5},{5... | collective-permute-start | bytes 1572872 | tf_op jit(solution)/shard_map/ppermute | solution.py:97
  74.4 18.5 %collective-permute-start = (bf16[128,1024]{1,0:T(8,128)(2,1)}, bf16[128,1024]{1,0:T(8,128)(2,1)}, u32[]{:S(2)}, u32[]{:S(2)}) collective-permute-start(bf16[128,1024]{1,0:T(8,128)(2,1)} %get-tuple-element.98.refs_0_.refs_1_), channel_id=1, source_target_pairs={{0,1},{1,0},{2,3},{3,2},{4,5},{5,4},{6,7},{7,6},{8,9},{9,8},{10,11... | collective-permute-start | bytes 786440 | tf_op jit(solution)/shard_map/ppermute | solution.py:100
  78.7 17.8 %collective-permute-start.1 = (bf16[128,1024]{1,0:T(8,128)(2,1)}, bf16[128,1024]{1,0:T(8,128)(2,1)}, u32[]{:S(2)}, u32[]{:S(2)}) collective-permute-start(bf16[128,1024]{1,0:T(8,128)(2,1)} %get-tuple-element.98.refs_0_.refs_1_), channel_id=1, source_target_pairs={{0,2},{1,3},{2,0},{3,1},{4,6},{5,7},{6,4},{7,5},{8,10},{9,11},{10,... | collective-permute-start | bytes 786440 | tf_op jit(solution)/shard_map/ppermute | solution.py:100
  80.3 16.2 %collective-permute-start.2 = (bf16[128,1024]{1,0:T(8,128)(2,1)}, bf16[128,1024]{1,0:T(8,128)(2,1)}, u32[]{:S(2)}, u32[]{:S(2)}) collective-permute-start(bf16[128,1024]{1,0:T(8,128)(2,1)} %get-tuple-element.98.refs_0_.refs_1_), channel_id=1, source_target_pairs={{0,3},{1,2},{2,1},{3,0},{4,7},{5,6},{6,5},{7,4},{8,11},{9,10},{10,... | collective-permute-start | bytes 786440 | tf_op jit(solution)/shard_map/ppermute | solution.py:100
  92.9 57.5 %collective-permute-start.19 = (bf16[1,512,1024]{2,1,0:T(8,128)(2,1)}, bf16[1,512,1024]{2,1,0:T(8,128)(2,1)}, u32[]{:S(2)}, u32[]{:S(2)}) collective-permute-start(bf16[1,512,1024]{2,1,0:T(8,128)(2,1)} %pad_maximum_fusion.refs_4_.refs_11_), channel_id=1, source_target_pairs={{0,4},{4,0},{8,12},{12,8},{16,20},{20,16},{24,28},{28,24},{1,5},{5... | collective-permute-start | bytes 3145736 | tf_op jit(solution)/shard_map/ppermute | solution.py:97
  122.6 31.1 %collective-permute-start.27 = (bf16[128,1024]{1,0:T(8,128)(2,1)}, bf16[128,1024]{1,0:T(8,128)(2,1)}, u32[]{:S(2)}, u32[]{:S(2)}) collective-permute-start(bf16[128,1024]{1,0:T(8,128)(2,1)} %get-tuple-element.113.refs_0_.refs_4_.refs_9_), channel_id=1, source_target_pairs={{0,1},{1,0},{2,3},{3,2},{4,5},{5,4},{6,7},{7,6},{8,9},{9,8},{10,11... | collective-permute-start | bytes 786440 | tf_op jit(solution)/shard_map/ppermute | solution.py:100
  122.7 33.1 %collective-permute-start.28 = (bf16[128,1024]{1,0:T(8,128)(2,1)}, bf16[128,1024]{1,0:T(8,128)(2,1)}, u32[]{:S(2)}, u32[]{:S(2)}) collective-permute-start(bf16[128,1024]{1,0:T(8,128)(2,1)} %get-tuple-element.113.refs_0_.refs_4_.refs_9_), channel_id=1, source_target_pairs={{0,2},{1,3},{2,0},{3,1},{4,6},{5,7},{6,4},{7,5},{8,10},{9,11},{10,... | collective-permute-start | bytes 786440 | tf_op jit(solution)/shard_map/ppermute | solution.py:100
  153.8 23.4 %collective-permute-start.21 = (bf16[128,1024]{1,0:T(8,128)(2,1)}, bf16[128,1024]{1,0:T(8,128)(2,1)}, u32[]{:S(2)}, u32[]{:S(2)}) collective-permute-start(bf16[128,1024]{1,0:T(8,128)(2,1)} %get-tuple-element.111.refs_0_), channel_id=1, source_target_pairs={{0,2},{1,3},{2,0},{3,1},{4,6},{5,7},{6,4},{7,5},{8,10},{9,11},{10,... | collective-permute-start | bytes 786440 | tf_op jit(solution)/shard_map/ppermute | solution.py:100
  155.8 21.4 %collective-permute-start.22 = (bf16[128,1024]{1,0:T(8,128)(2,1)}, bf16[128,1024]{1,0:T(8,128)(2,1)}, u32[]{:S(2)}, u32[]{:S(2)}) collective-permute-start(bf16[128,1024]{1,0:T(8,128)(2,1)} %get-tuple-element.111.refs_0_), channel_id=1, source_target_pairs={{0,3},{1,2},{2,1},{3,0},{4,7},{5,6},{6,5},{7,4},{8,11},{9,10},{10,... | collective-permute-start | bytes 786440 | tf_op jit(solution)/shard_map/ppermute | solution.py:100
  194.9 19.6 %collective-permute-start.33 = (bf16[3,512,1152]{2,1,0:T(8,128)(2,1)}, bf16[3,512,1152]{2,1,0:T(8,128)(2,1)S(1)}, u32[]{:S(2)}, u32[]{:S(2)}) collective-permute-start(bf16[3,512,1152]{2,1,0:T(8,128)(2,1)} %shard_map.224), channel_id=1, source_target_pairs={{0,4},{4,0},{8,12},{12,8},{16,20},{20,16},{24,28},{28,24},{1,5},{5... | collective-permute-start | bytes 10616840 | tf_op jit(solution)/shard_map/ppermute | solution.py:97
  194.9 29.1 %collective-permute-start.30 = (bf16[128,1024]{1,0:T(8,128)(2,1)}, bf16[128,1024]{1,0:T(8,128)(2,1)}, u32[]{:S(2)}, u32[]{:S(2)}) collective-permute-start(bf16[128,1024]{1,0:T(8,128)(2,1)} %get-tuple-element.115), channel_id=1, source_target_pairs={{0,1},{1,0},{2,3},{3,2},{4,5},{5,4},{6,7},{7,6},{8,9},{9,8},{10,11... | collective-permute-start | bytes 786440 | tf_op jit(solution)/shard_map/ppermute | solution.py:100
  199.6 24.5 %collective-permute-start.31 = (bf16[128,1024]{1,0:T(8,128)(2,1)}, bf16[128,1024]{1,0:T(8,128)(2,1)}, u32[]{:S(2)}, u32[]{:S(2)}) collective-permute-start(bf16[128,1024]{1,0:T(8,128)(2,1)} %get-tuple-element.116), channel_id=1, source_target_pairs={{0,2},{1,3},{2,0},{3,1},{4,6},{5,7},{6,4},{7,5},{8,10},{9,11},{10,... | collective-permute-start | bytes 786440 | tf_op jit(solution)/shard_map/ppermute | solution.py:100
  199.8 24.3 %collective-permute-start.32 = (bf16[128,1024]{1,0:T(8,128)(2,1)}, bf16[128,1024]{1,0:T(8,128)(2,1)}, u32[]{:S(2)}, u32[]{:S(2)}) collective-permute-start(bf16[128,1024]{1,0:T(8,128)(2,1)} %get-tuple-element.117), channel_id=1, source_target_pairs={{0,3},{1,2},{2,1},{3,0},{4,7},{5,6},{6,5},{7,4},{8,11},{9,10},{10,... | collective-permute-start | bytes 786440 | tf_op jit(solution)/shard_map/ppermute | solution.py:100
  247.4 37.7 %collective-permute-start.51 = (bf16[256,1024]{1,0:T(8,128)(2,1)}, bf16[256,1024]{1,0:T(8,128)(2,1)S(1)}, u32[]{:S(2)}, u32[]{:S(2)}) collective-permute-start(bf16[256,1024]{1,0:T(8,128)(2,1)} %get-tuple-element.157), channel_id=1, source_target_pairs={{0,1},{1,0},{2,3},{3,2},{4,5},{5,4},{6,7},{7,6},{8,9},{9,8},{10,11... | collective-permute-start | bytes 1572872 | tf_op jit(solution)/shard_map/ppermute | solution.py:100
  250.0 38.2 %collective-permute-start.52 = (bf16[256,1024]{1,0:T(8,128)(2,1)S(1)}, bf16[256,1024]{1,0:T(8,128)(2,1)S(1)}, u32[]{:S(2)}, u32[]{:S(2)}) collective-permute-start(bf16[256,1024]{1,0:T(8,128)(2,1)S(1)} %copy-done.26), channel_id=1, source_target_pairs={{0,2},{1,3},{2,0},{3,1},{4,6},{5,7},{6,4},{7,5},{8,10},{9,11},{10,... | collective-permute-start | bytes 1572872 | tf_op jit(solution)/shard_map/ppermute | solution.py:100
  250.3 37.9 %collective-permute-start.53 = (bf16[256,1024]{1,0:T(8,128)(2,1)S(1)}, bf16[256,1024]{1,0:T(8,128)(2,1)S(1)}, u32[]{:S(2)}, u32[]{:S(2)}) collective-permute-start(bf16[256,1024]{1,0:T(8,128)(2,1)S(1)} %copy-done.25), channel_id=1, source_target_pairs={{0,3},{1,2},{2,1},{3,0},{4,7},{5,6},{6,5},{7,4},{8,11},{9,10},{10,... | collective-permute-start | bytes 1572872 | tf_op jit(solution)/shard_map/ppermute | solution.py:100
  253.6 21.7 %collective-permute-start.38 = (bf16[512,256]{1,0:T(8,128)(2,1)S(1)}, bf16[512,256]{1,0:T(8,128)(2,1)S(1)}, u32[]{:S(2)}, u32[]{:S(2)}) collective-permute-start(bf16[512,256]{1,0:T(8,128)(2,1)S(1)} %fusion), channel_id=1, source_target_pairs={{8,0},{12,4},{9,1},{13,5},{10,2},{14,6},{11,3},{15,7},{24,16},{28,... | collective-permute-start | bytes 786440 | tf_op jit(solution)/shard_map/ppermute | solution.py:104
  292.7 69.2 %collective-permute-start.54 = (bf16[3,512,256]{2,1,0:T(8,128)(2,1)}, bf16[3,512,256]{2,1,0:T(8,128)(2,1)S(1)}, u32[]{:S(2)}, u32[]{:S(2)}) collective-permute-start(bf16[3,512,256]{2,1,0:T(8,128)(2,1)} %get-tuple-element.164), channel_id=1, source_target_pairs={{0,4},{4,0},{8,12},{12,8},{16,20},{20,16},{24,28},{28,24},{1,5},{5... | collective-permute-start | bytes 2359304 | tf_op jit(solution)/shard_map/ppermute | solution.py:97
  292.7 73.5 %collective-permute-start.48 = (bf16[3,128,1152]{2,1,0:T(8,128)(2,1)}, bf16[3,128,1152]{2,1,0:T(8,128)(2,1)S(1)}, u32[]{:S(2)}, u32[]{:S(2)}) collective-permute-start(bf16[3,128,1152]{2,1,0:T(8,128)(2,1)} %get-tuple-element.152), channel_id=1, source_target_pairs={{0,8},{4,12},{8,0},{12,4},{16,24},{20,28},{24,16},{28,20},{1,9},{5... | collective-permute-start | bytes 2654216 | tf_op jit(solution)/shard_map/ppermute | solution.py:97
  307.1 61.1 %collective-permute-start.49 = (bf16[3,128,1152]{2,1,0:T(8,128)(2,1)}, bf16[3,128,1152]{2,1,0:T(8,128)(2,1)S(1)}, u32[]{:S(2)}, u32[]{:S(2)}) collective-permute-start(bf16[3,128,1152]{2,1,0:T(8,128)(2,1)} %get-tuple-element.153), channel_id=1, source_target_pairs={{0,16},{4,20},{8,24},{12,28},{16,0},{20,4},{24,8},{28,12},{1,17},{... | collective-permute-start | bytes 2654216 | tf_op jit(solution)/shard_map/ppermute | solution.py:97
  310.0 58.8 %collective-permute-start.50 = (bf16[3,128,1152]{2,1,0:T(8,128)(2,1)}, bf16[3,128,1152]{2,1,0:T(8,128)(2,1)S(1)}, u32[]{:S(2)}, u32[]{:S(2)}) collective-permute-start(bf16[3,128,1152]{2,1,0:T(8,128)(2,1)} %get-tuple-element.154), channel_id=1, source_target_pairs={{0,24},{4,28},{8,16},{12,20},{16,8},{20,12},{24,0},{28,4},{1,25},{... | collective-permute-start | bytes 2654216 | tf_op jit(solution)/shard_map/ppermute | solution.py:97
  311.2 35.7 %collective-permute-start.43 = (f32[24,128]{1,0:T(8,128)S(1)}, f32[24,128]{1,0:T(8,128)S(1)}, u32[]{:S(2)}, u32[]{:S(2)}) collective-permute-start(f32[24,128]{1,0:T(8,128)S(1)} %add.56), channel_id=1, source_target_pairs={{0,8},{4,12},{8,0},{12,4},{16,24},{20,28},{24,16},{28,20},{1,9},{5... | collective-permute-start | bytes 36872 | tf_op jit(solution)/shard_map/ppermute | solution.py:97
  351.5 19.2 %collective-permute-start.45 = (f32[24,128]{1,0:T(8,128)S(1)}, f32[24,128]{1,0:T(8,128)S(1)}, u32[]{:S(2)}, u32[]{:S(2)}) collective-permute-start(f32[24,128]{1,0:T(8,128)S(1)} %add.58), channel_id=1, source_target_pairs={{0,1},{1,0},{2,3},{3,2},{4,5},{5,4},{6,7},{7,6},{8,9},{9,8},{10,11... | collective-permute-start | bytes 36872 | tf_op jit(solution)/shard_map/ppermute | solution.py:100
  366.2 32.0 %collective-permute-start.39 = (bf16[128,1024]{1,0:T(8,128)(2,1)}, bf16[128,1024]{1,0:T(8,128)(2,1)S(1)}, u32[]{:S(2)}, u32[]{:S(2)}) collective-permute-start(bf16[128,1024]{1,0:T(8,128)(2,1)} %get-tuple-element.147), channel_id=1, source_target_pairs={{0,1},{1,0},{2,3},{3,2},{4,5},{5,4},{6,7},{7,6},{8,9},{9,8},{10,11... | collective-permute-start | bytes 786440 | tf_op jit(solution)/shard_map/ppermute | solution.py:100
  368.2 30.0 %collective-permute-start.40 = (bf16[128,1024]{1,0:T(8,128)(2,1)}, bf16[128,1024]{1,0:T(8,128)(2,1)S(1)}, u32[]{:S(2)}, u32[]{:S(2)}) collective-permute-start(bf16[128,1024]{1,0:T(8,128)(2,1)} %get-tuple-element.148), channel_id=1, source_target_pairs={{0,2},{1,3},{2,0},{3,1},{4,6},{5,7},{6,4},{7,5},{8,10},{9,11},{10,... | collective-permute-start | bytes 786440 | tf_op jit(solution)/shard_map/ppermute | solution.py:100
  368.7 29.4 %collective-permute-start.41 = (bf16[128,1024]{1,0:T(8,128)(2,1)}, bf16[128,1024]{1,0:T(8,128)(2,1)S(1)}, u32[]{:S(2)}, u32[]{:S(2)}) collective-permute-start(bf16[128,1024]{1,0:T(8,128)(2,1)} %get-tuple-element.149), channel_id=1, source_target_pairs={{0,3},{1,2},{2,1},{3,0},{4,7},{5,6},{6,5},{7,4},{8,11},{9,10},{10,... | collective-permute-start | bytes 786440 | tf_op jit(solution)/shard_map/ppermute | solution.py:100
  370.7 15.9 %collective-permute-start.47 = (f32[24,128]{1,0:T(8,128)S(1)}, f32[24,128]{1,0:T(8,128)S(1)}, u32[]{:S(2)}, u32[]{:S(2)}) collective-permute-start(f32[24,128]{1,0:T(8,128)S(1)} %add.58), channel_id=1, source_target_pairs={{0,3},{1,2},{2,1},{3,0},{4,7},{5,6},{6,5},{7,4},{8,11},{9,10},{10,... | collective-permute-start | bytes 36872 | tf_op jit(solution)/shard_map/ppermute | solution.py:100
  372.6 15.8 %collective-permute-start.55 = (bf16[3,128,256]{2,1,0:T(8,128)(2,1)}, bf16[3,128,256]{2,1,0:T(8,128)(2,1)}, u32[]{:S(2)}, u32[]{:S(2)}) collective-permute-start(bf16[3,128,256]{2,1,0:T(8,128)(2,1)} %get-tuple-element.166), channel_id=1, source_target_pairs={{0,8},{4,12},{8,0},{12,4},{16,24},{20,28},{24,16},{28,20},{1,9},{5... | collective-permute-start | bytes 589832 | tf_op jit(solution)/shard_map/ppermute | solution.py:97
  (60 other events, 649.1 us)

commit v6 on v5

--- a/solution.py
+++ b/solution.py
@@ -113,35 +113,16 @@
         mine = jnp.concatenate(near, axis=1)
         return mine, plane(mine, 1)
 
-    def merge_core(mine, got):
-        kinds, half, cols = mine.shape
-        m = half * 2 // N
-
-        def body(a, b, first, *rest):
-            for i in range(N // 2):
-                rows = slice(i * m, (i + 1) * m)
-                total = a[0, rows].astype(f32) + b[0, rows].astype(f32)
-                if i == 0:
-                    first[0] = total
-                else:
-                    rest[i - 1][0] = total.astype(bf16)
-
-        part = 384 if cols % 384 == 0 else cols
-        big = pl.BlockSpec((1, half, part), lambda k, i: (k, 0, i))
-        small = pl.BlockSpec((1, m, part), lambda k, i: (k, 0, i))
-        own, *sends = pl.pallas_call(
-            body,
-            grid=(kinds, cols // part),
-            out_shape=[sds((kinds, m, cols), f32)] + [sds((kinds, m, cols), bf16)] * (N // 2 - 1),
-            in_specs=[big, big],
-            out_specs=[small] * (N // 2),
-            cost_estimate=pl.CostEstimate(
-                flops=kinds * half * cols, bytes_accessed=7 * kinds * half * cols, transcendentals=0
-            ),
-        )(mine, got)
-        return own, sends
-
-    def close_sum(own, parts):
+    def share_out(refs, total, k):
+        m = total.shape[0] * 2 // N
+        for i, ref in enumerate(refs):
+            ref[k] = total[i * m : (i + 1) * m].astype(ref.dtype)
+
+    def share_shapes(kinds, cols):
+        shape = (kinds, H * 2 // N, cols)
+        return [sds(shape, f32)] + [sds(shape, bf16)] * (N // 2 - 1)
+
+    def close_sum(own, parts, turned):
         kinds, m, cols = own.shape
 
         def body(first, *refs):
@@ -150,12 +131,12 @@
                 total = first[k]
                 for p in parts:
                     total = total + p[k].astype(f32)
-                outs[k][...] = total if k < kinds - 1 else total.T
+                outs[k][...] = total if k < kinds - turned else total.T
 
         parts_in = parts
         return whole_call(
             body,
-            [sds((m, cols), f32)] * (kinds - 1) + [sds((cols, m), f32)],
+            [sds((m, cols), f32)] * (kinds - turned) + [sds((cols, m), f32)] * turned,
             (own, *parts),
             own.size * N,
             scalars=False,
@@ -379,15 +360,24 @@
         wm, wo, out = refs[NT:]
         c = join_slots(refs[:NT])
         for cols in chunks:
-            out[:, cols] = mm(c[:, :H], wm[2, :, cols]) + mm(c[:, H:], wo[2, :, cols])
-
-    (grad_mid,) = whole_call(
-        hidden_body, [sds((B, F), f32)], (*cot_pieces, ffn_m, ffn_o), 2 * B * W * F, scalars=False
-    )
+            out[:, cols] = mm(c[:, :H], wm[0, :, cols]) + mm(c[:, H:], wo[0, :, cols])
+
+    down_spec = pl.BlockSpec((1, H, F), lambda k: (2, 0, 0))
+    grad_mid = pl.pallas_call(
+        hidden_body,
+        grid=(1,),
+        out_shape=sds((B, F), f32),
+        in_specs=[pl.BlockSpec((R, W), lambda k: (0, 0))] * NT + [down_spec] * 2,
+        out_specs=pl.BlockSpec((B, F), lambda k: (0, 0)),
+        cost_estimate=pl.CostEstimate(
+            flops=2 * B * W * F, bytes_accessed=2 * W * F + 6 * B * F, transcendentals=0
+        ),
+        name="hidden_back",
+    )(*cot_pieces, ffn_m, ffn_o)
 
     def ffn_body(*refs):
-        wm, wo, gmid_r, mid_r, dg_r, du_r = refs[NT : NT + 6]
-        gnfs = refs[NT + 6 :]
+        wm, wo, gmid_r, hid = refs[NT : NT + 4]
+        gnfs = refs[NT + 4 :]
         r = join_slots(refs[:NT])
         rl, rr = r[:, :H], r[:, H:]
         for cols in chunks:
@@ -396,63 +386,85 @@
             gmid = gmid_r[:, cols]
             sig = jax.nn.sigmoid(gate)
             act = gate * sig
-            mid_r[:, cols] = (act * up).astype(bf16)
-            dg_r[:, cols] = (gmid * up * sig * (1.0 + gate * (1.0 - sig))).astype(bf16)
-            du_r[:, cols] = (gmid * act).astype(bf16)
+            hid[0, :, cols] = (gmid * up * sig * (1.0 + gate * (1.0 - sig))).astype(bf16)
+            hid[1, :, cols] = (gmid * act).astype(bf16)
+            hid[2, :, cols] = (act * up).astype(bf16)
         for w, cols in ((wm, slice(0, H)), (wo, slice(H, W))):
-            g = mm_nt(dg_r[...], w[0]) + mm_nt(du_r[...], w[1])
+            g = mm_nt(hid[0], w[0]) + mm_nt(hid[1], w[1])
             for k, ref in enumerate(gnfs):
                 ref[:, cols] = g[k * R : (k + 1) * R].astype(bf16)
 
-    mid, dgate, dup, *gnf_slots = whole_call(
+    hidden, *gnf_slots = whole_call(
         ffn_body,
-        [sds((B, F), bf16)] * 3 + [sds((R, W), bf16)] * NT,
+        [sds((3, B, F), bf16)] + [sds((R, W), bf16)] * NT,
         (*second_pieces, ffn_m, ffn_o, grad_mid),
         8 * B * W * F,
         scalars=False,
     )
     gnf_pieces = spread_column(gnf_slots)
 
+    one = lambda shape: pl.BlockSpec(shape, lambda k: (0,) * len(shape))
+    kind = lambda rows: pl.BlockSpec((1, rows, F), lambda k: (k, 0, 0))
+
     def dw_body(cols, *refs):
-        c_in, (mid_r, dg_r, du_r, out) = refs[NT : 2 * NT], refs[2 * NT :]
-        rt = jnp.concatenate([ref[:, cols] for ref in refs[:NT]], axis=0).T
-        ct = jnp.concatenate([ref[:, cols] for ref in c_in], axis=0).T
-        for k, (lhs, rhs) in enumerate(((rt, dg_r), (rt, du_r), (ct, mid_r))):
-            out[k] = mm(lhs, rhs[...]).astype(bf16)
-
-    def half_weights(cols, dg):
-        return whole_call(
+        r_in, c_in, (h_ref, *rest) = refs[:NT], refs[NT : 2 * NT], refs[2 * NT :]
+        lt = rest[-1]
+        k = pl.program_id(0)
+
+        @pl.when(k == 0)
+        def _():
+            lt[0] = jnp.concatenate([ref[:, cols] for ref in r_in], axis=0).T
+            lt[1] = jnp.concatenate([ref[:, cols] for ref in c_in], axis=0).T
+
+        total = mm(lt[k // 2], h_ref[0])
+        if len(rest) == 2:
+            rest[0][0] = total.astype(bf16)
+        else:
+            share_out(rest[1:-1], total + rest[0][0].astype(f32), 0)
+
+    def half_weights(cols, hid, got):
+        outs = share_shapes(3, F) if got else [sds((3, H, F), bf16)]
+        return pl.pallas_call(
             functools.partial(dw_body, cols),
-            [sds((3, H, F), bf16)],
-            (*second_pieces, *cot_pieces, mid, dg, dup),
-            3 * B * W * F,
-            scalars=False,
-        )[0]
-
-    dwf_o = half_weights(slice(H, W), dgate)
-    dwf_m = half_weights(slice(0, H), after(dgate, dwf_o))
-
-    def out_part_body(m_ref, wm, wo, *outs):
+            grid=(3,),
+            out_shape=outs,
+            in_specs=[one((R, W))] * (2 * NT) + [kind(B)] + [kind(H)] * len(got),
+            out_specs=[kind(o.shape[1]) for o in outs],
+            scratch_shapes=[pltpu.VMEM((2, H, B), bf16)],
+            cost_estimate=pl.CostEstimate(
+                flops=3 * B * W * F, bytes_accessed=3 * W * F + 6 * B * F, transcendentals=0
+            ),
+        )(*second_pieces, *cot_pieces, hid, *got)
+
+    (dwf_o,) = half_weights(slice(H, W), hidden, [])
+    dwf_got = plane(dwf_o, 1)
+
+    def out_part_body(h_ref, wm, wo, *outs):
         for w, cols in ((wm, slice(0, H)), (wo, slice(H, W))):
-            o = mm_nt(m_ref[...], w[2])
+            o = mm_nt(h_ref[0], w[0])
             for k, ref in enumerate(outs):
                 ref[:, cols] = o[k * R : (k + 1) * R].astype(bf16)
 
-    ffn_slots = whole_call(
+    third = lambda rows: pl.BlockSpec((1, rows, F), lambda k: (2, 0, 0))
+    ffn_slots = pl.pallas_call(
         out_part_body,
-        [sds((R, W), bf16)] * NT,
-        (after(mid, dwf_m), ffn_m, ffn_o),
-        2 * B * W * F,
-        scalars=False,
-    )
-    ffn_own, ffn_sends = merge_core(dwf_m, plane(dwf_o, 1))
-    gnf_pieces, ffn_own, ffn_sends = lax.optimization_barrier((gnf_pieces, ffn_own, ffn_sends))
+        grid=(1,),
+        out_shape=[sds((R, W), bf16)] * NT,
+        in_specs=[third(B), third(H), third(H)],
+        out_specs=[one((R, W))] * NT,
+        cost_estimate=pl.CostEstimate(
+            flops=2 * B * W * F, bytes_accessed=2 * W * F + 2 * B * F, transcendentals=0
+        ),
+        name="ffn_out",
+    )(after(hidden, dwf_o), ffn_m, ffn_o)
+    ffn_own, *ffn_sends = half_weights(slice(0, H), hidden, [dwf_got])
+    gnf_pieces, ffn_own, ffn_sends, ffn_slots = lax.optimization_barrier(
+        (gnf_pieces, ffn_own, ffn_sends, ffn_slots)
+    )
     ffn_got = [plane(v, 2 * (i + 1)) for i, v in enumerate(ffn_sends)]
 
     def back_body(*refs):
-        pieces, outs_in = refs[:NT], refs[NT : 2 * NT]
-        res, c_ref, g_ref, om, oo, gres, gg, *more = refs[2 * NT :]
-        gas, both = more[:NT], more[NT:]
+        pieces, (res, c_ref, g_ref, om, oo, gres, gg, rg, *gas) = refs[:NT], refs[NT:]
         grad = sum(p[...].astype(f32) for p in pieces)
         x = res[...]
         inv = lax.rsqrt(jnp.mean(x * x, axis=-1, keepdims=True) + epsilon)
@@ -463,25 +475,43 @@
         total = c_ref[...].astype(f32) + through
         gres[...] = total
         half = total.astype(bf16)
-        for k, ref in enumerate(both):
-            ref[:R] = half
-            ref[R:] = outs_in[k][...]
+        rg[...] = half
         ga = (mm(half[:, :H], om[0]) + mm(half[:, H:], oo[0])).astype(bf16)
         for k, ref in enumerate(gas):
             ref[...] = ga[:, k * C : (k + 1) * C]
 
-    grad_resid, ffn_gain_part, *ga_slots = whole_call(
+    grad_resid, ffn_gain_part, rg16, *ga_slots = whole_call(
         back_body,
-        [sds((R, W), f32), sds((1, W), f32)]
-        + [sds((R, C), bf16)] * NT
-        + [sds((2 * R, W), bf16)] * NT,
-        (*gnf_pieces, *ffn_slots[:NT], resid, cot, gain2, out_m, out_o),
+        [sds((R, W), f32), sds((1, W), f32), sds((R, W), bf16)] + [sds((R, C), bf16)] * NT,
+        (*gnf_pieces, resid, cot, gain2, out_m, out_o),
         2 * R * W * W,
         scalars=False,
     )
-    ga_slots, both_slots = ga_slots[:NT], ga_slots[NT:]
     ga_pieces = spread_column(ga_slots)
-    both_pieces = spread_column(both_slots)
+    ffn_pieces = spread_column(ffn_slots)
+
+    def dwo_body(cols, g_ref, *refs):
+        g = g_ref[:, cols].T
+        a = jnp.concatenate([ref[...] for ref in refs[:NT]], axis=1)
+        total = mm(g, a)
+        rest = refs[NT:]
+        if len(rest) == 1:
+            rest[0][0] = total.astype(bf16)
+        else:
+            share_out(rest[1:], total + rest[0][0].astype(f32), 0)
+
+    def half_out(cols, got):
+        return whole_call(
+            functools.partial(dwo_body, cols),
+            share_shapes(1, NT * C) if got else [sds((1, H, NT * C), bf16)],
+            (rg16, *att_pieces, *got),
+            R * W * NT * C,
+            scalars=False,
+        )
+
+    (dwo_o,) = half_out(slice(H, W), [])
+    out_own, *out_sends = half_out(slice(0, H), [plane(dwo_o, 1)])
+    out_got = [plane(v, 2 * (i + 1)) for i, v in enumerate(out_sends)]
 
     def bwd_body(s_ref, q_ref, a_ref, l_ref, *refs):
         d_in, kv_in = refs[:NT], refs[NT : NT + NC]
@@ -632,39 +662,61 @@
     )
     gna_pieces = spread_column(gna_slots)
 
-    def proj_body(*refs):
-        b_ref, gm, go = refs[NT:]
-        rt = join_slots(refs[:NT]).T
-        for ref, rows in ((gm, slice(0, H)), (go, slice(H, W))):
-            full = mm(rt[rows], b_ref[...]).astype(bf16)
-            ref[0] = full[:, :C]
-            ref[1] = full[:, C:]
-
-    proj_m, proj_o = whole_call(
-        proj_body, [sds((2, H, C), bf16)] * 2, (*first_pieces, both16), 4 * B * W * C, scalars=False
-    )
-
-    def last_body(*refs):
-        g_in, (a_ref, pm, po, gm, go) = refs[:NT], refs[NT:]
-        gt = jnp.concatenate([ref[:R] for ref in g_in], axis=0).T
-        for ref, part, rows in ((gm, pm, slice(0, H)), (go, po, slice(H, W))):
-            ref[:2] = part[...]
-            ref[2] = mm(gt[rows], a_ref[...]).astype(bf16)
-
-    last_m, last_o = whole_call(
-        last_body,
-        [sds((3, H, C), bf16)] * 2,
-        (*both_pieces, attended, proj_m, proj_o),
-        2 * B * W * C,
+    def proj_body(cols, *refs):
+        b_ref, *rest = refs[NT:]
+        rt = jnp.concatenate([ref[:, cols] for ref in refs[:NT]], axis=0).T
+        full = mm(rt, b_ref[...])
+        for k in range(2):
+            part = full[:, k * C : (k + 1) * C]
+            if len(rest) == 1:
+                rest[0][k] = part.astype(bf16)
+            else:
+                share_out(rest[1:], part + rest[0][k].astype(f32), k)
+
+    def half_proj(cols, got):
+        return whole_call(
+            functools.partial(proj_body, cols),
+            share_shapes(2, C) if got else [sds((2, H, C), bf16)],
+            (*first_pieces, both16, *got),
+            2 * B * W * C,
+            scalars=False,
+        )
+
+    (proj_o,) = half_proj(slice(H, W), [])
+    att_own, *att_sends = half_proj(slice(0, H), [plane(proj_o, 1)])
+    att_got = [plane(v, 2 * (i + 1)) for i, v in enumerate(att_sends)]
+
+    def out_sum_body(first, *refs):
+        parts, outs = refs[: len(out_got)], refs[len(out_got) :]
+        total = first[0]
+        for p in parts:
+            total = total + p[0].astype(f32)
+        for k, ref in enumerate(outs):
+            ref[...] = total[:, k * C : (k + 1) * C].astype(bf16)
+
+    out_slots = whole_call(
+        out_sum_body,
+        [sds((blk, C), bf16)] * NT,
+        (out_own, *out_got),
+        blk * NT * C * 4,
         scalars=False,
     )
-    att_own, att_sends = merge_core(last_m, plane(last_o, 1))
-    att_got = [plane(v, 2 * (i + 1)) for i, v in enumerate(att_sends)]
+    out_pieces = spread_column(out_slots)
+
+    def out_close_body(*refs):
+        total = refs[0][...].astype(f32)
+        for ref in refs[1:NT]:
+            total = total + ref[...].astype(f32)
+        refs[NT][...] = total.T
+
+    (grad_output,) = whole_call(
+        out_close_body, [sds((C, blk), f32)], out_pieces, blk * C * 4, scalars=False
+    )
 
     def block_body(*refs):
         index = refs[0][0]
         fp, (res, bo) = refs[1 : NT + 1], refs[NT + 1 :]
-        block = (res[...] + sum(p[R:].astype(f32) for p in fp)).astype(bf16)
+        block = (res[...] + sum(p[...].astype(f32) for p in fp)).astype(bf16)
         for s, mask in enumerate(masks):
             src = slice(s * blk, (s + 1) * blk)
             if aligned:
@@ -674,7 +726,7 @@
             bo[:, dst] = block[:, src]
 
     (block_out,) = whole_call(
-        block_body, [sds((R, W), bf16)], (where, *both_pieces, resid), R * W * 8
+        block_body, [sds((R, W), bf16)], (where, *ffn_pieces, resid), R * W * 8
     )
 
     bit = 1
@@ -683,8 +735,8 @@
         bit *= 2
     packed = sum(gather_column(packed))
 
-    grad_gate, grad_up, grad_down = close_sum(ffn_own, ffn_got)
-    grad_query, grad_pairs, grad_output = close_sum(att_own, att_got)
+    grad_gate, grad_up, grad_down = close_sum(ffn_own, ffn_got, 1)
+    grad_query, grad_pairs = close_sum(att_own, att_got, 0)
 
     def end_body(*refs):
         s_ref, rest = refs[0], refs[1:]
@@ -704,8 +756,10 @@
                 dst = src
             gt[:, dst] = total[:, src]
 
-    gna_pieces, packed, grad_down, grad_output, block_out = lax.optimization_barrier(
-        (gna_pieces, packed, grad_down, grad_output, block_out)
+    gna_pieces, packed, grad_down, grad_output, grad_query, block_out = (
+        lax.optimization_barrier(
+            (gna_pieces, packed, grad_down, grad_output, grad_query, block_out)
+        )
     )
     (grad_tokens,) = whole_call(
         end_body, [sds((R, W), f32)], (where, *gna_pieces, tok, grad_resid, gain2), R * W * 16

time: 407 us -> 389 us (0.956)
  waiting for transfers between devices: 158 us -> 150 us
  Pallas kernels: 98 us -> 91.6 us
  starting transfers between devices: 110 us -> 105 us
    pallas_call x16, Pallas kernels: 75.1 us -> 55.4 us  [whole_call(): pl.pallas_call(body, out_shape=list(outs), in_specs=specs, out_specs=[VM]...]
    pallas_call x2 -> x4, Pallas kernels: 10.9 us -> 24.2 us  [the longest x2 14.7 us: half_weights(): pl.pallas_call(functools.partial(dw_body, cols), grid=(3,), out_shape=out...]
    ppermute x23 -> x27, waiting for transfers between devices: 88.4 us -> 80.9 us  [plane(): return lax.ppermute(v, ('dp', 'ctx'), [(i, i ^ mask) for i in range(N)])]
    ppermute x23 -> x27, starting transfers between devices: 38.1 us -> 33.3 us  [plane(): return lax.ppermute(v, ('dp', 'ctx'), [(i, i ^ mask) for i in range(N)])]
    ppermute x30 -> x33, waiting for transfers between devices: 46.4 us -> 49.5 us  [column(): return lax.ppermute(v, 'tp', [(i, i ^ mask) for i in range(NT)])]
    ppermute x30 -> x33, starting transfers between devices: 63.5 us -> 62.2 us  [column(): return lax.ppermute(v, 'tp', [(i, i ^ mask) for i in range(NT)])]
    unnamed x75 -> x85, local copies, waits for them, and re-layouts: 13.5 us -> 13.4 us
  transfers between devices with their start and end apart: 58 -> 65, of which waited for: 20 -> 21; matrix products, arithmetic and copies ran while one was open for 5% -> 6% of each run, Pallas kernels for 15% -> 15%
where the time goes in v6:
time: 389 us; the launch traced here: 382 us
  waiting for transfers between devices  150 us (39%)
  starting transfers between devices  105 us (27%)
  Pallas kernels  91.6 us (24%)
  local copies, waits for them, and re-layouts  23.9 us (6%)
  other arithmetic  11.4 us (3%)
    ppermute x27, waiting for transfers between devices, plane(): return lax.ppermute(v, ('dp', 'ctx'), [(i, i ^ mask) for i in range(N)])  80.9 us
    ppermute x33, starting transfers between devices, column(): return lax.ppermute(v, 'tp', [(i, i ^ mask) for i in range(NT)])  62.2 us
    pallas_call x16, Pallas kernels, whole_call(): pl.pallas_call(body, out_shape=list(outs), in_specs=specs, out_specs=[VM]...  55.4 us
    ppermute x33, waiting for transfers between devices, column(): return lax.ppermute(v, 'tp', [(i, i ^ mask) for i in range(NT)])  49.5 us
    ppermute x27, starting transfers between devices, plane(): return lax.ppermute(v, ('dp', 'ctx'), [(i, i ^ mask) for i in range(N)])  33.3 us
    ppermute x4, waiting for transfers between devices, along(): return lax.ppermute(v, 'ctx', pairs)  19.5 us
    pallas_call x2, Pallas kernels, half_weights(): pl.pallas_call(functools.partial(dw_body, cols), grid=(3,), out_shape=out...  14.7 us
    unnamed x85, local copies, waits for them, and re-layouts  13.4 us
  transfers between devices with their start and end apart: 65, of which 21 were waited for; matrix products, arithmetic and copies ran while one was open for 6% of the time, Pallas kernels for 15%

profile of v6, /device:TPU:0, one launch (start us, length us, event | category | flops | bytes accessed | tf_op | source)
XLA Modules:
  0.0 382.3 jit_solution(2640211874585136389)
XLA Ops:
  13.8 17.9 %collective-permute-done.23 = bf16[3,128,1152]{2,1,0:T(8,128)(2,1)S(1)} collective-permute-done((bf16[3,128,1152]{2,1,0:T(8,128)(2,1)}, bf16[3,128,1152]{2,1,0:T(8,128)(2,1)S(1)}, u32[]{:S(2)}, u32[]{:S(2)}) %collective-permute-start.23) | collective-permute-done | bytes 884768 | tf_op jit(solution)/shard_map/ppermute | solution.py:97
  31.8 19.4 %collective-permute-done.24 = bf16[3,128,1152]{2,1,0:T(8,128)(2,1)S(1)} collective-permute-done((bf16[3,128,1152]{2,1,0:T(8,128)(2,1)}, bf16[3,128,1152]{2,1,0:T(8,128)(2,1)S(1)}, u32[]{:S(2)}, u32[]{:S(2)}) %collective-permute-start.24) | collective-permute-done | bytes 884768 | tf_op jit(solution)/shard_map/ppermute | solution.py:97
  70.3 4.1 %collective-permute-done.16 = bf16[1,128,1024]{2,1,0:T(8,128)(2,1)S(1)} collective-permute-done((bf16[1,128,1024]{2,1,0:T(8,128)(2,1)S(1)}, bf16[1,128,1024]{2,1,0:T(8,128)(2,1)S(1)}, u32[]{:S(2)}, u32[]{:S(2)}) %collective-permute-start.16) | collective-permute-done | bytes 262176 | tf_op jit(solution)/shard_map/ppermute | solution.py:97
  74.8 4.0 %collective-permute-done.17 = bf16[1,128,1024]{2,1,0:T(8,128)(2,1)S(1)} collective-permute-done((bf16[1,128,1024]{2,1,0:T(8,128)(2,1)S(1)}, bf16[1,128,1024]{2,1,0:T(8,128)(2,1)S(1)}, u32[]{:S(2)}, u32[]{:S(2)}) %collective-permute-start.17) | collective-permute-done | bytes 262176 | tf_op jit(solution)/shard_map/ppermute | solution.py:97
  92.9 3.7 collective-permute-done.1.refs_2_.refs_3_
  97.2 4.5 %shard_map.220 = (bf16[512,256]{1,0:T(8,128)(2,1)}, bf16[512,256]{1,0:T(8,128)(2,1)}, f32[512,256]{1,0:T(8,128)}, f32[512,256]{1,0:T(8,128)}) custom-call(bf16[128,1024]{1,0:T(8,128)(2,1)} %get-tuple-element.100.refs_0_.refs_1_, bf16[128,1024]{1,0:T(8,128)(2,1)} %collective-permute-done.refs_1_.refs_2_, ...), custom_call_target="tpu_custom_call" | custom-call | flops 536870912 | bytes 4720640 | tf_op jit(solution)/shard_map/pallas_call | solution.py:48
  101.7 5.2 %collective-permute-start.8 = (bf16[512,256]{1,0:T(8,128)(2,1)}, bf16[512,256]{1,0:T(8,128)(2,1)S(1)}, u32[]{:S(2)}, u32[]{:S(2)}) collective-permute-start(bf16[512,256]{1,0:T(8,128)(2,1)} %get-tuple-element.103.refs_0_.refs_4_), channel_id=1, source_target_pairs={{0,8},{4,12},{1,9},{5,13},{2,10},{6,14},{3,11},{7,15},{16,24},{20,... | collective-permute-start | bytes 786440 | tf_op jit(solution)/shard_map/ppermute | solution.py:104
  114.0 4.7 %attention_forward.1 = (bf16[128,256]{1,0:T(8,128)(2,1)}, bf16[128,256]{1,0:T(8,128)(2,1)}, bf16[128,256]{1,0:T(8,128)(2,1)}, bf16[128,256]{1,0:T(8,128)(2,1)}, ...) custom-call(s32[3]{0:T(128)} %pad_add_fusion.s_ref.refs_0_, bf16[512,256]{1,0:T(8,128)(2,1)} %get-tuple-element.102.q_ref, ...), custom_call_target="tpu_custom_call" | custom-call | flops 2147483648 | bytes 1048576 | tf_op jit(solution)/shard_map/attention_forward/pallas_call | solution.py:319
  118.7 4.1 %collective-permute-start.10 = (bf16[128,256]{1,0:T(8,128)(2,1)}, bf16[128,256]{1,0:T(8,128)(2,1)}, u32[]{:S(2)}, u32[]{:S(2)}) collective-permute-start(bf16[128,256]{1,0:T(8,128)(2,1)} %get-tuple-element.107), channel_id=1, source_target_pairs={{0,1},{1,0},{2,3},{3,2},{4,5},{5,4},{6,7},{7,6},{8,9},{9,8},{10,11... | collective-permute-start | bytes 196616 | tf_op jit(solution)/shard_map/ppermute | solution.py:100
  122.9 3.9 %collective-permute-start.28 = (bf16[128,1024]{1,0:T(8,128)(2,1)}, bf16[128,1024]{1,0:T(8,128)(2,1)}, u32[]{:S(2)}, u32[]{:S(2)}) collective-permute-start(bf16[128,1024]{1,0:T(8,128)(2,1)} %get-tuple-element.115.refs_0_.refs_4_.refs_5_), channel_id=1, source_target_pairs={{0,2},{1,3},{2,0},{3,1},{4,6},{5,7},{6,4},{7,5},{8,10},{9,11},{10,... | collective-permute-start | bytes 786440 | tf_op jit(solution)/shard_map/ppermute | solution.py:100
  130.0 11.6 %collective-permute-done.11.refs_2_ = bf16[128,256]{1,0:T(8,128)(2,1)} collective-permute-done((bf16[128,256]{1,0:T(8,128)(2,1)}, bf16[128,256]{1,0:T(8,128)(2,1)}, u32[]{:S(2)}, u32[]{:S(2)}) %collective-permute-start.11) | collective-permute-done | bytes 65568 | tf_op jit(solution)/shard_map/ppermute | solution.py:100
  144.1 4.1 %collective-permute-done.12.refs_3_ = bf16[128,256]{1,0:T(8,128)(2,1)} collective-permute-done((bf16[128,256]{1,0:T(8,128)(2,1)}, bf16[128,256]{1,0:T(8,128)(2,1)}, u32[]{:S(2)}, u32[]{:S(2)}) %collective-permute-start.12) | collective-permute-done | bytes 65568 | tf_op jit(solution)/shard_map/ppermute | solution.py:100
  159.6 5.1 %hidden_back.1.refs_6_ = f32[512,1152]{1,0:T(8,128)} custom-call(bf16[128,1024]{1,0:T(8,128)(2,1)} %get-tuple-element.115.refs_0_.refs_4_.refs_5_, bf16[128,1024]{1,0:T(8,128)(2,1)} %collective-permute-done.27.refs_1_.refs_5_, bf16[128,1024]{1,0:T(8,128)(2,1)} %collective-permute-done.28.refs_2_.refs_6_, ...), custom_call_target="tpu_custom_call" | custom-call | flops 1207959552 | bytes 5898240 | tf_op jit(solution)/shard_map/hidden_back/pallas_call | solution.py:366
  166.8 10.5 %collective-permute-done.21.refs_2_ = bf16[128,1024]{1,0:T(8,128)(2,1)} collective-permute-done((bf16[128,1024]{1,0:T(8,128)(2,1)}, bf16[128,1024]{1,0:T(8,128)(2,1)}, u32[]{:S(2)}, u32[]{:S(2)}) %collective-permute-start.21) | collective-permute-done | bytes 262176 | tf_op jit(solution)/shard_map/ppermute | solution.py:100
  177.3 10.7 %shard_map.222 = (bf16[3,512,1152]{2,1,0:T(8,128)(2,1)}, bf16[128,1024]{1,0:T(8,128)(2,1)}, bf16[128,1024]{1,0:T(8,128)(2,1)}, bf16[128,1024]{1,0:T(8,128)(2,1)}, bf16[128,1024]{1,0:T(8,128)(2,1)}) custom-call(bf16[128,1024]{1,0:T(8,128)(2,1)} %get-tuple-element.113.refs_0_, bf16[128,1024]{1,0:T(8,128)(2,1)} %collective-permute-done.20.refs_1_, ...), custom_call_target="tpu_custom_call" | custom-call | flops 4831838208 | bytes 15073280 | tf_op jit(solution)/shard_map/pallas_call | solution.py:48
  188.0 6.7 %shard_map.223 = bf16[3,512,1152]{2,1,0:T(8,128)(2,1)} custom-call(bf16[128,1024]{1,0:T(8,128)(2,1)} %get-tuple-element.113.refs_0_, bf16[128,1024]{1,0:T(8,128)(2,1)} %collective-permute-done.20.refs_1_, bf16[128,1024]{1,0:T(8,128)(2,1)} %collective-permute-done.21.refs_2_, bf16[128,1024]{1,0:T(8,128)(2,1)} %collective-permute-done.22.refs_3_, ...), custom_call_target="tpu_custom_call" | custom-call | flops 1811939328 | bytes 7077888 | tf_op jit(solution)/shard_map/pallas_call | solution.py:427
  194.8 4.7 %collective-permute-start.30 = (bf16[128,1024]{1,0:T(8,128)(2,1)}, bf16[128,1024]{1,0:T(8,128)(2,1)}, u32[]{:S(2)}, u32[]{:S(2)}) collective-permute-start(bf16[128,1024]{1,0:T(8,128)(2,1)} %get-tuple-element.117), channel_id=1, source_target_pairs={{0,1},{1,0},{2,3},{3,2},{4,5},{5,4},{6,7},{7,6},{8,9},{9,8},{10,11... | collective-permute-start | bytes 786440 | tf_op jit(solution)/shard_map/ppermute | solution.py:100
  201.9 4.4 %ffn_out.1 = (bf16[128,1024]{1,0:T(8,128)(2,1)}, bf16[128,1024]{1,0:T(8,128)(2,1)}, bf16[128,1024]{1,0:T(8,128)(2,1)}, bf16[128,1024]{1,0:T(8,128)(2,1)}) custom-call(bf16[3,512,1152]{2,1,0:T(8,128)(2,1)} %get-tuple-element.125.refs_8_.h_ref, bf16[3,512,1152]{2,1,0:T(8,128)(2,1)} %copy-done, bf16[3,512,1152]{2,1,0:T(8,128)(2,1)} %collective-permute-done.26.refs_5_.wo), custom_call_target="tpu_custom_call" | custom-call | flops 1207959552 | bytes 3538944 | tf_op jit(solution)/shard_map/ffn_out/pallas_call | solution.py:449
  208.1 8.0 %shard_map.224 = (f32[3,128,1152]{2,1,0:T(8,128)}, bf16[3,128,1152]{2,1,0:T(8,128)(2,1)}, bf16[3,128,1152]{2,1,0:T(8,128)(2,1)}, bf16[3,128,1152]{2,1,0:T(8,128)(2,1)}) custom-call(bf16[128,1024]{1,0:T(8,128)(2,1)} %get-tuple-element.113.refs_0_, bf16[128,1024]{1,0:T(8,128)(2,1)} %collective-permute-done.20.refs_1_, ...), custom_call_target="tpu_custom_call" | custom-call | flops 1811939328 | bytes 7077888 | tf_op jit(solution)/shard_map/pallas_call | solution.py:427
  216.1 5.0 %collective-permute-done.31.refs_2_ = bf16[128,1024]{1,0:T(8,128)(2,1)} collective-permute-done((bf16[128,1024]{1,0:T(8,128)(2,1)}, bf16[128,1024]{1,0:T(8,128)(2,1)}, u32[]{:S(2)}, u32[]{:S(2)}) %collective-permute-start.31) | collective-permute-done | bytes 262176 | tf_op jit(solution)/shard_map/ppermute | solution.py:100
  221.1 3.5 shard_map.225
  224.7 5.4 %collective-permute-start.34 = (bf16[128,256]{1,0:T(8,128)(2,1)}, bf16[128,256]{1,0:T(8,128)(2,1)S(1)}, u32[]{:S(2)}, u32[]{:S(2)}) collective-permute-start(bf16[128,256]{1,0:T(8,128)(2,1)} %get-tuple-element.136), channel_id=1, source_target_pairs={{0,1},{1,0},{2,3},{3,2},{4,5},{5,4},{6,7},{7,6},{8,9},{9,8},{10,11... | collective-permute-start | bytes 196616 | tf_op jit(solution)/shard_map/ppermute | solution.py:100
  232.6 5.0 %collective-permute-done.35.refs_2_ = bf16[128,256]{1,0:T(8,128)(2,1)S(1)} collective-permute-done((bf16[128,256]{1,0:T(8,128)(2,1)}, bf16[128,256]{1,0:T(8,128)(2,1)S(1)}, u32[]{:S(2)}, u32[]{:S(2)}) %collective-permute-start.35) | collective-permute-done | bytes 65568 | tf_op jit(solution)/shard_map/ppermute | solution.py:100
  238.2 7.2 %attention_backward.1 = (f32[512,256]{1,0:T(8,128)}, bf16[2,512,256]{2,1,0:T(8,128)(2,1)}, bf16[2,512,256]{2,1,0:T(8,128)(2,1)}) custom-call(s32[3]{0:T(128)} %pad_add_fusion.s_ref.refs_0_, bf16[512,256]{1,0:T(8,128)(2,1)} %get-tuple-element.102.q_ref, bf16[512,256]{1,0:T(8,128)(2,1)} %get-tuple-element.104.a_ref, f32[4,1,512]{2,1,0:T(1,128)} %get-tuple-element.105.l_ref, ...), custom_call_target="tpu_custom_call" | custom-call | flops 5368709120 | bytes 2097152 | tf_op jit(solution)/shard_map/attention_backward/pallas_call | solution.py:586
  255.9 16.6 %collective-permute-done.38.refs_0_ = bf16[512,256]{1,0:T(8,128)(2,1)S(1)} collective-permute-done((bf16[512,256]{1,0:T(8,128)(2,1)S(1)}, bf16[512,256]{1,0:T(8,128)(2,1)S(1)}, u32[]{:S(2)}, u32[]{:S(2)}) %collective-permute-start.38) | collective-permute-done | bytes 262176 | tf_op jit(solution)/shard_map/ppermute | solution.py:104
  273.2 6.2 %shard_map.226 = (bf16[128,1024]{1,0:T(8,128)(2,1)}, bf16[128,1024]{1,0:T(8,128)(2,1)}, bf16[128,1024]{1,0:T(8,128)(2,1)}, bf16[128,1024]{1,0:T(8,128)(2,1)}, bf...) custom-call(s32[3]{0:T(128)} %pad_add_fusion.s_ref.refs_0_, f32[512,256]{1,0:T(8,128)} %get-tuple-element.139.dq, ...), custom_call_target="tpu_custom_call" | custom-call | flops 536870912 | bytes 7628812 | tf_op jit(solution)/shard_map/pallas_call | solution.py:48
  283.1 8.4 %collective-permute-start.50 = (bf16[3,128,1152]{2,1,0:T(8,128)(2,1)}, bf16[3,128,1152]{2,1,0:T(8,128)(2,1)}, u32[]{:S(2)}, u32[]{:S(2)}) collective-permute-start(bf16[3,128,1152]{2,1,0:T(8,128)(2,1)} %get-tuple-element.153), channel_id=1, source_target_pairs={{0,24},{4,28},{8,16},{12,20},{16,8},{20,12},{24,0},{28,4},{1,25},{... | collective-permute-start | bytes 2654216 | tf_op jit(solution)/shard_map/ppermute | solution.py:97
  297.2 17.3 %collective-permute-done.43 = f32[24,128]{1,0:T(8,128)S(1)} collective-permute-done((f32[24,128]{1,0:T(8,128)S(1)}, f32[24,128]{1,0:T(8,128)S(1)}, u32[]{:S(2)}, u32[]{:S(2)}) %collective-permute-start.43) | collective-permute-done | bytes 12320 | tf_op jit(solution)/shard_map/ppermute | solution.py:97
  320.1 7.6 %collective-permute-done.53.refs_1_ = bf16[1,128,1024]{2,1,0:T(8,128)(2,1)S(1)} collective-permute-done((bf16[1,128,1024]{2,1,0:T(8,128)(2,1)}, bf16[1,128,1024]{2,1,0:T(8,128)(2,1)S(1)}, u32[]{:S(2)}, u32[]{:S(2)}) %collective-permute-start.53) | collective-permute-done | bytes 262176 | tf_op jit(solution)/shard_map/ppermute | solution.py:97
  330.2 6.3 %collective-permute-done.54.refs_2_ = bf16[1,128,1024]{2,1,0:T(8,128)(2,1)S(1)} collective-permute-done((bf16[1,128,1024]{2,1,0:T(8,128)(2,1)}, bf16[1,128,1024]{2,1,0:T(8,128)(2,1)S(1)}, u32[]{:S(2)}, u32[]{:S(2)}) %collective-permute-start.54) | collective-permute-done | bytes 262176 | tf_op jit(solution)/shard_map/ppermute | solution.py:97
  359.9 3.8 shard_map.227
  363.7 5.3 %collective-permute-done.57.refs_3_ = bf16[128,256]{1,0:T(8,128)(2,1)S(1)} collective-permute-done((bf16[128,256]{1,0:T(8,128)(2,1)}, bf16[128,256]{1,0:T(8,128)(2,1)S(1)}, u32[]{:S(2)}, u32[]{:S(2)}) %collective-permute-start.57) | collective-permute-done | bytes 65568 | tf_op jit(solution)/shard_map/ppermute | solution.py:100
  (239 shorter events, 145.9 us)
Async XLA Ops:
  8.0 23.7 %collective-permute-start.23 = (bf16[3,128,1152]{2,1,0:T(8,128)(2,1)}, bf16[3,128,1152]{2,1,0:T(8,128)(2,1)S(1)}, u32[]{:S(2)}, u32[]{:S(2)}) collective-permute-start(bf16[3,128,1152]{2,1,0:T(8,128)(2,1)} %pad_maximum_fusion.1), channel_id=1, source_target_pairs={{0,8},{4,12},{8,0},{12,4},{16,24},{20,28},{24,16},{28,20},{1,9},{5... | collective-permute-start | bytes 2654216 | tf_op jit(solution)/shard_map/ppermute | solution.py:97
  11.0 40.3 %collective-permute-start.24 = (bf16[3,128,1152]{2,1,0:T(8,128)(2,1)}, bf16[3,128,1152]{2,1,0:T(8,128)(2,1)S(1)}, u32[]{:S(2)}, u32[]{:S(2)}) collective-permute-start(bf16[3,128,1152]{2,1,0:T(8,128)(2,1)} %pad_maximum_fusion.1), channel_id=1, source_target_pairs={{0,16},{4,20},{8,24},{12,28},{16,0},{20,4},{24,8},{28,12},{1,17},{... | collective-permute-start | bytes 2654216 | tf_op jit(solution)/shard_map/ppermute | solution.py:97
  12.5 38.9 %collective-permute-start.25 = (bf16[3,128,1152]{2,1,0:T(8,128)(2,1)}, bf16[3,128,1152]{2,1,0:T(8,128)(2,1)S(1)}, u32[]{:S(2)}, u32[]{:S(2)}) collective-permute-start(bf16[3,128,1152]{2,1,0:T(8,128)(2,1)} %pad_maximum_fusion.1), channel_id=1, source_target_pairs={{0,24},{4,28},{8,16},{12,20},{16,8},{20,12},{24,0},{28,4},{1,25},{... | collective-permute-start | bytes 2654216 | tf_op jit(solution)/shard_map/ppermute | solution.py:97
  51.6 108.0 %collective-permute-start.26 = (bf16[3,512,1152]{2,1,0:T(8,128)(2,1)S(1)}, bf16[3,512,1152]{2,1,0:T(8,128)(2,1)}, u32[]{:S(2)}, u32[]{:S(2)}) collective-permute-start(bf16[3,512,1152]{2,1,0:T(8,128)(2,1)S(1)} %constant_dynamic-update-slice_fusion.4.refs_4_.wm), channel_id=1, source_target_pairs={{0,4},{4,0},{8,12},{12,8},{16,20},{20,16},{24,28},{28,24},{1,5},{5... | collective-permute-start | bytes 10616840 | tf_op jit(solution)/shard_map/ppermute | solution.py:97
  70.3 26.3 %collective-permute-start.6 = (bf16[2,512,256]{2,1,0:T(8,128)(2,1)}, bf16[2,512,256]{2,1,0:T(8,128)(2,1)}, u32[]{:S(2)}, u32[]{:S(2)}) collective-permute-start(bf16[2,512,256]{2,1,0:T(8,128)(2,1)} %constant_dynamic-update-slice_fusion.refs_4_.wm), channel_id=1, source_target_pairs={{0,4},{4,0},{8,12},{12,8},{16,20},{20,16},{24,28},{28,24},{1,5},{5... | collective-permute-start | bytes 1572872 | tf_op jit(solution)/shard_map/ppermute | solution.py:97
  74.4 18.4 %collective-permute-start = (bf16[128,1024]{1,0:T(8,128)(2,1)}, bf16[128,1024]{1,0:T(8,128)(2,1)}, u32[]{:S(2)}, u32[]{:S(2)}) collective-permute-start(bf16[128,1024]{1,0:T(8,128)(2,1)} %get-tuple-element.100.refs_0_.refs_1_), channel_id=1, source_target_pairs={{0,1},{1,0},{2,3},{3,2},{4,5},{5,4},{6,7},{7,6},{8,9},{9,8},{10,11... | collective-permute-start | bytes 786440 | tf_op jit(solution)/shard_map/ppermute | solution.py:100
  78.7 17.8 %collective-permute-start.1 = (bf16[128,1024]{1,0:T(8,128)(2,1)}, bf16[128,1024]{1,0:T(8,128)(2,1)}, u32[]{:S(2)}, u32[]{:S(2)}) collective-permute-start(bf16[128,1024]{1,0:T(8,128)(2,1)} %get-tuple-element.100.refs_0_.refs_1_), channel_id=1, source_target_pairs={{0,2},{1,3},{2,0},{3,1},{4,6},{5,7},{6,4},{7,5},{8,10},{9,11},{10,... | collective-permute-start | bytes 786440 | tf_op jit(solution)/shard_map/ppermute | solution.py:100
  80.4 16.2 %collective-permute-start.2 = (bf16[128,1024]{1,0:T(8,128)(2,1)}, bf16[128,1024]{1,0:T(8,128)(2,1)}, u32[]{:S(2)}, u32[]{:S(2)}) collective-permute-start(bf16[128,1024]{1,0:T(8,128)(2,1)} %get-tuple-element.100.refs_0_.refs_1_), channel_id=1, source_target_pairs={{0,3},{1,2},{2,1},{3,0},{4,7},{5,6},{6,5},{7,4},{8,11},{9,10},{10,... | collective-permute-start | bytes 786440 | tf_op jit(solution)/shard_map/ppermute | solution.py:100
  92.8 57.7 %collective-permute-start.19 = (bf16[1,512,1024]{2,1,0:T(8,128)(2,1)}, bf16[1,512,1024]{2,1,0:T(8,128)(2,1)}, u32[]{:S(2)}, u32[]{:S(2)}) collective-permute-start(bf16[1,512,1024]{2,1,0:T(8,128)(2,1)} %pad_maximum_fusion.refs_4_.refs_7_), channel_id=1, source_target_pairs={{0,4},{4,0},{8,12},{12,8},{16,20},{20,16},{24,28},{28,24},{1,5},{5... | collective-permute-start | bytes 3145736 | tf_op jit(solution)/shard_map/ppermute | solution.py:97
  122.8 31.2 %collective-permute-start.27 = (bf16[128,1024]{1,0:T(8,128)(2,1)}, bf16[128,1024]{1,0:T(8,128)(2,1)}, u32[]{:S(2)}, u32[]{:S(2)}) collective-permute-start(bf16[128,1024]{1,0:T(8,128)(2,1)} %get-tuple-element.115.refs_0_.refs_4_.refs_5_), channel_id=1, source_target_pairs={{0,1},{1,0},{2,3},{3,2},{4,5},{5,4},{6,7},{7,6},{8,9},{9,8},{10,11... | collective-permute-start | bytes 786440 | tf_op jit(solution)/shard_map/ppermute | solution.py:100
  122.9 33.1 %collective-permute-start.28 = (bf16[128,1024]{1,0:T(8,128)(2,1)}, bf16[128,1024]{1,0:T(8,128)(2,1)}, u32[]{:S(2)}, u32[]{:S(2)}) collective-permute-start(bf16[128,1024]{1,0:T(8,128)(2,1)} %get-tuple-element.115.refs_0_.refs_4_.refs_5_), channel_id=1, source_target_pairs={{0,2},{1,3},{2,0},{3,1},{4,6},{5,7},{6,4},{7,5},{8,10},{9,11},{10,... | collective-permute-start | bytes 786440 | tf_op jit(solution)/shard_map/ppermute | solution.py:100
  126.8 14.9 %collective-permute-start.11 = (bf16[128,256]{1,0:T(8,128)(2,1)}, bf16[128,256]{1,0:T(8,128)(2,1)}, u32[]{:S(2)}, u32[]{:S(2)}) collective-permute-start(bf16[128,256]{1,0:T(8,128)(2,1)} %get-tuple-element.108), channel_id=1, source_target_pairs={{0,2},{1,3},{2,0},{3,1},{4,6},{5,7},{6,4},{7,5},{8,10},{9,11},{10,... | collective-permute-start | bytes 196616 | tf_op jit(solution)/shard_map/ppermute | solution.py:100
  154.0 23.3 %collective-permute-start.21 = (bf16[128,1024]{1,0:T(8,128)(2,1)}, bf16[128,1024]{1,0:T(8,128)(2,1)}, u32[]{:S(2)}, u32[]{:S(2)}) collective-permute-start(bf16[128,1024]{1,0:T(8,128)(2,1)} %get-tuple-element.113.refs_0_), channel_id=1, source_target_pairs={{0,2},{1,3},{2,0},{3,1},{4,6},{5,7},{6,4},{7,5},{8,10},{9,11},{10,... | collective-permute-start | bytes 786440 | tf_op jit(solution)/shard_map/ppermute | solution.py:100
  156.0 21.3 %collective-permute-start.22 = (bf16[128,1024]{1,0:T(8,128)(2,1)}, bf16[128,1024]{1,0:T(8,128)(2,1)}, u32[]{:S(2)}, u32[]{:S(2)}) collective-permute-start(bf16[128,1024]{1,0:T(8,128)(2,1)} %get-tuple-element.113.refs_0_), channel_id=1, source_target_pairs={{0,3},{1,2},{2,1},{3,0},{4,7},{5,6},{6,5},{7,4},{8,11},{9,10},{10,... | collective-permute-start | bytes 786440 | tf_op jit(solution)/shard_map/ppermute | solution.py:100
  194.8 21.4 %collective-permute-start.30 = (bf16[128,1024]{1,0:T(8,128)(2,1)}, bf16[128,1024]{1,0:T(8,128)(2,1)}, u32[]{:S(2)}, u32[]{:S(2)}) collective-permute-start(bf16[128,1024]{1,0:T(8,128)(2,1)} %get-tuple-element.117), channel_id=1, source_target_pairs={{0,1},{1,0},{2,3},{3,2},{4,5},{5,4},{6,7},{7,6},{8,9},{9,8},{10,11... | collective-permute-start | bytes 786440 | tf_op jit(solution)/shard_map/ppermute | solution.py:100
  199.4 21.7 %collective-permute-start.31 = (bf16[128,1024]{1,0:T(8,128)(2,1)}, bf16[128,1024]{1,0:T(8,128)(2,1)}, u32[]{:S(2)}, u32[]{:S(2)}) collective-permute-start(bf16[128,1024]{1,0:T(8,128)(2,1)} %get-tuple-element.118), channel_id=1, source_target_pairs={{0,2},{1,3},{2,0},{3,1},{4,6},{5,7},{6,4},{7,5},{8,10},{9,11},{10,... | collective-permute-start | bytes 786440 | tf_op jit(solution)/shard_map/ppermute | solution.py:100
  199.6 21.5 %collective-permute-start.32 = (bf16[128,1024]{1,0:T(8,128)(2,1)}, bf16[128,1024]{1,0:T(8,128)(2,1)}, u32[]{:S(2)}, u32[]{:S(2)}) collective-permute-start(bf16[128,1024]{1,0:T(8,128)(2,1)} %get-tuple-element.119), channel_id=1, source_target_pairs={{0,3},{1,2},{2,1},{3,0},{4,7},{5,6},{6,5},{7,4},{8,11},{9,10},{10,... | collective-permute-start | bytes 786440 | tf_op jit(solution)/shard_map/ppermute | solution.py:100
  248.3 44.0 %collective-permute-start.51 = (bf16[1,512,1024]{2,1,0:T(8,128)(2,1)}, bf16[1,512,1024]{2,1,0:T(8,128)(2,1)S(1)}, u32[]{:S(2)}, u32[]{:S(2)}) collective-permute-start(bf16[1,512,1024]{2,1,0:T(8,128)(2,1)} %shard_map.228), channel_id=1, source_target_pairs={{0,4},{4,0},{8,12},{12,8},{16,20},{20,16},{24,28},{28,24},{1,5},{5... | collective-permute-start | bytes 3145736 | tf_op jit(solution)/shard_map/ppermute | solution.py:97
  249.6 22.9 %collective-permute-start.38 = (bf16[512,256]{1,0:T(8,128)(2,1)S(1)}, bf16[512,256]{1,0:T(8,128)(2,1)S(1)}, u32[]{:S(2)}, u32[]{:S(2)}) collective-permute-start(bf16[512,256]{1,0:T(8,128)(2,1)S(1)} %fusion), channel_id=1, source_target_pairs={{8,0},{12,4},{9,1},{13,5},{10,2},{14,6},{11,3},{15,7},{24,16},{28,... | collective-permute-start | bytes 786440 | tf_op jit(solution)/shard_map/ppermute | solution.py:104
  250.9 28.6 %collective-permute-start.62 = (bf16[128,1024]{1,0:T(8,128)(2,1)}, bf16[128,1024]{1,0:T(8,128)(2,1)S(1)}, u32[]{:S(2)}, u32[]{:S(2)}) collective-permute-start(bf16[128,1024]{1,0:T(8,128)(2,1)} %get-tuple-element.171), channel_id=1, source_target_pairs={{0,1},{1,0},{2,3},{3,2},{4,5},{5,4},{6,7},{7,6},{8,9},{9,8},{10,11... | collective-permute-start | bytes 786440 | tf_op jit(solution)/shard_map/ppermute | solution.py:100
  253.5 26.7 %collective-permute-start.63 = (bf16[128,1024]{1,0:T(8,128)(2,1)S(1)}, bf16[128,1024]{1,0:T(8,128)(2,1)}, u32[]{:S(2)}, u32[]{:S(2)}) collective-permute-start(bf16[128,1024]{1,0:T(8,128)(2,1)S(1)} %copy-done.32), channel_id=1, source_target_pairs={{0,2},{1,3},{2,0},{3,1},{4,6},{5,7},{6,4},{7,5},{8,10},{9,11},{10,... | collective-permute-start | bytes 786440 | tf_op jit(solution)/shard_map/ppermute | solution.py:100
  253.7 42.4 %collective-permute-start.64 = (bf16[128,1024]{1,0:T(8,128)(2,1)}, bf16[128,1024]{1,0:T(8,128)(2,1)}, u32[]{:S(2)}, u32[]{:S(2)}) collective-permute-start(bf16[128,1024]{1,0:T(8,128)(2,1)} %get-tuple-element.173), channel_id=1, source_target_pairs={{0,3},{1,2},{2,1},{3,0},{4,7},{5,6},{6,5},{7,4},{8,11},{9,10},{10,... | collective-permute-start | bytes 786440 | tf_op jit(solution)/shard_map/ppermute | solution.py:100
  272.5 67.4 %collective-permute-start.48 = (bf16[3,128,1152]{2,1,0:T(8,128)(2,1)}, bf16[3,128,1152]{2,1,0:T(8,128)(2,1)S(1)}, u32[]{:S(2)}, u32[]{:S(2)}) collective-permute-start(bf16[3,128,1152]{2,1,0:T(8,128)(2,1)} %get-tuple-element.151), channel_id=1, source_target_pairs={{0,8},{4,12},{8,0},{12,4},{16,24},{20,28},{24,16},{28,20},{1,9},{5... | collective-permute-start | bytes 2654216 | tf_op jit(solution)/shard_map/ppermute | solution.py:97
  280.2 62.9 %collective-permute-start.49 = (bf16[3,128,1152]{2,1,0:T(8,128)(2,1)}, bf16[3,128,1152]{2,1,0:T(8,128)(2,1)S(1)}, u32[]{:S(2)}, u32[]{:S(2)}) collective-permute-start(bf16[3,128,1152]{2,1,0:T(8,128)(2,1)} %get-tuple-element.152), channel_id=1, source_target_pairs={{0,16},{4,20},{8,24},{12,28},{16,0},{20,4},{24,8},{28,12},{1,17},{... | collective-permute-start | bytes 2654216 | tf_op jit(solution)/shard_map/ppermute | solution.py:97
  283.1 62.0 %collective-permute-start.50 = (bf16[3,128,1152]{2,1,0:T(8,128)(2,1)}, bf16[3,128,1152]{2,1,0:T(8,128)(2,1)}, u32[]{:S(2)}, u32[]{:S(2)}) collective-permute-start(bf16[3,128,1152]{2,1,0:T(8,128)(2,1)} %get-tuple-element.153), channel_id=1, source_target_pairs={{0,24},{4,28},{8,16},{12,20},{16,8},{20,12},{24,0},{28,4},{1,25},{... | collective-permute-start | bytes 2654216 | tf_op jit(solution)/shard_map/ppermute | solution.py:97
  292.2 22.3 %collective-permute-start.43 = (f32[24,128]{1,0:T(8,128)S(1)}, f32[24,128]{1,0:T(8,128)S(1)}, u32[]{:S(2)}, u32[]{:S(2)}) collective-permute-start(f32[24,128]{1,0:T(8,128)S(1)} %add.56), channel_id=1, source_target_pairs={{0,8},{4,12},{8,0},{12,4},{16,24},{20,28},{24,16},{28,20},{1,9},{5... | collective-permute-start | bytes 36872 | tf_op jit(solution)/shard_map/ppermute | solution.py:97
  296.1 24.0 %collective-permute-start.52 = (bf16[1,128,1024]{2,1,0:T(8,128)(2,1)}, bf16[1,128,1024]{2,1,0:T(8,128)(2,1)S(1)}, u32[]{:S(2)}, u32[]{:S(2)}) collective-permute-start(bf16[1,128,1024]{2,1,0:T(8,128)(2,1)} %get-tuple-element.157), channel_id=1, source_target_pairs={{0,8},{4,12},{8,0},{12,4},{16,24},{20,28},{24,16},{28,20},{1,9},{5... | collective-permute-start | bytes 786440 | tf_op jit(solution)/shard_map/ppermute | solution.py:97
  320.0 25.6 %collective-permute-start.58 = (bf16[2,512,256]{2,1,0:T(8,128)(2,1)}, bf16[2,512,256]{2,1,0:T(8,128)(2,1)S(1)}, u32[]{:S(2)}, u32[]{:S(2)}) collective-permute-start(bf16[2,512,256]{2,1,0:T(8,128)(2,1)} %shard_map.232), channel_id=1, source_target_pairs={{0,4},{4,0},{8,12},{12,8},{16,20},{20,16},{24,28},{28,24},{1,5},{5... | collective-permute-start | bytes 1572872 | tf_op jit(solution)/shard_map/ppermute | solution.py:97
  341.9 14.8 %collective-permute-start.56 = (bf16[128,256]{1,0:T(8,128)(2,1)}, bf16[128,256]{1,0:T(8,128)(2,1)S(1)}, u32[]{:S(2)}, u32[]{:S(2)}) collective-permute-start(bf16[128,256]{1,0:T(8,128)(2,1)} %get-tuple-element.162), channel_id=1, source_target_pairs={{0,2},{1,3},{2,0},{3,1},{4,6},{5,7},{6,4},{7,5},{8,10},{9,11},{10,... | collective-permute-start | bytes 196616 | tf_op jit(solution)/shard_map/ppermute | solution.py:100
  350.3 28.2 %collective-permute-start.39 = (bf16[128,1024]{1,0:T(8,128)(2,1)}, bf16[128,1024]{1,0:T(8,128)(2,1)S(1)}, u32[]{:S(2)}, u32[]{:S(2)}) collective-permute-start(bf16[128,1024]{1,0:T(8,128)(2,1)} %get-tuple-element.146), channel_id=1, source_target_pairs={{0,1},{1,0},{2,3},{3,2},{4,5},{5,4},{6,7},{7,6},{8,9},{9,8},{10,11... | collective-permute-start | bytes 786440 | tf_op jit(solution)/shard_map/ppermute | solution.py:100
  351.4 27.1 %collective-permute-start.40 = (bf16[128,1024]{1,0:T(8,128)(2,1)}, bf16[128,1024]{1,0:T(8,128)(2,1)S(1)}, u32[]{:S(2)}, u32[]{:S(2)}) collective-permute-start(bf16[128,1024]{1,0:T(8,128)(2,1)} %get-tuple-element.147), channel_id=1, source_target_pairs={{0,2},{1,3},{2,0},{3,1},{4,6},{5,7},{6,4},{7,5},{8,10},{9,11},{10,... | collective-permute-start | bytes 786440 | tf_op jit(solution)/shard_map/ppermute | solution.py:100
  352.9 25.6 %collective-permute-start.41 = (bf16[128,1024]{1,0:T(8,128)(2,1)}, bf16[128,1024]{1,0:T(8,128)(2,1)S(1)}, u32[]{:S(2)}, u32[]{:S(2)}) collective-permute-start(bf16[128,1024]{1,0:T(8,128)(2,1)} %get-tuple-element.148), channel_id=1, source_target_pairs={{0,3},{1,2},{2,1},{3,0},{4,7},{5,6},{6,5},{7,4},{8,11},{9,10},{10,... | collective-permute-start | bytes 786440 | tf_op jit(solution)/shard_map/ppermute | solution.py:100
  (72 other events, 779.7 us)

commit v7 on v6

--- a/solution.py
+++ b/solution.py
@@ -662,29 +662,74 @@
     )
     gna_pieces = spread_column(gna_slots)
 
+    G = 2 * N + 8
+    X = -(-G // 16) * 16
+    gain_pieces = gather_column(packed)
+
+    def put_gains(ref, at, gains):
+        high = gains.astype(bf16)
+        low = (gains - high.astype(f32)).astype(bf16)
+        for k, part in enumerate((high, low)):
+            ref[k, at : at + X] = jnp.zeros((X, C), bf16)
+            ref[k, at : at + G, :blk] = part
+
+    def read_gains(ref, at):
+        return sum(ref[k, at : at + G, :blk].astype(f32) for k in range(2))
+
     def proj_body(cols, *refs):
-        b_ref, *rest = refs[NT:]
+        gains = sum(ref[...] for ref in refs[NT : 2 * NT])
+        b_ref, *rest = refs[2 * NT :]
         rt = jnp.concatenate([ref[:, cols] for ref in refs[:NT]], axis=0).T
         full = mm(rt, b_ref[...])
+        if len(rest) == 1:
+            for k in range(2):
+                rest[0][k, :H] = full[:, k * C : (k + 1) * C].astype(bf16)
+            put_gains(rest[0], H, gains)
+            return
+        got, total_gains, own, *sends = rest
+        gains = gains + read_gains(got, H)
+        total_gains[...] = gains
         for k in range(2):
-            part = full[:, k * C : (k + 1) * C]
-            if len(rest) == 1:
-                rest[0][k] = part.astype(bf16)
-            else:
-                share_out(rest[1:], part + rest[0][k].astype(f32), k)
-
-    def half_proj(cols, got):
+            part = full[:, k * C : (k + 1) * C] + got[k, :H].astype(f32)
+            own[k] = part[:blk]
+            for i, ref in enumerate(sends):
+                ref[k, :blk] = part[(i + 1) * blk : (i + 2) * blk].astype(bf16)
+        for ref in sends:
+            put_gains(ref, blk, gains)
+
+    def half_proj(cols, outs, got):
         return whole_call(
             functools.partial(proj_body, cols),
-            share_shapes(2, C) if got else [sds((2, H, C), bf16)],
-            (*first_pieces, both16, *got),
+            outs,
+            (*first_pieces, *gain_pieces, both16, *got),
             2 * B * W * C,
             scalars=False,
         )
 
-    (proj_o,) = half_proj(slice(H, W), [])
-    att_own, *att_sends = half_proj(slice(0, H), [plane(proj_o, 1)])
+    (proj_o,) = half_proj(slice(H, W), [sds((2, H + X, C), bf16)], [])
+    plane_gains, att_own, *att_sends = half_proj(
+        slice(0, H),
+        [sds((G, blk), f32), sds((2, blk, C), f32)] + [sds((2, blk + X, C), bf16)] * (N // 2 - 1),
+        [plane(proj_o, 1)],
+    )
     att_got = [plane(v, 2 * (i + 1)) for i, v in enumerate(att_sends)]
+
+    def att_close_body(gains, own, *refs):
+        parts, (out_q, out_p, out_g) = refs[: len(att_got)], refs[len(att_got) :]
+        for k, ref in enumerate((out_q, out_p)):
+            total = own[k]
+            for p in parts:
+                total = total + p[k, :blk].astype(f32)
+            ref[...] = total
+        out_g[...] = gains[...] + sum(read_gains(p, blk) for p in parts)
+
+    grad_query, grad_pairs, packed = whole_call(
+        att_close_body,
+        [sds((blk, C), f32)] * 2 + [sds((G, blk), f32)],
+        (plane_gains, att_own, *att_got),
+        blk * C * 8,
+        scalars=False,
+    )
 
     def out_sum_body(first, *refs):
         parts, outs = refs[: len(out_got)], refs[len(out_got) :]
@@ -729,14 +774,7 @@
         block_body, [sds((R, W), bf16)], (where, *ffn_pieces, resid), R * W * 8
     )
 
-    bit = 1
-    while bit < N:
-        packed = packed + plane(packed, bit)
-        bit *= 2
-    packed = sum(gather_column(packed))
-
     grad_gate, grad_up, grad_down = close_sum(ffn_own, ffn_got, 1)
-    grad_query, grad_pairs = close_sum(att_own, att_got, 0)
 
     def end_body(*refs):
         s_ref, rest = refs[0], refs[1:]

time: 389 us -> 413 us (1.062)
  waiting for transfers between devices: 150 us -> 166 us
  starting transfers between devices: 105 us -> 112 us
    ppermute x33, waiting for transfers between devices: 49.5 us -> 73 us  [column(): return lax.ppermute(v, 'tp', [(i, i ^ mask) for i in range(NT)])]
    ppermute x4, waiting for transfers between devices: 19.5 us -> 3.63 us  [along(): return lax.ppermute(v, 'ctx', pairs)]
    ppermute x27 -> x24, waiting for transfers between devices: 80.9 us -> 87.3 us  [plane(): return lax.ppermute(v, ('dp', 'ctx'), [(i, i ^ mask) for i in range(N)])]
    ppermute x33, starting transfers between devices: 62.2 us -> 66.4 us  [column(): return lax.ppermute(v, 'tp', [(i, i ^ mask) for i in range(NT)])]
    ppermute x27 -> x24, starting transfers between devices: 33.3 us -> 35.9 us  [plane(): return lax.ppermute(v, ('dp', 'ctx'), [(i, i ^ mask) for i in range(N)])]
    unnamed x85 -> x79, local copies, waits for them, and re-layouts: 13.4 us -> 14 us
  transfers between devices with their start and end apart: 65 -> 62, of which waited for: 21 -> 22; matrix products, arithmetic and copies ran while one was open for 6% -> 5% of each run, Pallas kernels for 15% -> 16%
where the time goes in v7:
time: 413 us; the launch traced here: 407 us
  waiting for transfers between devices  166 us (40%)
  starting transfers between devices  112 us (27%)
  Pallas kernels  91.6 us (22%)
  local copies, waits for them, and re-layouts  26 us (6%)
  other arithmetic  10.7 us (3%)
    ppermute x24, waiting for transfers between devices, plane(): return lax.ppermute(v, ('dp', 'ctx'), [(i, i ^ mask) for i in range(N)])  87.3 us
    ppermute x33, waiting for transfers between devices, column(): return lax.ppermute(v, 'tp', [(i, i ^ mask) for i in range(NT)])  73 us
    ppermute x33, starting transfers between devices, column(): return lax.ppermute(v, 'tp', [(i, i ^ mask) for i in range(NT)])  66.4 us
    pallas_call x16, Pallas kernels, whole_call(): pl.pallas_call(body, out_shape=list(outs), in_specs=specs, out_specs=[VM]...  55.6 us
    ppermute x24, starting transfers between devices, plane(): return lax.ppermute(v, ('dp', 'ctx'), [(i, i ^ mask) for i in range(N)])  35.9 us
    pallas_call x2, Pallas kernels, half_weights(): pl.pallas_call(functools.partial(dw_body, cols), grid=(3,), out_shape=out...  14.7 us
    unnamed x79, local copies, waits for them, and re-layouts  14 us
    ppermute x4, starting transfers between devices, along(): return lax.ppermute(v, 'ctx', pairs)  8.62 us
  transfers between devices with their start and end apart: 62, of which 22 were waited for; matrix products, arithmetic and copies ran while one was open for 5% of the time, Pallas kernels for 16%

profile of v7, /device:TPU:0, one launch (start us, length us, event | category | flops | bytes accessed | tf_op | source)
XLA Modules:
  0.0 406.6 jit_solution(189885223845981490)
XLA Ops:
  13.8 17.9 %collective-permute-done.23 = bf16[3,128,1152]{2,1,0:T(8,128)(2,1)S(1)} collective-permute-done((bf16[3,128,1152]{2,1,0:T(8,128)(2,1)}, bf16[3,128,1152]{2,1,0:T(8,128)(2,1)S(1)}, u32[]{:S(2)}, u32[]{:S(2)}) %collective-permute-start.23) | collective-permute-done | bytes 884768 | tf_op jit(solution)/shard_map/ppermute | solution.py:97
  31.8 19.4 %collective-permute-done.24 = bf16[3,128,1152]{2,1,0:T(8,128)(2,1)S(1)} collective-permute-done((bf16[3,128,1152]{2,1,0:T(8,128)(2,1)}, bf16[3,128,1152]{2,1,0:T(8,128)(2,1)S(1)}, u32[]{:S(2)}, u32[]{:S(2)}) %collective-permute-start.24) | collective-permute-done | bytes 884768 | tf_op jit(solution)/shard_map/ppermute | solution.py:97
  70.3 4.1 %collective-permute-done.16 = bf16[1,128,1024]{2,1,0:T(8,128)(2,1)S(1)} collective-permute-done((bf16[1,128,1024]{2,1,0:T(8,128)(2,1)S(1)}, bf16[1,128,1024]{2,1,0:T(8,128)(2,1)S(1)}, u32[]{:S(2)}, u32[]{:S(2)}) %collective-permute-start.16) | collective-permute-done | bytes 262176 | tf_op jit(solution)/shard_map/ppermute | solution.py:97
  74.8 4.0 collective-permute-done.17
  92.9 3.7 collective-permute-done.1.refs_2_.refs_3_
  97.2 4.5 %shard_map.220 = (bf16[512,256]{1,0:T(8,128)(2,1)}, bf16[512,256]{1,0:T(8,128)(2,1)}, f32[512,256]{1,0:T(8,128)}, f32[512,256]{1,0:T(8,128)}) custom-call(bf16[128,1024]{1,0:T(8,128)(2,1)} %get-tuple-element.102.refs_0_.refs_1_, bf16[128,1024]{1,0:T(8,128)(2,1)} %collective-permute-done.refs_1_.refs_2_, ...), custom_call_target="tpu_custom_call" | custom-call | flops 536870912 | bytes 4720640 | tf_op jit(solution)/shard_map/pallas_call | solution.py:48
  101.7 5.2 %collective-permute-start.8 = (bf16[512,256]{1,0:T(8,128)(2,1)}, bf16[512,256]{1,0:T(8,128)(2,1)S(1)}, u32[]{:S(2)}, u32[]{:S(2)}) collective-permute-start(bf16[512,256]{1,0:T(8,128)(2,1)} %get-tuple-element.105.refs_0_.refs_4_), channel_id=1, source_target_pairs={{0,8},{4,12},{1,9},{5,13},{2,10},{6,14},{3,11},{7,15},{16,24},{20,... | collective-permute-start | bytes 786440 | tf_op jit(solution)/shard_map/ppermute | solution.py:104
  114.0 4.7 %attention_forward.1 = (bf16[128,256]{1,0:T(8,128)(2,1)}, bf16[128,256]{1,0:T(8,128)(2,1)}, bf16[128,256]{1,0:T(8,128)(2,1)}, bf16[128,256]{1,0:T(8,128)(2,1)}, ...) custom-call(s32[3]{0:T(128)} %pad_add_fusion.s_ref.refs_0_, bf16[512,256]{1,0:T(8,128)(2,1)} %get-tuple-element.104.q_ref, ...), custom_call_target="tpu_custom_call" | custom-call | flops 2147483648 | bytes 1048576 | tf_op jit(solution)/shard_map/attention_forward/pallas_call | solution.py:319
  118.8 4.1 %collective-permute-start.10 = (bf16[128,256]{1,0:T(8,128)(2,1)}, bf16[128,256]{1,0:T(8,128)(2,1)}, u32[]{:S(2)}, u32[]{:S(2)}) collective-permute-start(bf16[128,256]{1,0:T(8,128)(2,1)} %get-tuple-element.109), channel_id=1, source_target_pairs={{0,1},{1,0},{2,3},{3,2},{4,5},{5,4},{6,7},{7,6},{8,9},{9,8},{10,11... | collective-permute-start | bytes 196616 | tf_op jit(solution)/shard_map/ppermute | solution.py:100
  122.9 3.9 collective-permute-start.28
  130.1 11.7 %collective-permute-done.11.refs_2_ = bf16[128,256]{1,0:T(8,128)(2,1)} collective-permute-done((bf16[128,256]{1,0:T(8,128)(2,1)}, bf16[128,256]{1,0:T(8,128)(2,1)}, u32[]{:S(2)}, u32[]{:S(2)}) %collective-permute-start.11) | collective-permute-done | bytes 65568 | tf_op jit(solution)/shard_map/ppermute | solution.py:100
  144.1 4.1 %collective-permute-done.12.refs_3_ = bf16[128,256]{1,0:T(8,128)(2,1)} collective-permute-done((bf16[128,256]{1,0:T(8,128)(2,1)}, bf16[128,256]{1,0:T(8,128)(2,1)}, u32[]{:S(2)}, u32[]{:S(2)}) %collective-permute-start.12) | collective-permute-done | bytes 65568 | tf_op jit(solution)/shard_map/ppermute | solution.py:100
  150.6 3.4 shard_map.221
  159.6 4.9 %hidden_back.1.refs_6_ = f32[512,1152]{1,0:T(8,128)} custom-call(bf16[128,1024]{1,0:T(8,128)(2,1)} %get-tuple-element.117.refs_0_.refs_4_.refs_5_, bf16[128,1024]{1,0:T(8,128)(2,1)} %collective-permute-done.27.refs_1_.refs_5_, bf16[128,1024]{1,0:T(8,128)(2,1)} %collective-permute-done.28.refs_2_.refs_6_, ...), custom_call_target="tpu_custom_call" | custom-call | flops 1207959552 | bytes 5898240 | tf_op jit(solution)/shard_map/hidden_back/pallas_call | solution.py:366
  166.8 10.6 %collective-permute-done.21.refs_2_ = bf16[128,1024]{1,0:T(8,128)(2,1)} collective-permute-done((bf16[128,1024]{1,0:T(8,128)(2,1)}, bf16[128,1024]{1,0:T(8,128)(2,1)}, u32[]{:S(2)}, u32[]{:S(2)}) %collective-permute-start.21) | collective-permute-done | bytes 262176 | tf_op jit(solution)/shard_map/ppermute | solution.py:100
  177.3 10.7 %shard_map.222 = (bf16[3,512,1152]{2,1,0:T(8,128)(2,1)}, bf16[128,1024]{1,0:T(8,128)(2,1)}, bf16[128,1024]{1,0:T(8,128)(2,1)}, bf16[128,1024]{1,0:T(8,128)(2,1)}, bf16[128,1024]{1,0:T(8,128)(2,1)}) custom-call(bf16[128,1024]{1,0:T(8,128)(2,1)} %get-tuple-element.115.refs_0_, bf16[128,1024]{1,0:T(8,128)(2,1)} %collective-permute-done.20.refs_1_, ...), custom_call_target="tpu_custom_call" | custom-call | flops 4831838208 | bytes 15073280 | tf_op jit(solution)/shard_map/pallas_call | solution.py:48
  188.1 6.7 %shard_map.223 = bf16[3,512,1152]{2,1,0:T(8,128)(2,1)} custom-call(bf16[128,1024]{1,0:T(8,128)(2,1)} %get-tuple-element.115.refs_0_, bf16[128,1024]{1,0:T(8,128)(2,1)} %collective-permute-done.20.refs_1_, bf16[128,1024]{1,0:T(8,128)(2,1)} %collective-permute-done.21.refs_2_, bf16[128,1024]{1,0:T(8,128)(2,1)} %collective-permute-done.22.refs_3_, ...), custom_call_target="tpu_custom_call" | custom-call | flops 1811939328 | bytes 7077888 | tf_op jit(solution)/shard_map/pallas_call | solution.py:427
  194.7 4.7 %collective-permute-start.30 = (bf16[128,1024]{1,0:T(8,128)(2,1)}, bf16[128,1024]{1,0:T(8,128)(2,1)}, u32[]{:S(2)}, u32[]{:S(2)}) collective-permute-start(bf16[128,1024]{1,0:T(8,128)(2,1)} %get-tuple-element.119), channel_id=1, source_target_pairs={{0,1},{1,0},{2,3},{3,2},{4,5},{5,4},{6,7},{7,6},{8,9},{9,8},{10,11... | collective-permute-start | bytes 786440 | tf_op jit(solution)/shard_map/ppermute | solution.py:100
  201.9 4.4 %ffn_out.1 = (bf16[128,1024]{1,0:T(8,128)(2,1)}, bf16[128,1024]{1,0:T(8,128)(2,1)}, bf16[128,1024]{1,0:T(8,128)(2,1)}, bf16[128,1024]{1,0:T(8,128)(2,1)}) custom-call(bf16[3,512,1152]{2,1,0:T(8,128)(2,1)} %get-tuple-element.127.refs_8_.h_ref, bf16[3,512,1152]{2,1,0:T(8,128)(2,1)} %copy-done, bf16[3,512,1152]{2,1,0:T(8,128)(2,1)} %collective-permute-done.26.refs_5_.wo), custom_call_target="tpu_custom_call" | custom-call | flops 1207959552 | bytes 3538944 | tf_op jit(solution)/shard_map/ffn_out/pallas_call | solution.py:449
  208.0 8.0 %shard_map.224 = (f32[3,128,1152]{2,1,0:T(8,128)}, bf16[3,128,1152]{2,1,0:T(8,128)(2,1)}, bf16[3,128,1152]{2,1,0:T(8,128)(2,1)}, bf16[3,128,1152]{2,1,0:T(8,128)(2,1)}) custom-call(bf16[128,1024]{1,0:T(8,128)(2,1)} %get-tuple-element.115.refs_0_, bf16[128,1024]{1,0:T(8,128)(2,1)} %collective-permute-done.20.refs_1_, ...), custom_call_target="tpu_custom_call" | custom-call | flops 1811939328 | bytes 7077888 | tf_op jit(solution)/shard_map/pallas_call | solution.py:427
  216.0 5.0 %collective-permute-done.31.refs_2_ = bf16[128,1024]{1,0:T(8,128)(2,1)} collective-permute-done((bf16[128,1024]{1,0:T(8,128)(2,1)}, bf16[128,1024]{1,0:T(8,128)(2,1)}, u32[]{:S(2)}, u32[]{:S(2)}) %collective-permute-start.31) | collective-permute-done | bytes 262176 | tf_op jit(solution)/shard_map/ppermute | solution.py:100
  221.1 3.5 shard_map.225
  224.6 5.4 %collective-permute-start.34 = (bf16[128,256]{1,0:T(8,128)(2,1)}, bf16[128,256]{1,0:T(8,128)(2,1)S(1)}, u32[]{:S(2)}, u32[]{:S(2)}) collective-permute-start(bf16[128,256]{1,0:T(8,128)(2,1)} %get-tuple-element.138), channel_id=1, source_target_pairs={{0,1},{1,0},{2,3},{3,2},{4,5},{5,4},{6,7},{7,6},{8,9},{9,8},{10,11... | collective-permute-start | bytes 196616 | tf_op jit(solution)/shard_map/ppermute | solution.py:100
  238.2 7.2 %attention_backward.1 = (f32[512,256]{1,0:T(8,128)}, bf16[2,512,256]{2,1,0:T(8,128)(2,1)}, bf16[2,512,256]{2,1,0:T(8,128)(2,1)}) custom-call(s32[3]{0:T(128)} %pad_add_fusion.s_ref.refs_0_, bf16[512,256]{1,0:T(8,128)(2,1)} %get-tuple-element.104.q_ref, bf16[512,256]{1,0:T(8,128)(2,1)} %get-tuple-element.106.a_ref, f32[4,1,512]{2,1,0:T(1,128)} %get-tuple-element.107.l_ref, ...), custom_call_target="tpu_custom_call" | custom-call | flops 5368709120 | bytes 2097152 | tf_op jit(solution)/shard_map/attention_backward/pallas_call | solution.py:586
  256.6 14.3 %collective-permute-start.53 = (bf16[1,128,1024]{2,1,0:T(8,128)(2,1)}, bf16[1,128,1024]{2,1,0:T(8,128)(2,1)S(1)}, u32[]{:S(2)}, u32[]{:S(2)}) collective-permute-start(bf16[1,128,1024]{2,1,0:T(8,128)(2,1)} %get-tuple-element.166), channel_id=1, source_target_pairs={{0,8},{4,12},{8,0},{12,4},{16,24},{20,28},{24,16},{28,20},{1,9},{5... | collective-permute-start | bytes 786440 | tf_op jit(solution)/shard_map/ppermute | solution.py:97
  272.3 6.1 %shard_map.226 = (bf16[128,1024]{1,0:T(8,128)(2,1)}, bf16[128,1024]{1,0:T(8,128)(2,1)}, bf16[128,1024]{1,0:T(8,128)(2,1)}, bf16[128,1024]{1,0:T(8,128)(2,1)}, bf...) custom-call(s32[3]{0:T(128)} %pad_add_fusion.s_ref.refs_0_, f32[512,256]{1,0:T(8,128)} %get-tuple-element.141.dq, ...), custom_call_target="tpu_custom_call" | custom-call | flops 536870912 | bytes 7628812 | tf_op jit(solution)/shard_map/pallas_call | solution.py:48
  296.9 3.8 collective-permute-done.54.refs_1_
  301.7 38.0 %collective-permute-done.55.refs_2_ = bf16[1,128,1024]{2,1,0:T(8,128)(2,1)S(1)} collective-permute-done((bf16[1,128,1024]{2,1,0:T(8,128)(2,1)}, bf16[1,128,1024]{2,1,0:T(8,128)(2,1)S(1)}, u32[]{:S(2)}, u32[]{:S(2)}) %collective-permute-start.55) | collective-permute-done | bytes 262176 | tf_op jit(solution)/shard_map/ppermute | solution.py:97
  347.3 12.3 %collective-permute-done.60.refs_3_ = bf16[128,1024]{1,0:T(8,128)(2,1)} collective-permute-done((bf16[128,1024]{1,0:T(8,128)(2,1)}, bf16[128,1024]{1,0:T(8,128)(2,1)}, u32[]{:S(2)}, u32[]{:S(2)}) %collective-permute-start.60) | collective-permute-done | bytes 262176 | tf_op jit(solution)/shard_map/ppermute | solution.py:100
  359.6 6.5 %collective-permute-start.57 = (bf16[128,256]{1,0:T(8,128)(2,1)}, bf16[128,256]{1,0:T(8,128)(2,1)}, u32[]{:S(2)}, u32[]{:S(2)}) collective-permute-start(bf16[128,256]{1,0:T(8,128)(2,1)} %get-tuple-element.171), channel_id=1, source_target_pairs={{0,2},{1,3},{2,0},{3,1},{4,6},{5,7},{6,4},{7,5},{8,10},{9,11},{10,... | collective-permute-start | bytes 196616 | tf_op jit(solution)/shard_map/ppermute | solution.py:100
  373.7 15.0 %collective-permute-done.58.refs_3_ = bf16[128,256]{1,0:T(8,128)(2,1)} collective-permute-done((bf16[128,256]{1,0:T(8,128)(2,1)}, bf16[128,256]{1,0:T(8,128)(2,1)}, u32[]{:S(2)}, u32[]{:S(2)}) %collective-permute-start.58) | collective-permute-done | bytes 65568 | tf_op jit(solution)/shard_map/ppermute | solution.py:100
  393.9 3.8 shard_map.230
  (223 shorter events, 143.8 us)
Async XLA Ops:
  8.0 23.7 %collective-permute-start.23 = (bf16[3,128,1152]{2,1,0:T(8,128)(2,1)}, bf16[3,128,1152]{2,1,0:T(8,128)(2,1)S(1)}, u32[]{:S(2)}, u32[]{:S(2)}) collective-permute-start(bf16[3,128,1152]{2,1,0:T(8,128)(2,1)} %pad_maximum_fusion.1), channel_id=1, source_target_pairs={{0,8},{4,12},{8,0},{12,4},{16,24},{20,28},{24,16},{28,20},{1,9},{5... | collective-permute-start | bytes 2654216 | tf_op jit(solution)/shard_map/ppermute | solution.py:97
  11.0 40.3 %collective-permute-start.24 = (bf16[3,128,1152]{2,1,0:T(8,128)(2,1)}, bf16[3,128,1152]{2,1,0:T(8,128)(2,1)S(1)}, u32[]{:S(2)}, u32[]{:S(2)}) collective-permute-start(bf16[3,128,1152]{2,1,0:T(8,128)(2,1)} %pad_maximum_fusion.1), channel_id=1, source_target_pairs={{0,16},{4,20},{8,24},{12,28},{16,0},{20,4},{24,8},{28,12},{1,17},{... | collective-permute-start | bytes 2654216 | tf_op jit(solution)/shard_map/ppermute | solution.py:97
  12.5 38.9 %collective-permute-start.25 = (bf16[3,128,1152]{2,1,0:T(8,128)(2,1)}, bf16[3,128,1152]{2,1,0:T(8,128)(2,1)S(1)}, u32[]{:S(2)}, u32[]{:S(2)}) collective-permute-start(bf16[3,128,1152]{2,1,0:T(8,128)(2,1)} %pad_maximum_fusion.1), channel_id=1, source_target_pairs={{0,24},{4,28},{8,16},{12,20},{16,8},{20,12},{24,0},{28,4},{1,25},{... | collective-permute-start | bytes 2654216 | tf_op jit(solution)/shard_map/ppermute | solution.py:97
  51.6 108.0 %collective-permute-start.26 = (bf16[3,512,1152]{2,1,0:T(8,128)(2,1)S(1)}, bf16[3,512,1152]{2,1,0:T(8,128)(2,1)}, u32[]{:S(2)}, u32[]{:S(2)}) collective-permute-start(bf16[3,512,1152]{2,1,0:T(8,128)(2,1)S(1)} %constant_dynamic-update-slice_fusion.4.refs_4_.wm), channel_id=1, source_target_pairs={{0,4},{4,0},{8,12},{12,8},{16,20},{20,16},{24,28},{28,24},{1,5},{5... | collective-permute-start | bytes 10616840 | tf_op jit(solution)/shard_map/ppermute | solution.py:97
  70.3 26.3 %collective-permute-start.6 = (bf16[2,512,256]{2,1,0:T(8,128)(2,1)}, bf16[2,512,256]{2,1,0:T(8,128)(2,1)}, u32[]{:S(2)}, u32[]{:S(2)}) collective-permute-start(bf16[2,512,256]{2,1,0:T(8,128)(2,1)} %constant_dynamic-update-slice_fusion.refs_4_.wm), channel_id=1, source_target_pairs={{0,4},{4,0},{8,12},{12,8},{16,20},{20,16},{24,28},{28,24},{1,5},{5... | collective-permute-start | bytes 1572872 | tf_op jit(solution)/shard_map/ppermute | solution.py:97
  74.4 18.4 %collective-permute-start = (bf16[128,1024]{1,0:T(8,128)(2,1)}, bf16[128,1024]{1,0:T(8,128)(2,1)}, u32[]{:S(2)}, u32[]{:S(2)}) collective-permute-start(bf16[128,1024]{1,0:T(8,128)(2,1)} %get-tuple-element.102.refs_0_.refs_1_), channel_id=1, source_target_pairs={{0,1},{1,0},{2,3},{3,2},{4,5},{5,4},{6,7},{7,6},{8,9},{9,8},{10,11... | collective-permute-start | bytes 786440 | tf_op jit(solution)/shard_map/ppermute | solution.py:100
  78.7 17.8 %collective-permute-start.1 = (bf16[128,1024]{1,0:T(8,128)(2,1)}, bf16[128,1024]{1,0:T(8,128)(2,1)}, u32[]{:S(2)}, u32[]{:S(2)}) collective-permute-start(bf16[128,1024]{1,0:T(8,128)(2,1)} %get-tuple-element.102.refs_0_.refs_1_), channel_id=1, source_target_pairs={{0,2},{1,3},{2,0},{3,1},{4,6},{5,7},{6,4},{7,5},{8,10},{9,11},{10,... | collective-permute-start | bytes 786440 | tf_op jit(solution)/shard_map/ppermute | solution.py:100
  80.4 16.2 %collective-permute-start.2 = (bf16[128,1024]{1,0:T(8,128)(2,1)}, bf16[128,1024]{1,0:T(8,128)(2,1)}, u32[]{:S(2)}, u32[]{:S(2)}) collective-permute-start(bf16[128,1024]{1,0:T(8,128)(2,1)} %get-tuple-element.102.refs_0_.refs_1_), channel_id=1, source_target_pairs={{0,3},{1,2},{2,1},{3,0},{4,7},{5,6},{6,5},{7,4},{8,11},{9,10},{10,... | collective-permute-start | bytes 786440 | tf_op jit(solution)/shard_map/ppermute | solution.py:100
  92.9 57.7 %collective-permute-start.19 = (bf16[1,512,1024]{2,1,0:T(8,128)(2,1)}, bf16[1,512,1024]{2,1,0:T(8,128)(2,1)}, u32[]{:S(2)}, u32[]{:S(2)}) collective-permute-start(bf16[1,512,1024]{2,1,0:T(8,128)(2,1)} %pad_maximum_fusion.refs_4_.refs_7_), channel_id=1, source_target_pairs={{0,4},{4,0},{8,12},{12,8},{16,20},{20,16},{24,28},{28,24},{1,5},{5... | collective-permute-start | bytes 3145736 | tf_op jit(solution)/shard_map/ppermute | solution.py:97
  122.9 31.2 %collective-permute-start.27 = (bf16[128,1024]{1,0:T(8,128)(2,1)}, bf16[128,1024]{1,0:T(8,128)(2,1)}, u32[]{:S(2)}, u32[]{:S(2)}) collective-permute-start(bf16[128,1024]{1,0:T(8,128)(2,1)} %get-tuple-element.117.refs_0_.refs_4_.refs_5_), channel_id=1, source_target_pairs={{0,1},{1,0},{2,3},{3,2},{4,5},{5,4},{6,7},{7,6},{8,9},{9,8},{10,11... | collective-permute-start | bytes 786440 | tf_op jit(solution)/shard_map/ppermute | solution.py:100
  122.9 33.1 %collective-permute-start.28 = (bf16[128,1024]{1,0:T(8,128)(2,1)}, bf16[128,1024]{1,0:T(8,128)(2,1)}, u32[]{:S(2)}, u32[]{:S(2)}) collective-permute-start(bf16[128,1024]{1,0:T(8,128)(2,1)} %get-tuple-element.117.refs_0_.refs_4_.refs_5_), channel_id=1, source_target_pairs={{0,2},{1,3},{2,0},{3,1},{4,6},{5,7},{6,4},{7,5},{8,10},{9,11},{10,... | collective-permute-start | bytes 786440 | tf_op jit(solution)/shard_map/ppermute | solution.py:100
  154.0 23.3 %collective-permute-start.21 = (bf16[128,1024]{1,0:T(8,128)(2,1)}, bf16[128,1024]{1,0:T(8,128)(2,1)}, u32[]{:S(2)}, u32[]{:S(2)}) collective-permute-start(bf16[128,1024]{1,0:T(8,128)(2,1)} %get-tuple-element.115.refs_0_), channel_id=1, source_target_pairs={{0,2},{1,3},{2,0},{3,1},{4,6},{5,7},{6,4},{7,5},{8,10},{9,11},{10,... | collective-permute-start | bytes 786440 | tf_op jit(solution)/shard_map/ppermute | solution.py:100
  156.0 21.3 %collective-permute-start.22 = (bf16[128,1024]{1,0:T(8,128)(2,1)}, bf16[128,1024]{1,0:T(8,128)(2,1)}, u32[]{:S(2)}, u32[]{:S(2)}) collective-permute-start(bf16[128,1024]{1,0:T(8,128)(2,1)} %get-tuple-element.115.refs_0_), channel_id=1, source_target_pairs={{0,3},{1,2},{2,1},{3,0},{4,7},{5,6},{6,5},{7,4},{8,11},{9,10},{10,... | collective-permute-start | bytes 786440 | tf_op jit(solution)/shard_map/ppermute | solution.py:100
  194.7 21.3 %collective-permute-start.30 = (bf16[128,1024]{1,0:T(8,128)(2,1)}, bf16[128,1024]{1,0:T(8,128)(2,1)}, u32[]{:S(2)}, u32[]{:S(2)}) collective-permute-start(bf16[128,1024]{1,0:T(8,128)(2,1)} %get-tuple-element.119), channel_id=1, source_target_pairs={{0,1},{1,0},{2,3},{3,2},{4,5},{5,4},{6,7},{7,6},{8,9},{9,8},{10,11... | collective-permute-start | bytes 786440 | tf_op jit(solution)/shard_map/ppermute | solution.py:100
  199.4 21.7 %collective-permute-start.31 = (bf16[128,1024]{1,0:T(8,128)(2,1)}, bf16[128,1024]{1,0:T(8,128)(2,1)}, u32[]{:S(2)}, u32[]{:S(2)}) collective-permute-start(bf16[128,1024]{1,0:T(8,128)(2,1)} %get-tuple-element.120), channel_id=1, source_target_pairs={{0,2},{1,3},{2,0},{3,1},{4,6},{5,7},{6,4},{7,5},{8,10},{9,11},{10,... | collective-permute-start | bytes 786440 | tf_op jit(solution)/shard_map/ppermute | solution.py:100
  199.6 21.5 %collective-permute-start.32 = (bf16[128,1024]{1,0:T(8,128)(2,1)}, bf16[128,1024]{1,0:T(8,128)(2,1)}, u32[]{:S(2)}, u32[]{:S(2)}) collective-permute-start(bf16[128,1024]{1,0:T(8,128)(2,1)} %get-tuple-element.121), channel_id=1, source_target_pairs={{0,3},{1,2},{2,1},{3,0},{4,7},{5,6},{6,5},{7,4},{8,11},{9,10},{10,... | collective-permute-start | bytes 786440 | tf_op jit(solution)/shard_map/ppermute | solution.py:100
  235.0 17.8 %collective-permute-start.52 = (bf16[1,512,1024]{2,1,0:T(8,128)(2,1)}, bf16[1,512,1024]{2,1,0:T(8,128)(2,1)S(1)}, u32[]{:S(2)}, u32[]{:S(2)}) collective-permute-start(bf16[1,512,1024]{2,1,0:T(8,128)(2,1)} %shard_map.231), channel_id=1, source_target_pairs={{0,4},{4,0},{8,12},{12,8},{16,20},{20,16},{24,28},{28,24},{1,5},{5... | collective-permute-start | bytes 3145736 | tf_op jit(solution)/shard_map/ppermute | solution.py:97
  249.1 22.6 %collective-permute-start.38 = (bf16[512,256]{1,0:T(8,128)(2,1)S(1)}, bf16[512,256]{1,0:T(8,128)(2,1)S(1)}, u32[]{:S(2)}, u32[]{:S(2)}) collective-permute-start(bf16[512,256]{1,0:T(8,128)(2,1)S(1)} %fusion), channel_id=1, source_target_pairs={{8,0},{12,4},{9,1},{13,5},{10,2},{14,6},{11,3},{15,7},{24,16},{28,... | collective-permute-start | bytes 786440 | tf_op jit(solution)/shard_map/ppermute | solution.py:104
  250.4 43.0 %collective-permute-start.59 = (bf16[128,1024]{1,0:T(8,128)(2,1)S(1)}, bf16[128,1024]{1,0:T(8,128)(2,1)S(1)}, u32[]{:S(2)}, u32[]{:S(2)}) collective-permute-start(bf16[128,1024]{1,0:T(8,128)(2,1)S(1)} %copy-done.31), channel_id=1, source_target_pairs={{0,1},{1,0},{2,3},{3,2},{4,5},{5,4},{6,7},{7,6},{8,9},{9,8},{10,11... | collective-permute-start | bytes 786440 | tf_op jit(solution)/shard_map/ppermute | solution.py:100
  256.6 37.5 %collective-permute-start.53 = (bf16[1,128,1024]{2,1,0:T(8,128)(2,1)}, bf16[1,128,1024]{2,1,0:T(8,128)(2,1)S(1)}, u32[]{:S(2)}, u32[]{:S(2)}) collective-permute-start(bf16[1,128,1024]{2,1,0:T(8,128)(2,1)} %get-tuple-element.166), channel_id=1, source_target_pairs={{0,8},{4,12},{8,0},{12,4},{16,24},{20,28},{24,16},{28,20},{1,9},{5... | collective-permute-start | bytes 786440 | tf_op jit(solution)/shard_map/ppermute | solution.py:97
  290.5 49.9 %collective-permute-start.45 = (bf16[2,544,256]{2,1,0:T(8,128)(2,1)}, bf16[2,544,256]{2,1,0:T(8,128)(2,1)S(1)}, u32[]{:S(2)}, u32[]{:S(2)}) collective-permute-start(bf16[2,544,256]{2,1,0:T(8,128)(2,1)} %shard_map.227), channel_id=1, source_target_pairs={{0,4},{4,0},{8,12},{12,8},{16,20},{20,16},{24,28},{28,24},{1,5},{5... | collective-permute-start | bytes 1671176 | tf_op jit(solution)/shard_map/ppermute | solution.py:97
  293.4 72.8 %collective-permute-start.49 = (bf16[3,128,1152]{2,1,0:T(8,128)(2,1)}, bf16[3,128,1152]{2,1,0:T(8,128)(2,1)S(1)}, u32[]{:S(2)}, u32[]{:S(2)}) collective-permute-start(bf16[3,128,1152]{2,1,0:T(8,128)(2,1)} %get-tuple-element.160), channel_id=1, source_target_pairs={{0,8},{4,12},{8,0},{12,4},{16,24},{20,28},{24,16},{28,20},{1,9},{5... | collective-permute-start | bytes 2654216 | tf_op jit(solution)/shard_map/ppermute | solution.py:97
  293.4 73.4 %collective-permute-start.50 = (bf16[3,128,1152]{2,1,0:T(8,128)(2,1)}, bf16[3,128,1152]{2,1,0:T(8,128)(2,1)S(1)}, u32[]{:S(2)}, u32[]{:S(2)}) collective-permute-start(bf16[3,128,1152]{2,1,0:T(8,128)(2,1)} %get-tuple-element.161), channel_id=1, source_target_pairs={{0,16},{4,20},{8,24},{12,28},{16,0},{20,4},{24,8},{28,12},{1,17},{... | collective-permute-start | bytes 2654216 | tf_op jit(solution)/shard_map/ppermute | solution.py:97
  294.1 72.7 %collective-permute-start.51 = (bf16[3,128,1152]{2,1,0:T(8,128)(2,1)}, bf16[3,128,1152]{2,1,0:T(8,128)(2,1)S(1)}, u32[]{:S(2)}, u32[]{:S(2)}) collective-permute-start(bf16[3,128,1152]{2,1,0:T(8,128)(2,1)} %get-tuple-element.162), channel_id=1, source_target_pairs={{0,24},{4,28},{8,16},{12,20},{16,8},{20,12},{24,0},{28,4},{1,25},{... | collective-permute-start | bytes 2654216 | tf_op jit(solution)/shard_map/ppermute | solution.py:97
  300.7 39.0 %collective-permute-start.55 = (bf16[1,128,1024]{2,1,0:T(8,128)(2,1)}, bf16[1,128,1024]{2,1,0:T(8,128)(2,1)S(1)}, u32[]{:S(2)}, u32[]{:S(2)}) collective-permute-start(bf16[1,128,1024]{2,1,0:T(8,128)(2,1)} %get-tuple-element.168), channel_id=1, source_target_pairs={{0,24},{4,28},{8,16},{12,20},{16,8},{20,12},{24,0},{28,4},{1,25},{... | collective-permute-start | bytes 786440 | tf_op jit(solution)/shard_map/ppermute | solution.py:97
  339.8 19.9 %collective-permute-start.60 = (bf16[128,1024]{1,0:T(8,128)(2,1)}, bf16[128,1024]{1,0:T(8,128)(2,1)}, u32[]{:S(2)}, u32[]{:S(2)}) collective-permute-start(bf16[128,1024]{1,0:T(8,128)(2,1)} %get-tuple-element.176), channel_id=1, source_target_pairs={{0,2},{1,3},{2,0},{3,1},{4,6},{5,7},{6,4},{7,5},{8,10},{9,11},{10,... | collective-permute-start | bytes 786440 | tf_op jit(solution)/shard_map/ppermute | solution.py:100
  340.5 19.2 %collective-permute-start.61 = (bf16[128,1024]{1,0:T(8,128)(2,1)}, bf16[128,1024]{1,0:T(8,128)(2,1)}, u32[]{:S(2)}, u32[]{:S(2)}) collective-permute-start(bf16[128,1024]{1,0:T(8,128)(2,1)} %get-tuple-element.177), channel_id=1, source_target_pairs={{0,3},{1,2},{2,1},{3,0},{4,7},{5,6},{6,5},{7,4},{8,11},{9,10},{10,... | collective-permute-start | bytes 786440 | tf_op jit(solution)/shard_map/ppermute | solution.py:100
  366.2 24.1 %collective-permute-start.46 = (bf16[2,160,256]{2,1,0:T(8,128)(2,1)}, bf16[2,160,256]{2,1,0:T(8,128)(2,1)}, u32[]{:S(2)}, u32[]{:S(2)}) collective-permute-start(bf16[2,160,256]{2,1,0:T(8,128)(2,1)} %get-tuple-element.155), channel_id=1, source_target_pairs={{0,8},{4,12},{8,0},{12,4},{16,24},{20,28},{24,16},{28,20},{1,9},{5... | collective-permute-start | bytes 491528 | tf_op jit(solution)/shard_map/ppermute | solution.py:97
  366.7 34.5 %collective-permute-start.39 = (bf16[128,1024]{1,0:T(8,128)(2,1)}, bf16[128,1024]{1,0:T(8,128)(2,1)S(1)}, u32[]{:S(2)}, u32[]{:S(2)}) collective-permute-start(bf16[128,1024]{1,0:T(8,128)(2,1)} %get-tuple-element.148), channel_id=1, source_target_pairs={{0,1},{1,0},{2,3},{3,2},{4,5},{5,4},{6,7},{7,6},{8,9},{9,8},{10,11... | collective-permute-start | bytes 786440 | tf_op jit(solution)/shard_map/ppermute | solution.py:100
  366.8 34.5 %collective-permute-start.40 = (bf16[128,1024]{1,0:T(8,128)(2,1)}, bf16[128,1024]{1,0:T(8,128)(2,1)S(1)}, u32[]{:S(2)}, u32[]{:S(2)}) collective-permute-start(bf16[128,1024]{1,0:T(8,128)(2,1)} %get-tuple-element.149), channel_id=1, source_target_pairs={{0,2},{1,3},{2,0},{3,1},{4,6},{5,7},{6,4},{7,5},{8,10},{9,11},{10,... | collective-permute-start | bytes 786440 | tf_op jit(solution)/shard_map/ppermute | solution.py:100
  369.3 32.0 %collective-permute-start.41 = (bf16[128,1024]{1,0:T(8,128)(2,1)}, bf16[128,1024]{1,0:T(8,128)(2,1)S(1)}, u32[]{:S(2)}, u32[]{:S(2)}) collective-permute-start(bf16[128,1024]{1,0:T(8,128)(2,1)} %get-tuple-element.150), channel_id=1, source_target_pairs={{0,3},{1,2},{2,1},{3,0},{4,7},{5,6},{6,5},{7,4},{8,11},{9,10},{10,... | collective-permute-start | bytes 786440 | tf_op jit(solution)/shard_map/ppermute | solution.py:100
  371.2 17.5 %collective-permute-start.58 = (bf16[128,256]{1,0:T(8,128)(2,1)}, bf16[128,256]{1,0:T(8,128)(2,1)}, u32[]{:S(2)}, u32[]{:S(2)}) collective-permute-start(bf16[128,256]{1,0:T(8,128)(2,1)} %get-tuple-element.172), channel_id=1, source_target_pairs={{0,3},{1,2},{2,1},{3,0},{4,7},{5,6},{6,5},{7,4},{8,11},{9,10},{10,... | collective-permute-start | bytes 196616 | tf_op jit(solution)/shard_map/ppermute | solution.py:100
  (66 other events, 852.0 us)

commit v8 on v7

--- a/solution.py
+++ b/solution.py
@@ -122,25 +122,30 @@
         shape = (kinds, H * 2 // N, cols)
         return [sds(shape, f32)] + [sds(shape, bf16)] * (N // 2 - 1)
 
-    def close_sum(own, parts, turned):
+    def close_sum(own, parts):
         kinds, m, cols = own.shape
+        part = 384 if cols % 384 == 0 else cols
+        n_parts = len(parts)
 
         def body(first, *refs):
-            parts, outs = refs[: len(parts_in)], refs[len(parts_in) :]
-            for k in range(kinds):
+            for k, out in enumerate(refs[n_parts:]):
                 total = first[k]
-                for p in parts:
+                for p in refs[:n_parts]:
                     total = total + p[k].astype(f32)
-                outs[k][...] = total if k < kinds - turned else total.T
-
-        parts_in = parts
-        return whole_call(
+                out[...] = total if k < kinds - 1 else total.T
+
+        block = pl.BlockSpec((kinds, m, part), lambda i: (0, 0, i))
+        return pl.pallas_call(
             body,
-            [sds((m, cols), f32)] * (kinds - turned) + [sds((cols, m), f32)] * turned,
-            (own, *parts),
-            own.size * N,
-            scalars=False,
-        )
+            grid=(cols // part,),
+            out_shape=[sds((m, cols), f32)] * (kinds - 1) + [sds((cols, m), f32)],
+            in_specs=[block] * (1 + n_parts),
+            out_specs=[pl.BlockSpec((m, part), lambda i: (0, i))] * (kinds - 1)
+            + [pl.BlockSpec((part, m), lambda i: (i, 0))],
+            cost_estimate=pl.CostEstimate(
+                flops=own.size * N, bytes_accessed=own.size * 14, transcendentals=0
+            ),
+        )(own, *parts)
 
     def gather_column(own):
         return [own] + [column(own, k) for k in range(1, NT)]
@@ -161,7 +166,7 @@
 
     own_qkv = jnp.stack([query_weight, key_value_weight])
 
-    def pre_body(s_ref, t_ref, c_ref, g_ref, o_ref, n_ref, t_out, c_out, g_out, ot_out):
+    def pre_body(s_ref, t_ref, c_ref, ga_ref, gf_ref, o_ref, n_ref, t_out, c_out, g_out, ot_out):
         index = s_ref[0]
         for s, mask in enumerate(masks):
             if aligned:
@@ -171,20 +176,23 @@
             dst = slice(s * blk, (s + 1) * blk)
             t_out[:, dst] = t_ref[:, src]
             c_out[:, dst] = c_ref[:, src]
-            g_out[:, dst] = g_ref[:, src]
+            g_out[0:1, dst] = ga_ref[:, src]
+            g_out[1:2, dst] = gf_ref[:, src]
         x = t_out[...].astype(f32)
         inv = lax.rsqrt(jnp.mean(x * x, axis=-1, keepdims=True) + epsilon)
         n_ref[...] = (x * inv * g_out[0:1, :]).astype(bf16)
         ot_out[...] = o_ref[...].T
 
-    gains = jnp.stack([attention_gain, ffn_gain])
-    t_in, c_in, g_in = tokens[0], cotangent[0], gains
+    t_in, c_in = tokens[0], cotangent[0]
+    ga_in, gf_in = attention_gain.reshape(1, W), ffn_gain.reshape(1, W)
     if not aligned:
-        t_in, c_in, g_in = (take_cols(v, me, blk, masks) for v in (t_in, c_in, g_in))
+        t_in, c_in, ga_in, gf_in = (
+            take_cols(v, me, blk, masks) for v in (t_in, c_in, ga_in, gf_in)
+        )
     normed, tok, cot, gain2, own_out = whole_call(
         pre_body,
         [sds((R, W), bf16)] * 3 + [sds((2, W), f32), sds((blk, C), bf16)],
-        (where, t_in, c_in, g_in, output_weight),
+        (where, t_in, c_in, ga_in, gf_in, output_weight),
         R * W * 8,
     )
     first_pieces = gather_column(normed)
@@ -374,6 +382,11 @@
         ),
         name="hidden_back",
     )(*cot_pieces, ffn_m, ffn_o)
+
+    lse_out = jnp.take(
+        lse.reshape(QH, NT, R), z ^ jnp.arange(NT, dtype=jnp.int32), axis=1
+    ).reshape(1, QH, B)
+    grad_mid, lse_out = lax.optimization_barrier((grad_mid, lse_out))
 
     def ffn_body(*refs):
         wm, wo, gmid_r, hid = refs[NT : NT + 4]
@@ -715,17 +728,21 @@
     att_got = [plane(v, 2 * (i + 1)) for i, v in enumerate(att_sends)]
 
     def att_close_body(gains, own, *refs):
-        parts, (out_q, out_p, out_g) = refs[: len(att_got)], refs[len(att_got) :]
+        parts, (out_q, out_p, *out_g) = refs[: len(att_got)], refs[len(att_got) :]
         for k, ref in enumerate((out_q, out_p)):
             total = own[k]
             for p in parts:
                 total = total + p[k, :blk].astype(f32)
             ref[...] = total
-        out_g[...] = gains[...] + sum(read_gains(p, blk) for p in parts)
-
-    grad_query, grad_pairs, packed = whole_call(
+        total = gains[...] + sum(read_gains(p, blk) for p in parts)
+        out_g[0][...] = total[:N]
+        out_g[1][...] = total[N : 2 * N]
+        out_g[2][...] = total[2 * N : 2 * N + 1, :hw]
+        out_g[3][...] = total[2 * N + 1 : 2 * N + 2, :hw]
+
+    grad_query, grad_pairs, *gain_sums = whole_call(
         att_close_body,
-        [sds((blk, C), f32)] * 2 + [sds((G, blk), f32)],
+        [sds((blk, C), f32)] * 2 + [sds((N, blk), f32)] * 2 + [sds((1, hw), f32)] * 2,
         (plane_gains, att_own, *att_got),
         blk * C * 8,
         scalars=False,
@@ -774,7 +791,7 @@
         block_body, [sds((R, W), bf16)], (where, *ffn_pieces, resid), R * W * 8
     )
 
-    grad_gate, grad_up, grad_down = close_sum(ffn_own, ffn_got, 1)
+    grad_gate, grad_up, grad_down = close_sum(ffn_own, ffn_got)
 
     def end_body(*refs):
         s_ref, rest = refs[0], refs[1:]
@@ -794,10 +811,11 @@
                 dst = src
             gt[:, dst] = total[:, src]
 
-    gna_pieces, packed, grad_down, grad_output, grad_query, block_out = (
-        lax.optimization_barrier(
-            (gna_pieces, packed, grad_down, grad_output, grad_query, block_out)
-        )
+    gain_sums = [gain_sums[0].reshape(W), gain_sums[1].reshape(W)] + [
+        v.reshape(hw) for v in gain_sums[2:]
+    ]
+    gna_pieces, gain_sums, grad_down, grad_output, block_out = lax.optimization_barrier(
+        (gna_pieces, gain_sums, grad_down, grad_output, block_out)
     )
     (grad_tokens,) = whole_call(
         end_body, [sds((R, W), f32)], (where, *gna_pieces, tok, grad_resid, gain2), R * W * 16
@@ -810,20 +828,17 @@
         ).reshape(R, W)
         grad_tokens, block_out = back_cols(grad_tokens), back_cols(block_out)
 
-    lse_out = jnp.take(
-        lse.reshape(QH, NT, R), z ^ jnp.arange(NT, dtype=jnp.int32), axis=1
-    ).reshape(1, QH, B)
     return (
         block_out[None],
         grad_tokens[None],
         lse_out,
-        packed[:N].reshape(W),
+        gain_sums[0],
         grad_query,
         grad_pairs,
-        packed[2 * N, :hw],
-        packed[2 * N + 1, :hw],
+        gain_sums[2],
+        gain_sums[3],
         grad_output,
-        packed[N : 2 * N].reshape(W),
+        gain_sums[1],
         grad_gate,
         grad_up,
         grad_down,

time: 413 us -> 394 us (0.954)
  starting transfers between devices: 112 us -> 78.5 us
  waiting for transfers between devices: 166 us -> 178 us
    ppermute x24, starting transfers between devices: 35.9 us -> 19.4 us  [plane(): return lax.ppermute(v, ('dp', 'ctx'), [(i, i ^ mask) for i in range(N)])]
    ppermute x33, starting transfers between devices: 66.4 us -> 51.6 us  [column(): return lax.ppermute(v, 'tp', [(i, i ^ mask) for i in range(NT)])]
    ppermute x4, waiting for transfers between devices: 3.63 us -> 16.7 us  [along(): return lax.ppermute(v, 'ctx', pairs)]
    ppermute x33, waiting for transfers between devices: 73 us -> 78 us  [column(): return lax.ppermute(v, 'tp', [(i, i ^ mask) for i in range(NT)])]
    ppermute x24, waiting for transfers between devices: 87.3 us -> 82.9 us  [plane(): return lax.ppermute(v, ('dp', 'ctx'), [(i, i ^ mask) for i in range(N)])]
    pallas_call x0 -> x1, Pallas kernels: none -> 4.22 us  [close_sum(): pl.pallas_call(body, grid=(cols // part,), out_shape=[sds((m, cols), f32)...]
    pallas_call x16 -> x15, Pallas kernels: 55.6 us -> 52 us  [whole_call(): pl.pallas_call(body, out_shape=list(outs), in_specs=specs, out_specs=[VM]...]
    unnamed x79 -> x73, local copies, waits for them, and re-layouts: 14 us -> 15.3 us
  transfers between devices with their start and end apart: 62 -> 62, of which waited for: 22 -> 23; matrix products, arithmetic and copies ran while one was open for 5% -> 7% of each run, Pallas kernels for 16% -> 15%
where the time goes in v8:
time: 394 us; the launch traced here: 387 us
  waiting for transfers between devices  178 us (45%)
  Pallas kernels  92.3 us (23%)
  starting transfers between devices  78.5 us (20%)
  local copies, waits for them, and re-layouts  25.8 us (7%)
  other arithmetic  11.2 us (3%)
    ppermute x24, waiting for transfers between devices, plane(): return lax.ppermute(v, ('dp', 'ctx'), [(i, i ^ mask) for i in range(N)])  82.9 us
    ppermute x33, waiting for transfers between devices, column(): return lax.ppermute(v, 'tp', [(i, i ^ mask) for i in range(NT)])  78 us
    pallas_call x15, Pallas kernels, whole_call(): pl.pallas_call(body, out_shape=list(outs), in_specs=specs, out_specs=[VM]...  52 us
    ppermute x33, starting transfers between devices, column(): return lax.ppermute(v, 'tp', [(i, i ^ mask) for i in range(NT)])  51.6 us
    ppermute x24, starting transfers between devices, plane(): return lax.ppermute(v, ('dp', 'ctx'), [(i, i ^ mask) for i in range(N)])  19.4 us
    ppermute x4, waiting for transfers between devices, along(): return lax.ppermute(v, 'ctx', pairs)  16.7 us
    unnamed x73, local copies, waits for them, and re-layouts  15.3 us
    pallas_call x2, Pallas kernels, half_weights(): pl.pallas_call(functools.partial(dw_body, cols), grid=(3,), out_shape=out...  14.8 us
  transfers between devices with their start and end apart: 62, of which 23 were waited for; matrix products, arithmetic and copies ran while one was open for 7% of the time, Pallas kernels for 15%

profile of v8, /device:TPU:0, one launch (start us, length us, event | category | flops | bytes accessed | tf_op | source)
XLA Modules:
  0.0 386.6 jit_solution(11738992853900419895)
XLA Ops:
  6.6 3.0 collective-permute-start.23
  12.5 17.9 %collective-permute-done.23 = bf16[3,128,1152]{2,1,0:T(8,128)(2,1)S(1)} collective-permute-done((bf16[3,128,1152]{2,1,0:T(8,128)(2,1)}, bf16[3,128,1152]{2,1,0:T(8,128)(2,1)S(1)}, u32[]{:S(2)}, u32[]{:S(2)}) %collective-permute-start.23) | collective-permute-done | bytes 884768 | tf_op jit(solution)/shard_map/ppermute | solution.py:97
  30.5 19.4 %collective-permute-done.24 = bf16[3,128,1152]{2,1,0:T(8,128)(2,1)S(1)} collective-permute-done((bf16[3,128,1152]{2,1,0:T(8,128)(2,1)}, bf16[3,128,1152]{2,1,0:T(8,128)(2,1)S(1)}, u32[]{:S(2)}, u32[]{:S(2)}) %collective-permute-start.24) | collective-permute-done | bytes 884768 | tf_op jit(solution)/shard_map/ppermute | solution.py:97
  50.3 3.7 collective-permute-start.15
  75.6 4.5 %collective-permute-done.2.refs_3_.refs_4_ = bf16[128,1024]{1,0:T(8,128)(2,1)} collective-permute-done((bf16[128,1024]{1,0:T(8,128)(2,1)}, bf16[128,1024]{1,0:T(8,128)(2,1)}, u32[]{:S(2)}, u32[]{:S(2)}) %collective-permute-start.2) | collective-permute-done | bytes 262176 | tf_op jit(solution)/shard_map/ppermute | solution.py:100
  81.0 14.3 %collective-permute-done.1.refs_2_.refs_3_ = bf16[128,1024]{1,0:T(8,128)(2,1)} collective-permute-done((bf16[128,1024]{1,0:T(8,128)(2,1)}, bf16[128,1024]{1,0:T(8,128)(2,1)}, u32[]{:S(2)}, u32[]{:S(2)}) %collective-permute-start.1) | collective-permute-done | bytes 262176 | tf_op jit(solution)/shard_map/ppermute | solution.py:100
  104.1 4.5 %shard_map.220 = (bf16[512,256]{1,0:T(8,128)(2,1)}, bf16[512,256]{1,0:T(8,128)(2,1)}, f32[512,256]{1,0:T(8,128)}, f32[512,256]{1,0:T(8,128)}) custom-call(bf16[128,1024]{1,0:T(8,128)(2,1)} %get-tuple-element.109.refs_0_.refs_1_, bf16[128,1024]{1,0:T(8,128)(2,1)} %collective-permute-done.refs_1_.refs_2_, ...), custom_call_target="tpu_custom_call" | custom-call | flops 536870912 | bytes 4720640 | tf_op jit(solution)/shard_map/pallas_call | solution.py:48
  122.1 4.7 %attention_forward.1 = (bf16[128,256]{1,0:T(8,128)(2,1)}, bf16[128,256]{1,0:T(8,128)(2,1)}, bf16[128,256]{1,0:T(8,128)(2,1)}, bf16[128,256]{1,0:T(8,128)(2,1)}, ...) custom-call(s32[3]{0:T(128)} %pad_add_fusion.s_ref.refs_0_, bf16[512,256]{1,0:T(8,128)(2,1)} %get-tuple-element.111.q_ref, ...), custom_call_target="tpu_custom_call" | custom-call | flops 2147483648 | bytes 1048576 | tf_op jit(solution)/shard_map/attention_forward/pallas_call | solution.py:327
  128.2 4.6 %collective-permute-done.10.refs_1_ = bf16[128,256]{1,0:T(8,128)(2,1)} collective-permute-done((bf16[128,256]{1,0:T(8,128)(2,1)}, bf16[128,256]{1,0:T(8,128)(2,1)}, u32[]{:S(2)}, u32[]{:S(2)}) %collective-permute-start.10) | collective-permute-done | bytes 65568 | tf_op jit(solution)/shard_map/ppermute | solution.py:100
  135.6 9.6 %collective-permute-done.11.refs_2_ = bf16[128,256]{1,0:T(8,128)(2,1)} collective-permute-done((bf16[128,256]{1,0:T(8,128)(2,1)}, bf16[128,256]{1,0:T(8,128)(2,1)}, u32[]{:S(2)}, u32[]{:S(2)}) %collective-permute-start.11) | collective-permute-done | bytes 65568 | tf_op jit(solution)/shard_map/ppermute | solution.py:100
  145.7 6.6 %collective-permute-done.12.refs_3_ = bf16[128,256]{1,0:T(8,128)(2,1)} collective-permute-done((bf16[128,256]{1,0:T(8,128)(2,1)}, bf16[128,256]{1,0:T(8,128)(2,1)}, u32[]{:S(2)}, u32[]{:S(2)}) %collective-permute-start.12) | collective-permute-done | bytes 65568 | tf_op jit(solution)/shard_map/ppermute | solution.py:100
  154.3 3.4 shard_map.221
  157.7 3.5 collective-permute-start.21
  163.3 4.9 %hidden_back.1.refs_6_ = f32[512,1152]{1,0:T(8,128)} custom-call(bf16[128,1024]{1,0:T(8,128)(2,1)} %get-tuple-element.124.refs_0_.refs_4_.refs_5_, bf16[128,1024]{1,0:T(8,128)(2,1)} %collective-permute-done.27.refs_1_.refs_5_, bf16[128,1024]{1,0:T(8,128)(2,1)} %collective-permute-done.28.refs_2_.refs_6_, ...), custom_call_target="tpu_custom_call" | custom-call | flops 1207959552 | bytes 5898240 | tf_op jit(solution)/shard_map/hidden_back/pallas_call | solution.py:374
  169.0 10.8 %collective-permute-done.21.refs_2_ = bf16[128,1024]{1,0:T(8,128)(2,1)} collective-permute-done((bf16[128,1024]{1,0:T(8,128)(2,1)}, bf16[128,1024]{1,0:T(8,128)(2,1)}, u32[]{:S(2)}, u32[]{:S(2)}) %collective-permute-start.21) | collective-permute-done | bytes 262176 | tf_op jit(solution)/shard_map/ppermute | solution.py:100
  179.8 10.8 %shard_map.222 = (bf16[3,512,1152]{2,1,0:T(8,128)(2,1)}, bf16[128,1024]{1,0:T(8,128)(2,1)}, bf16[128,1024]{1,0:T(8,128)(2,1)}, bf16[128,1024]{1,0:T(8,128)(2,1)}, bf16[128,1024]{1,0:T(8,128)(2,1)}) custom-call(bf16[128,1024]{1,0:T(8,128)(2,1)} %get-tuple-element.122.refs_0_, bf16[128,1024]{1,0:T(8,128)(2,1)} %collective-permute-done.20.refs_1_, ...), custom_call_target="tpu_custom_call" | custom-call | flops 4831838208 | bytes 15073280 | tf_op jit(solution)/shard_map/pallas_call | solution.py:48
  190.6 6.8 %shard_map.223 = bf16[3,512,1152]{2,1,0:T(8,128)(2,1)} custom-call(bf16[128,1024]{1,0:T(8,128)(2,1)} %get-tuple-element.122.refs_0_, bf16[128,1024]{1,0:T(8,128)(2,1)} %collective-permute-done.20.refs_1_, bf16[128,1024]{1,0:T(8,128)(2,1)} %collective-permute-done.21.refs_2_, bf16[128,1024]{1,0:T(8,128)(2,1)} %collective-permute-done.22.refs_3_, ...), custom_call_target="tpu_custom_call" | custom-call | flops 1811939328 | bytes 7077888 | tf_op jit(solution)/shard_map/pallas_call | solution.py:440
  201.8 4.4 %ffn_out.1 = (bf16[128,1024]{1,0:T(8,128)(2,1)}, bf16[128,1024]{1,0:T(8,128)(2,1)}, bf16[128,1024]{1,0:T(8,128)(2,1)}, bf16[128,1024]{1,0:T(8,128)(2,1)}) custom-call(bf16[3,512,1152]{2,1,0:T(8,128)(2,1)} %get-tuple-element.135.refs_8_.h_ref, bf16[3,512,1152]{2,1,0:T(8,128)(2,1)} %copy-done, bf16[3,512,1152]{2,1,0:T(8,128)(2,1)} %collective-permute-done.26.refs_5_.wo), custom_call_target="tpu_custom_call" | custom-call | flops 1207959552 | bytes 3538944 | tf_op jit(solution)/shard_map/ffn_out/pallas_call | solution.py:462
  207.9 8.1 %shard_map.224 = (f32[3,128,1152]{2,1,0:T(8,128)}, bf16[3,128,1152]{2,1,0:T(8,128)(2,1)}, bf16[3,128,1152]{2,1,0:T(8,128)(2,1)}, bf16[3,128,1152]{2,1,0:T(8,128)(2,1)}) custom-call(bf16[128,1024]{1,0:T(8,128)(2,1)} %get-tuple-element.122.refs_0_, bf16[128,1024]{1,0:T(8,128)(2,1)} %collective-permute-done.20.refs_1_, ...), custom_call_target="tpu_custom_call" | custom-call | flops 1811939328 | bytes 7077888 | tf_op jit(solution)/shard_map/pallas_call | solution.py:440
  216.0 3.1 collective-permute-done.31.refs_2_
  219.1 3.6 shard_map.225
  222.7 5.6 %collective-permute-start.34 = (bf16[128,256]{1,0:T(8,128)(2,1)}, bf16[128,256]{1,0:T(8,128)(2,1)S(1)}, u32[]{:S(2)}, u32[]{:S(2)}) collective-permute-start(bf16[128,256]{1,0:T(8,128)(2,1)} %get-tuple-element.146), channel_id=1, source_target_pairs={{0,1},{1,0},{2,3},{3,2},{4,5},{5,4},{6,7},{7,6},{8,9},{9,8},{10,11... | collective-permute-start | bytes 196616 | tf_op jit(solution)/shard_map/ppermute | solution.py:100
  230.8 5.2 %collective-permute-done.35.refs_2_ = bf16[128,256]{1,0:T(8,128)(2,1)S(1)} collective-permute-done((bf16[128,256]{1,0:T(8,128)(2,1)}, bf16[128,256]{1,0:T(8,128)(2,1)S(1)}, u32[]{:S(2)}, u32[]{:S(2)}) %collective-permute-start.35) | collective-permute-done | bytes 65568 | tf_op jit(solution)/shard_map/ppermute | solution.py:100
  236.7 7.2 %attention_backward.1 = (f32[512,256]{1,0:T(8,128)}, bf16[2,512,256]{2,1,0:T(8,128)(2,1)}, bf16[2,512,256]{2,1,0:T(8,128)(2,1)}) custom-call(s32[3]{0:T(128)} %pad_add_fusion.s_ref.refs_0_, bf16[512,256]{1,0:T(8,128)(2,1)} %get-tuple-element.111.q_ref, bf16[512,256]{1,0:T(8,128)(2,1)} %get-tuple-element.113.a_ref, f32[4,1,512]{2,1,0:T(1,128)} %get-tuple-element.114.l_ref, ...), custom_call_target="tpu_custom_call" | custom-call | flops 5368709120 | bytes 2097152 | tf_op jit(solution)/shard_map/attention_backward/pallas_call | solution.py:599
  252.1 16.1 %collective-permute-done.38.refs_0_ = bf16[512,256]{1,0:T(8,128)(2,1)S(1)} collective-permute-done((bf16[512,256]{1,0:T(8,128)(2,1)S(1)}, bf16[512,256]{1,0:T(8,128)(2,1)S(1)}, u32[]{:S(2)}, u32[]{:S(2)}) %collective-permute-start.38) | collective-permute-done | bytes 262176 | tf_op jit(solution)/shard_map/ppermute | solution.py:104
  268.9 6.3 %shard_map.226 = (bf16[128,1024]{1,0:T(8,128)(2,1)}, bf16[128,1024]{1,0:T(8,128)(2,1)}, bf16[128,1024]{1,0:T(8,128)(2,1)}, bf16[128,1024]{1,0:T(8,128)(2,1)}, bf...) custom-call(s32[3]{0:T(128)} %pad_add_fusion.s_ref.refs_0_, f32[512,256]{1,0:T(8,128)} %get-tuple-element.149.dq, ...), custom_call_target="tpu_custom_call" | custom-call | flops 536870912 | bytes 7628812 | tf_op jit(solution)/shard_map/pallas_call | solution.py:48
  294.1 33.3 %collective-permute-done.53.refs_0_ = bf16[1,128,1024]{2,1,0:T(8,128)(2,1)S(1)} collective-permute-done((bf16[1,128,1024]{2,1,0:T(8,128)(2,1)}, bf16[1,128,1024]{2,1,0:T(8,128)(2,1)S(1)}, u32[]{:S(2)}, u32[]{:S(2)}) %collective-permute-start.53) | collective-permute-done | bytes 262176 | tf_op jit(solution)/shard_map/ppermute | solution.py:97
  329.0 5.1 %collective-permute-done.54.refs_1_ = bf16[1,128,1024]{2,1,0:T(8,128)(2,1)S(1)} collective-permute-done((bf16[1,128,1024]{2,1,0:T(8,128)(2,1)}, bf16[1,128,1024]{2,1,0:T(8,128)(2,1)S(1)}, u32[]{:S(2)}, u32[]{:S(2)}) %collective-permute-start.54) | collective-permute-done | bytes 262176 | tf_op jit(solution)/shard_map/ppermute | solution.py:97
  339.4 3.0 collective-permute-done.55.refs_2_
  350.7 4.1 %collective-permute-start.41 = (bf16[128,1024]{1,0:T(8,128)(2,1)}, bf16[128,1024]{1,0:T(8,128)(2,1)S(1)}, u32[]{:S(2)}, u32[]{:S(2)}) collective-permute-start(bf16[128,1024]{1,0:T(8,128)(2,1)} %get-tuple-element.158), channel_id=1, source_target_pairs={{0,3},{1,2},{2,1},{3,0},{4,7},{5,6},{6,5},{7,4},{8,11},{9,10},{10,... | collective-permute-start | bytes 786440 | tf_op jit(solution)/shard_map/ppermute | solution.py:100
  355.9 13.7 %collective-permute-done.58.refs_3_ = bf16[128,256]{1,0:T(8,128)(2,1)S(1)} collective-permute-done((bf16[128,256]{1,0:T(8,128)(2,1)}, bf16[128,256]{1,0:T(8,128)(2,1)S(1)}, u32[]{:S(2)}, u32[]{:S(2)}) %collective-permute-start.58) | collective-permute-done | bytes 65568 | tf_op jit(solution)/shard_map/ppermute | solution.py:100
  374.5 4.2 %shard_map.230 = (f32[128,1152]{1,0:T(8,128)}, f32[128,1152]{1,0:T(8,128)}, f32[1152,128]{1,0:T(8,128)}) custom-call(f32[3,128,1152]{2,1,0:T(8,128)} %get-tuple-element.170.first, bf16[3,128,1152]{2,1,0:T(8,128)(2,1)} %copy-done.4, bf16[3,128,1152]{2,1,0:T(8,128)(2,1)} %copy-done.5, bf16[3,128,1152]{2,1,0:T(8,128)(2,1)} %collective-permute-done.51.refs_2_), custom_call_target="tpu_custom_call" | custom-call | flops 3538944 | bytes 6193152 | tf_op jit(solution)/shard_map/pallas_call | solution.py:138
  (214 shorter events, 129.6 us)
Async XLA Ops:
  6.6 23.7 %collective-permute-start.23 = (bf16[3,128,1152]{2,1,0:T(8,128)(2,1)}, bf16[3,128,1152]{2,1,0:T(8,128)(2,1)S(1)}, u32[]{:S(2)}, u32[]{:S(2)}) collective-permute-start(bf16[3,128,1152]{2,1,0:T(8,128)(2,1)} %pad_maximum_fusion.1), channel_id=1, source_target_pairs={{0,8},{4,12},{8,0},{12,4},{16,24},{20,28},{24,16},{28,20},{1,9},{5... | collective-permute-start | bytes 2654216 | tf_op jit(solution)/shard_map/ppermute | solution.py:97
  9.6 40.3 %collective-permute-start.24 = (bf16[3,128,1152]{2,1,0:T(8,128)(2,1)}, bf16[3,128,1152]{2,1,0:T(8,128)(2,1)S(1)}, u32[]{:S(2)}, u32[]{:S(2)}) collective-permute-start(bf16[3,128,1152]{2,1,0:T(8,128)(2,1)} %pad_maximum_fusion.1), channel_id=1, source_target_pairs={{0,16},{4,20},{8,24},{12,28},{16,0},{20,4},{24,8},{28,12},{1,17},{... | collective-permute-start | bytes 2654216 | tf_op jit(solution)/shard_map/ppermute | solution.py:97
  11.2 38.9 %collective-permute-start.25 = (bf16[3,128,1152]{2,1,0:T(8,128)(2,1)}, bf16[3,128,1152]{2,1,0:T(8,128)(2,1)S(1)}, u32[]{:S(2)}, u32[]{:S(2)}) collective-permute-start(bf16[3,128,1152]{2,1,0:T(8,128)(2,1)} %pad_maximum_fusion.1), channel_id=1, source_target_pairs={{0,24},{4,28},{8,16},{12,20},{16,8},{20,12},{24,0},{28,4},{1,25},{... | collective-permute-start | bytes 2654216 | tf_op jit(solution)/shard_map/ppermute | solution.py:97
  50.2 113.1 %collective-permute-start.26 = (bf16[3,512,1152]{2,1,0:T(8,128)(2,1)S(1)}, bf16[3,512,1152]{2,1,0:T(8,128)(2,1)}, u32[]{:S(2)}, u32[]{:S(2)}) collective-permute-start(bf16[3,512,1152]{2,1,0:T(8,128)(2,1)S(1)} %constant_dynamic-update-slice_fusion.4.refs_4_.wm), channel_id=1, source_target_pairs={{0,4},{4,0},{8,12},{12,8},{16,20},{20,16},{24,28},{28,24},{1,5},{5... | collective-permute-start | bytes 10616840 | tf_op jit(solution)/shard_map/ppermute | solution.py:97
  50.3 18.2 %collective-permute-start.15 = (bf16[128,256]{1,0:T(8,128)(2,1)}, bf16[128,256]{1,0:T(8,128)(2,1)}, u32[]{:S(2)}, u32[]{:S(2)}) collective-permute-start(bf16[128,256]{1,0:T(8,128)(2,1)} %get-tuple-element.119), channel_id=1, source_target_pairs={{0,3},{1,2},{2,1},{3,0},{4,7},{5,6},{6,5},{7,4},{8,11},{9,10},{10,... | collective-permute-start | bytes 196616 | tf_op jit(solution)/shard_map/ppermute | solution.py:100
  53.9 16.8 %collective-permute-start.14 = (bf16[128,256]{1,0:T(8,128)(2,1)}, bf16[128,256]{1,0:T(8,128)(2,1)}, u32[]{:S(2)}, u32[]{:S(2)}) collective-permute-start(bf16[128,256]{1,0:T(8,128)(2,1)} %get-tuple-element.119), channel_id=1, source_target_pairs={{0,2},{1,3},{2,0},{3,1},{4,6},{5,7},{6,4},{7,5},{8,10},{9,11},{10,... | collective-permute-start | bytes 196616 | tf_op jit(solution)/shard_map/ppermute | solution.py:100
  68.5 35.1 %collective-permute-start.6 = (bf16[2,512,256]{2,1,0:T(8,128)(2,1)}, bf16[2,512,256]{2,1,0:T(8,128)(2,1)}, u32[]{:S(2)}, u32[]{:S(2)}) collective-permute-start(bf16[2,512,256]{2,1,0:T(8,128)(2,1)} %constant_dynamic-update-slice_fusion.refs_4_.wm), channel_id=1, source_target_pairs={{0,4},{4,0},{8,12},{12,8},{16,20},{20,16},{24,28},{28,24},{1,5},{5... | collective-permute-start | bytes 1572872 | tf_op jit(solution)/shard_map/ppermute | solution.py:97
  70.8 24.6 %collective-permute-start.1 = (bf16[128,1024]{1,0:T(8,128)(2,1)}, bf16[128,1024]{1,0:T(8,128)(2,1)}, u32[]{:S(2)}, u32[]{:S(2)}) collective-permute-start(bf16[128,1024]{1,0:T(8,128)(2,1)} %get-tuple-element.109.refs_0_.refs_1_), channel_id=1, source_target_pairs={{0,2},{1,3},{2,0},{3,1},{4,6},{5,7},{6,4},{7,5},{8,10},{9,11},{10,... | collective-permute-start | bytes 786440 | tf_op jit(solution)/shard_map/ppermute | solution.py:100
  71.3 24.6 %collective-permute-start = (bf16[128,1024]{1,0:T(8,128)(2,1)}, bf16[128,1024]{1,0:T(8,128)(2,1)}, u32[]{:S(2)}, u32[]{:S(2)}) collective-permute-start(bf16[128,1024]{1,0:T(8,128)(2,1)} %get-tuple-element.109.refs_0_.refs_1_), channel_id=1, source_target_pairs={{0,1},{1,0},{2,3},{3,2},{4,5},{5,4},{6,7},{7,6},{8,9},{9,8},{10,11... | collective-permute-start | bytes 786440 | tf_op jit(solution)/shard_map/ppermute | solution.py:100
  80.0 31.5 %collective-permute-start.18 = (bf16[1,128,1024]{2,1,0:T(8,128)(2,1)}, bf16[1,128,1024]{2,1,0:T(8,128)(2,1)}, u32[]{:S(2)}, u32[]{:S(2)}) collective-permute-start(bf16[1,128,1024]{2,1,0:T(8,128)(2,1)} %maximum_bitcast_fusion), channel_id=1, source_target_pairs={{0,24},{4,28},{8,16},{12,20},{16,8},{20,12},{24,0},{28,4},{1,25},{... | collective-permute-start | bytes 786440 | tf_op jit(solution)/shard_map/ppermute | solution.py:97
  95.4 16.2 %collective-permute-start.17 = (bf16[1,128,1024]{2,1,0:T(8,128)(2,1)}, bf16[1,128,1024]{2,1,0:T(8,128)(2,1)}, u32[]{:S(2)}, u32[]{:S(2)}) collective-permute-start(bf16[1,128,1024]{2,1,0:T(8,128)(2,1)} %maximum_bitcast_fusion), channel_id=1, source_target_pairs={{0,16},{4,20},{8,24},{12,28},{16,0},{20,4},{24,8},{28,12},{1,17},{... | collective-permute-start | bytes 786440 | tf_op jit(solution)/shard_map/ppermute | solution.py:97
  113.8 40.5 %collective-permute-start.19 = (bf16[1,512,1024]{2,1,0:T(8,128)(2,1)}, bf16[1,512,1024]{2,1,0:T(8,128)(2,1)}, u32[]{:S(2)}, u32[]{:S(2)}) collective-permute-start(bf16[1,512,1024]{2,1,0:T(8,128)(2,1)} %pad_maximum_fusion.refs_4_.refs_7_), channel_id=1, source_target_pairs={{0,4},{4,0},{8,12},{12,8},{16,20},{20,16},{24,28},{28,24},{1,5},{5... | collective-permute-start | bytes 3145736 | tf_op jit(solution)/shard_map/ppermute | solution.py:97
  118.3 39.4 %collective-permute-start.29 = (bf16[128,1024]{1,0:T(8,128)(2,1)}, bf16[128,1024]{1,0:T(8,128)(2,1)}, u32[]{:S(2)}, u32[]{:S(2)}) collective-permute-start(bf16[128,1024]{1,0:T(8,128)(2,1)} %get-tuple-element.124.refs_0_.refs_4_.refs_5_), channel_id=1, source_target_pairs={{0,3},{1,2},{2,1},{3,0},{4,7},{5,6},{6,5},{7,4},{8,11},{9,10},{10,... | collective-permute-start | bytes 786440 | tf_op jit(solution)/shard_map/ppermute | solution.py:100
  120.7 40.5 %collective-permute-start.28 = (bf16[128,1024]{1,0:T(8,128)(2,1)}, bf16[128,1024]{1,0:T(8,128)(2,1)}, u32[]{:S(2)}, u32[]{:S(2)}) collective-permute-start(bf16[128,1024]{1,0:T(8,128)(2,1)} %get-tuple-element.124.refs_0_.refs_4_.refs_5_), channel_id=1, source_target_pairs={{0,2},{1,3},{2,0},{3,1},{4,6},{5,7},{6,4},{7,5},{8,10},{9,11},{10,... | collective-permute-start | bytes 786440 | tf_op jit(solution)/shard_map/ppermute | solution.py:100
  157.7 22.1 %collective-permute-start.21 = (bf16[128,1024]{1,0:T(8,128)(2,1)}, bf16[128,1024]{1,0:T(8,128)(2,1)}, u32[]{:S(2)}, u32[]{:S(2)}) collective-permute-start(bf16[128,1024]{1,0:T(8,128)(2,1)} %get-tuple-element.122.refs_0_), channel_id=1, source_target_pairs={{0,2},{1,3},{2,0},{3,1},{4,6},{5,7},{6,4},{7,5},{8,10},{9,11},{10,... | collective-permute-start | bytes 786440 | tf_op jit(solution)/shard_map/ppermute | solution.py:100
  161.2 18.6 %collective-permute-start.20 = (bf16[128,1024]{1,0:T(8,128)(2,1)}, bf16[128,1024]{1,0:T(8,128)(2,1)}, u32[]{:S(2)}, u32[]{:S(2)}) collective-permute-start(bf16[128,1024]{1,0:T(8,128)(2,1)} %get-tuple-element.122.refs_0_), channel_id=1, source_target_pairs={{0,1},{1,0},{2,3},{3,2},{4,5},{5,4},{6,7},{7,6},{8,9},{9,8},{10,11... | collective-permute-start | bytes 786440 | tf_op jit(solution)/shard_map/ppermute | solution.py:100
  197.4 18.7 %collective-permute-start.30 = (bf16[128,1024]{1,0:T(8,128)(2,1)}, bf16[128,1024]{1,0:T(8,128)(2,1)}, u32[]{:S(2)}, u32[]{:S(2)}) collective-permute-start(bf16[128,1024]{1,0:T(8,128)(2,1)} %get-tuple-element.127), channel_id=1, source_target_pairs={{0,1},{1,0},{2,3},{3,2},{4,5},{5,4},{6,7},{7,6},{8,9},{9,8},{10,11... | collective-permute-start | bytes 786440 | tf_op jit(solution)/shard_map/ppermute | solution.py:100
  197.4 21.7 %collective-permute-start.31 = (bf16[128,1024]{1,0:T(8,128)(2,1)}, bf16[128,1024]{1,0:T(8,128)(2,1)}, u32[]{:S(2)}, u32[]{:S(2)}) collective-permute-start(bf16[128,1024]{1,0:T(8,128)(2,1)} %get-tuple-element.128), channel_id=1, source_target_pairs={{0,2},{1,3},{2,0},{3,1},{4,6},{5,7},{6,4},{7,5},{8,10},{9,11},{10,... | collective-permute-start | bytes 786440 | tf_op jit(solution)/shard_map/ppermute | solution.py:100
  199.5 19.6 %collective-permute-start.32 = (bf16[128,1024]{1,0:T(8,128)(2,1)}, bf16[128,1024]{1,0:T(8,128)(2,1)}, u32[]{:S(2)}, u32[]{:S(2)}) collective-permute-start(bf16[128,1024]{1,0:T(8,128)(2,1)} %get-tuple-element.129), channel_id=1, source_target_pairs={{0,3},{1,2},{2,1},{3,0},{4,7},{5,6},{6,5},{7,4},{8,11},{9,10},{10,... | collective-permute-start | bytes 786440 | tf_op jit(solution)/shard_map/ppermute | solution.py:100
  246.6 42.5 %collective-permute-start.52 = (bf16[1,512,1024]{2,1,0:T(8,128)(2,1)}, bf16[1,512,1024]{2,1,0:T(8,128)(2,1)S(1)}, u32[]{:S(2)}, u32[]{:S(2)}) collective-permute-start(bf16[1,512,1024]{2,1,0:T(8,128)(2,1)} %shard_map.231), channel_id=1, source_target_pairs={{0,4},{4,0},{8,12},{12,8},{16,20},{20,16},{24,28},{28,24},{1,5},{5... | collective-permute-start | bytes 3145736 | tf_op jit(solution)/shard_map/ppermute | solution.py:97
  248.0 20.1 %collective-permute-start.38 = (bf16[512,256]{1,0:T(8,128)(2,1)S(1)}, bf16[512,256]{1,0:T(8,128)(2,1)S(1)}, u32[]{:S(2)}, u32[]{:S(2)}) collective-permute-start(bf16[512,256]{1,0:T(8,128)(2,1)S(1)} %fusion), channel_id=1, source_target_pairs={{8,0},{12,4},{9,1},{13,5},{10,2},{14,6},{11,3},{15,7},{24,16},{28,... | collective-permute-start | bytes 786440 | tf_op jit(solution)/shard_map/ppermute | solution.py:104
  249.3 39.8 %collective-permute-start.59 = (bf16[128,1024]{1,0:T(8,128)(2,1)}, bf16[128,1024]{1,0:T(8,128)(2,1)}, u32[]{:S(2)}, u32[]{:S(2)}) collective-permute-start(bf16[128,1024]{1,0:T(8,128)(2,1)} %get-tuple-element.185), channel_id=1, source_target_pairs={{0,1},{1,0},{2,3},{3,2},{4,5},{5,4},{6,7},{7,6},{8,9},{9,8},{10,11... | collective-permute-start | bytes 786440 | tf_op jit(solution)/shard_map/ppermute | solution.py:100
  252.0 41.0 %collective-permute-start.60 = (bf16[128,1024]{1,0:T(8,128)(2,1)}, bf16[128,1024]{1,0:T(8,128)(2,1)}, u32[]{:S(2)}, u32[]{:S(2)}) collective-permute-start(bf16[128,1024]{1,0:T(8,128)(2,1)} %get-tuple-element.186), channel_id=1, source_target_pairs={{0,2},{1,3},{2,0},{3,1},{4,6},{5,7},{6,4},{7,5},{8,10},{9,11},{10,... | collective-permute-start | bytes 786440 | tf_op jit(solution)/shard_map/ppermute | solution.py:100
  282.5 64.3 %collective-permute-start.49 = (bf16[3,128,1152]{2,1,0:T(8,128)(2,1)}, bf16[3,128,1152]{2,1,0:T(8,128)(2,1)S(1)}, u32[]{:S(2)}, u32[]{:S(2)}) collective-permute-start(bf16[3,128,1152]{2,1,0:T(8,128)(2,1)} %get-tuple-element.171), channel_id=1, source_target_pairs={{0,8},{4,12},{8,0},{12,4},{16,24},{20,28},{24,16},{28,20},{1,9},{5... | collective-permute-start | bytes 2654216 | tf_op jit(solution)/shard_map/ppermute | solution.py:97
  284.8 62.9 %collective-permute-start.50 = (bf16[3,128,1152]{2,1,0:T(8,128)(2,1)}, bf16[3,128,1152]{2,1,0:T(8,128)(2,1)S(1)}, u32[]{:S(2)}, u32[]{:S(2)}) collective-permute-start(bf16[3,128,1152]{2,1,0:T(8,128)(2,1)} %get-tuple-element.172), channel_id=1, source_target_pairs={{0,16},{4,20},{8,24},{12,28},{16,0},{20,4},{24,8},{28,12},{1,17},{... | collective-permute-start | bytes 2654216 | tf_op jit(solution)/shard_map/ppermute | solution.py:97
  289.1 46.2 %collective-permute-start.45 = (bf16[2,544,256]{2,1,0:T(8,128)(2,1)}, bf16[2,544,256]{2,1,0:T(8,128)(2,1)}, u32[]{:S(2)}, u32[]{:S(2)}) collective-permute-start(bf16[2,544,256]{2,1,0:T(8,128)(2,1)} %shard_map.227), channel_id=1, source_target_pairs={{0,4},{4,0},{8,12},{12,8},{16,20},{20,16},{24,28},{28,24},{1,5},{5... | collective-permute-start | bytes 1671176 | tf_op jit(solution)/shard_map/ppermute | solution.py:97
  289.1 60.6 %collective-permute-start.51 = (bf16[3,128,1152]{2,1,0:T(8,128)(2,1)}, bf16[3,128,1152]{2,1,0:T(8,128)(2,1)}, u32[]{:S(2)}, u32[]{:S(2)}) collective-permute-start(bf16[3,128,1152]{2,1,0:T(8,128)(2,1)} %get-tuple-element.173), channel_id=1, source_target_pairs={{0,24},{4,28},{8,16},{12,20},{16,8},{20,12},{24,0},{28,4},{1,25},{... | collective-permute-start | bytes 2654216 | tf_op jit(solution)/shard_map/ppermute | solution.py:97
  292.9 34.5 %collective-permute-start.53 = (bf16[1,128,1024]{2,1,0:T(8,128)(2,1)}, bf16[1,128,1024]{2,1,0:T(8,128)(2,1)S(1)}, u32[]{:S(2)}, u32[]{:S(2)}) collective-permute-start(bf16[1,128,1024]{2,1,0:T(8,128)(2,1)} %get-tuple-element.177), channel_id=1, source_target_pairs={{0,8},{4,12},{8,0},{12,4},{16,24},{20,28},{24,16},{28,20},{1,9},{5... | collective-permute-start | bytes 786440 | tf_op jit(solution)/shard_map/ppermute | solution.py:97
  342.3 27.7 %collective-permute-start.46 = (bf16[2,160,256]{2,1,0:T(8,128)(2,1)}, bf16[2,160,256]{2,1,0:T(8,128)(2,1)S(1)}, u32[]{:S(2)}, u32[]{:S(2)}) collective-permute-start(bf16[2,160,256]{2,1,0:T(8,128)(2,1)} %get-tuple-element.163), channel_id=1, source_target_pairs={{0,8},{4,12},{8,0},{12,4},{16,24},{20,28},{24,16},{28,20},{1,9},{5... | collective-permute-start | bytes 491528 | tf_op jit(solution)/shard_map/ppermute | solution.py:97
  347.8 35.3 %collective-permute-start.39 = (bf16[128,1024]{1,0:T(8,128)(2,1)}, bf16[128,1024]{1,0:T(8,128)(2,1)S(1)}, u32[]{:S(2)}, u32[]{:S(2)}) collective-permute-start(bf16[128,1024]{1,0:T(8,128)(2,1)} %get-tuple-element.156), channel_id=1, source_target_pairs={{0,1},{1,0},{2,3},{3,2},{4,5},{5,4},{6,7},{7,6},{8,9},{9,8},{10,11... | collective-permute-start | bytes 786440 | tf_op jit(solution)/shard_map/ppermute | solution.py:100
  349.7 33.3 %collective-permute-start.40 = (bf16[128,1024]{1,0:T(8,128)(2,1)}, bf16[128,1024]{1,0:T(8,128)(2,1)S(1)}, u32[]{:S(2)}, u32[]{:S(2)}) collective-permute-start(bf16[128,1024]{1,0:T(8,128)(2,1)} %get-tuple-element.157), channel_id=1, source_target_pairs={{0,2},{1,3},{2,0},{3,1},{4,6},{5,7},{6,4},{7,5},{8,10},{9,11},{10,... | collective-permute-start | bytes 786440 | tf_op jit(solution)/shard_map/ppermute | solution.py:100
  350.7 32.4 %collective-permute-start.41 = (bf16[128,1024]{1,0:T(8,128)(2,1)}, bf16[128,1024]{1,0:T(8,128)(2,1)S(1)}, u32[]{:S(2)}, u32[]{:S(2)}) collective-permute-start(bf16[128,1024]{1,0:T(8,128)(2,1)} %get-tuple-element.158), channel_id=1, source_target_pairs={{0,3},{1,2},{2,1},{3,0},{4,7},{5,6},{6,5},{7,4},{8,11},{9,10},{10,... | collective-permute-start | bytes 786440 | tf_op jit(solution)/shard_map/ppermute | solution.py:100
  (63 other events, 730.2 us)
